TPU v7x, 32 devices: a whole 2x2x4 slice. The times are simulated.
32 devices in a mesh: tile: 8 (over y, x, core), depth: 4 (over z).
Axes of the slice: x: 2, y: 2, z: 4, core: 2. Of those that a mesh axis runs over, the one named last changes fastest.
Arguments:
- initial_state: float32 [2, 32, 8192], P(None, 'depth', 'tile'), may hold values from -6 to 6
- observed: float32 [2, 32, 8192], P(None, 'depth', 'tile'), may hold values from -6 to 6
- edge_weight: float32 [8192], P('tile'), may hold values from 0.25 to 1
- land: int32 [8192], P('tile'), may hold values 0 or 1
- w_in: bfloat16 [64, 640], replicated, may hold values from -0.75 to 0.75
- b_in: float32 [640], replicated, may hold values from -3 to 3
- w_mid: bfloat16 [640, 640], replicated, may hold values from -0.25 to 0.25
- b_mid: float32 [640], replicated, may hold values from -3 to 3
- w_out: bfloat16 [640, 64], replicated, may hold values from -0.25 to 0.25
- b_out: float32 [64], replicated, may hold values from -3 to 3
Outputs:
- final_state: float32 [2, 32, 8192], P(None, 'depth', 'tile')
- sensitivity: float32 [2, 32, 8192], P(None, 'depth', 'tile')
- grad_w_in: float32 [64, 640], replicated
- grad_b_in: float32 [640], replicated
- grad_w_mid: float32 [640, 640], replicated
- grad_b_mid: float32 [640], replicated
- grad_w_out: float32 [640, 64], replicated
- grad_b_out: float32 [64], replicated
All inputs are finite; a program needn't handle non-finite values. No bound on the sum of `land` on one device may be relied on, other than what follows from the above.
Results may differ from a plain program's by a relative error of at most 0.0017.
Values may be sent and summed in bfloat16 or wider, within the bound.
No kernel may reach another device: no remote copies, remote signals or barrier semaphores. Data moves between devices by JAX's collectives and lax.ppermute only.
A program may use at most 64 MiB of HBM per device.

v0:
```python
import jax
import jax.numpy as jnp
from jax import lax
from jax.sharding import PartitionSpec as P

TILE_SIDE = 32
LEVELS = 32
TIME_STEPS = 2
FEATURES = 64
TILE_CELLS = 1024


diffuse_coef = 0.2
step_size = 0.5


def with_halo(cells, sides, width):
    for axis, dim in sides:
        count = lax.axis_size(axis)
        head = lax.slice_in_dim(cells, 0, width, axis=dim)
        tail = lax.slice_in_dim(cells, cells.shape[dim] - width, cells.shape[dim], axis=dim)
        cells = jnp.concatenate(
            [
                lax.ppermute(tail, axis, [(i, (i + 1) % count) for i in range(count)]),
                cells,
                lax.ppermute(head, axis, [((i + 1) % count, i) for i in range(count)]),
            ],
            axis=dim,
        )
    return cells


def passed_along(x, axis, by):
    length = lax.axis_size(axis)
    return lax.ppermute(x, axis, [(i, (i + by) % length) for i in range(length)])


def neighbour_sum(flat_rows):
    row_count = flat_rows.shape[0]
    tile_grid = flat_rows.reshape(row_count, TILE_SIDE, TILE_SIDE)
    zonal_pair = jnp.stack([tile_grid[:, :, -1], tile_grid[:, :, 0]], axis=1)
    padded = with_halo(zonal_pair[None], (("tile", 0),), 1)
    from_west = padded[0, :, 0, :]
    from_east = padded[2, :, 1, :]
    fold_pair = jnp.stack([tile_grid[:, 0, :], tile_grid[:, -1, :]], axis=1)
    across = passed_along(fold_pair, "tile", lax.axis_size("tile") // 2)[:, :, ::-1]
    west_cells = jnp.concatenate([from_west[:, :, None], tile_grid[:, :, :-1]], axis=2)
    east_cells = jnp.concatenate([tile_grid[:, :, 1:], from_east[:, :, None]], axis=2)
    south_cells = jnp.concatenate([across[:, 0, None, :], tile_grid[:, :-1, :]], axis=1)
    north_cells = jnp.concatenate([tile_grid[:, 1:, :], across[:, 1, None, :]], axis=1)
    return (west_cells + east_cells + south_cells + north_cells).reshape(row_count, TILE_CELLS)


def diffuse(tracer_field, weight, weight_sums):
    flat_rows = tracer_field.reshape(-1, TILE_CELLS)
    scaled = flat_rows * weight[None, :]
    result_rows = weight[None, :] * (neighbour_sum(scaled) - flat_rows * weight_sums[None, :])
    return result_rows.reshape(tracer_field.shape)


def silu_slope(pre_act):
    sigmoid_val = jax.nn.sigmoid(pre_act)
    return sigmoid_val * (1.0 + pre_act * (1.0 - sigmoid_val))


def closure_forward(inputs, params):
    w_in, b_in, w_mid, b_mid, w_out, b_out = params
    contract_rows = (((0,), (0,)), ((), ()))
    pre_one = (
        lax.dot_general(w_in, inputs, contract_rows, preferred_element_type=jnp.float32)
        + b_in[:, None]
    )
    hidden_one = jax.nn.silu(pre_one).astype(jnp.bfloat16)
    pre_two = (
        lax.dot_general(w_mid, hidden_one, contract_rows, preferred_element_type=jnp.float32)
        + b_mid[:, None]
    )
    hidden_two = jax.nn.silu(pre_two).astype(jnp.bfloat16)
    output = (
        lax.dot_general(w_out, hidden_two, contract_rows, preferred_element_type=jnp.float32)
        + b_out[:, None]
    )
    return (output, (inputs, pre_one, hidden_one, pre_two, hidden_two))


def closure_backward(upstream, saved_cache, params):
    w_in, b_in, w_mid, b_mid, w_out, b_out = params
    inputs, pre_one, hidden_one, pre_two, hidden_two = saved_cache
    contract_cols = (((1,), (1,)), ((), ()))
    grad_w_out = lax.dot_general(
        hidden_two, upstream, contract_cols, preferred_element_type=jnp.float32
    )
    grad_b_out = jnp.sum(upstream.astype(jnp.float32), axis=1)
    slope_two = (
        jnp.dot(w_out, upstream, preferred_element_type=jnp.float32) * silu_slope(pre_two)
    ).astype(jnp.bfloat16)
    grad_w_mid = lax.dot_general(
        hidden_one, slope_two, contract_cols, preferred_element_type=jnp.float32
    )
    grad_b_mid = jnp.sum(slope_two.astype(jnp.float32), axis=1)
    slope_one = (
        jnp.dot(w_mid, slope_two, preferred_element_type=jnp.float32) * silu_slope(pre_one)
    ).astype(jnp.bfloat16)
    grad_w_in = lax.dot_general(
        inputs, slope_one, contract_cols, preferred_element_type=jnp.float32
    )
    grad_b_in = jnp.sum(slope_one.astype(jnp.float32), axis=1)
    back_grad = jnp.dot(w_in, slope_one, preferred_element_type=jnp.float32)
    return (back_grad, (grad_w_in, grad_b_in, grad_w_mid, grad_b_mid, grad_w_out, grad_b_out))


def body(initial_state, observed, edge_weight, land, w_in, b_in, w_mid, b_mid, w_out, b_out):
    params = (w_in, b_in, w_mid, b_mid, w_out, b_out)
    ocean_mask = land.astype(jnp.float32)
    weight = edge_weight * ocean_mask
    weight_sums = neighbour_sum(weight[None, :])[0]

    def to_columns(segment):
        full_cols = lax.all_to_all(segment, "depth", split_axis=2, concat_axis=1, tiled=True)
        return full_cols.reshape(FEATURES, full_cols.shape[2])

    def to_segments(values):
        shaped = values.reshape(2, LEVELS, values.shape[1])
        segment_part = lax.all_to_all(shaped, "depth", split_axis=1, concat_axis=2, tiled=True)
        return segment_part

    state_now = initial_state
    caches = []
    for step_index in range(TIME_STEPS):
        inputs = to_columns(state_now.astype(jnp.bfloat16))
        tendency, saved_cache = closure_forward(inputs, params)
        caches.append(saved_cache)
        change = diffuse(state_now, weight, weight_sums)
        state_now = (
            state_now
            + diffuse_coef * change
            + step_size * ocean_mask[None, None, :] * to_segments(tendency)
        )
    adjoint = ocean_mask[None, None, :] * (state_now - observed)
    grad_list = []
    for step_index in reversed(range(TIME_STEPS)):
        upstream = to_columns(
            (step_size * ocean_mask[None, None, :] * adjoint).astype(jnp.bfloat16)
        )
        back_grad, param_grads = closure_backward(upstream, caches[step_index], params)
        grad_list.append(param_grads)
        spread = diffuse(adjoint, weight, weight_sums)
        adjoint = adjoint + diffuse_coef * spread + to_segments(back_grad)
    totals = grad_list[0]
    for param_grads in grad_list[1:]:
        totals = tuple((total + gradient for total, gradient in zip(totals, param_grads)))
    summed = lax.psum(totals, ("tile", "depth"))
    grad_scale = 1.0 / (lax.axis_size("tile") * TILE_CELLS)
    return (
        state_now,
        adjoint,
        summed[0] * grad_scale,
        summed[1] * grad_scale,
        summed[2] * grad_scale,
        summed[3] * grad_scale,
        summed[4] * grad_scale,
        summed[5] * grad_scale,
    )


def solution(mesh):
    return jax.shard_map(
        body,
        mesh=mesh,
        in_specs=(
            P(None, "depth", "tile"),
            P(None, "depth", "tile"),
            P("tile"),
            P("tile"),
            P(),
            P(),
            P(),
            P(),
            P(),
            P(),
        ),
        out_specs=(
            P(None, "depth", "tile"),
            P(None, "depth", "tile"),
            P(),
            P(),
            P(),
            P(),
            P(),
            P(),
        ),
        check_vma=False,
    )
```

profile of v0, /device:TPU:0, one launch (start us, length us, event | category | flops | bytes accessed | tf_op | source)
XLA Modules:
  0.0 276.7 jit_solution(8364587519596231876)
XLA Ops:
  8.2 3.4 %collective-permute-start.4 = (f32[1,1,2,32]{3,2,1,0:T(2,128)S(1)}, f32[1,1,2,32]{3,2,1,0:T(2,128)S(1)}, u32[]{:S(2)}, u32[]{:S(2)}) collective-permute-start(f32[1,1,2,32]{3,2,1,0:T(2,128)S(1)} %maximum_bitcast_fusion.4), channel_id=1, source_target_pairs={{4,0},{8,4},{12,8},{16,12},{20,16},{24,20},{28,24},{0,28},{5,1},{9... | collective-permute-start | bytes 776 | tf_op jit(solution)/shard_map/ppermute | solution.py:26
  11.7 1.0 reshape.230
  13.0 2.7 collective-permute-start.1
  17.5 1.1 reshape.252
  18.7 4.9 %all-to-all-start = ((bf16[4,2,2048]{2,1,0:T(2,128)(2,1)}), bf16[4,2,2048]{2,1,0:T(2,128)(2,1)S(1)}, u32[]{:S(2)}, u32[]{:S(2)}) async-start(bf16[4,2,2048]{2,1,0:T(2,128)(2,1)} %reshape.252), calls=%async_computation | async-start | bytes 65536 | tf_op jit(solution)/shard_map/all_to_all | solution.py:119
  25.2 1.5 collective-permute-start.2
  27.2 1.7 collective-permute-done.2
  32.7 1.3 multiply_convert_fusion.2
  35.0 5.1 %all-to-all-start.1 = ((f32[2,32,256]{2,0,1:T(2,128)}), f32[2,32,256]{2,0,1:T(2,128)}, u32[]{:S(2)}, u32[]{:S(2)}) async-start(f32[2,32,256]{2,0,1:T(2,128)} %copy.161), calls=%async_computation.1 | async-start | bytes 131072 | tf_op jit(solution)/shard_map/all_to_all | solution.py:124
  40.0 1.2 fusion.13
  41.3 4.5 %all-to-all-done.1 = f32[2,32,256]{2,0,1:T(2,128)} async-done(((f32[2,32,256]{2,0,1:T(2,128)}), f32[2,32,256]{2,0,1:T(2,128)}, u32[]{:S(2)}, u32[]{:S(2)}) %all-to-all-start.1) | async-done | bytes 65568 | tf_op jit(solution)/shard_map/all_to_all | solution.py:124
  48.7 1.6 collective-permute-start.8
  51.5 1.1 reshape.254
  52.6 3.3 %all-to-all-start.2 = ((bf16[4,2,2048]{2,1,0:T(2,128)(2,1)}), bf16[4,2,2048]{2,1,0:T(2,128)(2,1)S(1)}, u32[]{:S(2)}, u32[]{:S(2)}) async-start(bf16[4,2,2048]{2,1,0:T(2,128)(2,1)} %reshape.254), calls=%async_computation.2 | async-start | bytes 65536 | tf_op jit(solution)/shard_map/all_to_all | solution.py:119
  57.7 3.8 %all-to-all-done.2 = bf16[4,2,2048]{2,1,0:T(2,128)(2,1)S(1)} async-done(((bf16[4,2,2048]{2,1,0:T(2,128)(2,1)}), bf16[4,2,2048]{2,1,0:T(2,128)(2,1)S(1)}, u32[]{:S(2)}, u32[]{:S(2)}) %all-to-all-start.2) | async-done | bytes 32800 | tf_op jit(solution)/shard_map/all_to_all | solution.py:119
  63.4 2.3 multiply_convert_fusion
  66.6 3.9 %all-to-all-start.3 = ((f32[2,32,256]{2,0,1:T(2,128)}), f32[2,32,256]{2,0,1:T(2,128)}, u32[]{:S(2)}, u32[]{:S(2)}) async-start(f32[2,32,256]{2,0,1:T(2,128)} %copy.168), calls=%async_computation.3 | async-start | bytes 131072 | tf_op jit(solution)/shard_map/all_to_all | solution.py:124
  70.5 1.3 fusion.15
  72.0 4.4 %all-to-all-done.3 = f32[2,32,256]{2,0,1:T(2,128)} async-done(((f32[2,32,256]{2,0,1:T(2,128)}), f32[2,32,256]{2,0,1:T(2,128)}, u32[]{:S(2)}, u32[]{:S(2)}) %all-to-all-start.3) | async-done | bytes 65568 | tf_op jit(solution)/shard_map/all_to_all | solution.py:124
  77.2 1.5 multiply_convert_fusion.5
  81.8 1.1 reshape.256
  82.9 4.0 %all-to-all-start.4 = ((bf16[4,2,2048]{2,1,0:T(2,128)(2,1)}), bf16[4,2,2048]{2,1,0:T(2,128)(2,1)}, u32[]{:S(2)}, u32[]{:S(2)}) async-start(bf16[4,2,2048]{2,1,0:T(2,128)(2,1)} %reshape.256), calls=%async_computation.4 | async-start | bytes 65536 | tf_op jit(solution)/shard_map/all_to_all | solution.py:119
  88.8 1.3 fusion.17
  90.2 2.3 all-to-all-done.4
  92.5 1.4 reshape.257
  94.2 0.9 fusion.47
  95.1 1.5 convert_reduce_fusion.1
  96.6 1.1 convert_reduce_fusion.3
  97.7 1.7 fusion.22
  100.3 3.3 %all-to-all-start.5 = ((f32[2,32,256]{2,0,1:T(2,128)}), f32[2,32,256]{2,0,1:T(2,128)S(1)}, u32[]{:S(2)}, u32[]{:S(2)}) async-start(f32[2,32,256]{2,0,1:T(2,128)} %copy.175), calls=%async_computation.5 | async-start | bytes 131072 | tf_op jit(solution)/shard_map/all_to_all | solution.py:124
  103.6 0.9 fusion.46
  104.5 4.8 %all-to-all-done.5 = f32[2,32,256]{2,0,1:T(2,128)S(1)} async-done(((f32[2,32,256]{2,0,1:T(2,128)}), f32[2,32,256]{2,0,1:T(2,128)S(1)}, u32[]{:S(2)}, u32[]{:S(2)}) %all-to-all-start.5) | async-done | bytes 65568 | tf_op jit(solution)/shard_map/all_to_all | solution.py:124
  110.6 1.6 collective-permute-start.14
  113.3 1.1 reshape.258
  114.4 3.9 %all-to-all-start.6 = ((bf16[4,2,2048]{2,1,0:T(2,128)(2,1)}), bf16[4,2,2048]{2,1,0:T(2,128)(2,1)}, u32[]{:S(2)}, u32[]{:S(2)}) async-start(bf16[4,2,2048]{2,1,0:T(2,128)(2,1)} %reshape.258), calls=%async_computation.6 | async-start | bytes 65536 | tf_op jit(solution)/shard_map/all_to_all | solution.py:119
  119.0 1.2 fusion.19
  120.3 3.7 %all-to-all-done.6 = bf16[4,2,2048]{2,1,0:T(2,128)(2,1)} async-done(((bf16[4,2,2048]{2,1,0:T(2,128)(2,1)}), bf16[4,2,2048]{2,1,0:T(2,128)(2,1)}, u32[]{:S(2)}, u32[]{:S(2)}) %all-to-all-start.6) | async-done | bytes 32800 | tf_op jit(solution)/shard_map/all_to_all | solution.py:119
  124.0 1.4 reshape.259
  125.8 1.8 convolution_add_fusion.5
  127.6 1.5 convert_reduce_fusion
  130.0 0.9 fusion.11
  130.8 1.7 convolution_add_fusion
  134.3 3.3 %all-to-all-start.7 = ((f32[2,32,256]{2,0,1:T(2,128)}), f32[2,32,256]{2,0,1:T(2,128)S(1)}, u32[]{:S(2)}, u32[]{:S(2)}) async-start(f32[2,32,256]{2,0,1:T(2,128)} %copy.182), calls=%async_computation.7 | async-start | bytes 131072 | tf_op jit(solution)/shard_map/all_to_all | solution.py:124
  137.6 40.0 %all-reduce = (f32[640]{0:T(1024)S(1)}, f32[640]{0:T(1024)S(1)}, f32[64]{0:T(128)S(1)}) all-reduce(f32[640]{0:T(1024)S(1)} %add.309, f32[640]{0:T(1024)S(1)} %add.311, f32[64]{0:T(128)S(1)} %add.314), channel_id=1, replica_groups=mesh['tile'=8,'depth'=4] {'tile','depth'}, use_global_device_ids=true, to_apply=%region_3.4 | all-reduce | flops 1344 | bytes 10752 | tf_op jit(solution)/shard_map/psum | solution.py:152
  180.0 84.0 %all-reduce.4.cloned.1.call-done = (f32[64,640]{1,0:T(8,128)}, f32[640,640]{1,0:T(8,128)}, f32[640,64]{0,1:T(8,128)}) async-done(((f32[64,640]{1,0:T(8,128)}, f32[640,640]{1,0:T(8,128)}, f32[640,64]{0,1:T(8,128)}), (f32[64,640]{1,0:T(8,128)}, f32[640,640]{1,0:T(8,128)}, f32[640,64]{0,1:T(8,128)})) %all-reduce.4.cloned.1.call-update) | async-done | bytes 1966096 | tf_op jit(solution)/shard_map/psum | solution.py:152
  264.0 1.6 broadcast_multiply_fusion.6
  265.6 1.6 broadcast_multiply_fusion.5
  267.2 2.7 broadcast_multiply_fusion
  (208 shorter events, 34.3 us)
Async XLA Ops:
  7.2 25.5 %copy-start = (bf16[640,640]{1,0:T(8,128)(2,1)S(1)}, bf16[640,640]{1,0:T(8,128)(2,1)}, u32[]{:S(2)}) copy-start(bf16[640,640]{1,0:T(8,128)(2,1)} %param.16) | copy-start | bytes 2457604
  8.2 18.7 %collective-permute-start.4 = (f32[1,1,2,32]{3,2,1,0:T(2,128)S(1)}, f32[1,1,2,32]{3,2,1,0:T(2,128)S(1)}, u32[]{:S(2)}, u32[]{:S(2)}) collective-permute-start(f32[1,1,2,32]{3,2,1,0:T(2,128)S(1)} %maximum_bitcast_fusion.4), channel_id=1, source_target_pairs={{4,0},{8,4},{12,8},{16,12},{20,16},{24,20},{28,24},{0,28},{5,1},{9... | collective-permute-start | bytes 776 | tf_op jit(solution)/shard_map/ppermute | solution.py:26
  11.6 13.5 %collective-permute-start.3 = (f32[1,1,2,32]{3,2,1,0:T(2,128)S(1)}, f32[1,1,2,32]{3,2,1,0:T(2,128)S(1)}, u32[]{:S(2)}, u32[]{:S(2)}) collective-permute-start(f32[1,1,2,32]{3,2,1,0:T(2,128)S(1)} %maximum_bitcast_fusion.4), channel_id=1, source_target_pairs={{0,4},{4,8},{8,12},{12,16},{16,20},{20,24},{24,28},{28,0},{1,5},{5... | collective-permute-start | bytes 776 | tf_op jit(solution)/shard_map/ppermute | solution.py:24
  13.0 15.9 %collective-permute-start.1 = (f32[1,16,2,32]{3,1,2,0:T(8,128)S(1)}, f32[1,16,2,32]{3,1,2,0:T(8,128)S(1)}, u32[]{:S(2)}, u32[]{:S(2)}) collective-permute-start(f32[1,16,2,32]{3,1,2,0:T(8,128)S(1)} %maximum_bitcast_fusion), channel_id=1, source_target_pairs={{4,0},{8,4},{12,8},{16,12},{20,16},{24,20},{28,24},{0,28},{5,1},{9... | collective-permute-start | bytes 12296 | tf_op jit(solution)/shard_map/ppermute | solution.py:26
  15.7 13.2 %collective-permute-start = (f32[1,16,2,32]{3,1,2,0:T(8,128)S(1)}, f32[1,16,2,32]{3,1,2,0:T(8,128)S(1)}, u32[]{:S(2)}, u32[]{:S(2)}) collective-permute-start(f32[1,16,2,32]{3,1,2,0:T(8,128)S(1)} %maximum_bitcast_fusion), channel_id=1, source_target_pairs={{0,4},{4,8},{8,12},{12,16},{16,20},{20,24},{24,28},{28,0},{1,5},{5... | collective-permute-start | bytes 12296 | tf_op jit(solution)/shard_map/ppermute | solution.py:24
  15.7 10.9 %collective-permute-start.5 = (f32[1,2,32]{2,1,0:T(2,128)S(1)}, f32[1,2,32]{2,1,0:T(2,128)S(1)}, u32[]{:S(2)}, u32[]{:S(2)}) collective-permute-start(f32[1,2,32]{2,1,0:T(2,128)S(1)} %pad_maximum_fusion.4), channel_id=1, source_target_pairs={{0,16},{4,20},{8,24},{12,28},{16,0},{20,4},{24,8},{28,12},{1,17},{... | collective-permute-start | bytes 776 | tf_op jit(solution)/shard_map/ppermute | solution.py:35
  17.2 7.4 %copy-start.23 = (s32[1024]{0:T(1024)S(1)}, s32[1024]{0:T(1024)}, u32[]{:S(2)}) copy-start(s32[1024]{0:T(1024)} %param.13) | copy-start | bytes 12292
  18.7 12.1 %all-to-all-start = ((bf16[4,2,2048]{2,1,0:T(2,128)(2,1)}), bf16[4,2,2048]{2,1,0:T(2,128)(2,1)S(1)}, u32[]{:S(2)}, u32[]{:S(2)}) async-start(bf16[4,2,2048]{2,1,0:T(2,128)(2,1)} %reshape.252), calls=%async_computation | async-start | bytes 65536 | tf_op jit(solution)/shard_map/all_to_all | solution.py:119
  23.8 8.6 %copy-start.2 = (bf16[64,640]{1,0:T(8,128)(2,1)S(1)}, bf16[64,640]{1,0:T(8,128)(2,1)}, u32[]{:S(2)}) copy-start(bf16[64,640]{1,0:T(8,128)(2,1)} %param.14) | copy-start | bytes 245764
  23.8 8.6 %copy-start.21 = (f32[640]{0:T(1024)S(1)}, f32[640]{0:T(1024)}, u32[]{:S(2)}) copy-start(f32[640]{0:T(1024)} %param.15) | copy-start | bytes 7684
  24.5 8.1 %copy-start.27 = (f32[640]{0:T(1024)S(1)}, f32[640]{0:T(1024)}, u32[]{:S(2)}) copy-start(f32[640]{0:T(1024)} %param.17) | copy-start | bytes 7684
  25.2 3.7 %collective-permute-start.2 = (f32[16,2,32]{2,1,0:T(2,128)S(1)}, f32[16,2,32]{2,1,0:T(2,128)S(1)}, u32[]{:S(2)}, u32[]{:S(2)}) collective-permute-start(f32[16,2,32]{2,1,0:T(2,128)S(1)} %pad_maximum_fusion), channel_id=1, source_target_pairs={{0,16},{4,20},{8,24},{12,28},{16,0},{20,4},{24,8},{28,12},{1,17},{... | collective-permute-start | bytes 12296 | tf_op jit(solution)/shard_map/ppermute | solution.py:35
  32.7 1.4 copy-start.11
  32.7 1.4 copy-start.25
  34.0 12.7 %copy-start.10 = (f32[2,8,1024]{2,1,0:T(8,128)S(1)}, f32[2,8,1024]{2,1,0:T(8,128)}, u32[]{:S(2)}) copy-start(f32[2,8,1024]{2,1,0:T(8,128)} %param.10) | copy-start | bytes 196612
  35.0 10.9 %all-to-all-start.1 = ((f32[2,32,256]{2,0,1:T(2,128)}), f32[2,32,256]{2,0,1:T(2,128)}, u32[]{:S(2)}, u32[]{:S(2)}) async-start(f32[2,32,256]{2,0,1:T(2,128)} %copy.161), calls=%async_computation.1 | async-start | bytes 131072 | tf_op jit(solution)/shard_map/all_to_all | solution.py:124
  46.8 4.3 %copy-start.9 = (f32[2,8,1024]{2,1,0:T(8,128)}, f32[2,8,1024]{2,1,0:T(8,128)S(1)}, u32[]{:S(2)}) copy-start(f32[2,8,1024]{2,1,0:T(8,128)S(1)} %get-tuple-element.30) | copy-start | bytes 196612
  47.3 8.6 %collective-permute-start.7 = (f32[1,16,2,32]{3,1,2,0:T(8,128)S(1)}, f32[1,16,2,32]{3,1,2,0:T(8,128)S(1)}, u32[]{:S(2)}, u32[]{:S(2)}) collective-permute-start(f32[1,16,2,32]{3,1,2,0:T(8,128)S(1)} %maximum_bitcast_fusion.1), channel_id=1, source_target_pairs={{4,0},{8,4},{12,8},{16,12},{20,16},{24,20},{28,24},{0,28},{5,1},{9... | collective-permute-start | bytes 12296 | tf_op jit(solution)/shard_map/ppermute | solution.py:26
  47.4 8.6 %collective-permute-start.6 = (f32[1,16,2,32]{3,1,2,0:T(8,128)S(1)}, f32[1,16,2,32]{3,1,2,0:T(8,128)S(1)}, u32[]{:S(2)}, u32[]{:S(2)}) collective-permute-start(f32[1,16,2,32]{3,1,2,0:T(8,128)S(1)} %maximum_bitcast_fusion.1), channel_id=1, source_target_pairs={{0,4},{4,8},{8,12},{12,16},{16,20},{20,24},{24,28},{28,0},{1,5},{5... | collective-permute-start | bytes 12296 | tf_op jit(solution)/shard_map/ppermute | solution.py:24
  48.7 7.2 %collective-permute-start.8 = (f32[16,2,32]{2,1,0:T(2,128)S(1)}, f32[16,2,32]{2,1,0:T(2,128)S(1)}, u32[]{:S(2)}, u32[]{:S(2)}) collective-permute-start(f32[16,2,32]{2,1,0:T(2,128)S(1)} %pad_maximum_fusion.1), channel_id=1, source_target_pairs={{0,16},{4,20},{8,24},{12,28},{16,0},{20,4},{24,8},{28,12},{1,17},{... | collective-permute-start | bytes 12296 | tf_op jit(solution)/shard_map/ppermute | solution.py:35
  52.6 8.9 %all-to-all-start.2 = ((bf16[4,2,2048]{2,1,0:T(2,128)(2,1)}), bf16[4,2,2048]{2,1,0:T(2,128)(2,1)S(1)}, u32[]{:S(2)}, u32[]{:S(2)}) async-start(bf16[4,2,2048]{2,1,0:T(2,128)(2,1)} %reshape.254), calls=%async_computation.2 | async-start | bytes 65536 | tf_op jit(solution)/shard_map/all_to_all | solution.py:119
  63.4 2.3 copy-start.4
  63.4 2.3 copy-start.12
  63.4 2.3 copy-start.26
  63.4 7.1 %copy-start.3 = (f32[16,32,31]{2,1,0:T(8,128)S(1)}, f32[16,32,31]{2,1,0:T(8,128)}, u32[]{:S(2)}) copy-start(f32[16,32,31]{2,1,0:T(8,128)} %get-tuple-element.48) | copy-start | bytes 190468
  65.7 11.5 %copy-start.22 = (f32[1024]{0:T(1024)S(1)}, f32[1024]{0:T(1024)}, u32[]{:S(2)}) copy-start(f32[1024]{0:T(1024)} %convert_element_type.59) | copy-start | bytes 12292
  66.6 9.7 %all-to-all-start.3 = ((f32[2,32,256]{2,0,1:T(2,128)}), f32[2,32,256]{2,0,1:T(2,128)}, u32[]{:S(2)}, u32[]{:S(2)}) async-start(f32[2,32,256]{2,0,1:T(2,128)} %copy.168), calls=%async_computation.3 | async-start | bytes 131072 | tf_op jit(solution)/shard_map/all_to_all | solution.py:124
  79.2 9.4 %collective-permute-start.10 = (f32[1,16,2,32]{3,1,2,0:T(8,128)S(1)}, f32[1,16,2,32]{3,1,2,0:T(8,128)S(1)}, u32[]{:S(2)}, u32[]{:S(2)}) collective-permute-start(f32[1,16,2,32]{3,1,2,0:T(8,128)S(1)} %maximum_bitcast_fusion.2), channel_id=1, source_target_pairs={{4,0},{8,4},{12,8},{16,12},{20,16},{24,20},{28,24},{0,28},{5,1},{9... | collective-permute-start | bytes 12296 | tf_op jit(solution)/shard_map/ppermute | solution.py:26
  79.3 7.6 %collective-permute-start.9 = (f32[1,16,2,32]{3,1,2,0:T(8,128)S(1)}, f32[1,16,2,32]{3,1,2,0:T(8,128)S(1)}, u32[]{:S(2)}, u32[]{:S(2)}) collective-permute-start(f32[1,16,2,32]{3,1,2,0:T(8,128)S(1)} %maximum_bitcast_fusion.2), channel_id=1, source_target_pairs={{0,4},{4,8},{8,12},{12,16},{16,20},{20,24},{24,28},{28,0},{1,5},{5... | collective-permute-start | bytes 12296 | tf_op jit(solution)/shard_map/ppermute | solution.py:24
  80.0 7.0 %collective-permute-start.11 = (f32[16,2,32]{2,1,0:T(2,128)S(1)}, f32[16,2,32]{2,1,0:T(2,128)S(1)}, u32[]{:S(2)}, u32[]{:S(2)}) collective-permute-start(f32[16,2,32]{2,1,0:T(2,128)S(1)} %pad_maximum_fusion.2), channel_id=1, source_target_pairs={{0,16},{4,20},{8,24},{12,28},{16,0},{20,4},{24,8},{28,12},{1,17},{... | collective-permute-start | bytes 12296 | tf_op jit(solution)/shard_map/ppermute | solution.py:35
  82.9 9.6 %all-to-all-start.4 = ((bf16[4,2,2048]{2,1,0:T(2,128)(2,1)}), bf16[4,2,2048]{2,1,0:T(2,128)(2,1)}, u32[]{:S(2)}, u32[]{:S(2)}) async-start(bf16[4,2,2048]{2,1,0:T(2,128)(2,1)} %reshape.256), calls=%async_computation.4 | async-start | bytes 65536 | tf_op jit(solution)/shard_map/all_to_all | solution.py:119
  90.0 5.0 %copy-start.13 = (bf16[640,64]{0,1:T(8,128)(2,1)S(1)}, bf16[640,64]{0,1:T(8,128)(2,1)}, u32[]{:S(2)}) copy-start(bf16[640,64]{0,1:T(8,128)(2,1)} %param.18) | copy-start | bytes 245764
  94.2 2.4 copy-start.17
  95.1 1.6 copy-start.5
  97.7 5.9 %copy-start.16 = (bf16[2,4,8,256]{3,2,1,0:T(8,128)(2,1)S(1)}, bf16[2,4,8,256]{3,2,1,0:T(8,128)(2,1)}, u32[]{:S(2)}) copy-start(bf16[2,4,8,256]{3,2,1,0:T(8,128)(2,1)} %copy-done.15) | copy-start | bytes 98308
  97.7 11.6 %copy-start.8 = (f32[2,8,1024]{2,1,0:T(8,128)S(1)}, f32[2,8,1024]{2,1,0:T(8,128)}, u32[]{:S(2)}) copy-start(f32[2,8,1024]{2,1,0:T(8,128)} %copy-done.7) | copy-start | bytes 196612
  100.3 9.0 %all-to-all-start.5 = ((f32[2,32,256]{2,0,1:T(2,128)}), f32[2,32,256]{2,0,1:T(2,128)S(1)}, u32[]{:S(2)}, u32[]{:S(2)}) async-start(f32[2,32,256]{2,0,1:T(2,128)} %copy.175), calls=%async_computation.5 | async-start | bytes 131072 | tf_op jit(solution)/shard_map/all_to_all | solution.py:124
  109.9 8.9 %collective-permute-start.13 = (f32[1,16,2,32]{3,1,2,0:T(8,128)S(1)}, f32[1,16,2,32]{3,1,2,0:T(8,128)S(1)}, u32[]{:S(2)}, u32[]{:S(2)}) collective-permute-start(f32[1,16,2,32]{3,1,2,0:T(8,128)S(1)} %maximum_bitcast_fusion.3), channel_id=1, source_target_pairs={{4,0},{8,4},{12,8},{16,12},{20,16},{24,20},{28,24},{0,28},{5,1},{9... | collective-permute-start | bytes 12296 | tf_op jit(solution)/shard_map/ppermute | solution.py:26
  110.0 8.4 %collective-permute-start.12 = (f32[1,16,2,32]{3,1,2,0:T(8,128)S(1)}, f32[1,16,2,32]{3,1,2,0:T(8,128)S(1)}, u32[]{:S(2)}, u32[]{:S(2)}) collective-permute-start(f32[1,16,2,32]{3,1,2,0:T(8,128)S(1)} %maximum_bitcast_fusion.3), channel_id=1, source_target_pairs={{0,4},{4,8},{8,12},{12,16},{16,20},{20,24},{24,28},{28,0},{1,5},{5... | collective-permute-start | bytes 12296 | tf_op jit(solution)/shard_map/ppermute | solution.py:24
  110.6 7.7 %collective-permute-start.14 = (f32[16,2,32]{2,1,0:T(2,128)S(1)}, f32[16,2,32]{2,1,0:T(2,128)S(1)}, u32[]{:S(2)}, u32[]{:S(2)}) collective-permute-start(f32[16,2,32]{2,1,0:T(2,128)S(1)} %pad_maximum_fusion.3), channel_id=1, source_target_pairs={{0,16},{4,20},{8,24},{12,28},{16,0},{20,4},{24,8},{28,12},{1,17},{... | collective-permute-start | bytes 12296 | tf_op jit(solution)/shard_map/ppermute | solution.py:35
  114.4 9.6 %all-to-all-start.6 = ((bf16[4,2,2048]{2,1,0:T(2,128)(2,1)}), bf16[4,2,2048]{2,1,0:T(2,128)(2,1)}, u32[]{:S(2)}, u32[]{:S(2)}) async-start(bf16[4,2,2048]{2,1,0:T(2,128)(2,1)} %reshape.258), calls=%async_computation.6 | async-start | bytes 65536 | tf_op jit(solution)/shard_map/all_to_all | solution.py:119
  118.3 145.7 %all-reduce.4.cloned.1.call-start = ((), (), s32[]{:S(2)}) async-start(), calls=%async_computation.8 | async-start | bytes 3932160 | tf_op jit(solution)/shard_map/psum | solution.py:152
  120.2 7.4 %copy-start.14 = (bf16[640,64]{0,1:T(8,128)(2,1)S(1)}, bf16[640,64]{0,1:T(8,128)(2,1)}, u32[]{:S(2)}) copy-start(bf16[640,64]{0,1:T(8,128)(2,1)} %param.18) | copy-start | bytes 245764
  129.0 0.9 copy-start.6
  129.0 0.9 copy-start.20
  129.1 1.8 copy-start.1
  132.5 5.0 %copy-start.24 = (f32[640]{0:T(1024)S(1)}, f32[640]{0:T(1024)}, u32[]{:S(2)}) copy-start(f32[640]{0:T(1024)} %get-tuple-element.77) | copy-start | bytes 7684
  134.3 45.1 %all-to-all-start.7 = ((f32[2,32,256]{2,0,1:T(2,128)}), f32[2,32,256]{2,0,1:T(2,128)S(1)}, u32[]{:S(2)}, u32[]{:S(2)}) async-start(f32[2,32,256]{2,0,1:T(2,128)} %copy.182), calls=%async_computation.7 | async-start | bytes 131072 | tf_op jit(solution)/shard_map/all_to_all | solution.py:124
  (4 other events, 2.6 us)
Sparse Core Ops, SparseCore 0:
  132.7 131.2 all-reduce.3
where the time goes:
time: 278 us; the launch traced here: 277 us
  waiting for transfers between devices  109 us (39%)
  starting transfers between devices  45.2 us (16%)
  blocking collectives  40 us (14%)
  local copies, waits for them, and re-layouts  32.6 us (12%)
  other arithmetic  17.3 us (6%)
  matrix products  17.3 us (6%)
  between operations  15 us (5%)
    psum x1, waiting for transfers between devices, body(): summed = lax.psum(totals, ('tile', 'depth'))  84 us
    psum x1, blocking collectives, body(): summed = lax.psum(totals, ('tile', 'depth'))  40 us
    all_to_all x4, starting transfers between devices, to_columns(): lax.all_to_all(segment, 'depth', split_axis=2, concat_axis=1, tiled=True)  16.1 us
    all_to_all x4, starting transfers between devices, to_segments(): lax.all_to_all(shaped, 'depth', split_axis=1, concat_axis=2, tiled=True)  15.6 us
    all_to_all x4, waiting for transfers between devices, to_segments(): lax.all_to_all(shaped, 'depth', split_axis=1, concat_axis=2, tiled=True)  13.8 us
    unnamed x64, local copies, waits for them, and re-layouts  10.7 us
    all_to_all x4, waiting for transfers between devices, to_columns(): lax.all_to_all(segment, 'depth', split_axis=2, concat_axis=1, tiled=True)  9.74 us
    ppermute x5, starting transfers between devices, with_halo(): lax.ppermute(head, axis, [((i + 1) % count, i) for i in range(count)])  6.25 us
  transfers between devices with their start and end apart: 24, of which 8 were waited for; matrix products, arithmetic and copies ran while one was open for 11% of the time, Pallas kernels for 0%

commit v1 on v0

--- a/solution.py
+++ b/solution.py
@@ -107,6 +107,70 @@
     grad_b_in = jnp.sum(slope_one.astype(jnp.float32), axis=1)
     back_grad = jnp.dot(w_in, slope_one, preferred_element_type=jnp.float32)
     return (back_grad, (grad_w_in, grad_b_in, grad_w_mid, grad_b_mid, grad_w_out, grad_b_out))
+
+
+def is_power_of_two(count):
+    return count & (count - 1) == 0
+
+
+def swapped(x, axis, even_bit, odd_bit):
+    length = lax.axis_size(axis)
+    return lax.ppermute(x, axis, [(i, i ^ (odd_bit if i & 1 else even_bit)) for i in range(length)])
+
+
+def tile_rounds(length):
+    bits = [1 << k for k in range(length.bit_length() - 1)]
+    rounds = [(bits[0], bits[0])] if bits else []
+    rest = bits[1:]
+    for k in range(len(rest)):
+        rounds.append((rest[k], rest[(k + 1) % len(rest)]))
+    return rounds
+
+
+def all_summed(block):
+    tiles = lax.axis_size("tile")
+    depths = lax.axis_size("depth")
+    if not (is_power_of_two(tiles) and is_power_of_two(depths)):
+        return lax.psum(block, ("tile", "depth"))
+    width = block.shape[-1]
+    tile = lax.axis_index("tile")
+    rounds = tile_rounds(tiles)
+    sides = []
+    for even_bit, odd_bit in rounds:
+        bit = jnp.where(tile & 1 == 1, odd_bit, even_bit)
+        sides.append(((tile & bit) != 0).astype(jnp.int32))
+    for (even_bit, odd_bit), side in zip(rounds, sides):
+        halves = block.reshape(2, -1, width)
+        sent = lax.dynamic_index_in_dim(halves, 1 - side, 0, False)
+        kept = lax.dynamic_index_in_dim(halves, side, 0, False)
+        block = kept + swapped(sent, "tile", even_bit, odd_bit)
+    bit = 1
+    while bit < depths:
+        block = block + swapped(block, "depth", bit, bit)
+        bit *= 2
+    for (even_bit, odd_bit), side in zip(reversed(rounds), reversed(sides)):
+        other = swapped(block, "tile", even_bit, odd_bit)
+        block = jnp.where(side == 0, jnp.stack([block, other]), jnp.stack([other, block])).reshape(-1, width)
+    return block
+
+
+def reduced_gradients(totals):
+    grad_w_in, grad_b_in, grad_w_mid, grad_b_mid, grad_w_out, grad_b_out = totals
+    width = grad_w_mid.shape[1]
+    features = grad_w_in.shape[0]
+    bias_rows = jnp.zeros((8, width), jnp.float32)
+    bias_rows = bias_rows.at[0].set(grad_b_in).at[1].set(grad_b_mid).at[2, :features].set(grad_b_out)
+    parts = [grad_w_mid, grad_w_in, grad_w_out.T, bias_rows]
+    rows = sum(part.shape[0] for part in parts)
+    step = 8 * lax.axis_size("tile")
+    pad = -rows % step
+    block = jnp.concatenate(parts + [jnp.zeros((pad, width), jnp.float32)], axis=0)
+    block = all_summed(block)
+    top = width
+    out_in = block[top : top + features]
+    out_out = block[top + features : top + 2 * features].T
+    biases = block[top + 2 * features : top + 2 * features + 8]
+    return (out_in, biases[0], block[:width], biases[1], out_out, biases[2, :features])
 
 
 def body(initial_state, observed, edge_weight, land, w_in, b_in, w_mid, b_mid, w_out, b_out):
@@ -149,7 +213,7 @@
     totals = grad_list[0]
     for param_grads in grad_list[1:]:
         totals = tuple((total + gradient for total, gradient in zip(totals, param_grads)))
-    summed = lax.psum(totals, ("tile", "depth"))
+    summed = reduced_gradients(totals)
     grad_scale = 1.0 / (lax.axis_size("tile") * TILE_CELLS)
     return (
         state_now,

time: 278 us -> 193 us (0.69)
  blocking collectives: 40 us -> 0 us
  waiting for transfers between devices: 109 us -> 77.9 us
  between operations: 15 us -> 1.7 us
  starting transfers between devices: 45.2 us -> 49.9 us
  other arithmetic: 17.3 us -> 13.6 us
    psum x1 -> x0, waiting for transfers between devices: 84 us -> none  [body(): summed = lax.psum(totals, ('tile', 'depth'))]
    ppermute x0 -> x8, waiting for transfers between devices: none -> 43.1 us  [swapped(): lax.ppermute(x, axis, [(i, i ^ (odd_bit if i & 1 else even_bit)) for i in...]
    psum x1 -> x0, blocking collectives: 40 us -> none  [body(): summed = lax.psum(totals, ('tile', 'depth'))]
    ppermute x0 -> x8, starting transfers between devices: none -> 6.47 us  [swapped(): lax.ppermute(x, axis, [(i, i ^ (odd_bit if i & 1 else even_bit)) for i in...]
    all_to_all x4, waiting for transfers between devices: 13.8 us -> 19.7 us  [to_segments(): lax.all_to_all(shaped, 'depth', split_axis=1, concat_axis=2, tiled=True)]
    all_to_all x4, waiting for transfers between devices: 9.74 us -> 13.4 us  [to_columns(): lax.all_to_all(segment, 'depth', split_axis=2, concat_axis=1, tiled=True)]
    scatter x0 -> x3, local copies, waits for them, and re-layouts: none -> 3.31 us  [reduced_gradients(): bias_rows.at[0].set(grad_b_in).at[1].set(grad_b_mid).at[2, :features]]
    unnamed x64 -> x65, local copies, waits for them, and re-layouts: 10.7 us -> 9.16 us
  transfers between devices with their start and end apart: 24 -> 31, of which waited for: 8 -> 16; matrix products, arithmetic and copies ran while one was open for 11% -> 12% of each run, Pallas kernels for 0% -> 0%
where the time goes in v1:
time: 193 us; the launch traced here: 191 us
  waiting for transfers between devices  77.9 us (40%)
  starting transfers between devices  49.9 us (26%)
  local copies, waits for them, and re-layouts  32.4 us (17%)
  matrix products  15.8 us (8%)
  other arithmetic  13.6 us (7%)
    ppermute x8, waiting for transfers between devices, swapped(): lax.ppermute(x, axis, [(i, i ^ (odd_bit if i & 1 else even_bit)) for i in...  43.1 us
    all_to_all x4, waiting for transfers between devices, to_segments(): lax.all_to_all(shaped, 'depth', split_axis=1, concat_axis=2, tiled=True)  19.7 us
    all_to_all x4, starting transfers between devices, to_segments(): lax.all_to_all(shaped, 'depth', split_axis=1, concat_axis=2, tiled=True)  15.3 us
    all_to_all x4, starting transfers between devices, to_columns(): lax.all_to_all(segment, 'depth', split_axis=2, concat_axis=1, tiled=True)  14.8 us
    all_to_all x4, waiting for transfers between devices, to_columns(): lax.all_to_all(segment, 'depth', split_axis=2, concat_axis=1, tiled=True)  13.4 us
    unnamed x65, local copies, waits for them, and re-layouts  9.16 us
    ppermute x8, starting transfers between devices, swapped(): lax.ppermute(x, axis, [(i, i ^ (odd_bit if i & 1 else even_bit)) for i in...  6.47 us
    ppermute x5, starting transfers between devices, with_halo(): lax.ppermute(head, axis, [((i + 1) % count, i) for i in range(count)])  6.4 us
  transfers between devices with their start and end apart: 31, of which 16 were waited for; matrix products, arithmetic and copies ran while one was open for 12% of the time, Pallas kernels for 0%

profile of v1, /device:TPU:0, one launch (start us, length us, event | category | flops | bytes accessed | tf_op | source)
XLA Modules:
  0.0 191.3 jit_solution(9956939731741169588)
XLA Ops:
  1.7 3.4 %collective-permute-start.4 = (f32[1,1,2,32]{3,2,1,0:T(2,128)S(1)}, f32[1,1,2,32]{3,2,1,0:T(2,128)S(1)}, u32[]{:S(2)}, u32[]{:S(2)}) collective-permute-start(f32[1,1,2,32]{3,2,1,0:T(2,128)S(1)} %maximum_bitcast_fusion.4), channel_id=1, source_target_pairs={{4,0},{8,4},{12,8},{16,12},{20,16},{24,20},{28,24},{0,28},{5,1},{9... | collective-permute-start | bytes 776 | tf_op jit(solution)/shard_map/ppermute | solution.py:26
  6.5 2.7 %collective-permute-start.1 = (f32[1,16,2,32]{3,1,2,0:T(8,128)S(1)}, f32[1,16,2,32]{3,1,2,0:T(8,128)S(1)}, u32[]{:S(2)}, u32[]{:S(2)}) collective-permute-start(f32[1,16,2,32]{3,1,2,0:T(8,128)S(1)} %maximum_bitcast_fusion), channel_id=1, source_target_pairs={{4,0},{8,4},{12,8},{16,12},{20,16},{24,20},{28,24},{0,28},{5,1},{9... | collective-permute-start | bytes 12296 | tf_op jit(solution)/shard_map/ppermute | solution.py:26
  11.0 1.1 reshape.430
  12.1 4.9 %all-to-all-start = ((bf16[4,2,2048]{2,1,0:T(2,128)(2,1)}), bf16[4,2,2048]{2,1,0:T(2,128)(2,1)S(1)}, u32[]{:S(2)}, u32[]{:S(2)}) async-start(bf16[4,2,2048]{2,1,0:T(2,128)(2,1)} %reshape.430), calls=%async_computation | async-start | bytes 65536 | tf_op jit(solution)/shard_map/all_to_all | solution.py:183
  17.9 1.6 collective-permute-start.2
  20.1 1.7 collective-permute-done.2
  24.3 2.1 %multiply_convert_fusion.2 = (bf16[640,256]{0,1:T(8,128)(2,1)S(1)}, f32[640,256]{0,1:T(8,128)}) fusion(f32[640]{0:T(1024)} %param.23, bf16[640,640]{1,0:T(8,128)(2,1)S(1)} %copy-done, f32[640,256]{0,1:T(8,128)S(1)} %convolution_add_fusion.3), kind=kOutput, calls=%fused_computation.40 | convolution fusion | flops 211517440 | bytes 2460160 | tf_op jit(solution)/shard_map/dot_general | solution.py:75
  27.3 4.8 %all-to-all-start.1 = ((f32[2,32,256]{2,0,1:T(2,128)}), f32[2,32,256]{2,0,1:T(2,128)S(1)}, u32[]{:S(2)}, u32[]{:S(2)}) async-start(f32[2,32,256]{2,0,1:T(2,128)} %copy.161), calls=%async_computation.1 | async-start | bytes 131072 | tf_op jit(solution)/shard_map/all_to_all | solution.py:188
  32.5 5.4 %all-to-all-done.1 = f32[2,32,256]{2,0,1:T(2,128)S(1)} async-done(((f32[2,32,256]{2,0,1:T(2,128)}), f32[2,32,256]{2,0,1:T(2,128)S(1)}, u32[]{:S(2)}, u32[]{:S(2)}) %all-to-all-start.1) | async-done | bytes 65568 | tf_op jit(solution)/shard_map/all_to_all | solution.py:188
  39.2 1.6 collective-permute-start.8
  41.9 1.1 reshape.432
  43.0 3.3 %all-to-all-start.2 = ((bf16[4,2,2048]{2,1,0:T(2,128)(2,1)}), bf16[4,2,2048]{2,1,0:T(2,128)(2,1)S(1)}, u32[]{:S(2)}, u32[]{:S(2)}) async-start(bf16[4,2,2048]{2,1,0:T(2,128)(2,1)} %reshape.432), calls=%async_computation.2 | async-start | bytes 65536 | tf_op jit(solution)/shard_map/all_to_all | solution.py:183
  48.1 3.8 %all-to-all-done.2 = bf16[4,2,2048]{2,1,0:T(2,128)(2,1)S(1)} async-done(((bf16[4,2,2048]{2,1,0:T(2,128)(2,1)}), bf16[4,2,2048]{2,1,0:T(2,128)(2,1)S(1)}, u32[]{:S(2)}, u32[]{:S(2)}) %all-to-all-start.2) | async-done | bytes 32800 | tf_op jit(solution)/shard_map/all_to_all | solution.py:183
  53.2 2.3 %multiply_convert_fusion = (bf16[640,256]{0,1:T(8,128)(2,1)S(1)}, f32[640,256]{0,1:T(8,128)}) fusion(f32[640]{0:T(1024)} %param.23, bf16[640,640]{1,0:T(8,128)(2,1)S(1)} %copy-done, f32[640,256]{0,1:T(8,128)S(1)} %fusion.3), kind=kOutput, calls=%fused_computation.36 | convolution fusion | flops 211517440 | bytes 2460160 | tf_op jit(solution)/shard_map/dot_general | solution.py:75
  56.4 3.9 %all-to-all-start.3 = ((f32[2,32,256]{2,0,1:T(2,128)}), f32[2,32,256]{2,0,1:T(2,128)}, u32[]{:S(2)}, u32[]{:S(2)}) async-start(f32[2,32,256]{2,0,1:T(2,128)} %copy.168), calls=%async_computation.3 | async-start | bytes 131072 | tf_op jit(solution)/shard_map/all_to_all | solution.py:188
  61.4 4.7 %all-to-all-done.3 = f32[2,32,256]{2,0,1:T(2,128)} async-done(((f32[2,32,256]{2,0,1:T(2,128)}), f32[2,32,256]{2,0,1:T(2,128)}, u32[]{:S(2)}, u32[]{:S(2)}) %all-to-all-start.3) | async-done | bytes 65568 | tf_op jit(solution)/shard_map/all_to_all | solution.py:188
  67.0 1.5 multiply_convert_fusion.5
  70.7 1.1 reshape.434
  71.9 3.4 %all-to-all-start.4 = ((bf16[4,2,2048]{2,1,0:T(2,128)(2,1)}), bf16[4,2,2048]{2,1,0:T(2,128)(2,1)S(1)}, u32[]{:S(2)}, u32[]{:S(2)}) async-start(bf16[4,2,2048]{2,1,0:T(2,128)(2,1)} %reshape.434), calls=%async_computation.4 | async-start | bytes 65536 | tf_op jit(solution)/shard_map/all_to_all | solution.py:183
  76.3 4.6 %all-to-all-done.4 = bf16[4,2,2048]{2,1,0:T(2,128)(2,1)S(1)} async-done(((bf16[4,2,2048]{2,1,0:T(2,128)(2,1)}), bf16[4,2,2048]{2,1,0:T(2,128)(2,1)S(1)}, u32[]{:S(2)}, u32[]{:S(2)}) %all-to-all-start.4) | async-done | bytes 32800 | tf_op jit(solution)/shard_map/all_to_all | solution.py:183
  81.9 1.5 convert_reduce_fusion.1
  83.9 1.7 fusion.28
  86.5 3.3 %all-to-all-start.5 = ((f32[2,32,256]{2,0,1:T(2,128)}), f32[2,32,256]{2,0,1:T(2,128)S(1)}, u32[]{:S(2)}, u32[]{:S(2)}) async-start(f32[2,32,256]{2,0,1:T(2,128)} %copy.175), calls=%async_computation.5 | async-start | bytes 131072 | tf_op jit(solution)/shard_map/all_to_all | solution.py:188
  90.0 5.5 %all-to-all-done.5 = f32[2,32,256]{2,0,1:T(2,128)S(1)} async-done(((f32[2,32,256]{2,0,1:T(2,128)}), f32[2,32,256]{2,0,1:T(2,128)S(1)}, u32[]{:S(2)}, u32[]{:S(2)}) %all-to-all-start.5) | async-done | bytes 65568 | tf_op jit(solution)/shard_map/all_to_all | solution.py:188
  96.6 1.1 reshape.436
  97.7 3.3 %all-to-all-start.6 = ((bf16[4,2,2048]{2,1,0:T(2,128)(2,1)}), bf16[4,2,2048]{2,1,0:T(2,128)(2,1)S(1)}, u32[]{:S(2)}, u32[]{:S(2)}) async-start(bf16[4,2,2048]{2,1,0:T(2,128)(2,1)} %reshape.436), calls=%async_computation.6 | async-start | bytes 65536 | tf_op jit(solution)/shard_map/all_to_all | solution.py:183
  101.8 4.8 %all-to-all-done.6 = bf16[4,2,2048]{2,1,0:T(2,128)(2,1)S(1)} async-done(((bf16[4,2,2048]{2,1,0:T(2,128)(2,1)}), bf16[4,2,2048]{2,1,0:T(2,128)(2,1)S(1)}, u32[]{:S(2)}, u32[]{:S(2)}) %all-to-all-start.6) | async-done | bytes 32800 | tf_op jit(solution)/shard_map/all_to_all | solution.py:183
  107.9 1.5 convert_reduce_fusion
  109.4 1.2 convert_reduce_fusion.2
  112.4 1.3 scatter.11
  113.7 1.2 fusion.12
  115.9 1.3 scatter.14
  118.0 1.1 dynamic-slice_bitcast_fusion
  119.7 2.5 %collective-permute-done.15 = f32[416,640]{1,0:T(8,128)} collective-permute-done((f32[416,640]{1,0:T(8,128)}, f32[416,640]{1,0:T(8,128)}, u32[]{:S(2)}, u32[]{:S(2)}) %collective-permute-start.15) | collective-permute-done | bytes 1064992 | tf_op jit(solution)/shard_map/ppermute | solution.py:118
  122.1 1.7 bitcast_add_fusion
  124.7 8.5 %collective-permute-done.16 = f32[208,640]{1,0:T(8,128)S(1)} collective-permute-done((f32[208,640]{1,0:T(8,128)S(1)}, f32[208,640]{1,0:T(8,128)S(1)}, u32[]{:S(2)}, u32[]{:S(2)}) %collective-permute-start.16) | collective-permute-done | bytes 532512 | tf_op jit(solution)/shard_map/ppermute | solution.py:118
  133.3 1.6 collective-permute-start.17
  134.9 4.9 %collective-permute-done.17 = f32[104,640]{1,0:T(8,128)S(1)} collective-permute-done((f32[104,640]{1,0:T(8,128)S(1)}, f32[104,640]{1,0:T(8,128)S(1)}, u32[]{:S(2)}, u32[]{:S(2)}) %collective-permute-start.17) | collective-permute-done | bytes 266272 | tf_op jit(solution)/shard_map/ppermute | solution.py:118
  140.7 5.9 %collective-permute-done.18 = f32[104,640]{1,0:T(8,128)S(1)} collective-permute-done((f32[104,640]{1,0:T(8,128)S(1)}, f32[104,640]{1,0:T(8,128)S(1)}, u32[]{:S(2)}, u32[]{:S(2)}) %collective-permute-start.18) | collective-permute-done | bytes 266272 | tf_op jit(solution)/shard_map/ppermute | solution.py:118
  147.7 11.4 %collective-permute-done.19 = f32[104,640]{1,0:T(8,128)S(1)} collective-permute-done((f32[104,640]{1,0:T(8,128)S(1)}, f32[104,640]{1,0:T(8,128)S(1)}, u32[]{:S(2)}, u32[]{:S(2)}) %collective-permute-start.19) | collective-permute-done | bytes 266272 | tf_op jit(solution)/shard_map/ppermute | solution.py:118
  159.1 1.6 collective-permute-start.20
  161.2 4.6 %collective-permute-done.20 = f32[104,640]{1,0:T(8,128)S(1)} collective-permute-done((f32[104,640]{1,0:T(8,128)S(1)}, f32[104,640]{1,0:T(8,128)S(1)}, u32[]{:S(2)}, u32[]{:S(2)}) %collective-permute-start.20) | collective-permute-done | bytes 266272 | tf_op jit(solution)/shard_map/ppermute | solution.py:118
  166.7 1.3 collective-permute-start.14
  169.8 5.4 %collective-permute-done.21 = f32[208,640]{1,0:T(8,128)S(1)} collective-permute-done((f32[208,640]{1,0:T(8,128)S(1)}, f32[208,640]{1,0:T(8,128)S(1)}, u32[]{:S(2)}, u32[]{:S(2)}) %collective-permute-start.21) | collective-permute-done | bytes 532512 | tf_op jit(solution)/shard_map/ppermute | solution.py:118
  178.3 3.3 %all-to-all-start.7 = ((f32[2,32,256]{2,0,1:T(2,128)}), f32[2,32,256]{2,0,1:T(2,128)S(1)}, u32[]{:S(2)}, u32[]{:S(2)}) async-start(f32[2,32,256]{2,0,1:T(2,128)} %copy.182), calls=%async_computation.7 | async-start | bytes 131072 | tf_op jit(solution)/shard_map/all_to_all | solution.py:188
  181.6 1.6 fusion.21
  183.3 4.0 %all-to-all-done.7 = f32[2,32,256]{2,0,1:T(2,128)S(1)} async-done(((f32[2,32,256]{2,0,1:T(2,128)}), f32[2,32,256]{2,0,1:T(2,128)S(1)}, u32[]{:S(2)}, u32[]{:S(2)}) %all-to-all-start.7) | async-done | bytes 65568 | tf_op jit(solution)/shard_map/all_to_all | solution.py:188
  190.0 1.3 slice_multiply_fusion
  (236 shorter events, 42.5 us)
Async XLA Ops:
  0.6 23.6 %copy-start = (bf16[640,640]{1,0:T(8,128)(2,1)S(1)}, bf16[640,640]{1,0:T(8,128)(2,1)}, u32[]{:S(2)}) copy-start(bf16[640,640]{1,0:T(8,128)(2,1)} %param.22) | copy-start | bytes 2457604
  0.6 16.4 %copy-start.24 = (s32[1024]{0:T(1024)S(1)}, s32[1024]{0:T(1024)}, u32[]{:S(2)}) copy-start(s32[1024]{0:T(1024)} %param.19) | copy-start | bytes 12292
  1.7 18.1 %collective-permute-start.4 = (f32[1,1,2,32]{3,2,1,0:T(2,128)S(1)}, f32[1,1,2,32]{3,2,1,0:T(2,128)S(1)}, u32[]{:S(2)}, u32[]{:S(2)}) collective-permute-start(f32[1,1,2,32]{3,2,1,0:T(2,128)S(1)} %maximum_bitcast_fusion.4), channel_id=1, source_target_pairs={{4,0},{8,4},{12,8},{16,12},{20,16},{24,20},{28,24},{0,28},{5,1},{9... | collective-permute-start | bytes 776 | tf_op jit(solution)/shard_map/ppermute | solution.py:26
  5.1 12.8 %collective-permute-start.3 = (f32[1,1,2,32]{3,2,1,0:T(2,128)S(1)}, f32[1,1,2,32]{3,2,1,0:T(2,128)S(1)}, u32[]{:S(2)}, u32[]{:S(2)}) collective-permute-start(f32[1,1,2,32]{3,2,1,0:T(2,128)S(1)} %maximum_bitcast_fusion.4), channel_id=1, source_target_pairs={{0,4},{4,8},{8,12},{12,16},{16,20},{20,24},{24,28},{28,0},{1,5},{5... | collective-permute-start | bytes 776 | tf_op jit(solution)/shard_map/ppermute | solution.py:24
  6.5 15.3 %collective-permute-start.1 = (f32[1,16,2,32]{3,1,2,0:T(8,128)S(1)}, f32[1,16,2,32]{3,1,2,0:T(8,128)S(1)}, u32[]{:S(2)}, u32[]{:S(2)}) collective-permute-start(f32[1,16,2,32]{3,1,2,0:T(8,128)S(1)} %maximum_bitcast_fusion), channel_id=1, source_target_pairs={{4,0},{8,4},{12,8},{16,12},{20,16},{24,20},{28,24},{0,28},{5,1},{9... | collective-permute-start | bytes 12296 | tf_op jit(solution)/shard_map/ppermute | solution.py:26
  9.2 12.6 %collective-permute-start = (f32[1,16,2,32]{3,1,2,0:T(8,128)S(1)}, f32[1,16,2,32]{3,1,2,0:T(8,128)S(1)}, u32[]{:S(2)}, u32[]{:S(2)}) collective-permute-start(f32[1,16,2,32]{3,1,2,0:T(8,128)S(1)} %maximum_bitcast_fusion), channel_id=1, source_target_pairs={{0,4},{4,8},{8,12},{12,16},{16,20},{20,24},{24,28},{28,0},{1,5},{5... | collective-permute-start | bytes 12296 | tf_op jit(solution)/shard_map/ppermute | solution.py:24
  9.2 10.3 %collective-permute-start.5 = (f32[1,2,32]{2,1,0:T(2,128)S(1)}, f32[1,2,32]{2,1,0:T(2,128)S(1)}, u32[]{:S(2)}, u32[]{:S(2)}) collective-permute-start(f32[1,2,32]{2,1,0:T(2,128)S(1)} %pad_maximum_fusion.4), channel_id=1, source_target_pairs={{0,16},{4,20},{8,24},{12,28},{16,0},{20,4},{24,8},{28,12},{1,17},{... | collective-permute-start | bytes 776 | tf_op jit(solution)/shard_map/ppermute | solution.py:35
  12.1 10.5 %all-to-all-start = ((bf16[4,2,2048]{2,1,0:T(2,128)(2,1)}), bf16[4,2,2048]{2,1,0:T(2,128)(2,1)S(1)}, u32[]{:S(2)}, u32[]{:S(2)}) async-start(bf16[4,2,2048]{2,1,0:T(2,128)(2,1)} %reshape.430), calls=%async_computation | async-start | bytes 65536 | tf_op jit(solution)/shard_map/all_to_all | solution.py:183
  17.7 6.0 %copy-start.3 = (bf16[64,640]{1,0:T(8,128)(2,1)S(1)}, bf16[64,640]{1,0:T(8,128)(2,1)}, u32[]{:S(2)}) copy-start(bf16[64,640]{1,0:T(8,128)(2,1)} %param.20) | copy-start | bytes 245764
  17.7 6.0 %copy-start.22 = (f32[640]{0:T(1024)S(1)}, f32[640]{0:T(1024)}, u32[]{:S(2)}) copy-start(f32[640]{0:T(1024)} %param.21) | copy-start | bytes 7684
  17.9 3.8 %collective-permute-start.2 = (f32[16,2,32]{2,1,0:T(2,128)S(1)}, f32[16,2,32]{2,1,0:T(2,128)S(1)}, u32[]{:S(2)}, u32[]{:S(2)}) collective-permute-start(f32[16,2,32]{2,1,0:T(2,128)S(1)} %pad_maximum_fusion), channel_id=1, source_target_pairs={{0,16},{4,20},{8,24},{12,28},{16,0},{20,4},{24,8},{28,12},{1,17},{... | collective-permute-start | bytes 12296 | tf_op jit(solution)/shard_map/ppermute | solution.py:35
  26.4 11.5 %copy-start.12 = (f32[2,8,1024]{2,1,0:T(8,128)S(1)}, f32[2,8,1024]{2,1,0:T(8,128)}, u32[]{:S(2)}) copy-start(f32[2,8,1024]{2,1,0:T(8,128)} %param.16) | copy-start | bytes 196612
  27.3 10.6 %all-to-all-start.1 = ((f32[2,32,256]{2,0,1:T(2,128)}), f32[2,32,256]{2,0,1:T(2,128)S(1)}, u32[]{:S(2)}, u32[]{:S(2)}) async-start(f32[2,32,256]{2,0,1:T(2,128)} %copy.161), calls=%async_computation.1 | async-start | bytes 131072 | tf_op jit(solution)/shard_map/all_to_all | solution.py:188
  38.4 7.8 %collective-permute-start.7 = (f32[1,16,2,32]{3,1,2,0:T(8,128)S(1)}, f32[1,16,2,32]{3,1,2,0:T(8,128)S(1)}, u32[]{:S(2)}, u32[]{:S(2)}) collective-permute-start(f32[1,16,2,32]{3,1,2,0:T(8,128)S(1)} %maximum_bitcast_fusion.1), channel_id=1, source_target_pairs={{4,0},{8,4},{12,8},{16,12},{20,16},{24,20},{28,24},{0,28},{5,1},{9... | collective-permute-start | bytes 12296 | tf_op jit(solution)/shard_map/ppermute | solution.py:26
  38.5 7.8 %collective-permute-start.6 = (f32[1,16,2,32]{3,1,2,0:T(8,128)S(1)}, f32[1,16,2,32]{3,1,2,0:T(8,128)S(1)}, u32[]{:S(2)}, u32[]{:S(2)}) collective-permute-start(f32[1,16,2,32]{3,1,2,0:T(8,128)S(1)} %maximum_bitcast_fusion.1), channel_id=1, source_target_pairs={{0,4},{4,8},{8,12},{12,16},{16,20},{20,24},{24,28},{28,0},{1,5},{5... | collective-permute-start | bytes 12296 | tf_op jit(solution)/shard_map/ppermute | solution.py:24
  39.2 7.1 %collective-permute-start.8 = (f32[16,2,32]{2,1,0:T(2,128)S(1)}, f32[16,2,32]{2,1,0:T(2,128)S(1)}, u32[]{:S(2)}, u32[]{:S(2)}) collective-permute-start(f32[16,2,32]{2,1,0:T(2,128)S(1)} %pad_maximum_fusion.1), channel_id=1, source_target_pairs={{0,16},{4,20},{8,24},{12,28},{16,0},{20,4},{24,8},{28,12},{1,17},{... | collective-permute-start | bytes 12296 | tf_op jit(solution)/shard_map/ppermute | solution.py:35
  43.0 8.9 %all-to-all-start.2 = ((bf16[4,2,2048]{2,1,0:T(2,128)(2,1)}), bf16[4,2,2048]{2,1,0:T(2,128)(2,1)S(1)}, u32[]{:S(2)}, u32[]{:S(2)}) async-start(bf16[4,2,2048]{2,1,0:T(2,128)(2,1)} %reshape.432), calls=%async_computation.2 | async-start | bytes 65536 | tf_op jit(solution)/shard_map/all_to_all | solution.py:183
  52.9 2.6 %copy-start.18 = (bf16[2,4,8,256]{3,2,1,0:T(8,128)(2,1)}, bf16[2,4,8,256]{3,2,1,0:T(8,128)(2,1)S(1)}, u32[]{:S(2)}) copy-start(bf16[2,4,8,256]{3,2,1,0:T(8,128)(2,1)S(1)} %copy.167) | copy-start | bytes 98308
  53.2 2.3 %copy-start.8 = (f32[640,256]{0,1:T(8,128)}, f32[640,256]{0,1:T(8,128)S(1)}, u32[]{:S(2)}) copy-start(f32[640,256]{0,1:T(8,128)S(1)} %fusion.3) | copy-start | bytes 1966084
  53.2 2.3 %copy-start.15 = (bf16[640,64]{0,1:T(8,128)(2,1)S(1)}, bf16[640,64]{0,1:T(8,128)(2,1)}, u32[]{:S(2)}) copy-start(bf16[640,64]{0,1:T(8,128)(2,1)} %param.24) | copy-start | bytes 245764
  53.2 7.1 %copy-start.4 = (f32[16,31,32]{2,1,0:T(8,128)S(1)}, f32[16,31,32]{2,1,0:T(8,128)}, u32[]{:S(2)}) copy-start(f32[16,31,32]{2,1,0:T(8,128)} %get-tuple-element.78) | copy-start | bytes 190468
  55.5 11.5 %copy-start.23 = (f32[1024]{0:T(1024)S(1)}, f32[1024]{0:T(1024)}, u32[]{:S(2)}) copy-start(f32[1024]{0:T(1024)} %convert_element_type.68) | copy-start | bytes 12292
  56.4 9.7 %all-to-all-start.3 = ((f32[2,32,256]{2,0,1:T(2,128)}), f32[2,32,256]{2,0,1:T(2,128)}, u32[]{:S(2)}, u32[]{:S(2)}) async-start(f32[2,32,256]{2,0,1:T(2,128)} %copy.168), calls=%async_computation.3 | async-start | bytes 131072 | tf_op jit(solution)/shard_map/all_to_all | solution.py:188
  69.0 6.7 %collective-permute-start.10 = (f32[1,16,2,32]{3,1,2,0:T(8,128)S(1)}, f32[1,16,2,32]{3,1,2,0:T(8,128)S(1)}, u32[]{:S(2)}, u32[]{:S(2)}) collective-permute-start(f32[1,16,2,32]{3,1,2,0:T(8,128)S(1)} %maximum_bitcast_fusion.2), channel_id=1, source_target_pairs={{4,0},{8,4},{12,8},{16,12},{20,16},{24,20},{28,24},{0,28},{5,1},{9... | collective-permute-start | bytes 12296 | tf_op jit(solution)/shard_map/ppermute | solution.py:26
  69.1 6.2 %collective-permute-start.9 = (f32[1,16,2,32]{3,1,2,0:T(8,128)S(1)}, f32[1,16,2,32]{3,1,2,0:T(8,128)S(1)}, u32[]{:S(2)}, u32[]{:S(2)}) collective-permute-start(f32[1,16,2,32]{3,1,2,0:T(8,128)S(1)} %maximum_bitcast_fusion.2), channel_id=1, source_target_pairs={{0,4},{4,8},{8,12},{12,16},{16,20},{20,24},{24,28},{28,0},{1,5},{5... | collective-permute-start | bytes 12296 | tf_op jit(solution)/shard_map/ppermute | solution.py:24
  69.7 5.5 %collective-permute-start.11 = (f32[16,2,32]{2,1,0:T(2,128)S(1)}, f32[16,2,32]{2,1,0:T(2,128)S(1)}, u32[]{:S(2)}, u32[]{:S(2)}) collective-permute-start(f32[16,2,32]{2,1,0:T(2,128)S(1)} %pad_maximum_fusion.2), channel_id=1, source_target_pairs={{0,16},{4,20},{8,24},{12,28},{16,0},{20,4},{24,8},{28,12},{1,17},{... | collective-permute-start | bytes 12296 | tf_op jit(solution)/shard_map/ppermute | solution.py:35
  71.9 10.0 %copy-start.16 = (bf16[640,64]{0,1:T(8,128)(2,1)S(1)}, bf16[640,64]{0,1:T(8,128)(2,1)}, u32[]{:S(2)}) copy-start(bf16[640,64]{0,1:T(8,128)(2,1)} %param.24) | copy-start | bytes 245764
  71.9 9.0 %all-to-all-start.4 = ((bf16[4,2,2048]{2,1,0:T(2,128)(2,1)}), bf16[4,2,2048]{2,1,0:T(2,128)(2,1)S(1)}, u32[]{:S(2)}, u32[]{:S(2)}) async-start(bf16[4,2,2048]{2,1,0:T(2,128)(2,1)} %reshape.434), calls=%async_computation.4 | async-start | bytes 65536 | tf_op jit(solution)/shard_map/all_to_all | solution.py:183
  83.9 11.7 %copy-start.11 = (f32[2,8,1024]{2,1,0:T(8,128)S(1)}, f32[2,8,1024]{2,1,0:T(8,128)}, u32[]{:S(2)}) copy-start(f32[2,8,1024]{2,1,0:T(8,128)} %copy-done.10) | copy-start | bytes 196612
  85.6 15.4 %copy-start.19 = (bf16[2,4,8,256]{3,2,1,0:T(8,128)(2,1)S(1)}, bf16[2,4,8,256]{3,2,1,0:T(8,128)(2,1)}, u32[]{:S(2)}) copy-start(bf16[2,4,8,256]{3,2,1,0:T(8,128)(2,1)} %copy-done.18) | copy-start | bytes 98308
  85.8 22.1 %copy-start.17 = (bf16[640,64]{0,1:T(8,128)(2,1)S(1)}, bf16[640,64]{0,1:T(8,128)(2,1)}, u32[]{:S(2)}) copy-start(bf16[640,64]{0,1:T(8,128)(2,1)} %param.24) | copy-start | bytes 245764
  86.5 9.0 %all-to-all-start.5 = ((f32[2,32,256]{2,0,1:T(2,128)}), f32[2,32,256]{2,0,1:T(2,128)S(1)}, u32[]{:S(2)}, u32[]{:S(2)}) async-start(f32[2,32,256]{2,0,1:T(2,128)} %copy.175), calls=%async_computation.5 | async-start | bytes 131072 | tf_op jit(solution)/shard_map/all_to_all | solution.py:188
  97.7 8.9 %all-to-all-start.6 = ((bf16[4,2,2048]{2,1,0:T(2,128)(2,1)}), bf16[4,2,2048]{2,1,0:T(2,128)(2,1)S(1)}, u32[]{:S(2)}, u32[]{:S(2)}) async-start(bf16[4,2,2048]{2,1,0:T(2,128)(2,1)} %reshape.436), calls=%async_computation.6 | async-start | bytes 65536 | tf_op jit(solution)/shard_map/all_to_all | solution.py:183
  107.9 2.8 %copy-start.21 = (bf16[2,4,8,256]{3,2,1,0:T(8,128)(2,1)}, bf16[2,4,8,256]{3,2,1,0:T(8,128)(2,1)S(1)}, u32[]{:S(2)}) copy-start(bf16[2,4,8,256]{3,2,1,0:T(8,128)(2,1)S(1)} %copy.181) | copy-start | bytes 98308
  119.1 3.0 %collective-permute-start.15 = (f32[416,640]{1,0:T(8,128)}, f32[416,640]{1,0:T(8,128)}, u32[]{:S(2)}, u32[]{:S(2)}) collective-permute-start(f32[416,640]{1,0:T(8,128)} %dynamic-slice_bitcast_fusion), channel_id=1, source_target_pairs={{0,4},{4,0},{8,12},{12,8},{16,20},{20,16},{24,28},{28,24},{1,5},{5... | collective-permute-start | bytes 3194888 | tf_op jit(solution)/shard_map/ppermute | solution.py:118
  123.8 16.8 %copy-start.13 = (f32[2,8,1024]{2,1,0:T(8,128)S(1)}, f32[2,8,1024]{2,1,0:T(8,128)}, u32[]{:S(2)}) copy-start(f32[2,8,1024]{2,1,0:T(8,128)} %get-tuple-element.57) | copy-start | bytes 196612
  123.8 9.3 %collective-permute-start.16 = (f32[208,640]{1,0:T(8,128)S(1)}, f32[208,640]{1,0:T(8,128)S(1)}, u32[]{:S(2)}, u32[]{:S(2)}) collective-permute-start(f32[208,640]{1,0:T(8,128)S(1)} %dynamic-slice_bitcast_fusion.1), channel_id=1, source_target_pairs={{0,8},{4,20},{8,0},{12,28},{16,24},{20,4},{24,16},{28,12},{1,9},{5... | collective-permute-start | bytes 1597448 | tf_op jit(solution)/shard_map/ppermute | solution.py:118
  133.3 6.5 %collective-permute-start.17 = (f32[104,640]{1,0:T(8,128)S(1)}, f32[104,640]{1,0:T(8,128)S(1)}, u32[]{:S(2)}, u32[]{:S(2)}) collective-permute-start(f32[104,640]{1,0:T(8,128)S(1)} %dynamic-slice_bitcast_fusion.2), channel_id=1, source_target_pairs={{0,16},{4,12},{8,24},{12,4},{16,0},{20,28},{24,8},{28,20},{1,17},{... | collective-permute-start | bytes 798728 | tf_op jit(solution)/shard_map/ppermute | solution.py:118
  139.8 6.8 %collective-permute-start.18 = (f32[104,640]{1,0:T(8,128)S(1)}, f32[104,640]{1,0:T(8,128)S(1)}, u32[]{:S(2)}, u32[]{:S(2)}) collective-permute-start(f32[104,640]{1,0:T(8,128)S(1)} %bitcast_add_fusion.2), channel_id=1, source_target_pairs={{0,1},{1,0},{2,3},{3,2},{4,5},{5,4},{6,7},{7,6},{8,9},{9,8},{10,11... | collective-permute-start | bytes 798728 | tf_op jit(solution)/shard_map/ppermute | solution.py:118
  146.6 12.5 %collective-permute-start.19 = (f32[104,640]{1,0:T(8,128)S(1)}, f32[104,640]{1,0:T(8,128)S(1)}, u32[]{:S(2)}, u32[]{:S(2)}) collective-permute-start(f32[104,640]{1,0:T(8,128)S(1)} %add.383), channel_id=1, source_target_pairs={{0,2},{1,3},{2,0},{3,1},{4,6},{5,7},{6,4},{7,5},{8,10},{9,11},{10,... | collective-permute-start | bytes 798728 | tf_op jit(solution)/shard_map/ppermute | solution.py:118
  159.1 6.7 %collective-permute-start.20 = (f32[104,640]{1,0:T(8,128)S(1)}, f32[104,640]{1,0:T(8,128)S(1)}, u32[]{:S(2)}, u32[]{:S(2)}) collective-permute-start(f32[104,640]{1,0:T(8,128)S(1)} %add.384), channel_id=1, source_target_pairs={{0,16},{4,12},{8,24},{12,4},{16,0},{20,28},{24,8},{28,20},{1,17},{... | collective-permute-start | bytes 798728 | tf_op jit(solution)/shard_map/ppermute | solution.py:118
  160.7 15.8 %collective-permute-start.13 = (f32[1,16,2,32]{3,1,2,0:T(8,128)S(1)}, f32[1,16,2,32]{3,1,2,0:T(8,128)S(1)}, u32[]{:S(2)}, u32[]{:S(2)}) collective-permute-start(f32[1,16,2,32]{3,1,2,0:T(8,128)S(1)} %maximum_bitcast_fusion.3), channel_id=1, source_target_pairs={{4,0},{8,4},{12,8},{16,12},{20,16},{24,20},{28,24},{0,28},{5,1},{9... | collective-permute-start | bytes 12296 | tf_op jit(solution)/shard_map/ppermute | solution.py:26
  160.9 14.4 %collective-permute-start.12 = (f32[1,16,2,32]{3,1,2,0:T(8,128)S(1)}, f32[1,16,2,32]{3,1,2,0:T(8,128)S(1)}, u32[]{:S(2)}, u32[]{:S(2)}) collective-permute-start(f32[1,16,2,32]{3,1,2,0:T(8,128)S(1)} %maximum_bitcast_fusion.3), channel_id=1, source_target_pairs={{0,4},{4,8},{8,12},{12,16},{16,20},{20,24},{24,28},{28,0},{1,5},{5... | collective-permute-start | bytes 12296 | tf_op jit(solution)/shard_map/ppermute | solution.py:24
  165.8 9.3 %collective-permute-start.21 = (f32[208,640]{1,0:T(8,128)S(1)}, f32[208,640]{1,0:T(8,128)S(1)}, u32[]{:S(2)}, u32[]{:S(2)}) collective-permute-start(f32[208,640]{1,0:T(8,128)S(1)} %bitcast.194), channel_id=1, source_target_pairs={{0,8},{4,20},{8,0},{12,28},{16,24},{20,4},{24,16},{28,12},{1,9},{5... | collective-permute-start | bytes 1597448 | tf_op jit(solution)/shard_map/ppermute | solution.py:118
  166.7 8.6 %collective-permute-start.14 = (f32[16,2,32]{2,1,0:T(2,128)S(1)}, f32[16,2,32]{2,1,0:T(2,128)S(1)}, u32[]{:S(2)}, u32[]{:S(2)}) collective-permute-start(f32[16,2,32]{2,1,0:T(2,128)S(1)} %pad_maximum_fusion.3), channel_id=1, source_target_pairs={{0,16},{4,20},{8,24},{12,28},{16,0},{20,4},{24,8},{28,12},{1,17},{... | collective-permute-start | bytes 12296 | tf_op jit(solution)/shard_map/ppermute | solution.py:35
  168.9 8.5 %copy-start.2 = (bf16[640,256]{0,1:T(8,128)(2,1)S(1)}, bf16[640,256]{0,1:T(8,128)(2,1)}, u32[]{:S(2)}) copy-start(bf16[640,256]{0,1:T(8,128)(2,1)} %get-tuple-element.114) | copy-start | bytes 983044
  175.3 12.8 %collective-permute-start.22 = (f32[416,640]{1,0:T(8,128)S(1)}, f32[416,640]{1,0:T(8,128)S(1)}, u32[]{:S(2)}, u32[]{:S(2)}) collective-permute-start(f32[416,640]{1,0:T(8,128)S(1)} %bitcast.190), channel_id=1, source_target_pairs={{0,4},{4,0},{8,12},{12,8},{16,20},{20,16},{24,28},{28,24},{1,5},{5... | collective-permute-start | bytes 3194888 | tf_op jit(solution)/shard_map/ppermute | solution.py:118
  178.3 9.0 %all-to-all-start.7 = ((f32[2,32,256]{2,0,1:T(2,128)}), f32[2,32,256]{2,0,1:T(2,128)S(1)}, u32[]{:S(2)}, u32[]{:S(2)}) async-start(f32[2,32,256]{2,0,1:T(2,128)} %copy.182), calls=%async_computation.7 | async-start | bytes 131072 | tf_op jit(solution)/shard_map/all_to_all | solution.py:188
  (11 other events, 19.9 us)

commit v2 on v1

v2 whole, which is shorter than its diff:
```python
import functools

import jax
import jax.numpy as jnp
from jax import lax
from jax.experimental import pallas as pl
from jax.experimental.pallas import tpu as pltpu
from jax.sharding import PartitionSpec as P

TILE_SIDE = 32
LEVELS = 32
FEATURES = 64
TILE_CELLS = 1024
TRACERS = 2
LANES = 128

diffuse_coef = 0.2
step_size = 0.5


def pairings(tiles, depths):
    def at(t, d):
        return (t % tiles) * depths + d

    folds, rows, insides, outsides = [], [], [], []
    for t in range(tiles):
        for d in range(depths):
            me = at(t, d)
            ends = d in (0, depths - 1)
            folds.append((me, at(t + tiles // 2, d) if ends else at(t, d + 1 if d % 2 else d - 1)))
            rows.append((me, at(t, d - 1 if d % 2 else d + 1)))
            insides.append((me, at(t - 1 if t % 2 else t + 1, d)))
            outsides.append((me, at(t + 1 if t % 2 else t - 1, d)))
    return folds, rows, insides, outsides


def lane_of(shape):
    return lax.broadcasted_iota(jnp.int32, shape, 1)


def place_of(info):
    depth, last, tile = info[0], info[1], info[2]
    even_depth = depth % 2 == 0
    at_end = (depth == 0) | (depth == last)
    even_tile = tile % 2 == 0
    return even_depth, at_end, even_tile


def edges_of(scaled, info):
    even_depth, at_end, even_tile = place_of(info)
    half = scaled.shape[1] // 2
    lane = lane_of((scaled.shape[0], half))
    bottom = scaled[:, :half]
    top = pltpu.roll(scaled[:, half:], TILE_SIDE, 1)
    first = jnp.where(even_depth, bottom, top)
    second = jnp.where(even_depth, top, bottom)
    mirrored = first
    bit = 1
    while bit < TILE_SIDE:
        up = pltpu.roll(mirrored, bit, 1)
        down = pltpu.roll(mirrored, half - bit, 1)
        mirrored = jnp.where((lane & bit) != 0, up, down)
        bit *= 2
    first = jnp.where(at_end, mirrored, first)
    whole = scaled.shape[1]
    east = pltpu.roll(scaled, whole - (TILE_SIDE - 1), 1)

    def squeezed(cells):
        return jnp.where(lane % TILE_SIDE == 0, cells[:, :half], pltpu.roll(cells[:, half:], 1, 1))

    inside = squeezed(jnp.where(even_tile, east, scaled))
    outside = squeezed(jnp.where(even_tile, scaled, east))
    return first, second, inside, outside


def neighbour_sum(scaled, received, info):
    even_depth, _, even_tile = place_of(info)
    first, second, inside, outside = received
    whole = scaled.shape[1]
    half = whole // 2
    lane = lane_of(scaled.shape)
    place = lane % TILE_SIDE
    south = jnp.where(even_depth, first, second)
    north = pltpu.roll(jnp.where(even_depth, second, first), half - TILE_SIDE, 1)
    west = jnp.where(even_tile, outside, inside)
    east = jnp.where(even_tile, inside, outside)
    west = jnp.concatenate([west, pltpu.roll(west, half - 1, 1)], axis=1)
    east = jnp.concatenate([east, pltpu.roll(east, half - 1, 1)], axis=1)
    east = pltpu.roll(east, TILE_SIDE - 1, 1)
    south = jnp.concatenate([south, south], axis=1)
    north = jnp.concatenate([north, north], axis=1)
    west_cells = jnp.where(place == 0, west, pltpu.roll(scaled, 1, 1))
    east_cells = jnp.where(place == TILE_SIDE - 1, east, pltpu.roll(scaled, whole - 1, 1))
    south_cells = jnp.where(lane < TILE_SIDE, south, pltpu.roll(scaled, TILE_SIDE, 1))
    north_cells = jnp.where(lane >= whole - TILE_SIDE, north, pltpu.roll(scaled, whole - TILE_SIDE, 1))
    return west_cells + east_cells + south_cells + north_cells


def diffused(field, weight, weight_sums, received, info):
    sums = neighbour_sum(field * weight, received, info)
    return weight * (sums - field * weight_sums)


def mask_of(weight):
    return jnp.where(weight > 0.0, 1.0, 0.0)


def split_kernel(info, state_ref, observed_ref, *message_refs):
    depth = info[0]
    rows = state_ref.shape[0]
    width = message_refs[0].shape[1]
    for k, message_ref in enumerate(message_refs):
        start = pl.multiple_of((depth ^ k) * width, width)
        message_ref[:rows, :] = state_ref[:, pl.ds(start, width)]
        message_ref[rows:, :] = observed_ref[:, pl.ds(start, width)]


def gather_kernel(depths, info, edge_ref, land_ref, *refs):
    message_refs = refs[:depths]
    state_ref, observed_ref, weight_ref = refs[depths : depths + 3]
    edge_refs = refs[depths + 3 : depths + 7]
    held = refs[depths + 7]
    depth = info[0]
    width = state_ref.shape[1]
    levels = LEVELS // depths
    for k in range(depths):
        held[depth ^ k] = message_refs[k][...]
    for tracer in range(TRACERS):
        for d in range(depths):
            to = tracer * LEVELS + d * levels
            at = tracer * levels
            state_ref[to : to + levels, :] = held[d, at : at + levels, :]
            at = (TRACERS + tracer) * levels
            observed_ref[to : to + levels, :] = held[d, at : at + levels, :]
    start = pl.multiple_of(depth * width, width)
    land = land_ref[:, pl.ds(start, width)].astype(jnp.float32)
    weight = edge_ref[:, pl.ds(start, width)] * land
    weight_rows = jnp.broadcast_to(weight, weight_ref.shape)
    weight_ref[...] = weight_rows
    scaled = jnp.concatenate([state_ref[...] * weight, weight_rows], axis=0)
    for edge_out, edge in zip(edge_refs, edges_of(scaled, info)):
        edge_out[...] = edge


def sigmoid(z):
    return 0.5 * jnp.tanh(0.5 * z) + 0.5


def contract(a, b, dims):
    return lax.dot_general(a, b, ((dims[:1], dims[1:]), ((), ())), preferred_element_type=jnp.float32)


def forward_kernel(state_ref, w_in, b_in, w_mid, b_mid, w_out_t, b_out, q_ref, one_ref, slope_one_ref, two_ref, slope_two_ref):
    inputs = state_ref[...].astype(jnp.bfloat16)
    pre_one = contract(inputs, w_in[...], (0, 0)) + b_in[...]
    gate = sigmoid(pre_one)
    hidden = pre_one * gate
    slope_one_ref[...] = gate + hidden * (1.0 - gate)
    hidden_one = hidden.astype(jnp.bfloat16)
    one_ref[...] = hidden_one
    pre_two = contract(hidden_one, w_mid[...], (1, 0)) + b_mid[...]
    gate = sigmoid(pre_two)
    hidden = pre_two * gate
    slope_two_ref[...] = gate + hidden * (1.0 - gate)
    hidden_two = hidden.astype(jnp.bfloat16)
    two_ref[...] = hidden_two
    bias = b_out[...]
    bias = jnp.concatenate([bias, bias], axis=1)
    q_ref[...] = contract(w_out_t[...], hidden_two, (1, 1)) + bias


def first_step_kernel(info, state_ref, weight_ref, q_ref, e0, e1, e2, e3, next_ref, sums_ref, o0, o1, o2, o3):
    weight = weight_ref[0:1, :]
    state = state_ref[...]
    received = (e0[...], e1[...], e2[...], e3[...])
    scaled = jnp.concatenate([state * weight, weight_ref[...]], axis=0)
    sums = neighbour_sum(scaled, received, info)
    weight_sums = sums[FEATURES:, :]
    sums_ref[...] = weight_sums
    change = weight * (sums[:FEATURES, :] - state * weight_sums[0:1, :])
    state = state + diffuse_coef * change + step_size * mask_of(weight) * q_ref[...]
    next_ref[...] = state
    for edge_out, edge in zip((o0, o1, o2, o3), edges_of(state * weight, info)):
        edge_out[...] = edge


def last_step_kernel(
    info, state_ref, weight_ref, sums_ref, q_ref, observed_ref, e0, e1, e2, e3, next_ref, adjoint_ref, upstream_ref, o0, o1, o2, o3
):
    weight = weight_ref[0:1, :]
    mask = mask_of(weight)
    state = state_ref[...]
    received = (e0[...], e1[...], e2[...], e3[...])
    change = diffused(state, weight, sums_ref[0:1, :], received, info)
    state = state + diffuse_coef * change + step_size * mask * q_ref[...]
    next_ref[...] = state
    adjoint = mask * (state - observed_ref[...])
    adjoint_ref[...] = adjoint
    upstream_ref[...] = (step_size * mask * adjoint).astype(jnp.bfloat16)
    for edge_out, edge in zip((o0, o1, o2, o3), edges_of(adjoint * weight, info)):
        edge_out[...] = edge


def adjoint_kernel(info, adjoint_ref, weight_ref, sums_ref, back_ref, e0, e1, e2, e3, next_ref, upstream_ref, o0, o1, o2, o3):
    weight = weight_ref[0:1, :]
    adjoint = adjoint_ref[...]
    received = (e0[...], e1[...], e2[...], e3[...])
    adjoint = adjoint + diffuse_coef * diffused(adjoint, weight, sums_ref[0:1, :], received, info) + back_ref[...]
    next_ref[...] = adjoint
    upstream_ref[...] = (step_size * mask_of(weight) * adjoint).astype(jnp.bfloat16)
    for edge_out, edge in zip((o0, o1, o2, o3), edges_of(adjoint * weight, info)):
        edge_out[...] = edge


def end_kernel(depths, info, adjoint_ref, weight_ref, sums_ref, back_ref, final_ref, e0, e1, e2, e3, *refs):
    message_refs = refs[:depths]
    held = refs[depths]
    depth = info[0]
    weight = weight_ref[0:1, :]
    adjoint = adjoint_ref[...]
    received = (e0[...], e1[...], e2[...], e3[...])
    held[...] = adjoint + diffuse_coef * diffused(adjoint, weight, sums_ref[0:1, :], received, info) + back_ref[...]
    levels = LEVELS // depths
    for k in range(depths):
        for tracer in range(TRACERS):
            start = pl.multiple_of(tracer * LEVELS + (depth ^ k) * levels, levels)
            at = tracer * levels
            message_refs[k][at : at + levels, :] = final_ref[pl.ds(start, levels), :]
            at = (TRACERS + tracer) * levels
            message_refs[k][at : at + levels, :] = held[pl.ds(start, levels), :]


def join_kernel(depths, info, *refs):
    message_refs = refs[:depths]
    final_ref, sensitivity_ref = refs[depths:]
    depth = info[0]
    rows = final_ref.shape[0]
    width = message_refs[0].shape[1]
    for k, message_ref in enumerate(message_refs):
        start = pl.multiple_of((depth ^ k) * width, width)
        final_ref[:, pl.ds(start, width)] = message_ref[:rows, :]
        sensitivity_ref[:, pl.ds(start, width)] = message_ref[rows:, :]


CHUNKS = 8


def backward_kernel(with_sum, *refs):
    state_ref, upstream_ref, one_ref, slope_one_ref, two_ref, slope_two_ref, w_in, w_mid, w_out_t = refs[:9]
    if with_sum:
        earlier_ref, back_ref, total_ref = refs[9:]
    else:
        back_ref, total_ref = refs[9:]
    features = FEATURES
    width = w_mid.shape[0]
    mid_rows = width // CHUNKS
    side_rows = features // CHUNKS

    def store(first_row, rows, matrix):
        for c in range(CHUNKS):
            piece = matrix[c * rows : (c + 1) * rows, :]
            if with_sum:
                piece = piece + earlier_ref[c, first_row : first_row + rows, :]
            total_ref[c, first_row : first_row + rows, :] = piece

    upstream = upstream_ref[...]
    inputs = state_ref[...].astype(jnp.bfloat16)
    ones = jnp.ones((8, upstream.shape[1]), jnp.bfloat16)
    slope_two = (contract(upstream, w_out_t[...], (0, 0)) * slope_two_ref[...]).astype(jnp.bfloat16)
    slope_one = (contract(slope_two, w_mid[...], (1, 1)) * slope_one_ref[...]).astype(jnp.bfloat16)
    back_ref[...] = contract(w_in[...], slope_one, (1, 1))
    store(0, mid_rows, contract(one_ref[...], slope_two, (0, 0)))
    store(mid_rows, side_rows, contract(inputs, slope_one, (1, 0)))
    store(mid_rows + side_rows, side_rows, contract(upstream, two_ref[...], (1, 0)))
    bias_in = contract(ones, slope_one, (1, 0))
    bias_mid = contract(ones, slope_two, (1, 0))
    bias_out = contract(ones, upstream, (1, 1))
    bias_out = jnp.concatenate([bias_out, jnp.zeros((8, width - features), jnp.float32)], axis=1)
    first_row = mid_rows + 2 * side_rows
    for c in range(CHUNKS):
        rows = (bias_in, bias_mid, bias_out)[c] if c < 3 else jnp.zeros((8, width), jnp.float32)
        if with_sum:
            rows = rows + earlier_ref[c, first_row : first_row + 8, :]
        total_ref[c, first_row : first_row + 8, :] = rows


def spec_of(shape, dtype=jnp.float32):
    return jax.ShapeDtypeStruct(shape, dtype)


def called(kernel, outs, info, args, scratch=(), name=None):
    smem = pl.BlockSpec(memory_space=pltpu.SMEM)
    vmem = pl.BlockSpec(memory_space=pltpu.VMEM)
    in_specs = [smem] * len(info) + [vmem] * len(args)
    return pl.pallas_call(
        kernel,
        out_shape=tuple(outs),
        in_specs=in_specs,
        out_specs=tuple(vmem for _ in outs),
        scratch_shapes=list(scratch),
        compiler_params=pltpu.CompilerParams(vmem_limit_bytes=40 * 1024 * 1024),
        name=name,
    )(*info, *args)


def is_power_of_two(count):
    return count & (count - 1) == 0


def swapped(x, axis, even_bit, odd_bit):
    length = lax.axis_size(axis)
    return lax.ppermute(x, axis, [(i, i ^ (odd_bit if i & 1 else even_bit)) for i in range(length)])


def tile_rounds(length):
    bits = [1 << k for k in range(length.bit_length() - 1)]
    rounds = [(bits[0], bits[0])] if bits else []
    rest = bits[1:]
    for k in range(len(rest)):
        rounds.append((rest[k], rest[(k + 1) % len(rest)]))
    return rounds


def all_summed(block):
    tiles = lax.axis_size("tile")
    depths = lax.axis_size("depth")
    if not (is_power_of_two(tiles) and is_power_of_two(depths) and tiles <= CHUNKS):
        return lax.psum(block, ("tile", "depth"))
    tail = block.shape[1:]
    tile = lax.axis_index("tile")
    rounds = tile_rounds(tiles)
    sides = []
    for even_bit, odd_bit in rounds:
        bit = jnp.where(tile & 1 == 1, odd_bit, even_bit)
        sides.append(((tile & bit) != 0).astype(jnp.int32))
    for (even_bit, odd_bit), side in zip(rounds, sides):
        halves = block.reshape(2, block.shape[0] // 2, *tail)
        sent = lax.dynamic_index_in_dim(halves, 1 - side, 0, False)
        kept = lax.dynamic_index_in_dim(halves, side, 0, False)
        block = kept + swapped(sent, "tile", even_bit, odd_bit)
    bit = 1
    while bit < depths:
        block = block + swapped(block, "depth", bit, bit)
        bit *= 2
    for (even_bit, odd_bit), side in zip(reversed(rounds), reversed(sides)):
        other = swapped(block, "tile", even_bit, odd_bit)
        block = jnp.where(side == 0, jnp.stack([block, other]), jnp.stack([other, block]))
        block = block.reshape(block.shape[0] * block.shape[1], *tail)
    return block


def body(initial_state, observed, edge_weight, land, w_in, b_in, w_mid, b_mid, w_out, b_out):
    tiles = lax.axis_size("tile")
    depths = lax.axis_size("depth")
    tile = lax.axis_index("tile")
    depth = lax.axis_index("depth")
    info = (jnp.stack([depth, jnp.int32(depths - 1), tile]).astype(jnp.int32),)
    width = w_mid.shape[0]
    cells = TILE_CELLS // depths
    levels = LEVELS // depths
    rows = TRACERS * levels
    ways = pairings(tiles, depths)

    def exchanged(edges):
        return tuple(lax.ppermute(edge, ("tile", "depth"), way) for edge, way in zip(edges, ways))

    def across_depth(messages):
        out = [messages[0]]
        for k in range(1, depths):
            out.append(swapped(messages[k], "depth", k, k))
        return tuple(out)

    bias_in = b_in.reshape(1, width)
    bias_mid = b_mid.reshape(1, width)
    bias_out = jnp.broadcast_to(b_out[:, None], (FEATURES, LANES))
    w_out_t = w_out.T
    weights = (w_in, bias_in, w_mid, bias_mid, w_out_t, bias_out)
    field = spec_of((FEATURES, cells))
    half_field = spec_of((FEATURES, cells), jnp.bfloat16)
    edge = spec_of((FEATURES, LANES))
    cached = (
        field,
        spec_of((cells, width), jnp.bfloat16),
        spec_of((cells, width)),
        spec_of((cells, width), jnp.bfloat16),
        spec_of((cells, width)),
    )

    def closure(state):
        return called(forward_kernel, cached, (), (state, *weights), name="closure")

    message = spec_of((2 * rows, cells))
    messages = called(
        split_kernel,
        [message] * depths,
        info,
        (initial_state.reshape(rows, TILE_CELLS), observed.reshape(rows, TILE_CELLS)),
        name="split",
    )
    messages = across_depth(messages)
    first_edge = spec_of((FEATURES + 8, LANES))
    state_0, target, weight, *edges = called(
        functools.partial(gather_kernel, depths),
        (field, field, spec_of((8, cells)), first_edge, first_edge, first_edge, first_edge),
        info,
        (edge_weight.reshape(1, TILE_CELLS), land.reshape(1, TILE_CELLS), *messages),
        scratch=[pltpu.VMEM((depths, 2 * rows, cells), jnp.float32)],
        name="gather",
    )
    edges = exchanged(edges)
    q, *cache_0 = closure(state_0)
    state_1, weight_sums, *edges = called(
        first_step_kernel,
        (field, spec_of((8, cells)), edge, edge, edge, edge),
        info,
        (state_0, weight, q, *edges),
        name="step",
    )
    edges = exchanged(edges)
    q, *cache_1 = closure(state_1)
    state_2, adjoint, upstream, *edges = called(
        last_step_kernel,
        (field, field, half_field, edge, edge, edge, edge),
        info,
        (state_1, weight, weight_sums, q, target, *edges),
        name="last_step",
    )
    edges = exchanged(edges)
    total = spec_of((CHUNKS, width // CHUNKS + 2 * (FEATURES // CHUNKS) + 8, width))
    back, grads = called(
        functools.partial(backward_kernel, False),
        (field, total),
        (),
        (state_1, upstream, *cache_1, w_in, w_mid, w_out_t),
        name="backward",
    )
    adjoint, upstream, *edges = called(
        adjoint_kernel,
        (field, half_field, edge, edge, edge, edge),
        info,
        (adjoint, weight, weight_sums, back, *edges),
        name="adjoint",
    )
    edges = exchanged(edges)
    back, grads = called(
        functools.partial(backward_kernel, True),
        (field, total),
        (),
        (state_0, upstream, *cache_0, w_in, w_mid, w_out_t, grads),
        name="backward_sum",
    )
    messages = called(
        functools.partial(end_kernel, depths),
        [message] * depths,
        info,
        (adjoint, weight, weight_sums, back, state_2, *edges),
        scratch=[pltpu.VMEM((FEATURES, cells), jnp.float32)],
        name="end",
    )
    messages = across_depth(messages)
    whole = spec_of((rows, TILE_CELLS))
    final_state, sensitivity = called(functools.partial(join_kernel, depths), (whole, whole), info, messages, name="join")
    grads = all_summed(grads) * (1.0 / (tiles * TILE_CELLS))
    mid_rows = width // CHUNKS
    side_rows = FEATURES // CHUNKS
    first_row = mid_rows + 2 * side_rows
    grad_w_mid = grads[:, :mid_rows, :].reshape(width, width)
    grad_w_in = grads[:, mid_rows : mid_rows + side_rows, :].reshape(FEATURES, width)
    grad_w_out = grads[:, mid_rows + side_rows : first_row, :].reshape(FEATURES, width).T
    shape = (TRACERS, levels, TILE_CELLS)
    return (
        final_state.reshape(shape),
        sensitivity.reshape(shape),
        grad_w_in,
        grads[0, first_row],
        grad_w_mid,
        grads[1, first_row],
        grad_w_out,
        grads[2, first_row, :FEATURES],
    )


def solution(mesh):
    return jax.shard_map(
        body,
        mesh=mesh,
        in_specs=(
            P(None, "depth", "tile"),
            P(None, "depth", "tile"),
            P("tile"),
            P("tile"),
            P(),
            P(),
            P(),
            P(),
            P(),
            P(),
        ),
        out_specs=(
            P(None, "depth", "tile"),
            P(None, "depth", "tile"),
            P(),
            P(),
            P(),
            P(),
            P(),
            P(),
        ),
        check_vma=False,
    )
```

time: 193 us -> 127 us (0.66)
  starting transfers between devices: 49.9 us -> 30.1 us
  waiting for transfers between devices: 77.9 us -> 59.3 us
  matrix products: 15.8 us -> 0 us
  Pallas kernels: 0 us -> 12.5 us
  other arithmetic: 13.6 us -> 2 us
  local copies, waits for them, and re-layouts: 32.4 us -> 21 us
    all_to_all x8 -> x0, waiting for transfers between devices: 33.1 us -> none  [the longest x4 19.7 us: to_segments(): lax.all_to_all(shaped, 'depth', split_axis=1, concat_axis=2, tiled=True)]
    all_to_all x8 -> x0, starting transfers between devices: 30.1 us -> none  [the longest x4 15.3 us: to_segments(): lax.all_to_all(shaped, 'depth', split_axis=1, concat_axis=2, tiled=True)]
    dot_general x18 -> x0, matrix products: 15.8 us -> none  [the longest x2 4.36 us: closure_forward(): lax.dot_general(w_mid, hidden_one, contract_rows, preferred_element_type=...]
    ppermute x8 -> x14, waiting for transfers between devices: 43.1 us -> 56.3 us  [swapped(): lax.ppermute(x, axis, [(i, i ^ (odd_bit if i & 1 else even_bit)) for i in...]
    pallas_call x0 -> x11, Pallas kernels: none -> 12.5 us  [called(): pl.pallas_call(kernel, out_shape=tuple(outs), in_specs=in_specs, out_spec...]
    ppermute x8 -> x14, starting transfers between devices: 6.47 us -> 16.6 us  [swapped(): lax.ppermute(x, axis, [(i, i ^ (odd_bit if i & 1 else even_bit)) for i in...]
    unnamed x65 -> x68, local copies, waits for them, and re-layouts: 9.16 us -> 15.6 us
    slice x35 -> x2, local copies, waits for them, and re-layouts: 6.85 us -> 1.88 us  [the longest x1 1.27 us: body(): grad_w_mid = grads[:, :mid_rows, :].reshape(width, width)]
  transfers between devices with their start and end apart: 31 -> 30, of which waited for: 16 -> 15; matrix products, arithmetic and copies ran while one was open for 12% -> 2% of each run, Pallas kernels for 0% -> 4%
where the time goes in v2:
time: 127 us; the launch traced here: 126 us
  waiting for transfers between devices  59.3 us (47%)
  starting transfers between devices  30.1 us (24%)
  local copies, waits for them, and re-layouts  21 us (17%)
  Pallas kernels  12.5 us (10%)
  other arithmetic  2 us (2%)
    ppermute x14, waiting for transfers between devices, swapped(): lax.ppermute(x, axis, [(i, i ^ (odd_bit if i & 1 else even_bit)) for i in...  56.3 us
    ppermute x14, starting transfers between devices, swapped(): lax.ppermute(x, axis, [(i, i ^ (odd_bit if i & 1 else even_bit)) for i in...  16.6 us
    unnamed x68, local copies, waits for them, and re-layouts  15.6 us
    ppermute x16, starting transfers between devices, exchanged(): lax.ppermute(edge, ('tile', 'depth'), way)  13.6 us
    pallas_call x11, Pallas kernels, called(): pl.pallas_call(kernel, out_shape=tuple(outs), in_specs=in_specs, out_spec...  12.5 us
    ppermute x16, waiting for transfers between devices, exchanged(): lax.ppermute(edge, ('tile', 'depth'), way)  3.05 us
  transfers between devices with their start and end apart: 30, of which 15 were waited for; matrix products, arithmetic and copies ran while one was open for 2% of the time, Pallas kernels for 4%

profile of v2, /device:TPU:0, one launch (start us, length us, event | category | flops | bytes accessed | tf_op | source)
XLA Modules:
  0.0 125.9 jit_solution(9814170448934671146)
XLA Ops:
  0.7 0.8 copy-done.16
  1.6 0.8 copy-done.17
  3.0 3.1 %collective-permute-start = (f32[32,256]{1,0:T(8,128)S(1)}, f32[32,256]{1,0:T(8,128)S(1)}, u32[]{:S(2)}, u32[]{:S(2)}) collective-permute-start(f32[32,256]{1,0:T(8,128)S(1)} %get-tuple-element.59), channel_id=1, source_target_pairs={{0,1},{1,0},{2,3},{3,2},{4,5},{5,4},{6,7},{7,6},{8,9},{9,8},{10,11... | collective-permute-start | bytes 98312 | tf_op jit(solution)/shard_map/ppermute | solution.py:312
  6.1 2.6 %collective-permute-start.1 = (f32[32,256]{1,0:T(8,128)S(1)}, f32[32,256]{1,0:T(8,128)S(1)}, u32[]{:S(2)}, u32[]{:S(2)}) collective-permute-start(f32[32,256]{1,0:T(8,128)S(1)} %get-tuple-element.60), channel_id=1, source_target_pairs={{0,2},{1,3},{2,0},{3,1},{4,6},{5,7},{6,4},{7,5},{8,10},{9,11},{10,... | collective-permute-start | bytes 98312 | tf_op jit(solution)/shard_map/ppermute | solution.py:312
  8.7 2.8 %collective-permute-done.1.refs_2_ = f32[32,256]{1,0:T(8,128)S(1)} collective-permute-done((f32[32,256]{1,0:T(8,128)S(1)}, f32[32,256]{1,0:T(8,128)S(1)}, u32[]{:S(2)}, u32[]{:S(2)}) %collective-permute-start.1) | collective-permute-done | bytes 32800 | tf_op jit(solution)/shard_map/ppermute | solution.py:312
  11.5 2.9 %collective-permute-done.2.refs_3_ = f32[32,256]{1,0:T(8,128)S(1)} collective-permute-done((f32[32,256]{1,0:T(8,128)S(1)}, f32[32,256]{1,0:T(8,128)S(1)}, u32[]{:S(2)}, u32[]{:S(2)}) %collective-permute-start.2) | collective-permute-done | bytes 32800 | tf_op jit(solution)/shard_map/ppermute | solution.py:312
  15.7 1.1 gather.1
  16.8 1.6 %collective-permute-start.3 = (f32[72,128]{1,0:T(8,128)S(1)}, f32[72,128]{1,0:T(8,128)S(1)}, u32[]{:S(2)}, u32[]{:S(2)}) collective-permute-start(f32[72,128]{1,0:T(8,128)S(1)} %get-tuple-element.65), channel_id=1, source_target_pairs={{0,16},{1,2},{2,1},{3,19},{4,20},{5,6},{6,5},{7,23},{8,24},{9,10},... | collective-permute-start | bytes 110600 | tf_op jit(solution)/shard_map/ppermute | solution.py:365
  18.4 1.5 %collective-permute-start.6 = (f32[72,128]{1,0:T(8,128)S(1)}, f32[72,128]{1,0:T(8,128)S(1)}, u32[]{:S(2)}, u32[]{:S(2)}) collective-permute-start(f32[72,128]{1,0:T(8,128)S(1)} %get-tuple-element.68), channel_id=1, source_target_pairs={{0,28},{1,29},{2,30},{3,31},{4,8},{5,9},{6,10},{7,11},{8,4},{9,5},... | collective-permute-start | bytes 110600 | tf_op jit(solution)/shard_map/ppermute | solution.py:365
  22.1 1.1 copy-done
  23.2 0.9 copy-done.2
  24.1 0.9 copy-done.4
  25.0 1.0 closure.2
  27.6 1.2 step.1
  28.8 1.2 collective-permute-start.10
  30.5 1.5 %collective-permute-start.8 = (f32[64,128]{1,0:T(8,128)S(1)}, f32[64,128]{1,0:T(8,128)S(1)}, u32[]{:S(2)}, u32[]{:S(2)}) collective-permute-start(f32[64,128]{1,0:T(8,128)S(1)} %get-tuple-element.74), channel_id=1, source_target_pairs={{0,1},{1,0},{2,3},{3,2},{4,5},{5,4},{6,7},{7,6},{8,9},{9,8},{10,11... | collective-permute-start | bytes 98312 | tf_op jit(solution)/shard_map/ppermute | solution.py:365
  32.0 1.0 closure.3
  34.5 1.9 %last_step.1 = (f32[64,256]{1,0:T(8,128)S(1)}, f32[64,256]{1,0:T(8,128)S(1)}, bf16[64,256]{1,0:T(8,128)(2,1)S(1)}, f32[64,128]{1,0:T(8,128)}, f32[64,128]{1,0:T(...) custom-call(s32[3]{0:T(128)S(1)} %pad_add_fusion.info, f32[64,256]{1,0:T(8,128)S(1)} %get-tuple-element.69.state_ref.refs_0_, ...), custom_call_target="tpu_custom_call" | custom-call | tf_op jit(solution)/shard_map/last_step/pallas_call | solution.py:295
  37.0 1.4 %collective-permute-start.11 = (f32[64,128]{1,0:T(8,128)}, f32[64,128]{1,0:T(8,128)}, u32[]{:S(2)}, u32[]{:S(2)}) collective-permute-start(f32[64,128]{1,0:T(8,128)} %get-tuple-element.84), channel_id=1, source_target_pairs={{0,16},{1,2},{2,1},{3,19},{4,20},{5,6},{6,5},{7,23},{8,24},{9,10},... | collective-permute-start | bytes 98312 | tf_op jit(solution)/shard_map/ppermute | solution.py:365
  38.4 2.0 %collective-permute-start.12 = (f32[64,128]{1,0:T(8,128)}, f32[64,128]{1,0:T(8,128)}, u32[]{:S(2)}, u32[]{:S(2)}) collective-permute-start(f32[64,128]{1,0:T(8,128)} %get-tuple-element.85), channel_id=1, source_target_pairs={{0,1},{1,0},{2,3},{3,2},{4,5},{5,4},{6,7},{7,6},{8,9},{9,8},{10,11... | collective-permute-start | bytes 98312 | tf_op jit(solution)/shard_map/ppermute | solution.py:365
  41.3 1.0 copy-done.13
  42.3 1.0 copy-done.15
  43.2 1.1 backward.1
  45.1 1.5 %adjoint.1 = (f32[64,256]{1,0:T(8,128)S(1)}, bf16[64,256]{1,0:T(8,128)(2,1)S(1)}, f32[64,128]{1,0:T(8,128)S(1)}, f32[64,128]{1,0:T(8,128)S(1)}, f32[64,128]{1,0:T(8,128)S(1)}, /*index=5*/f32[64,128]{1,0:T(8,128)S(1)}) custom-call(s32[3]{0:T(128)S(1)} %pad_add_fusion.info, f32[64,256]{1,0:T(8,128)S(1)} %get-tuple-element.77.adjoint_ref, ...), custom_call_target="tpu_custom_call" | custom-call | tf_op jit(solution)/shard_map/adjoint/pallas_call | solution.py:295
  48.4 1.1 copy-done.9
  49.6 1.2 backward_sum.1
  51.4 2.8 %collective-permute-done.22 = f32[4,104,640]{2,1,0:T(8,128)} collective-permute-done((f32[4,104,640]{2,1,0:T(8,128)S(1)}, f32[4,104,640]{2,1,0:T(8,128)}, u32[]{:S(2)}, u32[]{:S(2)}) %collective-permute-start.22) | collective-permute-done | bytes 1064992 | tf_op jit(solution)/shard_map/ppermute | solution.py:312
  54.2 1.4 %bitcast_add_fusion = f32[4,104,640]{2,1,0:T(8,128)S(1)} fusion(f32[4,104,640]{2,1,0:T(8,128)} %collective-permute-done.22, f32[2,4,104,640]{3,2,1,0:T(8,128)S(1)} %bitcast.36, s32[]{:T(128)S(6)} %select_n.88), kind=kLoop, calls=%fused_computation.3 | loop fusion | flops 266240 | bytes 3194884 | tf_op jit(solution)/shard_map/add | solution.py:340
  55.6 0.9 collective-permute-start.23
  56.5 8.4 %collective-permute-done.23 = f32[2,104,640]{2,1,0:T(8,128)S(1)} collective-permute-done((f32[2,104,640]{2,1,0:T(8,128)S(1)}, f32[2,104,640]{2,1,0:T(8,128)S(1)}, u32[]{:S(2)}, u32[]{:S(2)}) %collective-permute-start.23) | collective-permute-done | bytes 532512 | tf_op jit(solution)/shard_map/ppermute | solution.py:312
  65.1 0.9 collective-permute-start.24
  66.0 5.5 %collective-permute-done.24 = f32[1,104,640]{2,1,0:T(8,128)S(1)} collective-permute-done((f32[1,104,640]{2,1,0:T(8,128)S(1)}, f32[1,104,640]{2,1,0:T(8,128)S(1)}, u32[]{:S(2)}, u32[]{:S(2)}) %collective-permute-start.24) | collective-permute-done | bytes 266272 | tf_op jit(solution)/shard_map/ppermute | solution.py:312
  72.1 6.3 %collective-permute-done.25 = f32[1,104,640]{2,1,0:T(8,128)S(1)} collective-permute-done((f32[1,104,640]{2,1,0:T(8,128)S(1)}, f32[1,104,640]{2,1,0:T(8,128)S(1)}, u32[]{:S(2)}, u32[]{:S(2)}) %collective-permute-start.25) | collective-permute-done | bytes 266272 | tf_op jit(solution)/shard_map/ppermute | solution.py:312
  78.4 1.7 %collective-permute-start.26 = (f32[1,104,640]{2,1,0:T(8,128)S(1)}, f32[1,104,640]{2,1,0:T(8,128)S(1)}, u32[]{:S(2)}, u32[]{:S(2)}) collective-permute-start(f32[1,104,640]{2,1,0:T(8,128)S(1)} %add.48), channel_id=1, source_target_pairs={{0,2},{1,3},{2,0},{3,1},{4,6},{5,7},{6,4},{7,5},{8,10},{9,11},{10,... | collective-permute-start | bytes 798728 | tf_op jit(solution)/shard_map/ppermute | solution.py:312
  80.1 10.7 %collective-permute-done.26 = f32[1,104,640]{2,1,0:T(8,128)S(1)} collective-permute-done((f32[1,104,640]{2,1,0:T(8,128)S(1)}, f32[1,104,640]{2,1,0:T(8,128)S(1)}, u32[]{:S(2)}, u32[]{:S(2)}) %collective-permute-start.26) | collective-permute-done | bytes 266272 | tf_op jit(solution)/shard_map/ppermute | solution.py:312
  90.9 1.0 collective-permute-start.27
  91.8 5.5 %collective-permute-done.27 = f32[1,104,640]{2,1,0:T(8,128)S(1)} collective-permute-done((f32[1,104,640]{2,1,0:T(8,128)S(1)}, f32[1,104,640]{2,1,0:T(8,128)S(1)}, u32[]{:S(2)}, u32[]{:S(2)}) %collective-permute-start.27) | collective-permute-done | bytes 266272 | tf_op jit(solution)/shard_map/ppermute | solution.py:312
  97.4 1.4 %collective-permute-start.28 = (f32[2,104,640]{2,1,0:T(8,128)S(1)}, f32[2,104,640]{2,1,0:T(8,128)S(1)}, u32[]{:S(2)}, u32[]{:S(2)}) collective-permute-start(f32[2,104,640]{2,1,0:T(8,128)S(1)} %maximum_select_fusion.3), channel_id=1, source_target_pairs={{0,8},{4,20},{8,0},{12,28},{16,24},{20,4},{24,16},{28,12},{1,9},{5... | collective-permute-start | bytes 1597448 | tf_op jit(solution)/shard_map/ppermute | solution.py:312
  98.9 7.8 %collective-permute-done.28 = f32[2,104,640]{2,1,0:T(8,128)S(1)} collective-permute-done((f32[2,104,640]{2,1,0:T(8,128)S(1)}, f32[2,104,640]{2,1,0:T(8,128)S(1)}, u32[]{:S(2)}, u32[]{:S(2)}) %collective-permute-start.28) | collective-permute-done | bytes 532512 | tf_op jit(solution)/shard_map/ppermute | solution.py:312
  107.5 0.9 collective-permute-start.15
  108.5 2.0 %collective-permute-start.18 = (f32[64,128]{1,0:T(8,128)S(1)}, f32[64,128]{1,0:T(8,128)S(1)}, u32[]{:S(2)}, u32[]{:S(2)}) collective-permute-start(f32[64,128]{1,0:T(8,128)S(1)} %copy-done.27), channel_id=1, source_target_pairs={{0,28},{1,29},{2,30},{3,31},{4,8},{5,9},{6,10},{7,11},{8,4},{9,5},... | collective-permute-start | bytes 98312 | tf_op jit(solution)/shard_map/ppermute | solution.py:365
  110.5 0.9 collective-permute-done.15.e0
  111.4 0.9 collective-permute-done.16.e1
  113.6 2.0 %collective-permute-start.19 = (f32[32,256]{1,0:T(8,128)S(1)}, f32[32,256]{1,0:T(8,128)S(1)}, u32[]{:S(2)}, u32[]{:S(2)}) collective-permute-start(f32[32,256]{1,0:T(8,128)S(1)} %get-tuple-element.102), channel_id=1, source_target_pairs={{0,1},{1,0},{2,3},{3,2},{4,5},{5,4},{6,7},{7,6},{8,9},{9,8},{10,11... | collective-permute-start | bytes 98312 | tf_op jit(solution)/shard_map/ppermute | solution.py:312
  115.6 2.5 %collective-permute-start.21 = (f32[32,256]{1,0:T(8,128)S(1)}, f32[32,256]{1,0:T(8,128)S(1)}, u32[]{:S(2)}, u32[]{:S(2)}) collective-permute-start(f32[32,256]{1,0:T(8,128)S(1)} %get-tuple-element.104), channel_id=1, source_target_pairs={{0,3},{1,2},{2,1},{3,0},{4,7},{5,6},{6,5},{7,4},{8,11},{9,10},{10,... | collective-permute-start | bytes 98312 | tf_op jit(solution)/shard_map/ppermute | solution.py:312
  118.1 2.7 %collective-permute-done.20.refs_2_ = f32[32,256]{1,0:T(8,128)S(1)} collective-permute-done((f32[32,256]{1,0:T(8,128)S(1)}, f32[32,256]{1,0:T(8,128)S(1)}, u32[]{:S(2)}, u32[]{:S(2)}) %collective-permute-start.20) | collective-permute-done | bytes 32800 | tf_op jit(solution)/shard_map/ppermute | solution.py:312
  121.5 1.2 join.1
  122.8 1.3 %slice.26 = f32[8,80,640]{2,1,0:T(8,128)} slice(f32[8,104,640]{2,1,0:T(8,128)S(1)} %bitcast.45), slice={[0:8], [0:80], [0:640]} | slice | bytes 3276800 | tf_op jit(solution)/shard_map/slice | solution.py:467
  (111 shorter events, 17.9 us)
Async XLA Ops:
  0.6 31.4 %copy-start.5 = (bf16[640,64]{0,1:T(8,128)(2,1)S(1)}, bf16[640,64]{0,1:T(8,128)(2,1)}, u32[]{:S(2)}) copy-start(bf16[640,64]{0,1:T(8,128)(2,1)} %param.18) | copy-start | bytes 245764
  0.6 31.4 %copy-start.3 = (bf16[64,640]{1,0:T(8,128)(2,1)S(1)}, bf16[64,640]{1,0:T(8,128)(2,1)}, u32[]{:S(2)}) copy-start(bf16[64,640]{1,0:T(8,128)(2,1)} %refs_6_.3) | copy-start | bytes 245764
  3.0 5.7 %collective-permute-start = (f32[32,256]{1,0:T(8,128)S(1)}, f32[32,256]{1,0:T(8,128)S(1)}, u32[]{:S(2)}, u32[]{:S(2)}) collective-permute-start(f32[32,256]{1,0:T(8,128)S(1)} %get-tuple-element.59), channel_id=1, source_target_pairs={{0,1},{1,0},{2,3},{3,2},{4,5},{5,4},{6,7},{7,6},{8,9},{9,8},{10,11... | collective-permute-start | bytes 98312 | tf_op jit(solution)/shard_map/ppermute | solution.py:312
  6.1 5.4 %collective-permute-start.1 = (f32[32,256]{1,0:T(8,128)S(1)}, f32[32,256]{1,0:T(8,128)S(1)}, u32[]{:S(2)}, u32[]{:S(2)}) collective-permute-start(f32[32,256]{1,0:T(8,128)S(1)} %get-tuple-element.60), channel_id=1, source_target_pairs={{0,2},{1,3},{2,0},{3,1},{4,6},{5,7},{6,4},{7,5},{8,10},{9,11},{10,... | collective-permute-start | bytes 98312 | tf_op jit(solution)/shard_map/ppermute | solution.py:312
  8.7 5.7 %collective-permute-start.2 = (f32[32,256]{1,0:T(8,128)S(1)}, f32[32,256]{1,0:T(8,128)S(1)}, u32[]{:S(2)}, u32[]{:S(2)}) collective-permute-start(f32[32,256]{1,0:T(8,128)S(1)} %get-tuple-element.61), channel_id=1, source_target_pairs={{0,3},{1,2},{2,1},{3,0},{4,7},{5,6},{6,5},{7,4},{8,11},{9,10},{10,... | collective-permute-start | bytes 98312 | tf_op jit(solution)/shard_map/ppermute | solution.py:312
  16.8 10.8 %collective-permute-start.3 = (f32[72,128]{1,0:T(8,128)S(1)}, f32[72,128]{1,0:T(8,128)S(1)}, u32[]{:S(2)}, u32[]{:S(2)}) collective-permute-start(f32[72,128]{1,0:T(8,128)S(1)} %get-tuple-element.65), channel_id=1, source_target_pairs={{0,16},{1,2},{2,1},{3,19},{4,20},{5,6},{6,5},{7,23},{8,24},{9,10},... | collective-permute-start | bytes 110600 | tf_op jit(solution)/shard_map/ppermute | solution.py:365
  18.4 9.2 %collective-permute-start.4 = (f32[72,128]{1,0:T(8,128)S(1)}, f32[72,128]{1,0:T(8,128)S(1)}, u32[]{:S(2)}, u32[]{:S(2)}) collective-permute-start(f32[72,128]{1,0:T(8,128)S(1)} %get-tuple-element.66), channel_id=1, source_target_pairs={{0,1},{1,0},{2,3},{3,2},{4,5},{5,4},{6,7},{7,6},{8,9},{9,8},{10,11... | collective-permute-start | bytes 110600 | tf_op jit(solution)/shard_map/ppermute | solution.py:365
  18.4 9.2 %collective-permute-start.5 = (f32[72,128]{1,0:T(8,128)S(1)}, f32[72,128]{1,0:T(8,128)S(1)}, u32[]{:S(2)}, u32[]{:S(2)}) collective-permute-start(f32[72,128]{1,0:T(8,128)S(1)} %get-tuple-element.67), channel_id=1, source_target_pairs={{0,4},{1,5},{2,6},{3,7},{4,0},{5,1},{6,2},{7,3},{8,12},{9,13},{10,... | collective-permute-start | bytes 110600 | tf_op jit(solution)/shard_map/ppermute | solution.py:365
  18.4 9.2 %collective-permute-start.6 = (f32[72,128]{1,0:T(8,128)S(1)}, f32[72,128]{1,0:T(8,128)S(1)}, u32[]{:S(2)}, u32[]{:S(2)}) collective-permute-start(f32[72,128]{1,0:T(8,128)S(1)} %get-tuple-element.68), channel_id=1, source_target_pairs={{0,28},{1,29},{2,30},{3,31},{4,8},{5,9},{6,10},{7,11},{8,4},{9,5},... | collective-permute-start | bytes 110600 | tf_op jit(solution)/shard_map/ppermute | solution.py:365
  22.1 1.1 copy-start
  25.0 7.1 %copy-start.1 = (bf16[640,640]{1,0:T(8,128)(2,1)S(1)}, bf16[640,640]{1,0:T(8,128)(2,1)}, u32[]{:S(2)}) copy-start(bf16[640,640]{1,0:T(8,128)(2,1)} %refs_7_.3) | copy-start | bytes 2457604
  27.6 16.8 %copy-start.8 = (f32[256,640]{1,0:T(8,128)}, f32[256,640]{1,0:T(8,128)S(1)}, u32[]{:S(2)}) copy-start(f32[256,640]{1,0:T(8,128)S(1)} %get-tuple-element.93.refs_5_) | copy-start | bytes 1966084
  28.8 5.7 %collective-permute-start.10 = (f32[64,128]{1,0:T(8,128)S(1)}, f32[64,128]{1,0:T(8,128)S(1)}, u32[]{:S(2)}, u32[]{:S(2)}) collective-permute-start(f32[64,128]{1,0:T(8,128)S(1)} %get-tuple-element.76), channel_id=1, source_target_pairs={{0,28},{1,29},{2,30},{3,31},{4,8},{5,9},{6,10},{7,11},{8,4},{9,5},... | collective-permute-start | bytes 98312 | tf_op jit(solution)/shard_map/ppermute | solution.py:365
  30.0 4.5 %collective-permute-start.7 = (f32[64,128]{1,0:T(8,128)S(1)}, f32[64,128]{1,0:T(8,128)S(1)}, u32[]{:S(2)}, u32[]{:S(2)}) collective-permute-start(f32[64,128]{1,0:T(8,128)S(1)} %get-tuple-element.73), channel_id=1, source_target_pairs={{0,16},{1,2},{2,1},{3,19},{4,20},{5,6},{6,5},{7,23},{8,24},{9,10},... | collective-permute-start | bytes 98312 | tf_op jit(solution)/shard_map/ppermute | solution.py:365
  30.5 4.0 %collective-permute-start.8 = (f32[64,128]{1,0:T(8,128)S(1)}, f32[64,128]{1,0:T(8,128)S(1)}, u32[]{:S(2)}, u32[]{:S(2)}) collective-permute-start(f32[64,128]{1,0:T(8,128)S(1)} %get-tuple-element.74), channel_id=1, source_target_pairs={{0,1},{1,0},{2,3},{3,2},{4,5},{5,4},{6,7},{7,6},{8,9},{9,8},{10,11... | collective-permute-start | bytes 98312 | tf_op jit(solution)/shard_map/ppermute | solution.py:365
  32.0 2.5 %collective-permute-start.9 = (f32[64,128]{1,0:T(8,128)S(1)}, f32[64,128]{1,0:T(8,128)S(1)}, u32[]{:S(2)}, u32[]{:S(2)}) collective-permute-start(f32[64,128]{1,0:T(8,128)S(1)} %get-tuple-element.75), channel_id=1, source_target_pairs={{0,4},{1,5},{2,6},{3,7},{4,0},{5,1},{6,2},{7,3},{8,12},{9,13},{10,... | collective-permute-start | bytes 98312 | tf_op jit(solution)/shard_map/ppermute | solution.py:365
  37.0 7.4 %collective-permute-start.11 = (f32[64,128]{1,0:T(8,128)}, f32[64,128]{1,0:T(8,128)}, u32[]{:S(2)}, u32[]{:S(2)}) collective-permute-start(f32[64,128]{1,0:T(8,128)} %get-tuple-element.84), channel_id=1, source_target_pairs={{0,16},{1,2},{2,1},{3,19},{4,20},{5,6},{6,5},{7,23},{8,24},{9,10},... | collective-permute-start | bytes 98312 | tf_op jit(solution)/shard_map/ppermute | solution.py:365
  38.4 6.0 %collective-permute-start.12 = (f32[64,128]{1,0:T(8,128)}, f32[64,128]{1,0:T(8,128)}, u32[]{:S(2)}, u32[]{:S(2)}) collective-permute-start(f32[64,128]{1,0:T(8,128)} %get-tuple-element.85), channel_id=1, source_target_pairs={{0,1},{1,0},{2,3},{3,2},{4,5},{5,4},{6,7},{7,6},{8,9},{9,8},{10,11... | collective-permute-start | bytes 98312 | tf_op jit(solution)/shard_map/ppermute | solution.py:365
  40.5 4.0 %collective-permute-start.13 = (f32[64,128]{1,0:T(8,128)}, f32[64,128]{1,0:T(8,128)}, u32[]{:S(2)}, u32[]{:S(2)}) collective-permute-start(f32[64,128]{1,0:T(8,128)} %get-tuple-element.86), channel_id=1, source_target_pairs={{0,4},{1,5},{2,6},{3,7},{4,0},{5,1},{6,2},{7,3},{8,12},{9,13},{10,... | collective-permute-start | bytes 98312 | tf_op jit(solution)/shard_map/ppermute | solution.py:365
  40.5 4.6 %collective-permute-start.14 = (f32[64,128]{1,0:T(8,128)}, f32[64,128]{1,0:T(8,128)}, u32[]{:S(2)}, u32[]{:S(2)}) collective-permute-start(f32[64,128]{1,0:T(8,128)} %get-tuple-element.87), channel_id=1, source_target_pairs={{0,28},{1,29},{2,30},{3,31},{4,8},{5,9},{6,10},{7,11},{8,4},{9,5},... | collective-permute-start | bytes 98312 | tf_op jit(solution)/shard_map/ppermute | solution.py:365
  41.3 1.0 copy-start.13
  42.3 1.0 copy-start.15
  43.2 5.2 %copy-start.7 = (f32[256,640]{1,0:T(8,128)S(1)}, f32[256,640]{1,0:T(8,128)}, u32[]{:S(2)}) copy-start(f32[256,640]{1,0:T(8,128)} %copy-done.6) | copy-start | bytes 1966084
  43.2 5.2 %copy-start.11 = (bf16[256,640]{1,0:T(8,128)(2,1)S(1)}, bf16[256,640]{1,0:T(8,128)(2,1)}, u32[]{:S(2)}) copy-start(bf16[256,640]{1,0:T(8,128)(2,1)} %copy-done.10) | copy-start | bytes 983044
  48.4 2.3 %copy-start.20 = (f32[64,256]{1,0:T(8,128)}, f32[64,256]{1,0:T(8,128)S(1)}, u32[]{:S(2)}) copy-start(f32[64,256]{1,0:T(8,128)S(1)} %get-tuple-element.88.adjoint_ref) | copy-start | bytes 196612
  48.4 2.3 %copy-start.30 = (f32[64,128]{1,0:T(8,128)}, f32[64,128]{1,0:T(8,128)S(1)}, u32[]{:S(2)}) copy-start(f32[64,128]{1,0:T(8,128)S(1)} %get-tuple-element.98) | copy-start | bytes 98308
  48.4 1.1 copy-start.9
  51.4 2.8 %collective-permute-start.22 = (f32[4,104,640]{2,1,0:T(8,128)S(1)}, f32[4,104,640]{2,1,0:T(8,128)}, u32[]{:S(2)}, u32[]{:S(2)}) collective-permute-start(f32[4,104,640]{2,1,0:T(8,128)S(1)} %dynamic-slice_bitcast_fusion), channel_id=1, source_target_pairs={{0,4},{4,0},{8,12},{12,8},{16,20},{20,16},{24,28},{28,24},{1,5},{5... | collective-permute-start | bytes 3194888 | tf_op jit(solution)/shard_map/ppermute | solution.py:312
  55.6 9.3 %collective-permute-start.23 = (f32[2,104,640]{2,1,0:T(8,128)S(1)}, f32[2,104,640]{2,1,0:T(8,128)S(1)}, u32[]{:S(2)}, u32[]{:S(2)}) collective-permute-start(f32[2,104,640]{2,1,0:T(8,128)S(1)} %dynamic-slice_bitcast_fusion.1), channel_id=1, source_target_pairs={{0,8},{4,20},{8,0},{12,28},{16,24},{20,4},{24,16},{28,12},{1,9},{5... | collective-permute-start | bytes 1597448 | tf_op jit(solution)/shard_map/ppermute | solution.py:312
  65.1 6.5 %collective-permute-start.24 = (f32[1,104,640]{2,1,0:T(8,128)S(1)}, f32[1,104,640]{2,1,0:T(8,128)S(1)}, u32[]{:S(2)}, u32[]{:S(2)}) collective-permute-start(f32[1,104,640]{2,1,0:T(8,128)S(1)} %constant_dynamic-slice_fusion), channel_id=1, source_target_pairs={{0,16},{4,12},{8,24},{12,4},{16,0},{20,28},{24,8},{28,20},{1,17},{... | collective-permute-start | bytes 798728 | tf_op jit(solution)/shard_map/ppermute | solution.py:312
  71.6 6.8 %collective-permute-start.25 = (f32[1,104,640]{2,1,0:T(8,128)S(1)}, f32[1,104,640]{2,1,0:T(8,128)S(1)}, u32[]{:S(2)}, u32[]{:S(2)}) collective-permute-start(f32[1,104,640]{2,1,0:T(8,128)S(1)} %dynamic-slice_add_fusion), channel_id=1, source_target_pairs={{0,1},{1,0},{2,3},{3,2},{4,5},{5,4},{6,7},{7,6},{8,9},{9,8},{10,11... | collective-permute-start | bytes 798728 | tf_op jit(solution)/shard_map/ppermute | solution.py:312
  78.4 12.4 %collective-permute-start.26 = (f32[1,104,640]{2,1,0:T(8,128)S(1)}, f32[1,104,640]{2,1,0:T(8,128)S(1)}, u32[]{:S(2)}, u32[]{:S(2)}) collective-permute-start(f32[1,104,640]{2,1,0:T(8,128)S(1)} %add.48), channel_id=1, source_target_pairs={{0,2},{1,3},{2,0},{3,1},{4,6},{5,7},{6,4},{7,5},{8,10},{9,11},{10,... | collective-permute-start | bytes 798728 | tf_op jit(solution)/shard_map/ppermute | solution.py:312
  90.9 6.5 %collective-permute-start.27 = (f32[1,104,640]{2,1,0:T(8,128)S(1)}, f32[1,104,640]{2,1,0:T(8,128)S(1)}, u32[]{:S(2)}, u32[]{:S(2)}) collective-permute-start(f32[1,104,640]{2,1,0:T(8,128)S(1)} %add.49), channel_id=1, source_target_pairs={{0,16},{4,12},{8,24},{12,4},{16,0},{20,28},{24,8},{28,20},{1,17},{... | collective-permute-start | bytes 798728 | tf_op jit(solution)/shard_map/ppermute | solution.py:312
  97.4 9.3 %collective-permute-start.28 = (f32[2,104,640]{2,1,0:T(8,128)S(1)}, f32[2,104,640]{2,1,0:T(8,128)S(1)}, u32[]{:S(2)}, u32[]{:S(2)}) collective-permute-start(f32[2,104,640]{2,1,0:T(8,128)S(1)} %maximum_select_fusion.3), channel_id=1, source_target_pairs={{0,8},{4,20},{8,0},{12,28},{16,24},{20,4},{24,16},{28,12},{1,9},{5... | collective-permute-start | bytes 1597448 | tf_op jit(solution)/shard_map/ppermute | solution.py:312
  106.7 1.6 %copy-start.31 = (f32[64,128]{1,0:T(8,128)S(1)}, f32[64,128]{1,0:T(8,128)}, u32[]{:S(2)}) copy-start(f32[64,128]{1,0:T(8,128)} %copy-done.30) | copy-start | bytes 98308
  106.7 1.6 %copy-start.29 = (f32[64,128]{1,0:T(8,128)S(1)}, f32[64,128]{1,0:T(8,128)}, u32[]{:S(2)}) copy-start(f32[64,128]{1,0:T(8,128)} %copy-done.28) | copy-start | bytes 98308
  106.7 1.7 %copy-start.27 = (f32[64,128]{1,0:T(8,128)S(1)}, f32[64,128]{1,0:T(8,128)}, u32[]{:S(2)}) copy-start(f32[64,128]{1,0:T(8,128)} %copy-done.26) | copy-start | bytes 98308
  106.8 6.1 %copy-start.19 = (f32[64,256]{1,0:T(8,128)S(1)}, f32[64,256]{1,0:T(8,128)}, u32[]{:S(2)}) copy-start(f32[64,256]{1,0:T(8,128)} %copy-done.18) | copy-start | bytes 196612
  106.8 6.1 %copy-start.21 = (f32[64,256]{1,0:T(8,128)S(1)}, f32[64,256]{1,0:T(8,128)}, u32[]{:S(2)}) copy-start(f32[64,256]{1,0:T(8,128)} %copy-done.20) | copy-start | bytes 196612
  106.8 6.1 %copy-start.23 = (f32[64,256]{1,0:T(8,128)S(1)}, f32[64,256]{1,0:T(8,128)}, u32[]{:S(2)}) copy-start(f32[64,256]{1,0:T(8,128)} %copy-done.22) | copy-start | bytes 196612
  106.9 15.8 %collective-permute-start.29 = (f32[4,104,640]{2,1,0:T(8,128)S(1)}, f32[4,104,640]{2,1,0:T(8,128)S(1)}, u32[]{:S(2)}, u32[]{:S(2)}) collective-permute-start(f32[4,104,640]{2,1,0:T(8,128)S(1)} %bitcast.49), channel_id=1, source_target_pairs={{0,4},{4,0},{8,12},{12,8},{16,20},{20,16},{24,28},{28,24},{1,5},{5... | collective-permute-start | bytes 3194888 | tf_op jit(solution)/shard_map/ppermute | solution.py:312
  107.5 3.9 %collective-permute-start.15 = (f32[64,128]{1,0:T(8,128)S(1)}, f32[64,128]{1,0:T(8,128)S(1)}, u32[]{:S(2)}, u32[]{:S(2)}) collective-permute-start(f32[64,128]{1,0:T(8,128)S(1)} %copy-done.33), channel_id=1, source_target_pairs={{0,16},{1,2},{2,1},{3,19},{4,20},{5,6},{6,5},{7,23},{8,24},{9,10},... | collective-permute-start | bytes 98312 | tf_op jit(solution)/shard_map/ppermute | solution.py:365
  108.4 3.9 %collective-permute-start.16 = (f32[64,128]{1,0:T(8,128)S(1)}, f32[64,128]{1,0:T(8,128)S(1)}, u32[]{:S(2)}, u32[]{:S(2)}) collective-permute-start(f32[64,128]{1,0:T(8,128)S(1)} %copy-done.31), channel_id=1, source_target_pairs={{0,1},{1,0},{2,3},{3,2},{4,5},{5,4},{6,7},{7,6},{8,9},{9,8},{10,11... | collective-permute-start | bytes 98312 | tf_op jit(solution)/shard_map/ppermute | solution.py:365
  108.4 3.9 %collective-permute-start.17 = (f32[64,128]{1,0:T(8,128)S(1)}, f32[64,128]{1,0:T(8,128)S(1)}, u32[]{:S(2)}, u32[]{:S(2)}) collective-permute-start(f32[64,128]{1,0:T(8,128)S(1)} %copy-done.29), channel_id=1, source_target_pairs={{0,4},{1,5},{2,6},{3,7},{4,0},{5,1},{6,2},{7,3},{8,12},{9,13},{10,... | collective-permute-start | bytes 98312 | tf_op jit(solution)/shard_map/ppermute | solution.py:365
  108.5 4.4 %collective-permute-start.18 = (f32[64,128]{1,0:T(8,128)S(1)}, f32[64,128]{1,0:T(8,128)S(1)}, u32[]{:S(2)}, u32[]{:S(2)}) collective-permute-start(f32[64,128]{1,0:T(8,128)S(1)} %copy-done.27), channel_id=1, source_target_pairs={{0,28},{1,29},{2,30},{3,31},{4,8},{5,9},{6,10},{7,11},{8,4},{9,5},... | collective-permute-start | bytes 98312 | tf_op jit(solution)/shard_map/ppermute | solution.py:365
  113.6 4.5 %collective-permute-start.19 = (f32[32,256]{1,0:T(8,128)S(1)}, f32[32,256]{1,0:T(8,128)S(1)}, u32[]{:S(2)}, u32[]{:S(2)}) collective-permute-start(f32[32,256]{1,0:T(8,128)S(1)} %get-tuple-element.102), channel_id=1, source_target_pairs={{0,1},{1,0},{2,3},{3,2},{4,5},{5,4},{6,7},{7,6},{8,9},{9,8},{10,11... | collective-permute-start | bytes 98312 | tf_op jit(solution)/shard_map/ppermute | solution.py:312
  115.6 5.2 %collective-permute-start.20 = (f32[32,256]{1,0:T(8,128)S(1)}, f32[32,256]{1,0:T(8,128)S(1)}, u32[]{:S(2)}, u32[]{:S(2)}) collective-permute-start(f32[32,256]{1,0:T(8,128)S(1)} %get-tuple-element.103), channel_id=1, source_target_pairs={{0,2},{1,3},{2,0},{3,1},{4,6},{5,7},{6,4},{7,5},{8,10},{9,11},{10,... | collective-permute-start | bytes 98312 | tf_op jit(solution)/shard_map/ppermute | solution.py:312
  115.6 5.8 %collective-permute-start.21 = (f32[32,256]{1,0:T(8,128)S(1)}, f32[32,256]{1,0:T(8,128)S(1)}, u32[]{:S(2)}, u32[]{:S(2)}) collective-permute-start(f32[32,256]{1,0:T(8,128)S(1)} %get-tuple-element.104), channel_id=1, source_target_pairs={{0,3},{1,2},{2,1},{3,0},{4,7},{5,6},{6,5},{7,4},{8,11},{9,10},{10,... | collective-permute-start | bytes 98312 | tf_op jit(solution)/shard_map/ppermute | solution.py:312
  (16 other events, 11.7 us)

commit v3 on v2

--- a/solution.py
+++ b/solution.py
@@ -321,14 +321,16 @@
     return rounds
 
 
-def all_summed(block):
+def halving_applies():
     tiles = lax.axis_size("tile")
+    return is_power_of_two(tiles) and is_power_of_two(lax.axis_size("depth")) and tiles == CHUNKS
+
+
+def all_summed(block, side_work):
+    tail = block.shape[1:]
     depths = lax.axis_size("depth")
-    if not (is_power_of_two(tiles) and is_power_of_two(depths) and tiles <= CHUNKS):
-        return lax.psum(block, ("tile", "depth"))
-    tail = block.shape[1:]
     tile = lax.axis_index("tile")
-    rounds = tile_rounds(tiles)
+    rounds = tile_rounds(lax.axis_size("tile"))
     sides = []
     for even_bit, odd_bit in rounds:
         bit = jnp.where(tile & 1 == 1, odd_bit, even_bit)
@@ -337,13 +339,18 @@
         halves = block.reshape(2, block.shape[0] // 2, *tail)
         sent = lax.dynamic_index_in_dim(halves, 1 - side, 0, False)
         kept = lax.dynamic_index_in_dim(halves, side, 0, False)
-        block = kept + swapped(sent, "tile", even_bit, odd_bit)
+        sent = swapped(sent, "tile", even_bit, odd_bit)
+        sent = side_work.send(sent)
+        block = kept + sent
     bit = 1
     while bit < depths:
-        block = block + swapped(block, "depth", bit, bit)
+        sent = swapped(block, "depth", bit, bit)
+        sent = side_work.send(sent)
+        block = block + sent
         bit *= 2
     for (even_bit, odd_bit), side in zip(reversed(rounds), reversed(sides)):
         other = swapped(block, "tile", even_bit, odd_bit)
+        other = side_work.send(other)
         block = jnp.where(side == 0, jnp.stack([block, other]), jnp.stack([other, block]))
         block = block.reshape(block.shape[0] * block.shape[1], *tail)
     return block
@@ -441,7 +448,6 @@
         (adjoint, weight, weight_sums, back, *edges),
         name="adjoint",
     )
-    edges = exchanged(edges)
     back, grads = called(
         functools.partial(backward_kernel, True),
         (field, total),
@@ -449,18 +455,55 @@
         (state_0, upstream, *cache_0, w_in, w_mid, w_out_t, grads),
         name="backward_sum",
     )
-    messages = called(
-        functools.partial(end_kernel, depths),
-        [message] * depths,
-        info,
-        (adjoint, weight, weight_sums, back, state_2, *edges),
-        scratch=[pltpu.VMEM((FEATURES, cells), jnp.float32)],
-        name="end",
-    )
-    messages = across_depth(messages)
     whole = spec_of((rows, TILE_CELLS))
-    final_state, sensitivity = called(functools.partial(join_kernel, depths), (whole, whole), info, messages, name="join")
-    grads = all_summed(grads) * (1.0 / (tiles * TILE_CELLS))
+    ended = []
+
+    def one_exchange(k, edge):
+        return lax.ppermute(edge, ("tile", "depth"), ways[k])
+
+    def last_transfers():
+        held = list(edges)
+        arrived = yield None
+        arrived, *held = lax.optimization_barrier((arrived, *held))
+        arrived = yield arrived
+        got = [one_exchange(0, held[0]), one_exchange(1, held[1])]
+        arrived, *rest = lax.optimization_barrier((arrived, *got, *held[2:]))
+        got, held = rest[:2], rest[2:]
+        arrived = yield arrived
+        got += [one_exchange(2, held[0]), one_exchange(3, held[1])]
+        arrived, *got = lax.optimization_barrier((arrived, *got))
+        arrived = yield arrived
+        messages = called(
+            functools.partial(end_kernel, depths),
+            [message] * depths,
+            info,
+            (adjoint, weight, weight_sums, back, state_2, *got),
+            scratch=[pltpu.VMEM((FEATURES, cells), jnp.float32)],
+            name="end",
+        )
+        out = [messages[0], swapped(messages[1], "depth", 1, 1)]
+        arrived, *rest = lax.optimization_barrier((arrived, *out, *messages[2:]))
+        out, messages = rest[:2], rest[2:]
+        arrived = yield arrived
+        out += [swapped(m, "depth", k + 2, k + 2) for k, m in enumerate(messages)]
+        arrived, *out = lax.optimization_barrier((arrived, *out))
+        arrived = yield arrived
+        both = called(functools.partial(join_kernel, depths), (whole, whole), info, out, name="join")
+        arrived, *both = lax.optimization_barrier((arrived, *both))
+        ended.extend(both)
+        while True:
+            arrived = yield arrived
+
+    side_work = last_transfers()
+    next(side_work)
+    if halving_applies():
+        grads = all_summed(grads, side_work)
+    else:
+        grads = lax.psum(grads, ("tile", "depth"))
+        for _ in range(6):
+            grads = side_work.send(grads)
+    final_state, sensitivity = ended
+    grads = grads * (1.0 / (tiles * TILE_CELLS))
     mid_rows = width // CHUNKS
     side_rows = FEATURES // CHUNKS
     first_row = mid_rows + 2 * side_rows

time: 127 us -> 119 us (0.937)
  waiting for transfers between devices: 59.3 us -> 50.2 us
    ppermute x14, waiting for transfers between devices: 56.3 us -> 42.5 us  [swapped(): lax.ppermute(x, axis, [(i, i ^ (odd_bit if i & 1 else even_bit)) for i in...]
    ppermute x0 -> x4, waiting for transfers between devices: none -> 6.99 us  [one_exchange(): return lax.ppermute(edge, ('tile', 'depth'), ways[k])]
    ppermute x0 -> x4, starting transfers between devices: none -> 3.49 us  [one_exchange(): return lax.ppermute(edge, ('tile', 'depth'), ways[k])]
    ppermute x16 -> x12, starting transfers between devices: 13.6 us -> 10.6 us  [exchanged(): lax.ppermute(edge, ('tile', 'depth'), way)]
    ppermute x16 -> x12, waiting for transfers between devices: 3.05 us -> 0.7 us  [exchanged(): lax.ppermute(edge, ('tile', 'depth'), way)]
    unnamed x68 -> x70, local copies, waits for them, and re-layouts: 15.6 us -> 15.1 us
  transfers between devices with their start and end apart: 30 -> 30, of which waited for: 15 -> 14; matrix products, arithmetic and copies ran while one was open for 2% -> 2% of each run, Pallas kernels for 4% -> 4%
where the time goes in v3:
time: 119 us; the launch traced here: 118 us
  waiting for transfers between devices  50.2 us (42%)
  starting transfers between devices  31.2 us (26%)
  local copies, waits for them, and re-layouts  20.5 us (17%)
  Pallas kernels  12.5 us (11%)
  other arithmetic  3.1 us (3%)
    ppermute x14, waiting for transfers between devices, swapped(): lax.ppermute(x, axis, [(i, i ^ (odd_bit if i & 1 else even_bit)) for i in...  42.5 us
    ppermute x14, starting transfers between devices, swapped(): lax.ppermute(x, axis, [(i, i ^ (odd_bit if i & 1 else even_bit)) for i in...  17.1 us
    unnamed x70, local copies, waits for them, and re-layouts  15.1 us
    pallas_call x11, Pallas kernels, called(): pl.pallas_call(kernel, out_shape=tuple(outs), in_specs=in_specs, out_spec...  12.5 us
    ppermute x12, starting transfers between devices, exchanged(): lax.ppermute(edge, ('tile', 'depth'), way)  10.6 us
    ppermute x4, waiting for transfers between devices, one_exchange(): return lax.ppermute(edge, ('tile', 'depth'), ways[k])  6.99 us
    ppermute x4, starting transfers between devices, one_exchange(): return lax.ppermute(edge, ('tile', 'depth'), ways[k])  3.49 us
    add x3, other arithmetic, all_summed(): block = kept + sent  2.55 us
  transfers between devices with their start and end apart: 30, of which 14 were waited for; matrix products, arithmetic and copies ran while one was open for 2% of the time, Pallas kernels for 4%

profile of v3, /device:TPU:0, one launch (start us, length us, event | category | flops | bytes accessed | tf_op | source)
XLA Modules:
  0.0 118.4 jit_solution(15859314775028881125)
XLA Ops:
  3.0 3.1 %collective-permute-start = (f32[32,256]{1,0:T(8,128)S(1)}, f32[32,256]{1,0:T(8,128)S(1)}, u32[]{:S(2)}, u32[]{:S(2)}) collective-permute-start(f32[32,256]{1,0:T(8,128)S(1)} %get-tuple-element.87), channel_id=1, source_target_pairs={{0,1},{1,0},{2,3},{3,2},{4,5},{5,4},{6,7},{7,6},{8,9},{9,8},{10,11... | collective-permute-start | bytes 98312 | tf_op jit(solution)/shard_map/ppermute | solution.py:312
  6.1 2.6 %collective-permute-start.1 = (f32[32,256]{1,0:T(8,128)S(1)}, f32[32,256]{1,0:T(8,128)S(1)}, u32[]{:S(2)}, u32[]{:S(2)}) collective-permute-start(f32[32,256]{1,0:T(8,128)S(1)} %get-tuple-element.88), channel_id=1, source_target_pairs={{0,2},{1,3},{2,0},{3,1},{4,6},{5,7},{6,4},{7,5},{8,10},{9,11},{10,... | collective-permute-start | bytes 98312 | tf_op jit(solution)/shard_map/ppermute | solution.py:312
  8.7 2.8 %collective-permute-done.1.refs_2_ = f32[32,256]{1,0:T(8,128)S(1)} collective-permute-done((f32[32,256]{1,0:T(8,128)S(1)}, f32[32,256]{1,0:T(8,128)S(1)}, u32[]{:S(2)}, u32[]{:S(2)}) %collective-permute-start.1) | collective-permute-done | bytes 32800 | tf_op jit(solution)/shard_map/ppermute | solution.py:312
  11.5 2.9 %collective-permute-done.2.refs_3_ = f32[32,256]{1,0:T(8,128)S(1)} collective-permute-done((f32[32,256]{1,0:T(8,128)S(1)}, f32[32,256]{1,0:T(8,128)S(1)}, u32[]{:S(2)}, u32[]{:S(2)}) %collective-permute-start.2) | collective-permute-done | bytes 32800 | tf_op jit(solution)/shard_map/ppermute | solution.py:312
  15.7 1.1 gather.1
  16.8 1.6 %collective-permute-start.3 = (f32[72,128]{1,0:T(8,128)S(1)}, f32[72,128]{1,0:T(8,128)S(1)}, u32[]{:S(2)}, u32[]{:S(2)}) collective-permute-start(f32[72,128]{1,0:T(8,128)S(1)} %get-tuple-element.93), channel_id=1, source_target_pairs={{0,16},{1,2},{2,1},{3,19},{4,20},{5,6},{6,5},{7,23},{8,24},{9,10},... | collective-permute-start | bytes 110600 | tf_op jit(solution)/shard_map/ppermute | solution.py:372
  18.4 1.5 %collective-permute-start.6 = (f32[72,128]{1,0:T(8,128)S(1)}, f32[72,128]{1,0:T(8,128)S(1)}, u32[]{:S(2)}, u32[]{:S(2)}) collective-permute-start(f32[72,128]{1,0:T(8,128)S(1)} %get-tuple-element.96), channel_id=1, source_target_pairs={{0,28},{1,29},{2,30},{3,31},{4,8},{5,9},{6,10},{7,11},{8,4},{9,5},... | collective-permute-start | bytes 110600 | tf_op jit(solution)/shard_map/ppermute | solution.py:372
  22.1 1.1 copy-done
  23.2 0.9 copy-done.2
  24.1 0.9 copy-done.4
  25.0 1.0 closure.2
  27.6 1.2 %step.1 = (f32[64,256]{1,0:T(8,128)S(1)}, f32[8,256]{1,0:T(8,128)S(1)}, f32[64,128]{1,0:T(8,128)S(1)}, f32[64,128]{1,0:T(8,128)S(1)}, f32[64,128]{1,0:T(8,128)S(1)}, /*index=5*/f32[64,128]{1,0:T(8,128)S(1)}) custom-call(s32[3]{0:T(128)S(1)} %pad_add_fusion.info, f32[64,256]{1,0:T(8,128)S(1)} %get-tuple-element.90.state_ref.refs_0_, ...), custom_call_target="tpu_custom_call" | custom-call | tf_op jit(solution)/shard_map/step/pallas_call | solution.py:295
  28.8 1.2 collective-permute-start.10
  30.5 1.5 %collective-permute-start.8 = (f32[64,128]{1,0:T(8,128)S(1)}, f32[64,128]{1,0:T(8,128)S(1)}, u32[]{:S(2)}, u32[]{:S(2)}) collective-permute-start(f32[64,128]{1,0:T(8,128)S(1)} %get-tuple-element.102), channel_id=1, source_target_pairs={{0,1},{1,0},{2,3},{3,2},{4,5},{5,4},{6,7},{7,6},{8,9},{9,8},{10,11... | collective-permute-start | bytes 98312 | tf_op jit(solution)/shard_map/ppermute | solution.py:372
  32.0 1.0 closure.3
  34.6 1.9 %last_step.1 = (f32[64,256]{1,0:T(8,128)S(1)}, f32[64,256]{1,0:T(8,128)S(1)}, bf16[64,256]{1,0:T(8,128)(2,1)S(1)}, f32[64,128]{1,0:T(8,128)}, f32[64,128]{1,0:T(...) custom-call(s32[3]{0:T(128)S(1)} %pad_add_fusion.info, f32[64,256]{1,0:T(8,128)S(1)} %get-tuple-element.97.state_ref.refs_0_, ...), custom_call_target="tpu_custom_call" | custom-call | tf_op jit(solution)/shard_map/last_step/pallas_call | solution.py:295
  37.0 1.4 %collective-permute-start.11 = (f32[64,128]{1,0:T(8,128)}, f32[64,128]{1,0:T(8,128)}, u32[]{:S(2)}, u32[]{:S(2)}) collective-permute-start(f32[64,128]{1,0:T(8,128)} %get-tuple-element.112), channel_id=1, source_target_pairs={{0,16},{1,2},{2,1},{3,19},{4,20},{5,6},{6,5},{7,23},{8,24},{9,10},... | collective-permute-start | bytes 98312 | tf_op jit(solution)/shard_map/ppermute | solution.py:372
  38.4 2.0 %collective-permute-start.12 = (f32[64,128]{1,0:T(8,128)}, f32[64,128]{1,0:T(8,128)}, u32[]{:S(2)}, u32[]{:S(2)}) collective-permute-start(f32[64,128]{1,0:T(8,128)} %get-tuple-element.113), channel_id=1, source_target_pairs={{0,1},{1,0},{2,3},{3,2},{4,5},{5,4},{6,7},{7,6},{8,9},{9,8},{10,11... | collective-permute-start | bytes 98312 | tf_op jit(solution)/shard_map/ppermute | solution.py:372
  41.3 1.0 copy-done.13
  42.3 1.0 copy-done.15
  43.2 1.1 backward.1
  45.1 1.5 %adjoint.1 = (f32[64,256]{1,0:T(8,128)S(1)}, bf16[64,256]{1,0:T(8,128)(2,1)S(1)}, f32[64,128]{1,0:T(8,128)S(1)}, f32[64,128]{1,0:T(8,128)S(1)}, f32[64,128]{1,0:T(8,128)S(1)}, /*index=5*/f32[64,128]{1,0:T(8,128)S(1)}) custom-call(s32[3]{0:T(128)S(1)} %pad_add_fusion.info, f32[64,256]{1,0:T(8,128)S(1)} %get-tuple-element.105.adjoint_ref, ...), custom_call_target="tpu_custom_call" | custom-call | tf_op jit(solution)/shard_map/adjoint/pallas_call | solution.py:295
  48.4 1.1 copy-done.9
  49.5 1.2 backward_sum.1
  51.4 2.8 %collective-permute-done.15 = f32[4,104,640]{2,1,0:T(8,128)} collective-permute-done((f32[4,104,640]{2,1,0:T(8,128)S(1)}, f32[4,104,640]{2,1,0:T(8,128)}, u32[]{:S(2)}, u32[]{:S(2)}) %collective-permute-start.15) | collective-permute-done | bytes 1064992 | tf_op jit(solution)/shard_map/ppermute | solution.py:312
  54.2 1.4 %bitcast_add_fusion = f32[4,104,640]{2,1,0:T(8,128)S(1)} fusion(f32[4,104,640]{2,1,0:T(8,128)} %collective-permute-done.15, f32[2,4,104,640]{3,2,1,0:T(8,128)S(1)} %bitcast.36, s32[]{:T(128)S(6)} %select_n.83), kind=kLoop, calls=%fused_computation.3 | loop fusion | flops 266240 | bytes 3194884 | tf_op jit(solution)/shard_map/add | solution.py:344
  55.6 0.9 collective-permute-start.16
  56.5 0.9 collective-permute-start.17
  57.5 1.1 collective-permute-start.18
  58.5 2.4 %collective-permute-done.17.e0 = f32[64,128]{1,0:T(8,128)S(1)} collective-permute-done((f32[64,128]{1,0:T(8,128)S(1)}, f32[64,128]{1,0:T(8,128)S(1)}, u32[]{:S(2)}, u32[]{:S(2)}) %collective-permute-start.17) | collective-permute-done | bytes 32800 | tf_op jit(solution)/shard_map/ppermute | solution.py:462
  61.4 3.6 %collective-permute-done.16 = f32[2,104,640]{2,1,0:T(8,128)S(1)} collective-permute-done((f32[2,104,640]{2,1,0:T(8,128)S(1)}, f32[2,104,640]{2,1,0:T(8,128)S(1)}, u32[]{:S(2)}, u32[]{:S(2)}) %collective-permute-start.16) | collective-permute-done | bytes 532512 | tf_op jit(solution)/shard_map/ppermute | solution.py:312
  65.0 1.1 bitcast_add_fusion.1
  66.2 0.9 collective-permute-start.19
  67.1 1.5 %collective-permute-start.21 = (f32[64,128]{1,0:T(8,128)S(1)}, f32[64,128]{1,0:T(8,128)S(1)}, u32[]{:S(2)}, u32[]{:S(2)}) collective-permute-start(f32[64,128]{1,0:T(8,128)S(1)} %copy-done.27), channel_id=1, source_target_pairs={{0,28},{1,29},{2,30},{3,31},{4,8},{5,9},{6,10},{7,11},{8,4},{9,5},... | collective-permute-start | bytes 98312 | tf_op jit(solution)/shard_map/ppermute | solution.py:462
  68.7 4.1 %collective-permute-done.21.e3 = f32[64,128]{1,0:T(8,128)S(1)} collective-permute-done((f32[64,128]{1,0:T(8,128)S(1)}, f32[64,128]{1,0:T(8,128)S(1)}, u32[]{:S(2)}, u32[]{:S(2)}) %collective-permute-start.21) | collective-permute-done | bytes 32800 | tf_op jit(solution)/shard_map/ppermute | solution.py:462
  74.3 1.7 %collective-permute-start.23 = (f32[32,256]{1,0:T(8,128)S(1)}, f32[32,256]{1,0:T(8,128)S(1)}, u32[]{:S(2)}, u32[]{:S(2)}) collective-permute-start(f32[32,256]{1,0:T(8,128)S(1)} %get-tuple-element.146), channel_id=1, source_target_pairs={{0,1},{1,0},{2,3},{3,2},{4,5},{5,4},{6,7},{7,6},{8,9},{9,8},{10,11... | collective-permute-start | bytes 98312 | tf_op jit(solution)/shard_map/ppermute | solution.py:312
  76.0 5.3 %collective-permute-done.23.refs_1_ = f32[32,256]{1,0:T(8,128)S(1)} collective-permute-done((f32[32,256]{1,0:T(8,128)S(1)}, f32[32,256]{1,0:T(8,128)S(1)}, u32[]{:S(2)}, u32[]{:S(2)}) %collective-permute-start.23) | collective-permute-done | bytes 32800 | tf_op jit(solution)/shard_map/ppermute | solution.py:312
  81.3 0.9 collective-permute-start.24
  82.2 2.0 %collective-permute-start.25 = (f32[32,256]{1,0:T(8,128)S(1)}, f32[32,256]{1,0:T(8,128)S(1)}, u32[]{:S(2)}, u32[]{:S(2)}) collective-permute-start(f32[32,256]{1,0:T(8,128)S(1)} %get-tuple-element.152), channel_id=1, source_target_pairs={{0,2},{1,3},{2,0},{3,1},{4,6},{5,7},{6,4},{7,5},{8,10},{9,11},{10,... | collective-permute-start | bytes 98312 | tf_op jit(solution)/shard_map/ppermute | solution.py:312
  84.3 1.2 collective-permute-start.26
  85.5 10.8 %collective-permute-done.25.refs_2_ = f32[32,256]{1,0:T(8,128)S(1)} collective-permute-done((f32[32,256]{1,0:T(8,128)S(1)}, f32[32,256]{1,0:T(8,128)S(1)}, u32[]{:S(2)}, u32[]{:S(2)}) %collective-permute-start.25) | collective-permute-done | bytes 32800 | tf_op jit(solution)/shard_map/ppermute | solution.py:312
  96.3 1.3 %collective-permute-start.27 = (f32[1,104,640]{2,1,0:T(8,128)S(1)}, f32[1,104,640]{2,1,0:T(8,128)S(1)}, u32[]{:S(2)}, u32[]{:S(2)}) collective-permute-start(f32[1,104,640]{2,1,0:T(8,128)S(1)} %add.49), channel_id=1, source_target_pairs={{0,16},{4,12},{8,24},{12,4},{16,0},{20,28},{24,8},{28,20},{1,17},{... | collective-permute-start | bytes 798728 | tf_op jit(solution)/shard_map/ppermute | solution.py:312
  97.6 1.2 %join.1 = (f32[16,1024]{1,0:T(8,128)}, f32[16,1024]{1,0:T(8,128)}) custom-call(s32[3]{0:T(128)S(1)} %pad_add_fusion.info, f32[32,256]{1,0:T(8,128)S(1)} %get-tuple-element.155.refs_0_, f32[32,256]{1,0:T(8,128)S(1)} %collective-permute-done.23.refs_1_, f32[32,256]{1,0:T(8,128)S(1)} %collective-permute-done.25.refs_2_, ...), custom_call_target="tpu_custom_call" | custom-call | tf_op jit(solution)/shard_map/join/pallas_call | solution.py:295
  98.8 4.0 %collective-permute-done.27 = f32[1,104,640]{2,1,0:T(8,128)S(1)} collective-permute-done((f32[1,104,640]{2,1,0:T(8,128)S(1)}, f32[1,104,640]{2,1,0:T(8,128)S(1)}, u32[]{:S(2)}, u32[]{:S(2)}) %collective-permute-start.27) | collective-permute-done | bytes 266272 | tf_op jit(solution)/shard_map/ppermute | solution.py:312
  102.9 1.9 %collective-permute-start.28 = (f32[2,104,640]{2,1,0:T(8,128)S(1)}, f32[2,104,640]{2,1,0:T(8,128)S(1)}, u32[]{:S(2)}, u32[]{:S(2)}) collective-permute-start(f32[2,104,640]{2,1,0:T(8,128)S(1)} %maximum_select_fusion.3), channel_id=1, source_target_pairs={{0,8},{4,20},{8,0},{12,28},{16,24},{20,4},{24,16},{28,12},{1,9},{5... | collective-permute-start | bytes 1597448 | tf_op jit(solution)/shard_map/ppermute | solution.py:312
  104.8 7.4 %collective-permute-done.28 = f32[2,104,640]{2,1,0:T(8,128)S(1)} collective-permute-done((f32[2,104,640]{2,1,0:T(8,128)S(1)}, f32[2,104,640]{2,1,0:T(8,128)S(1)}, u32[]{:S(2)}, u32[]{:S(2)}) %collective-permute-start.28) | collective-permute-done | bytes 532512 | tf_op jit(solution)/shard_map/ppermute | solution.py:312
  112.4 2.7 %collective-permute-done.29 = f32[4,104,640]{2,1,0:T(8,128)S(1)} collective-permute-done((f32[4,104,640]{2,1,0:T(8,128)S(1)}, f32[4,104,640]{2,1,0:T(8,128)S(1)}, u32[]{:S(2)}, u32[]{:S(2)}) %collective-permute-start.29) | collective-permute-done | bytes 1064992 | tf_op jit(solution)/shard_map/ppermute | solution.py:312
  115.2 1.3 %slice.26 = f32[8,80,640]{2,1,0:T(8,128)} slice(f32[8,104,640]{2,1,0:T(8,128)S(1)} %bitcast.45), slice={[0:8], [0:80], [0:640]} | slice | bytes 3276800 | tf_op jit(solution)/shard_map/slice | solution.py:510
  (113 shorter events, 18.4 us)
Async XLA Ops:
  0.6 31.4 %copy-start.5 = (bf16[640,64]{0,1:T(8,128)(2,1)S(1)}, bf16[640,64]{0,1:T(8,128)(2,1)}, u32[]{:S(2)}) copy-start(bf16[640,64]{0,1:T(8,128)(2,1)} %param.18) | copy-start | bytes 245764
  0.6 31.4 %copy-start.3 = (bf16[64,640]{1,0:T(8,128)(2,1)S(1)}, bf16[64,640]{1,0:T(8,128)(2,1)}, u32[]{:S(2)}) copy-start(bf16[64,640]{1,0:T(8,128)(2,1)} %refs_6_.3) | copy-start | bytes 245764
  3.0 5.7 %collective-permute-start = (f32[32,256]{1,0:T(8,128)S(1)}, f32[32,256]{1,0:T(8,128)S(1)}, u32[]{:S(2)}, u32[]{:S(2)}) collective-permute-start(f32[32,256]{1,0:T(8,128)S(1)} %get-tuple-element.87), channel_id=1, source_target_pairs={{0,1},{1,0},{2,3},{3,2},{4,5},{5,4},{6,7},{7,6},{8,9},{9,8},{10,11... | collective-permute-start | bytes 98312 | tf_op jit(solution)/shard_map/ppermute | solution.py:312
  6.1 5.4 %collective-permute-start.1 = (f32[32,256]{1,0:T(8,128)S(1)}, f32[32,256]{1,0:T(8,128)S(1)}, u32[]{:S(2)}, u32[]{:S(2)}) collective-permute-start(f32[32,256]{1,0:T(8,128)S(1)} %get-tuple-element.88), channel_id=1, source_target_pairs={{0,2},{1,3},{2,0},{3,1},{4,6},{5,7},{6,4},{7,5},{8,10},{9,11},{10,... | collective-permute-start | bytes 98312 | tf_op jit(solution)/shard_map/ppermute | solution.py:312
  8.7 5.7 %collective-permute-start.2 = (f32[32,256]{1,0:T(8,128)S(1)}, f32[32,256]{1,0:T(8,128)S(1)}, u32[]{:S(2)}, u32[]{:S(2)}) collective-permute-start(f32[32,256]{1,0:T(8,128)S(1)} %get-tuple-element.89), channel_id=1, source_target_pairs={{0,3},{1,2},{2,1},{3,0},{4,7},{5,6},{6,5},{7,4},{8,11},{9,10},{10,... | collective-permute-start | bytes 98312 | tf_op jit(solution)/shard_map/ppermute | solution.py:312
  16.8 10.8 %collective-permute-start.3 = (f32[72,128]{1,0:T(8,128)S(1)}, f32[72,128]{1,0:T(8,128)S(1)}, u32[]{:S(2)}, u32[]{:S(2)}) collective-permute-start(f32[72,128]{1,0:T(8,128)S(1)} %get-tuple-element.93), channel_id=1, source_target_pairs={{0,16},{1,2},{2,1},{3,19},{4,20},{5,6},{6,5},{7,23},{8,24},{9,10},... | collective-permute-start | bytes 110600 | tf_op jit(solution)/shard_map/ppermute | solution.py:372
  18.4 9.2 %collective-permute-start.4 = (f32[72,128]{1,0:T(8,128)S(1)}, f32[72,128]{1,0:T(8,128)S(1)}, u32[]{:S(2)}, u32[]{:S(2)}) collective-permute-start(f32[72,128]{1,0:T(8,128)S(1)} %get-tuple-element.94), channel_id=1, source_target_pairs={{0,1},{1,0},{2,3},{3,2},{4,5},{5,4},{6,7},{7,6},{8,9},{9,8},{10,11... | collective-permute-start | bytes 110600 | tf_op jit(solution)/shard_map/ppermute | solution.py:372
  18.4 9.2 %collective-permute-start.5 = (f32[72,128]{1,0:T(8,128)S(1)}, f32[72,128]{1,0:T(8,128)S(1)}, u32[]{:S(2)}, u32[]{:S(2)}) collective-permute-start(f32[72,128]{1,0:T(8,128)S(1)} %get-tuple-element.95), channel_id=1, source_target_pairs={{0,4},{1,5},{2,6},{3,7},{4,0},{5,1},{6,2},{7,3},{8,12},{9,13},{10,... | collective-permute-start | bytes 110600 | tf_op jit(solution)/shard_map/ppermute | solution.py:372
  18.4 9.2 %collective-permute-start.6 = (f32[72,128]{1,0:T(8,128)S(1)}, f32[72,128]{1,0:T(8,128)S(1)}, u32[]{:S(2)}, u32[]{:S(2)}) collective-permute-start(f32[72,128]{1,0:T(8,128)S(1)} %get-tuple-element.96), channel_id=1, source_target_pairs={{0,28},{1,29},{2,30},{3,31},{4,8},{5,9},{6,10},{7,11},{8,4},{9,5},... | collective-permute-start | bytes 110600 | tf_op jit(solution)/shard_map/ppermute | solution.py:372
  22.1 1.1 copy-start
  25.0 7.1 %copy-start.1 = (bf16[640,640]{1,0:T(8,128)(2,1)S(1)}, bf16[640,640]{1,0:T(8,128)(2,1)}, u32[]{:S(2)}) copy-start(bf16[640,640]{1,0:T(8,128)(2,1)} %refs_7_.3) | copy-start | bytes 2457604
  27.6 16.8 %copy-start.8 = (f32[256,640]{1,0:T(8,128)}, f32[256,640]{1,0:T(8,128)S(1)}, u32[]{:S(2)}) copy-start(f32[256,640]{1,0:T(8,128)S(1)} %get-tuple-element.120.refs_5_) | copy-start | bytes 1966084
  28.8 5.7 %collective-permute-start.10 = (f32[64,128]{1,0:T(8,128)S(1)}, f32[64,128]{1,0:T(8,128)S(1)}, u32[]{:S(2)}, u32[]{:S(2)}) collective-permute-start(f32[64,128]{1,0:T(8,128)S(1)} %get-tuple-element.104), channel_id=1, source_target_pairs={{0,28},{1,29},{2,30},{3,31},{4,8},{5,9},{6,10},{7,11},{8,4},{9,5},... | collective-permute-start | bytes 98312 | tf_op jit(solution)/shard_map/ppermute | solution.py:372
  30.0 4.5 %collective-permute-start.7 = (f32[64,128]{1,0:T(8,128)S(1)}, f32[64,128]{1,0:T(8,128)S(1)}, u32[]{:S(2)}, u32[]{:S(2)}) collective-permute-start(f32[64,128]{1,0:T(8,128)S(1)} %get-tuple-element.101), channel_id=1, source_target_pairs={{0,16},{1,2},{2,1},{3,19},{4,20},{5,6},{6,5},{7,23},{8,24},{9,10},... | collective-permute-start | bytes 98312 | tf_op jit(solution)/shard_map/ppermute | solution.py:372
  30.5 4.0 %collective-permute-start.8 = (f32[64,128]{1,0:T(8,128)S(1)}, f32[64,128]{1,0:T(8,128)S(1)}, u32[]{:S(2)}, u32[]{:S(2)}) collective-permute-start(f32[64,128]{1,0:T(8,128)S(1)} %get-tuple-element.102), channel_id=1, source_target_pairs={{0,1},{1,0},{2,3},{3,2},{4,5},{5,4},{6,7},{7,6},{8,9},{9,8},{10,11... | collective-permute-start | bytes 98312 | tf_op jit(solution)/shard_map/ppermute | solution.py:372
  32.0 2.5 %collective-permute-start.9 = (f32[64,128]{1,0:T(8,128)S(1)}, f32[64,128]{1,0:T(8,128)S(1)}, u32[]{:S(2)}, u32[]{:S(2)}) collective-permute-start(f32[64,128]{1,0:T(8,128)S(1)} %get-tuple-element.103), channel_id=1, source_target_pairs={{0,4},{1,5},{2,6},{3,7},{4,0},{5,1},{6,2},{7,3},{8,12},{9,13},{10,... | collective-permute-start | bytes 98312 | tf_op jit(solution)/shard_map/ppermute | solution.py:372
  37.0 7.4 %collective-permute-start.11 = (f32[64,128]{1,0:T(8,128)}, f32[64,128]{1,0:T(8,128)}, u32[]{:S(2)}, u32[]{:S(2)}) collective-permute-start(f32[64,128]{1,0:T(8,128)} %get-tuple-element.112), channel_id=1, source_target_pairs={{0,16},{1,2},{2,1},{3,19},{4,20},{5,6},{6,5},{7,23},{8,24},{9,10},... | collective-permute-start | bytes 98312 | tf_op jit(solution)/shard_map/ppermute | solution.py:372
  38.4 6.0 %collective-permute-start.12 = (f32[64,128]{1,0:T(8,128)}, f32[64,128]{1,0:T(8,128)}, u32[]{:S(2)}, u32[]{:S(2)}) collective-permute-start(f32[64,128]{1,0:T(8,128)} %get-tuple-element.113), channel_id=1, source_target_pairs={{0,1},{1,0},{2,3},{3,2},{4,5},{5,4},{6,7},{7,6},{8,9},{9,8},{10,11... | collective-permute-start | bytes 98312 | tf_op jit(solution)/shard_map/ppermute | solution.py:372
  40.5 4.0 %collective-permute-start.13 = (f32[64,128]{1,0:T(8,128)}, f32[64,128]{1,0:T(8,128)}, u32[]{:S(2)}, u32[]{:S(2)}) collective-permute-start(f32[64,128]{1,0:T(8,128)} %get-tuple-element.114), channel_id=1, source_target_pairs={{0,4},{1,5},{2,6},{3,7},{4,0},{5,1},{6,2},{7,3},{8,12},{9,13},{10,... | collective-permute-start | bytes 98312 | tf_op jit(solution)/shard_map/ppermute | solution.py:372
  40.5 4.6 %collective-permute-start.14 = (f32[64,128]{1,0:T(8,128)}, f32[64,128]{1,0:T(8,128)}, u32[]{:S(2)}, u32[]{:S(2)}) collective-permute-start(f32[64,128]{1,0:T(8,128)} %get-tuple-element.115), channel_id=1, source_target_pairs={{0,28},{1,29},{2,30},{3,31},{4,8},{5,9},{6,10},{7,11},{8,4},{9,5},... | collective-permute-start | bytes 98312 | tf_op jit(solution)/shard_map/ppermute | solution.py:372
  43.2 5.2 %copy-start.7 = (f32[256,640]{1,0:T(8,128)S(1)}, f32[256,640]{1,0:T(8,128)}, u32[]{:S(2)}) copy-start(f32[256,640]{1,0:T(8,128)} %copy-done.6) | copy-start | bytes 1966084
  43.2 5.2 %copy-start.11 = (bf16[256,640]{1,0:T(8,128)(2,1)S(1)}, bf16[256,640]{1,0:T(8,128)(2,1)}, u32[]{:S(2)}) copy-start(bf16[256,640]{1,0:T(8,128)(2,1)} %copy-done.10) | copy-start | bytes 983044
  48.4 2.3 %copy-start.20 = (f32[64,256]{1,0:T(8,128)}, f32[64,256]{1,0:T(8,128)S(1)}, u32[]{:S(2)}) copy-start(f32[64,256]{1,0:T(8,128)S(1)} %get-tuple-element.138.adjoint_ref) | copy-start | bytes 196612
  48.4 2.3 %copy-start.30 = (f32[64,128]{1,0:T(8,128)}, f32[64,128]{1,0:T(8,128)S(1)}, u32[]{:S(2)}) copy-start(f32[64,128]{1,0:T(8,128)S(1)} %get-tuple-element.129) | copy-start | bytes 98308
  48.4 1.1 copy-start.9
  51.3 2.8 %collective-permute-start.15 = (f32[4,104,640]{2,1,0:T(8,128)S(1)}, f32[4,104,640]{2,1,0:T(8,128)}, u32[]{:S(2)}, u32[]{:S(2)}) collective-permute-start(f32[4,104,640]{2,1,0:T(8,128)S(1)} %dynamic-slice_bitcast_fusion), channel_id=1, source_target_pairs={{0,4},{4,0},{8,12},{12,8},{16,20},{20,16},{24,28},{28,24},{1,5},{5... | collective-permute-start | bytes 3194888 | tf_op jit(solution)/shard_map/ppermute | solution.py:312
  55.6 3.0 %copy-start.34 = (f32[4,104,640]{2,1,0:T(8,128)}, f32[4,104,640]{2,1,0:T(8,128)S(1)}, u32[]{:S(2)}) copy-start(f32[4,104,640]{2,1,0:T(8,128)S(1)} %bitcast_add_fusion) | copy-start | bytes 3194884
  55.6 1.0 copy-start.33
  55.6 1.9 %copy-start.31 = (f32[64,128]{1,0:T(8,128)S(1)}, f32[64,128]{1,0:T(8,128)}, u32[]{:S(2)}) copy-start(f32[64,128]{1,0:T(8,128)} %copy-done.30) | copy-start | bytes 98308
  55.6 9.3 %collective-permute-start.16 = (f32[2,104,640]{2,1,0:T(8,128)S(1)}, f32[2,104,640]{2,1,0:T(8,128)S(1)}, u32[]{:S(2)}, u32[]{:S(2)}) collective-permute-start(f32[2,104,640]{2,1,0:T(8,128)S(1)} %dynamic-slice_bitcast_fusion.1), channel_id=1, source_target_pairs={{0,8},{4,20},{8,0},{12,28},{16,24},{20,4},{24,16},{28,12},{1,9},{5... | collective-permute-start | bytes 1597448 | tf_op jit(solution)/shard_map/ppermute | solution.py:312
  56.5 4.3 %collective-permute-start.17 = (f32[64,128]{1,0:T(8,128)S(1)}, f32[64,128]{1,0:T(8,128)S(1)}, u32[]{:S(2)}, u32[]{:S(2)}) collective-permute-start(f32[64,128]{1,0:T(8,128)S(1)} %copy-done.33), channel_id=1, source_target_pairs={{0,16},{1,2},{2,1},{3,19},{4,20},{5,6},{6,5},{7,23},{8,24},{9,10},... | collective-permute-start | bytes 98312 | tf_op jit(solution)/shard_map/ppermute | solution.py:462
  57.5 3.9 %collective-permute-start.18 = (f32[64,128]{1,0:T(8,128)S(1)}, f32[64,128]{1,0:T(8,128)S(1)}, u32[]{:S(2)}, u32[]{:S(2)}) collective-permute-start(f32[64,128]{1,0:T(8,128)S(1)} %copy-done.31), channel_id=1, source_target_pairs={{0,1},{1,0},{2,3},{3,2},{4,5},{5,4},{6,7},{7,6},{8,9},{9,8},{10,11... | collective-permute-start | bytes 98312 | tf_op jit(solution)/shard_map/ppermute | solution.py:462
  58.5 8.6 %copy-start.29 = (f32[64,128]{1,0:T(8,128)S(1)}, f32[64,128]{1,0:T(8,128)}, u32[]{:S(2)}) copy-start(f32[64,128]{1,0:T(8,128)} %copy-done.28) | copy-start | bytes 98308
  58.5 8.6 %copy-start.27 = (f32[64,128]{1,0:T(8,128)S(1)}, f32[64,128]{1,0:T(8,128)}, u32[]{:S(2)}) copy-start(f32[64,128]{1,0:T(8,128)} %copy-done.26) | copy-start | bytes 98308
  66.1 7.4 %copy-start.19 = (f32[64,256]{1,0:T(8,128)S(1)}, f32[64,256]{1,0:T(8,128)}, u32[]{:S(2)}) copy-start(f32[64,256]{1,0:T(8,128)} %copy-done.18) | copy-start | bytes 196612
  66.1 7.4 %copy-start.21 = (f32[64,256]{1,0:T(8,128)S(1)}, f32[64,256]{1,0:T(8,128)}, u32[]{:S(2)}) copy-start(f32[64,256]{1,0:T(8,128)} %copy-done.20) | copy-start | bytes 196612
  66.1 7.4 %copy-start.23 = (f32[64,256]{1,0:T(8,128)S(1)}, f32[64,256]{1,0:T(8,128)}, u32[]{:S(2)}) copy-start(f32[64,256]{1,0:T(8,128)} %copy-done.22) | copy-start | bytes 196612
  66.2 6.8 %collective-permute-start.19 = (f32[1,104,640]{2,1,0:T(8,128)S(1)}, f32[1,104,640]{2,1,0:T(8,128)S(1)}, u32[]{:S(2)}, u32[]{:S(2)}) collective-permute-start(f32[1,104,640]{2,1,0:T(8,128)S(1)} %constant_dynamic-slice_fusion), channel_id=1, source_target_pairs={{0,16},{4,12},{8,24},{12,4},{16,0},{20,28},{24,8},{28,20},{1,17},{... | collective-permute-start | bytes 798728 | tf_op jit(solution)/shard_map/ppermute | solution.py:312
  67.1 1.5 %collective-permute-start.20 = (f32[64,128]{1,0:T(8,128)S(1)}, f32[64,128]{1,0:T(8,128)S(1)}, u32[]{:S(2)}, u32[]{:S(2)}) collective-permute-start(f32[64,128]{1,0:T(8,128)S(1)} %copy-done.29), channel_id=1, source_target_pairs={{0,4},{1,5},{2,6},{3,7},{4,0},{5,1},{6,2},{7,3},{8,12},{9,13},{10,... | collective-permute-start | bytes 98312 | tf_op jit(solution)/shard_map/ppermute | solution.py:462
  67.1 5.7 %collective-permute-start.21 = (f32[64,128]{1,0:T(8,128)S(1)}, f32[64,128]{1,0:T(8,128)S(1)}, u32[]{:S(2)}, u32[]{:S(2)}) collective-permute-start(f32[64,128]{1,0:T(8,128)S(1)} %copy-done.27), channel_id=1, source_target_pairs={{0,28},{1,29},{2,30},{3,31},{4,8},{5,9},{6,10},{7,11},{8,4},{9,5},... | collective-permute-start | bytes 98312 | tf_op jit(solution)/shard_map/ppermute | solution.py:462
  73.0 8.2 %collective-permute-start.22 = (f32[1,104,640]{2,1,0:T(8,128)S(1)}, f32[1,104,640]{2,1,0:T(8,128)S(1)}, u32[]{:S(2)}, u32[]{:S(2)}) collective-permute-start(f32[1,104,640]{2,1,0:T(8,128)S(1)} %dynamic-slice_add_fusion), channel_id=1, source_target_pairs={{0,1},{1,0},{2,3},{3,2},{4,5},{5,4},{6,7},{7,6},{8,9},{9,8},{10,11... | collective-permute-start | bytes 798728 | tf_op jit(solution)/shard_map/ppermute | solution.py:312
  74.3 7.0 %collective-permute-start.23 = (f32[32,256]{1,0:T(8,128)S(1)}, f32[32,256]{1,0:T(8,128)S(1)}, u32[]{:S(2)}, u32[]{:S(2)}) collective-permute-start(f32[32,256]{1,0:T(8,128)S(1)} %get-tuple-element.146), channel_id=1, source_target_pairs={{0,1},{1,0},{2,3},{3,2},{4,5},{5,4},{6,7},{7,6},{8,9},{9,8},{10,11... | collective-permute-start | bytes 98312 | tf_op jit(solution)/shard_map/ppermute | solution.py:312
  81.3 15.0 %collective-permute-start.24 = (f32[1,104,640]{2,1,0:T(8,128)S(1)}, f32[1,104,640]{2,1,0:T(8,128)S(1)}, u32[]{:S(2)}, u32[]{:S(2)}) collective-permute-start(f32[1,104,640]{2,1,0:T(8,128)S(1)} %add.48), channel_id=1, source_target_pairs={{0,2},{1,3},{2,0},{3,1},{4,6},{5,7},{6,4},{7,5},{8,10},{9,11},{10,... | collective-permute-start | bytes 798728 | tf_op jit(solution)/shard_map/ppermute | solution.py:312
  82.2 14.0 %collective-permute-start.25 = (f32[32,256]{1,0:T(8,128)S(1)}, f32[32,256]{1,0:T(8,128)S(1)}, u32[]{:S(2)}, u32[]{:S(2)}) collective-permute-start(f32[32,256]{1,0:T(8,128)S(1)} %get-tuple-element.152), channel_id=1, source_target_pairs={{0,2},{1,3},{2,0},{3,1},{4,6},{5,7},{6,4},{7,5},{8,10},{9,11},{10,... | collective-permute-start | bytes 98312 | tf_op jit(solution)/shard_map/ppermute | solution.py:312
  84.3 12.0 %collective-permute-start.26 = (f32[32,256]{1,0:T(8,128)S(1)}, f32[32,256]{1,0:T(8,128)S(1)}, u32[]{:S(2)}, u32[]{:S(2)}) collective-permute-start(f32[32,256]{1,0:T(8,128)S(1)} %get-tuple-element.153), channel_id=1, source_target_pairs={{0,3},{1,2},{2,1},{3,0},{4,7},{5,6},{6,5},{7,4},{8,11},{9,10},{10,... | collective-permute-start | bytes 98312 | tf_op jit(solution)/shard_map/ppermute | solution.py:312
  96.3 6.5 %collective-permute-start.27 = (f32[1,104,640]{2,1,0:T(8,128)S(1)}, f32[1,104,640]{2,1,0:T(8,128)S(1)}, u32[]{:S(2)}, u32[]{:S(2)}) collective-permute-start(f32[1,104,640]{2,1,0:T(8,128)S(1)} %add.49), channel_id=1, source_target_pairs={{0,16},{4,12},{8,24},{12,4},{16,0},{20,28},{24,8},{28,20},{1,17},{... | collective-permute-start | bytes 798728 | tf_op jit(solution)/shard_map/ppermute | solution.py:312
  102.9 9.3 %collective-permute-start.28 = (f32[2,104,640]{2,1,0:T(8,128)S(1)}, f32[2,104,640]{2,1,0:T(8,128)S(1)}, u32[]{:S(2)}, u32[]{:S(2)}) collective-permute-start(f32[2,104,640]{2,1,0:T(8,128)S(1)} %maximum_select_fusion.3), channel_id=1, source_target_pairs={{0,8},{4,20},{8,0},{12,28},{16,24},{20,4},{24,16},{28,12},{1,9},{5... | collective-permute-start | bytes 1597448 | tf_op jit(solution)/shard_map/ppermute | solution.py:312
  112.3 2.7 %collective-permute-start.29 = (f32[4,104,640]{2,1,0:T(8,128)S(1)}, f32[4,104,640]{2,1,0:T(8,128)S(1)}, u32[]{:S(2)}, u32[]{:S(2)}) collective-permute-start(f32[4,104,640]{2,1,0:T(8,128)S(1)} %bitcast.49), channel_id=1, source_target_pairs={{0,4},{4,0},{8,12},{12,8},{16,20},{20,16},{24,28},{28,24},{1,5},{5... | collective-permute-start | bytes 3194888 | tf_op jit(solution)/shard_map/ppermute | solution.py:312
  (17 other events, 12.9 us)

commit v4 on v3

v4 whole, which is shorter than its diff:
```python
import functools

import jax
import jax.numpy as jnp
from jax import lax
from jax.experimental import pallas as pl
from jax.experimental.pallas import tpu as pltpu
from jax.sharding import PartitionSpec as P

TILE_SIDE = 32
LEVELS = 32
FEATURES = 64
TILE_CELLS = 1024
TRACERS = 2
LANES = 128
VMEM_LIMIT = 24 * 1024 * 1024

diffuse_coef = 0.2
step_size = 0.5


def pairings(tiles):
    fold = [(t, (t + tiles // 2) % tiles) for t in range(tiles)]
    inside = [(t, t ^ 1) for t in range(tiles)]
    outside = [(t, (t + 1 if t % 2 else t - 1) % tiles) for t in range(tiles)]
    return fold, inside, outside


def lane_of(shape):
    return lax.broadcasted_iota(jnp.int32, shape, 1)


def edges_of(scaled, info):
    even_tile = info[1] % 2 == 0
    rows, whole = scaled.shape
    lane = lane_of((rows, LANES))
    across = jnp.where(lane < LANES // 2, scaled[:, :LANES], scaled[:, whole - LANES :])
    bit = 1
    while bit < TILE_SIDE:
        up = pltpu.roll(across, bit, 1)
        down = pltpu.roll(across, LANES - bit, 1)
        across = jnp.where((lane & bit) != 0, up, down)
        bit *= 2
    place = lane % TILE_SIDE

    def squeezed(last):
        shift = LANES - (TILE_SIDE - 1) if last else 0
        out = None
        for k in range(whole // LANES):
            piece = scaled[:, k * LANES : (k + 1) * LANES]
            turn = (shift + k) % LANES
            piece = pltpu.roll(piece, turn, 1) if turn else piece
            out = piece if out is None else jnp.where(place == k, piece, out)
        return out

    west, east = squeezed(False), squeezed(True)
    return across, jnp.where(even_tile, east, west), jnp.where(even_tile, west, east)


def neighbour_sum(scaled, received, info):
    even_tile = info[1] % 2 == 0
    across, inside, outside = received
    whole = scaled.shape[1]
    count = whole // LANES
    lane = lane_of(scaled.shape)
    place = lane % TILE_SIDE
    west = jnp.where(even_tile, outside, inside)
    east = jnp.where(even_tile, inside, outside)

    def spread(edge, shift):
        turns = [(shift - k) % LANES for k in range(count)]
        return jnp.concatenate([pltpu.roll(edge, turn, 1) if turn else edge for turn in turns], axis=1)

    everywhere = jnp.concatenate([across] * count, axis=1)
    west_cells = jnp.where(place == 0, spread(west, 0), pltpu.roll(scaled, 1, 1))
    east_cells = jnp.where(place == TILE_SIDE - 1, spread(east, TILE_SIDE - 1), pltpu.roll(scaled, whole - 1, 1))
    south_cells = jnp.where(lane < TILE_SIDE, everywhere, pltpu.roll(scaled, TILE_SIDE, 1))
    north_cells = jnp.where(lane >= whole - TILE_SIDE, everywhere, pltpu.roll(scaled, whole - TILE_SIDE, 1))
    return west_cells + east_cells + south_cells + north_cells


def diffused(field, weight, weight_sums, received, info):
    sums = neighbour_sum(field * weight, received, info)
    return weight * (sums - field * weight_sums)


def mask_of(weight):
    return jnp.where(weight > 0.0, 1.0, 0.0)


def in_order(depths, info, message_refs, held, out_ref):
    for k in range(depths):
        held[info[0] ^ k] = message_refs[k][...]
    levels = LEVELS // depths
    for tracer in range(TRACERS):
        for d in range(depths):
            to = tracer * LEVELS + d * levels
            out_ref[to : to + levels, :] = held[d, tracer * levels : (tracer + 1) * levels, :]


def own_levels(depths, info, from_ref, to_ref):
    levels = LEVELS // depths
    for tracer in range(TRACERS):
        start = pl.multiple_of(tracer * LEVELS + info[0] * levels, levels)
        to_ref[tracer * levels : (tracer + 1) * levels, :] = from_ref[pl.ds(start, levels), :]


def gather_kernel(depths, info, edge_ref, land_ref, *refs):
    message_refs = refs[:depths]
    state_ref, weight_ref = refs[depths : depths + 2]
    edge_refs = refs[depths + 2 : depths + 5]
    in_order(depths, info, message_refs, refs[depths + 5], state_ref)
    weight = edge_ref[...] * land_ref[...].astype(jnp.float32)
    weight_rows = jnp.broadcast_to(weight, weight_ref.shape)
    weight_ref[...] = weight_rows
    scaled = jnp.concatenate([state_ref[...] * weight, weight_rows], axis=0)
    for edge_out, edge in zip(edge_refs, edges_of(scaled, info)):
        edge_out[...] = edge


def sigmoid(z):
    return 0.5 * jnp.tanh(0.5 * z) + 0.5


def contract(a, b, dims):
    return lax.dot_general(a, b, ((dims[:1], dims[1:]), ((), ())), preferred_element_type=jnp.float32)


def forward_kernel(state_ref, w_in, b_in, w_mid, b_mid, w_out_t, b_out, q_ref, one_ref, slope_one_ref, two_ref, slope_two_ref):
    inputs = state_ref[...].astype(jnp.bfloat16)
    pre_one = contract(inputs, w_in[...], (0, 0)) + b_in[...]
    gate = sigmoid(pre_one)
    hidden = pre_one * gate
    slope_one_ref[...] = gate + hidden * (1.0 - gate)
    hidden_one = hidden.astype(jnp.bfloat16)
    one_ref[...] = hidden_one
    pre_two = contract(hidden_one, w_mid[...], (1, 0)) + b_mid[...]
    gate = sigmoid(pre_two)
    hidden = pre_two * gate
    slope_two_ref[...] = gate + hidden * (1.0 - gate)
    hidden_two = hidden.astype(jnp.bfloat16)
    two_ref[...] = hidden_two
    bias = b_out[...]
    bias = jnp.concatenate([bias] * (q_ref.shape[1] // LANES), axis=1)
    q_ref[...] = contract(w_out_t[...], hidden_two, (1, 1)) + bias


def first_step_kernel(info, state_ref, weight_ref, q_ref, e0, e1, e2, next_ref, sums_ref, o0, o1, o2):
    weight = weight_ref[0:1, :]
    state = state_ref[...]
    received = (e0[...], e1[...], e2[...])
    scaled = jnp.concatenate([state * weight, weight_ref[...]], axis=0)
    sums = neighbour_sum(scaled, received, info)
    weight_sums = sums[FEATURES:, :]
    sums_ref[...] = weight_sums
    change = weight * (sums[:FEATURES, :] - state * weight_sums[0:1, :])
    state = state + diffuse_coef * change + step_size * mask_of(weight) * q_ref[...]
    next_ref[...] = state
    for edge_out, edge in zip((o0, o1, o2), edges_of(state * weight, info)):
        edge_out[...] = edge


def last_step_kernel(depths, info, state_ref, weight_ref, sums_ref, q_ref, e0, e1, e2, *refs):
    message_refs = refs[:depths]
    final_ref, adjoint_ref, upstream_ref, o0, o1, o2, held, ordered = refs[depths:]
    weight = weight_ref[0:1, :]
    mask = mask_of(weight)
    state = state_ref[...]
    received = (e0[...], e1[...], e2[...])
    change = diffused(state, weight, sums_ref[0:1, :], received, info)
    state = state + diffuse_coef * change + step_size * mask * q_ref[...]
    adjoint_ref[...] = state
    own_levels(depths, info, adjoint_ref, final_ref)
    in_order(depths, info, message_refs, held, ordered)
    adjoint = mask * (state - ordered[...])
    adjoint_ref[...] = adjoint
    upstream_ref[...] = (step_size * mask * adjoint).astype(jnp.bfloat16)
    for edge_out, edge in zip((o0, o1, o2), edges_of(adjoint * weight, info)):
        edge_out[...] = edge


def adjoint_kernel(depths, info, adjoint_ref, weight_ref, sums_ref, back_ref, e0, e1, e2, own_ref, upstream_ref, o0, o1, o2, held):
    weight = weight_ref[0:1, :]
    adjoint = adjoint_ref[...]
    received = (e0[...], e1[...], e2[...])
    adjoint = adjoint + diffuse_coef * diffused(adjoint, weight, sums_ref[0:1, :], received, info) + back_ref[...]
    upstream_ref[...] = (step_size * mask_of(weight) * adjoint).astype(jnp.bfloat16)
    held[...] = adjoint
    own_levels(depths, info, held, own_ref)
    for edge_out, edge in zip((o0, o1, o2), edges_of(own_ref[...] * weight, info)):
        edge_out[...] = edge


def end_kernel(depths, info, adjoint_ref, weight_ref, sums_ref, back_ref, e0, e1, e2, sensitivity_ref, own):
    weight = weight_ref[0:1, :]
    adjoint = adjoint_ref[...]
    received = (e0[...], e1[...], e2[...])
    own_levels(depths, info, back_ref, own)
    sensitivity_ref[...] = adjoint + diffuse_coef * diffused(adjoint, weight, sums_ref[0:1, :], received, info) + own[...]


CHUNKS = 8


def backward_kernel(with_sum, *refs):
    state_ref, upstream_ref, one_ref, slope_one_ref, two_ref, slope_two_ref, w_in, w_mid, w_out_t = refs[:9]
    if with_sum:
        earlier_ref, back_ref, total_ref = refs[9:]
    else:
        back_ref, total_ref = refs[9:]
    features = FEATURES
    width = w_mid.shape[0]
    mid_rows = width // CHUNKS
    side_rows = features // CHUNKS

    def store(first_row, rows, matrix):
        for c in range(CHUNKS):
            piece = matrix[c * rows : (c + 1) * rows, :]
            if with_sum:
                piece = piece + earlier_ref[c, first_row : first_row + rows, :]
            total_ref[c, first_row : first_row + rows, :] = piece

    upstream = upstream_ref[...]
    inputs = state_ref[...].astype(jnp.bfloat16)
    ones = jnp.ones((8, upstream.shape[1]), jnp.bfloat16)
    slope_two = (contract(upstream, w_out_t[...], (0, 0)) * slope_two_ref[...]).astype(jnp.bfloat16)
    slope_one = (contract(slope_two, w_mid[...], (1, 1)) * slope_one_ref[...]).astype(jnp.bfloat16)
    back_ref[...] = contract(w_in[...], slope_one, (1, 1))
    store(0, mid_rows, contract(one_ref[...], slope_two, (0, 0)))
    store(mid_rows, side_rows, contract(inputs, slope_one, (1, 0)))
    store(mid_rows + side_rows, side_rows, contract(upstream, two_ref[...], (1, 0)))
    bias_in = contract(ones, slope_one, (1, 0))
    bias_mid = contract(ones, slope_two, (1, 0))
    bias_out = contract(ones, upstream, (1, 1))
    bias_out = jnp.concatenate([bias_out, jnp.zeros((8, width - features), jnp.float32)], axis=1)
    first_row = mid_rows + 2 * side_rows
    for c in range(CHUNKS):
        rows = (bias_in, bias_mid, bias_out)[c] if c < 3 else jnp.zeros((8, width), jnp.float32)
        if with_sum:
            rows = rows + earlier_ref[c, first_row : first_row + 8, :]
        total_ref[c, first_row : first_row + 8, :] = rows


def spec_of(shape, dtype=jnp.float32):
    return jax.ShapeDtypeStruct(shape, dtype)


def called(kernel, outs, info, args, scratch=(), name=None):
    smem = pl.BlockSpec(memory_space=pltpu.SMEM)
    vmem = pl.BlockSpec(memory_space=pltpu.VMEM)
    in_specs = [smem] * len(info) + [vmem] * len(args)
    return pl.pallas_call(
        kernel,
        out_shape=tuple(outs),
        in_specs=in_specs,
        out_specs=tuple(vmem for _ in outs),
        scratch_shapes=list(scratch),
        compiler_params=pltpu.CompilerParams(vmem_limit_bytes=VMEM_LIMIT),
        name=name,
    )(*info, *args)


def is_power_of_two(count):
    return count & (count - 1) == 0


def swapped(x, axis, even_bit, odd_bit):
    length = lax.axis_size(axis)
    return lax.ppermute(x, axis, [(i, i ^ (odd_bit if i & 1 else even_bit)) for i in range(length)])


def tile_rounds(length):
    bits = [1 << k for k in range(length.bit_length() - 1)]
    rounds = [(bits[0], bits[0])] if bits else []
    rest = bits[1:]
    for k in range(len(rest)):
        rounds.append((rest[k], rest[(k + 1) % len(rest)]))
    return rounds


def halving_applies():
    tiles = lax.axis_size("tile")
    return tiles == CHUNKS


def all_summed(block, side_work):
    tail = block.shape[1:]
    tile = lax.axis_index("tile")
    rounds = tile_rounds(lax.axis_size("tile"))
    sides = []
    for even_bit, odd_bit in rounds:
        bit = jnp.where(tile & 1 == 1, odd_bit, even_bit)
        sides.append(((tile & bit) != 0).astype(jnp.int32))
    for (even_bit, odd_bit), side in zip(rounds, sides):
        halves = block.reshape(2, block.shape[0] // 2, *tail)
        sent = lax.dynamic_index_in_dim(halves, 1 - side, 0, False)
        kept = lax.dynamic_index_in_dim(halves, side, 0, False)
        sent = swapped(sent, "tile", even_bit, odd_bit)
        sent = side_work.send(sent)
        block = kept + sent
    for (even_bit, odd_bit), side in zip(reversed(rounds), reversed(sides)):
        other = swapped(block, "tile", even_bit, odd_bit)
        other = side_work.send(other)
        block = jnp.where(side == 0, jnp.stack([block, other]), jnp.stack([other, block]))
        block = block.reshape(block.shape[0] * block.shape[1], *tail)
    return block


def body(initial_state, observed, edge_weight, land, w_in, b_in, w_mid, b_mid, w_out, b_out):
    tiles = lax.axis_size("tile")
    depths = lax.axis_size("depth")
    info = (jnp.stack([lax.axis_index("depth"), lax.axis_index("tile")]).astype(jnp.int32),)
    width = w_mid.shape[0]
    levels = LEVELS // depths
    rows = TRACERS * levels
    ways = pairings(tiles)

    def exchanged(edges):
        return tuple(lax.ppermute(edge, "tile", way) for edge, way in zip(edges, ways))

    def from_depths(own):
        return (own, *(swapped(own, "depth", k, k) for k in range(1, depths)))

    bias_in = b_in.reshape(1, width)
    bias_mid = b_mid.reshape(1, width)
    bias_out = jnp.broadcast_to(b_out[:, None], (FEATURES, LANES))
    w_out_t = w_out.T
    weights = (w_in, bias_in, w_mid, bias_mid, w_out_t, bias_out)
    field = spec_of((FEATURES, TILE_CELLS))
    half_field = spec_of((FEATURES, TILE_CELLS), jnp.bfloat16)
    own_field = spec_of((rows, TILE_CELLS))
    weight_rows = spec_of((8, TILE_CELLS))
    edge = spec_of((FEATURES, LANES))
    first_edge = spec_of((FEATURES + 8, LANES))
    own_edge = spec_of((rows, LANES))
    held = pltpu.VMEM((depths, rows, TILE_CELLS), jnp.float32)
    whole = pltpu.VMEM((FEATURES, TILE_CELLS), jnp.float32)
    cached = (
        field,
        spec_of((TILE_CELLS, width), jnp.bfloat16),
        spec_of((TILE_CELLS, width)),
        spec_of((TILE_CELLS, width), jnp.bfloat16),
        spec_of((TILE_CELLS, width)),
    )

    def closure(state):
        return called(forward_kernel, cached, (), (state, *weights), name="closure")

    messages = from_depths(initial_state.reshape(rows, TILE_CELLS))
    state_0, weight, *edges = called(
        functools.partial(gather_kernel, depths),
        (field, weight_rows, first_edge, first_edge, first_edge),
        info,
        (edge_weight.reshape(1, TILE_CELLS), land.reshape(1, TILE_CELLS), *messages),
        scratch=[held],
        name="gather",
    )
    edges = exchanged(edges)
    state_0, target = lax.optimization_barrier((state_0, observed.reshape(rows, TILE_CELLS)))
    targets = from_depths(target)
    q, *cache_0 = closure(state_0)
    state_1, weight_sums, *edges = called(
        first_step_kernel,
        (field, weight_rows, edge, edge, edge),
        info,
        (state_0, weight, q, *edges),
        name="step",
    )
    edges = exchanged(edges)
    q, *cache_1 = closure(state_1)
    final_state, adjoint, upstream, *edges = called(
        functools.partial(last_step_kernel, depths),
        (own_field, field, half_field, edge, edge, edge),
        info,
        (state_1, weight, weight_sums, q, *edges, *targets),
        scratch=[held, whole],
        name="last_step",
    )
    edges = exchanged(edges)
    total = spec_of((CHUNKS, width // CHUNKS + 2 * (FEATURES // CHUNKS) + 8, width))
    back, grads = called(
        functools.partial(backward_kernel, False),
        (field, total),
        (),
        (state_1, upstream, *cache_1, w_in, w_mid, w_out_t),
        name="backward",
    )
    adjoint, upstream, *edges = called(
        functools.partial(adjoint_kernel, depths),
        (own_field, half_field, own_edge, own_edge, own_edge),
        info,
        (adjoint, weight, weight_sums, back, *edges),
        scratch=[whole],
        name="adjoint",
    )
    back, grads = called(
        functools.partial(backward_kernel, True),
        (field, total),
        (),
        (state_0, upstream, *cache_0, w_in, w_mid, w_out_t, grads),
        name="backward_sum",
    )
    ended = []

    def last_transfers():
        arrived = yield None
        arrived, *held = lax.optimization_barrier((arrived, *edges))
        arrived = yield arrived
        got = exchanged(held)
        arrived, *got = lax.optimization_barrier((arrived, *got))
        arrived = yield arrived
        (sensitivity,) = called(
            functools.partial(end_kernel, depths),
            (own_field,),
            info,
            (adjoint, weight, weight_sums, back, *got),
            scratch=[pltpu.VMEM((rows, TILE_CELLS), jnp.float32)],
            name="end",
        )
        arrived, sensitivity = lax.optimization_barrier((arrived, sensitivity))
        ended.append(sensitivity)
        while True:
            arrived = yield arrived

    side_work = last_transfers()
    next(side_work)
    if halving_applies():
        grads = all_summed(grads, side_work)
    else:
        grads = lax.psum(grads, "tile")
        for _ in range(3):
            grads = side_work.send(grads)
    (sensitivity,) = ended
    grads = grads * (1.0 / (tiles * TILE_CELLS))
    mid_rows = width // CHUNKS
    side_rows = FEATURES // CHUNKS
    first_row = mid_rows + 2 * side_rows
    grad_w_mid = grads[:, :mid_rows, :].reshape(width, width)
    grad_w_in = grads[:, mid_rows : mid_rows + side_rows, :].reshape(FEATURES, width)
    grad_w_out = grads[:, mid_rows + side_rows : first_row, :].reshape(FEATURES, width).T
    shape = (TRACERS, levels, TILE_CELLS)
    return (
        final_state.reshape(shape),
        sensitivity.reshape(shape),
        grad_w_in,
        grads[0, first_row],
        grad_w_mid,
        grads[1, first_row],
        grad_w_out,
        grads[2, first_row, :FEATURES],
    )


def solution(mesh):
    return jax.shard_map(
        body,
        mesh=mesh,
        in_specs=(
            P(None, "depth", "tile"),
            P(None, "depth", "tile"),
            P("tile"),
            P("tile"),
            P(),
            P(),
            P(),
            P(),
            P(),
            P(),
        ),
        out_specs=(
            P(None, "depth", "tile"),
            P(None, "depth", "tile"),
            P(),
            P(),
            P(),
            P(),
            P(),
            P(),
        ),
        check_vma=False,
    )
```

time: 119 us -> 115 us (0.966)
  waiting for transfers between devices: 50.2 us -> 36.5 us
  local copies, waits for them, and re-layouts: 20.5 us -> 31 us
  Pallas kernels: 12.5 us -> 21.1 us
  starting transfers between devices: 31.2 us -> 23.1 us
    unnamed x70 -> x100, local copies, waits for them, and re-layouts: 15.1 us -> 25.6 us
    ppermute x14 -> x12, waiting for transfers between devices: 42.5 us -> 33 us  [swapped(): lax.ppermute(x, axis, [(i, i ^ (odd_bit if i & 1 else even_bit)) for i in...]
    pallas_call x11 -> x9, Pallas kernels: 12.5 us -> 21.1 us  [called(): pl.pallas_call(kernel, out_shape=tuple(outs), in_specs=in_specs, out_spec...]
    ppermute x14 -> x12, starting transfers between devices: 17.1 us -> 11.2 us  [swapped(): lax.ppermute(x, axis, [(i, i ^ (odd_bit if i & 1 else even_bit)) for i in...]
    ppermute x16 -> x12, waiting for transfers between devices: 7.7 us -> 3.54 us  [exchanged(): lax.ppermute(edge, 'tile', way)]
    ppermute x16 -> x12, starting transfers between devices: 14.1 us -> 11.9 us  [exchanged(): lax.ppermute(edge, 'tile', way)]
  transfers between devices with their start and end apart: 30 -> 24, of which waited for: 14 -> 10; matrix products, arithmetic and copies ran while one was open for 2% -> 2% of each run, Pallas kernels for 4% -> 11%
where the time goes in v4:
time: 115 us
  waiting for transfers between devices  36.5 us (32%)
  local copies, waits for them, and re-layouts  31 us (27%)
  starting transfers between devices  23.1 us (20%)
  Pallas kernels  21.1 us (18%)
  other arithmetic  1.98 us (2%)
    ppermute x12, waiting for transfers between devices, swapped(): lax.ppermute(x, axis, [(i, i ^ (odd_bit if i & 1 else even_bit)) for i in...  33 us
    unnamed x100, local copies, waits for them, and re-layouts  25.6 us
    pallas_call x9, Pallas kernels, called(): pl.pallas_call(kernel, out_shape=tuple(outs), in_specs=in_specs, out_spec...  21.1 us
    ppermute x12, starting transfers between devices, exchanged(): lax.ppermute(edge, 'tile', way)  11.9 us
    ppermute x12, starting transfers between devices, swapped(): lax.ppermute(x, axis, [(i, i ^ (odd_bit if i & 1 else even_bit)) for i in...  11.2 us
    ppermute x12, waiting for transfers between devices, exchanged(): lax.ppermute(edge, 'tile', way)  3.54 us
  transfers between devices with their start and end apart: 24, of which 10 were waited for; matrix products, arithmetic and copies ran while one was open for 2% of the time, Pallas kernels for 11%

profile of v4, /device:TPU:0, one launch (start us, length us, event | category | flops | bytes accessed | tf_op | source)
XLA Modules:
  0.0 114.7 jit_solution(2706277833313429933)
XLA Ops:
  0.6 3.1 %collective-permute-start = (f32[16,1024]{1,0:T(8,128)}, f32[16,1024]{1,0:T(8,128)S(1)}, u32[]{:S(2)}, u32[]{:S(2)}) collective-permute-start(f32[16,1024]{1,0:T(8,128)} %bitcast.45), channel_id=1, source_target_pairs={{0,1},{1,0},{2,3},{3,2},{4,5},{5,4},{6,7},{7,6},{8,9},{9,8},{10,11... | collective-permute-start | bytes 196616 | tf_op jit(solution)/shard_map/ppermute | solution.py:269
  3.7 2.6 %collective-permute-start.1 = (f32[16,1024]{1,0:T(8,128)}, f32[16,1024]{1,0:T(8,128)S(1)}, u32[]{:S(2)}, u32[]{:S(2)}) collective-permute-start(f32[16,1024]{1,0:T(8,128)} %bitcast.46), channel_id=1, source_target_pairs={{0,2},{1,3},{2,0},{3,1},{4,6},{5,7},{6,4},{7,5},{8,10},{9,11},{10,... | collective-permute-start | bytes 196616 | tf_op jit(solution)/shard_map/ppermute | solution.py:269
  6.4 4.8 %collective-permute-done.1.refs_2_ = f32[16,1024]{1,0:T(8,128)S(1)} collective-permute-done((f32[16,1024]{1,0:T(8,128)}, f32[16,1024]{1,0:T(8,128)S(1)}, u32[]{:S(2)}, u32[]{:S(2)}) %collective-permute-start.1) | collective-permute-done | bytes 65568 | tf_op jit(solution)/shard_map/ppermute | solution.py:269
  11.2 1.4 %collective-permute-done.2.refs_3_ = f32[16,1024]{1,0:T(8,128)S(1)} collective-permute-done((f32[16,1024]{1,0:T(8,128)}, f32[16,1024]{1,0:T(8,128)S(1)}, u32[]{:S(2)}, u32[]{:S(2)}) %collective-permute-start.2) | collective-permute-done | bytes 65568 | tf_op jit(solution)/shard_map/ppermute | solution.py:269
  14.8 1.0 gather.1
  15.8 1.6 %collective-permute-start.3 = (f32[72,128]{1,0:T(8,128)S(1)}, f32[72,128]{1,0:T(8,128)S(1)}, u32[]{:S(2)}, u32[]{:S(2)}) collective-permute-start(f32[72,128]{1,0:T(8,128)S(1)} %get-tuple-element.59), channel_id=1, source_target_pairs={{0,16},{4,20},{8,24},{12,28},{16,0},{20,4},{24,8},{28,12},{1,17},{... | collective-permute-start | bytes 110600 | tf_op jit(solution)/shard_map/ppermute | solution.py:319
  17.4 1.6 %collective-permute-start.10 = (f32[16,1024]{1,0:T(8,128)}, f32[16,1024]{1,0:T(8,128)S(1)}, u32[]{:S(2)}, u32[]{:S(2)}) collective-permute-start(f32[16,1024]{1,0:T(8,128)} %bitcast.41), channel_id=1, source_target_pairs={{0,2},{1,3},{2,0},{3,1},{4,6},{5,7},{6,4},{7,5},{8,10},{9,11},{10,... | collective-permute-start | bytes 196616 | tf_op jit(solution)/shard_map/ppermute | solution.py:269
  19.0 1.5 %collective-permute-start.5 = (f32[72,128]{1,0:T(8,128)S(1)}, f32[72,128]{1,0:T(8,128)S(1)}, u32[]{:S(2)}, u32[]{:S(2)}) collective-permute-start(f32[72,128]{1,0:T(8,128)S(1)} %get-tuple-element.61), channel_id=1, source_target_pairs={{0,28},{4,8},{8,4},{12,16},{16,12},{20,24},{24,20},{28,0},{1,29},{... | collective-permute-start | bytes 110600 | tf_op jit(solution)/shard_map/ppermute | solution.py:319
  21.2 1.3 %collective-permute-start.9 = (f32[16,1024]{1,0:T(8,128)}, f32[16,1024]{1,0:T(8,128)S(1)}, u32[]{:S(2)}, u32[]{:S(2)}) collective-permute-start(f32[16,1024]{1,0:T(8,128)} %bitcast.43), channel_id=1, source_target_pairs={{0,1},{1,0},{2,3},{3,2},{4,5},{5,4},{6,7},{7,6},{8,9},{9,8},{10,11... | collective-permute-start | bytes 196616 | tf_op jit(solution)/shard_map/ppermute | solution.py:269
  24.6 1.1 copy-done
  25.7 0.9 copy-done.13
  26.6 0.9 copy-done.15
  27.5 2.7 %closure.2 = (f32[64,1024]{1,0:T(8,128)S(1)}, bf16[1024,640]{1,0:T(8,128)(2,1)S(1)}, f32[1024,640]{1,0:T(8,128)S(1)}, bf16[1024,640]{1,0:T(8,128)(2,1)S(1)}, f32[1024,640]{1,0:T(8,128)S(1)}) custom-call(f32[64,1024]{1,0:T(8,128)S(1)} %get-tuple-element.56.state_ref.refs_0_, bf16[64,640]{1,0:T(8,128)(2,1)S(1)} %copy-done.13, f32[1,640]{1,0:T(1,128)S(1)} %reshape.177.b_in, ...), custom_call_target="tpu_custom_call" | custom-call | tf_op jit(solution)/shard_map/closure/pallas_call | solution.py:252
  30.2 1.5 %copy-done.2 = f32[1024,640]{1,0:T(8,128)} copy-done((f32[1024,640]{1,0:T(8,128)}, f32[1024,640]{1,0:T(8,128)S(1)}, u32[]{:S(2)}) %copy-start.2) | copy-done | bytes 2621464
  31.6 1.1 copy-done.22
  32.7 1.1 copy-done.24
  33.8 1.6 %step.1 = (f32[64,1024]{1,0:T(8,128)S(1)}, f32[8,1024]{1,0:T(8,128)S(1)}, f32[64,128]{1,0:T(8,128)S(1)}, f32[64,128]{1,0:T(8,128)S(1)}, f32[64,128]{1,0:T(8,128)S(1)}) custom-call(s32[2]{0:T(128)S(1)} %pad_add_fusion.info, f32[64,1024]{1,0:T(8,128)S(1)} %get-tuple-element.56.state_ref.refs_0_, f32[8,1024]{1,0:T(8,128)S(1)} %get-tuple-element.57.weight_ref, ...), custom_call_target="tpu_custom_call" | custom-call | tf_op jit(solution)/shard_map/step/pallas_call | solution.py:252
  35.4 1.6 %collective-permute-start.6 = (f32[64,128]{1,0:T(8,128)S(1)}, f32[64,128]{1,0:T(8,128)S(1)}, u32[]{:S(2)}, u32[]{:S(2)}) collective-permute-start(f32[64,128]{1,0:T(8,128)S(1)} %get-tuple-element.65), channel_id=1, source_target_pairs={{0,16},{4,20},{8,24},{12,28},{16,0},{20,4},{24,8},{28,12},{1,17},{... | collective-permute-start | bytes 98312 | tf_op jit(solution)/shard_map/ppermute | solution.py:319
  37.7 2.7 %closure.3 = (f32[64,1024]{1,0:T(8,128)S(1)}, bf16[1024,640]{1,0:T(8,128)(2,1)S(1)}, f32[1024,640]{1,0:T(8,128)S(1)}, bf16[1024,640]{1,0:T(8,128)(2,1)S(1)}, f32[1024,640]{1,0:T(8,128)S(1)}) custom-call(f32[64,1024]{1,0:T(8,128)S(1)} %get-tuple-element.62.state_ref.refs_0_, bf16[64,640]{1,0:T(8,128)(2,1)S(1)} %copy-done.14, f32[1,640]{1,0:T(1,128)S(1)} %reshape.177.b_in, ...), custom_call_target="tpu_custom_call" | custom-call | tf_op jit(solution)/shard_map/closure/pallas_call | solution.py:252
  40.4 1.5 %copy-done.4 = f32[1024,640]{1,0:T(8,128)} copy-done((f32[1024,640]{1,0:T(8,128)}, f32[1024,640]{1,0:T(8,128)S(1)}, u32[]{:S(2)}) %copy-start.4) | copy-done | bytes 2621464
  41.9 1.5 %copy-done.6 = f32[1024,640]{1,0:T(8,128)} copy-done((f32[1024,640]{1,0:T(8,128)}, f32[1024,640]{1,0:T(8,128)S(1)}, u32[]{:S(2)}) %copy-start.6) | copy-done | bytes 2621464
  43.4 1.1 copy-done.18
  44.5 1.1 copy-done.20
  45.6 2.3 %last_step.1 = (f32[16,1024]{1,0:T(8,128)}, f32[64,1024]{1,0:T(8,128)S(1)}, bf16[64,1024]{1,0:T(8,128)(2,1)S(1)}, f32[64,128]{1,0:T(8,128)}, f32[64,128]{1,0:T(8,128)}, /*index=5*/f32[64,128]{1,0:T(8,128)}) custom-call(s32[2]{0:T(128)S(1)} %pad_add_fusion.info, f32[64,1024]{1,0:T(8,128)S(1)} %get-tuple-element.62.state_ref.refs_0_, ...), custom_call_target="tpu_custom_call" | custom-call | tf_op jit(solution)/shard_map/last_step/pallas_call | solution.py:252
  49.8 2.6 %collective-permute-start.14 = (f32[64,128]{1,0:T(8,128)}, f32[64,128]{1,0:T(8,128)}, u32[]{:S(2)}, u32[]{:S(2)}) collective-permute-start(f32[64,128]{1,0:T(8,128)} %get-tuple-element.79), channel_id=1, source_target_pairs={{0,28},{4,8},{8,4},{12,16},{16,12},{20,24},{24,20},{28,0},{1,29},{... | collective-permute-start | bytes 98312 | tf_op jit(solution)/shard_map/ppermute | solution.py:319
  52.3 1.7 %copy-done.5 = f32[1024,640]{1,0:T(8,128)S(1)} copy-done((f32[1024,640]{1,0:T(8,128)S(1)}, f32[1024,640]{1,0:T(8,128)}, u32[]{:S(2)}) %copy-start.5) | copy-done | bytes 2621464
  54.1 1.7 %copy-done.7 = f32[1024,640]{1,0:T(8,128)S(1)} copy-done((f32[1024,640]{1,0:T(8,128)S(1)}, f32[1024,640]{1,0:T(8,128)}, u32[]{:S(2)}) %copy-start.7) | copy-done | bytes 2621464
  55.8 0.9 copy-done.9
  56.7 0.9 copy-done.17
  57.6 1.3 %copy-done.19 = bf16[1024,640]{1,0:T(8,128)(2,1)S(1)} copy-done((bf16[1024,640]{1,0:T(8,128)(2,1)S(1)}, bf16[1024,640]{1,0:T(8,128)(2,1)}, u32[]{:S(2)}) %copy-start.19) | copy-done | bytes 1310744
  59.0 1.3 %copy-done.21 = bf16[1024,640]{1,0:T(8,128)(2,1)S(1)} copy-done((bf16[1024,640]{1,0:T(8,128)(2,1)S(1)}, bf16[1024,640]{1,0:T(8,128)(2,1)}, u32[]{:S(2)}) %copy-start.21) | copy-done | bytes 1310744
  60.3 0.9 copy-done.34
  61.2 3.9 %backward.1 = (f32[64,1024]{1,0:T(8,128)S(1)}, f32[8,104,640]{2,1,0:T(8,128)S(1)}) custom-call(f32[64,1024]{1,0:T(8,128)S(1)} %copy-done.9, bf16[64,1024]{1,0:T(8,128)(2,1)S(1)} %copy-done.34, bf16[1024,640]{1,0:T(8,128)(2,1)S(1)} %copy-done.19, f32[1024,640]{1,0:T(8,128)S(1)} %copy-done.5, bf16[1024,640]{1,0:T(8,128)(2,1)S(1)} %copy-done.21, ...), custom_call_target="tpu_custom_call" | custom-call | tf_op jit(solution)/shard_map/backward/pallas_call | solution.py:252
  65.2 1.7 %adjoint.1 = (f32[16,1024]{1,0:T(8,128)S(1)}, bf16[64,1024]{1,0:T(8,128)(2,1)S(1)}, f32[16,128]{1,0:T(8,128)S(1)}, f32[16,128]{1,0:T(8,128)S(1)}, f32[16,128]{1,0:T(8,128)S(1)}) custom-call(s32[2]{0:T(128)S(1)} %copy-done.40, f32[64,1024]{1,0:T(8,128)S(1)} %copy-done.32, f32[8,1024]{1,0:T(8,128)S(1)} %get-tuple-element.57.weight_ref, ...), custom_call_target="tpu_custom_call" | custom-call | tf_op jit(solution)/shard_map/adjoint/pallas_call | solution.py:252
  66.9 4.0 %backward_sum.1 = (f32[64,1024]{1,0:T(8,128)S(1)}, f32[8,104,640]{2,1,0:T(8,128)S(1)}) custom-call(f32[64,1024]{1,0:T(8,128)S(1)} %copy-done.11, bf16[64,1024]{1,0:T(8,128)(2,1)S(1)} %get-tuple-element.80.refs_1_, bf16[1024,640]{1,0:T(8,128)(2,1)S(1)} %copy-done.23, f32[1024,640]{1,0:T(8,128)S(1)} %get-tuple-element.82.refs_3_, ...), custom_call_target="tpu_custom_call" | custom-call | tf_op jit(solution)/shard_map/backward_sum/pallas_call | solution.py:252
  71.0 1.3 %copy-done.12 = f32[8,104,640]{2,1,0:T(8,128)} copy-done((f32[8,104,640]{2,1,0:T(8,128)}, f32[8,104,640]{2,1,0:T(8,128)S(1)}, u32[]{:S(2)}) %copy-start.12) | copy-done | bytes 2129944
  72.5 2.7 %collective-permute-done.15 = f32[4,104,640]{2,1,0:T(8,128)S(1)} collective-permute-done((f32[4,104,640]{2,1,0:T(8,128)S(1)}, f32[4,104,640]{2,1,0:T(8,128)S(1)}, u32[]{:S(2)}, u32[]{:S(2)}) %collective-permute-start.15) | collective-permute-done | bytes 1064992 | tf_op jit(solution)/shard_map/ppermute | solution.py:269
  75.1 1.4 %bitcast_add_fusion = f32[4,104,640]{2,1,0:T(8,128)S(1)} fusion(f32[4,104,640]{2,1,0:T(8,128)S(1)} %collective-permute-done.15, f32[2,4,104,640]{3,2,1,0:T(8,128)} %bitcast.36, s32[]{:T(128)S(6)} %select_n.83), kind=kLoop, calls=%fused_computation.3 | loop fusion | flops 266240 | bytes 3194884 | tf_op jit(solution)/shard_map/add | solution.py:300
  76.9 0.9 collective-permute-start.17
  78.3 2.0 %collective-permute-start.19 = (f32[16,128]{1,0:T(8,128)S(1)}, f32[16,128]{1,0:T(8,128)S(1)}, u32[]{:S(2)}, u32[]{:S(2)}) collective-permute-start(f32[16,128]{1,0:T(8,128)S(1)} %copy-done.45), channel_id=1, source_target_pairs={{0,28},{4,8},{8,4},{12,16},{16,12},{20,24},{24,20},{28,0},{1,29},{... | collective-permute-start | bytes 24584 | tf_op jit(solution)/shard_map/ppermute | solution.py:319
  80.6 3.2 %collective-permute-done.19.e2 = f32[16,128]{1,0:T(8,128)S(1)} collective-permute-done((f32[16,128]{1,0:T(8,128)S(1)}, f32[16,128]{1,0:T(8,128)S(1)}, u32[]{:S(2)}, u32[]{:S(2)}) %collective-permute-start.19) | collective-permute-done | bytes 8224 | tf_op jit(solution)/shard_map/ppermute | solution.py:319
  83.8 2.2 %collective-permute-done.16 = f32[2,104,640]{2,1,0:T(8,128)S(1)} collective-permute-done((f32[2,104,640]{2,1,0:T(8,128)S(1)}, f32[2,104,640]{2,1,0:T(8,128)S(1)}, u32[]{:S(2)}, u32[]{:S(2)}) %collective-permute-start.16) | collective-permute-done | bytes 532512 | tf_op jit(solution)/shard_map/ppermute | solution.py:269
  86.9 1.4 %end.1 = f32[16,1024]{1,0:T(8,128)} custom-call(s32[2]{0:T(128)S(1)} %copy-done.41, f32[16,1024]{1,0:T(8,128)S(1)} %copy-done.38, f32[8,1024]{1,0:T(8,128)S(1)} %get-tuple-element.57.weight_ref, f32[8,1024]{1,0:T(8,128)S(1)} %copy-done.28, f32[64,1024]{1,0:T(8,128)S(1)} %copy-done.30, f32[16,128]{1,0:T(8,128)S(1)} %collective-permute-done.17.e0, ...), custom_call_target="tpu_custom_call" | custom-call | tf_op jit(solution)/shard_map/end/pallas_call | solution.py:252
  88.3 4.4 %collective-permute-done.20 = f32[1,104,640]{2,1,0:T(8,128)S(1)} collective-permute-done((f32[1,104,640]{2,1,0:T(8,128)S(1)}, f32[1,104,640]{2,1,0:T(8,128)S(1)}, u32[]{:S(2)}, u32[]{:S(2)}) %collective-permute-start.20) | collective-permute-done | bytes 266272 | tf_op jit(solution)/shard_map/ppermute | solution.py:269
  93.4 5.7 %collective-permute-done.21 = f32[1,104,640]{2,1,0:T(8,128)S(1)} collective-permute-done((f32[1,104,640]{2,1,0:T(8,128)S(1)}, f32[1,104,640]{2,1,0:T(8,128)S(1)}, u32[]{:S(2)}, u32[]{:S(2)}) %collective-permute-start.21) | collective-permute-done | bytes 266272 | tf_op jit(solution)/shard_map/ppermute | solution.py:269
  99.5 9.1 %collective-permute-done.22 = f32[2,104,640]{2,1,0:T(8,128)S(1)} collective-permute-done((f32[2,104,640]{2,1,0:T(8,128)S(1)}, f32[2,104,640]{2,1,0:T(8,128)S(1)}, u32[]{:S(2)}, u32[]{:S(2)}) %collective-permute-start.22) | collective-permute-done | bytes 532512 | tf_op jit(solution)/shard_map/ppermute | solution.py:269
  108.8 2.7 %collective-permute-done.23 = f32[4,104,640]{2,1,0:T(8,128)S(1)} collective-permute-done((f32[4,104,640]{2,1,0:T(8,128)S(1)}, f32[4,104,640]{2,1,0:T(8,128)S(1)}, u32[]{:S(2)}, u32[]{:S(2)}) %collective-permute-start.23) | collective-permute-done | bytes 1064992 | tf_op jit(solution)/shard_map/ppermute | solution.py:269
  111.6 1.3 %slice.26 = f32[8,80,640]{2,1,0:T(8,128)} slice(f32[8,104,640]{2,1,0:T(8,128)S(1)} %bitcast.51), slice={[0:8], [0:80], [0:640]} | slice | bytes 3276800 | tf_op jit(solution)/shard_map/slice | solution.py:438
  (127 shorter events, 13.2 us)
Async XLA Ops:
  0.6 37.0 %copy-start.14 = (bf16[64,640]{1,0:T(8,128)(2,1)S(1)}, bf16[64,640]{1,0:T(8,128)(2,1)}, u32[]{:S(2)}) copy-start(bf16[64,640]{1,0:T(8,128)(2,1)} %refs_6_.3) | copy-start | bytes 245764
  0.6 5.8 %collective-permute-start = (f32[16,1024]{1,0:T(8,128)}, f32[16,1024]{1,0:T(8,128)S(1)}, u32[]{:S(2)}, u32[]{:S(2)}) collective-permute-start(f32[16,1024]{1,0:T(8,128)} %bitcast.45), channel_id=1, source_target_pairs={{0,1},{1,0},{2,3},{3,2},{4,5},{5,4},{6,7},{7,6},{8,9},{9,8},{10,11... | collective-permute-start | bytes 196616 | tf_op jit(solution)/shard_map/ppermute | solution.py:269
  3.7 7.5 %collective-permute-start.1 = (f32[16,1024]{1,0:T(8,128)}, f32[16,1024]{1,0:T(8,128)S(1)}, u32[]{:S(2)}, u32[]{:S(2)}) collective-permute-start(f32[16,1024]{1,0:T(8,128)} %bitcast.46), channel_id=1, source_target_pairs={{0,2},{1,3},{2,0},{3,1},{4,6},{5,7},{6,4},{7,5},{8,10},{9,11},{10,... | collective-permute-start | bytes 196616 | tf_op jit(solution)/shard_map/ppermute | solution.py:269
  6.3 6.3 %collective-permute-start.2 = (f32[16,1024]{1,0:T(8,128)}, f32[16,1024]{1,0:T(8,128)S(1)}, u32[]{:S(2)}, u32[]{:S(2)}) collective-permute-start(f32[16,1024]{1,0:T(8,128)} %bitcast.47), channel_id=1, source_target_pairs={{0,3},{1,2},{2,1},{3,0},{4,7},{5,6},{6,5},{7,4},{8,11},{9,10},{10,... | collective-permute-start | bytes 196616 | tf_op jit(solution)/shard_map/ppermute | solution.py:269
  6.3 31.4 %copy-start.16 = (bf16[640,64]{0,1:T(8,128)(2,1)S(1)}, bf16[640,64]{0,1:T(8,128)(2,1)}, u32[]{:S(2)}) copy-start(bf16[640,64]{0,1:T(8,128)(2,1)} %param.18) | copy-start | bytes 245764
  6.4 39.2 %copy-start.39 = (s32[2]{0:T(128)}, s32[2]{0:T(128)S(1)}, u32[]{:S(2)}) copy-start(s32[2]{0:T(128)S(1)} %pad_add_fusion.info) | copy-start | bytes 28
  15.8 21.9 %copy-start.10 = (f32[64,1024]{1,0:T(8,128)}, f32[64,1024]{1,0:T(8,128)S(1)}, u32[]{:S(2)}) copy-start(f32[64,1024]{1,0:T(8,128)S(1)} %get-tuple-element.56.state_ref.refs_0_) | copy-start | bytes 786436
  15.8 5.4 %collective-permute-start.3 = (f32[72,128]{1,0:T(8,128)S(1)}, f32[72,128]{1,0:T(8,128)S(1)}, u32[]{:S(2)}, u32[]{:S(2)}) collective-permute-start(f32[72,128]{1,0:T(8,128)S(1)} %get-tuple-element.59), channel_id=1, source_target_pairs={{0,16},{4,20},{8,24},{12,28},{16,0},{20,4},{24,8},{28,12},{1,17},{... | collective-permute-start | bytes 110600 | tf_op jit(solution)/shard_map/ppermute | solution.py:319
  17.4 19.6 %collective-permute-start.10 = (f32[16,1024]{1,0:T(8,128)}, f32[16,1024]{1,0:T(8,128)S(1)}, u32[]{:S(2)}, u32[]{:S(2)}) collective-permute-start(f32[16,1024]{1,0:T(8,128)} %bitcast.41), channel_id=1, source_target_pairs={{0,2},{1,3},{2,0},{3,1},{4,6},{5,7},{6,4},{7,5},{8,10},{9,11},{10,... | collective-permute-start | bytes 196616 | tf_op jit(solution)/shard_map/ppermute | solution.py:269
  19.0 14.8 %collective-permute-start.4 = (f32[72,128]{1,0:T(8,128)S(1)}, f32[72,128]{1,0:T(8,128)S(1)}, u32[]{:S(2)}, u32[]{:S(2)}) collective-permute-start(f32[72,128]{1,0:T(8,128)S(1)} %get-tuple-element.60), channel_id=1, source_target_pairs={{0,4},{4,0},{8,12},{12,8},{16,20},{20,16},{24,28},{28,24},{1,5},{5... | collective-permute-start | bytes 110600 | tf_op jit(solution)/shard_map/ppermute | solution.py:319
  19.0 14.8 %collective-permute-start.5 = (f32[72,128]{1,0:T(8,128)S(1)}, f32[72,128]{1,0:T(8,128)S(1)}, u32[]{:S(2)}, u32[]{:S(2)}) collective-permute-start(f32[72,128]{1,0:T(8,128)S(1)} %get-tuple-element.61), channel_id=1, source_target_pairs={{0,28},{4,8},{8,4},{12,16},{16,12},{20,24},{24,20},{28,0},{1,29},{... | collective-permute-start | bytes 110600 | tf_op jit(solution)/shard_map/ppermute | solution.py:319
  20.5 25.1 %collective-permute-start.11 = (f32[16,1024]{1,0:T(8,128)}, f32[16,1024]{1,0:T(8,128)S(1)}, u32[]{:S(2)}, u32[]{:S(2)}) collective-permute-start(f32[16,1024]{1,0:T(8,128)} %bitcast.42), channel_id=1, source_target_pairs={{0,3},{1,2},{2,1},{3,0},{4,7},{5,6},{6,5},{7,4},{8,11},{9,10},{10,... | collective-permute-start | bytes 196616 | tf_op jit(solution)/shard_map/ppermute | solution.py:269
  21.2 24.4 %collective-permute-start.9 = (f32[16,1024]{1,0:T(8,128)}, f32[16,1024]{1,0:T(8,128)S(1)}, u32[]{:S(2)}, u32[]{:S(2)}) collective-permute-start(f32[16,1024]{1,0:T(8,128)} %bitcast.43), channel_id=1, source_target_pairs={{0,1},{1,0},{2,3},{3,2},{4,5},{5,4},{6,7},{7,6},{8,9},{9,8},{10,11... | collective-permute-start | bytes 196616 | tf_op jit(solution)/shard_map/ppermute | solution.py:269
  27.5 10.2 %copy-start.1 = (bf16[640,640]{1,0:T(8,128)(2,1)S(1)}, bf16[640,640]{1,0:T(8,128)(2,1)}, u32[]{:S(2)}) copy-start(bf16[640,640]{1,0:T(8,128)(2,1)} %refs_7_.3) | copy-start | bytes 2457604
  27.5 18.1 %copy-start.35 = (f32[2,8,1024]{2,1,0:T(8,128)S(1)}, f32[2,8,1024]{2,1,0:T(8,128)}, u32[]{:S(2)}) copy-start(f32[2,8,1024]{2,1,0:T(8,128)} %param.11) | copy-start | bytes 196612
  35.4 10.2 %copy-start.8 = (f32[64,1024]{1,0:T(8,128)}, f32[64,1024]{1,0:T(8,128)S(1)}, u32[]{:S(2)}) copy-start(f32[64,1024]{1,0:T(8,128)S(1)} %get-tuple-element.62.state_ref.refs_0_) | copy-start | bytes 786436
  35.4 12.5 %copy-start.26 = (f32[8,1024]{1,0:T(8,128)}, f32[8,1024]{1,0:T(8,128)S(1)}, u32[]{:S(2)}) copy-start(f32[8,1024]{1,0:T(8,128)S(1)} %get-tuple-element.63.sums_ref) | copy-start | bytes 98308
  35.4 10.2 %collective-permute-start.6 = (f32[64,128]{1,0:T(8,128)S(1)}, f32[64,128]{1,0:T(8,128)S(1)}, u32[]{:S(2)}, u32[]{:S(2)}) collective-permute-start(f32[64,128]{1,0:T(8,128)S(1)} %get-tuple-element.65), channel_id=1, source_target_pairs={{0,16},{4,20},{8,24},{12,28},{16,0},{20,4},{24,8},{28,12},{1,17},{... | collective-permute-start | bytes 98312 | tf_op jit(solution)/shard_map/ppermute | solution.py:319
  37.0 8.6 %collective-permute-start.7 = (f32[64,128]{1,0:T(8,128)S(1)}, f32[64,128]{1,0:T(8,128)S(1)}, u32[]{:S(2)}, u32[]{:S(2)}) collective-permute-start(f32[64,128]{1,0:T(8,128)S(1)} %get-tuple-element.66), channel_id=1, source_target_pairs={{0,4},{4,0},{8,12},{12,8},{16,20},{20,16},{24,28},{28,24},{1,5},{5... | collective-permute-start | bytes 98312 | tf_op jit(solution)/shard_map/ppermute | solution.py:319
  37.0 8.6 %collective-permute-start.8 = (f32[64,128]{1,0:T(8,128)S(1)}, f32[64,128]{1,0:T(8,128)S(1)}, u32[]{:S(2)}, u32[]{:S(2)}) collective-permute-start(f32[64,128]{1,0:T(8,128)S(1)} %get-tuple-element.67), channel_id=1, source_target_pairs={{0,28},{4,8},{8,4},{12,16},{16,12},{20,24},{24,20},{28,0},{1,29},{... | collective-permute-start | bytes 98312 | tf_op jit(solution)/shard_map/ppermute | solution.py:319
  49.2 15.9 %collective-permute-start.12 = (f32[64,128]{1,0:T(8,128)}, f32[64,128]{1,0:T(8,128)}, u32[]{:S(2)}, u32[]{:S(2)}) collective-permute-start(f32[64,128]{1,0:T(8,128)} %get-tuple-element.77), channel_id=1, source_target_pairs={{0,16},{4,20},{8,24},{12,28},{16,0},{20,4},{24,8},{28,12},{1,17},{... | collective-permute-start | bytes 98312 | tf_op jit(solution)/shard_map/ppermute | solution.py:319
  49.8 15.3 %collective-permute-start.13 = (f32[64,128]{1,0:T(8,128)}, f32[64,128]{1,0:T(8,128)}, u32[]{:S(2)}, u32[]{:S(2)}) collective-permute-start(f32[64,128]{1,0:T(8,128)} %get-tuple-element.78), channel_id=1, source_target_pairs={{0,4},{4,0},{8,12},{12,8},{16,20},{20,16},{24,28},{28,24},{1,5},{5... | collective-permute-start | bytes 98312 | tf_op jit(solution)/shard_map/ppermute | solution.py:319
  49.8 15.4 %collective-permute-start.14 = (f32[64,128]{1,0:T(8,128)}, f32[64,128]{1,0:T(8,128)}, u32[]{:S(2)}, u32[]{:S(2)}) collective-permute-start(f32[64,128]{1,0:T(8,128)} %get-tuple-element.79), channel_id=1, source_target_pairs={{0,28},{4,8},{8,4},{12,16},{16,12},{20,24},{24,20},{28,0},{1,29},{... | collective-permute-start | bytes 98312 | tf_op jit(solution)/shard_map/ppermute | solution.py:319
  61.2 4.0 %copy-start.27 = (f32[8,1024]{1,0:T(8,128)S(1)}, f32[8,1024]{1,0:T(8,128)}, u32[]{:S(2)}) copy-start(f32[8,1024]{1,0:T(8,128)} %copy-done.26) | copy-start | bytes 98308
  61.2 4.0 %copy-start.32 = (f32[64,1024]{1,0:T(8,128)S(1)}, f32[64,1024]{1,0:T(8,128)}, u32[]{:S(2)}) copy-start(f32[64,1024]{1,0:T(8,128)} %copy-done.31) | copy-start | bytes 786436
  61.2 4.0 %copy-start.40 = (s32[2]{0:T(128)S(1)}, s32[2]{0:T(128)}, u32[]{:S(2)}) copy-start(s32[2]{0:T(128)} %copy-done.39) | copy-start | bytes 28
  61.2 5.7 %copy-start.3 = (f32[1024,640]{1,0:T(8,128)S(1)}, f32[1024,640]{1,0:T(8,128)}, u32[]{:S(2)}) copy-start(f32[1024,640]{1,0:T(8,128)} %copy-done.2) | copy-start | bytes 7864324
  61.2 5.7 %copy-start.11 = (f32[64,1024]{1,0:T(8,128)S(1)}, f32[64,1024]{1,0:T(8,128)}, u32[]{:S(2)}) copy-start(f32[64,1024]{1,0:T(8,128)} %copy-done.10) | copy-start | bytes 786436
  61.2 5.7 %copy-start.23 = (bf16[1024,640]{1,0:T(8,128)(2,1)S(1)}, bf16[1024,640]{1,0:T(8,128)(2,1)}, u32[]{:S(2)}) copy-start(bf16[1024,640]{1,0:T(8,128)(2,1)} %copy-done.22) | copy-start | bytes 3932164
  61.2 5.7 %copy-start.25 = (bf16[1024,640]{1,0:T(8,128)(2,1)S(1)}, bf16[1024,640]{1,0:T(8,128)(2,1)}, u32[]{:S(2)}) copy-start(bf16[1024,640]{1,0:T(8,128)(2,1)} %copy-done.24) | copy-start | bytes 3932164
  66.8 4.1 %copy-start.37 = (f32[16,1024]{1,0:T(8,128)}, f32[16,1024]{1,0:T(8,128)S(1)}, u32[]{:S(2)}) copy-start(f32[16,1024]{1,0:T(8,128)S(1)} %get-tuple-element.95.adjoint_ref) | copy-start | bytes 196612
  66.8 4.1 %copy-start.44 = (f32[16,128]{1,0:T(8,128)}, f32[16,128]{1,0:T(8,128)S(1)}, u32[]{:S(2)}) copy-start(f32[16,128]{1,0:T(8,128)S(1)} %get-tuple-element.93) | copy-start | bytes 24580
  66.8 4.1 %copy-start.46 = (f32[16,128]{1,0:T(8,128)}, f32[16,128]{1,0:T(8,128)S(1)}, u32[]{:S(2)}) copy-start(f32[16,128]{1,0:T(8,128)S(1)} %get-tuple-element.92) | copy-start | bytes 24580
  66.9 4.1 %copy-start.48 = (f32[16,128]{1,0:T(8,128)}, f32[16,128]{1,0:T(8,128)S(1)}, u32[]{:S(2)}) copy-start(f32[16,128]{1,0:T(8,128)S(1)} %get-tuple-element.91) | copy-start | bytes 24580
  72.4 2.7 %collective-permute-start.15 = (f32[4,104,640]{2,1,0:T(8,128)S(1)}, f32[4,104,640]{2,1,0:T(8,128)S(1)}, u32[]{:S(2)}, u32[]{:S(2)}) collective-permute-start(f32[4,104,640]{2,1,0:T(8,128)S(1)} %dynamic-slice_bitcast_fusion), channel_id=1, source_target_pairs={{0,4},{4,0},{8,12},{12,8},{16,20},{20,16},{24,28},{28,24},{1,5},{5... | collective-permute-start | bytes 3194888 | tf_op jit(solution)/shard_map/ppermute | solution.py:269
  75.1 3.2 %copy-start.45 = (f32[16,128]{1,0:T(8,128)S(1)}, f32[16,128]{1,0:T(8,128)}, u32[]{:S(2)}) copy-start(f32[16,128]{1,0:T(8,128)} %copy-done.44) | copy-start | bytes 24580
  76.6 10.3 %copy-start.28 = (f32[8,1024]{1,0:T(8,128)S(1)}, f32[8,1024]{1,0:T(8,128)}, u32[]{:S(2)}) copy-start(f32[8,1024]{1,0:T(8,128)} %copy-done.26) | copy-start | bytes 98308
  76.6 10.3 %copy-start.30 = (f32[64,1024]{1,0:T(8,128)S(1)}, f32[64,1024]{1,0:T(8,128)}, u32[]{:S(2)}) copy-start(f32[64,1024]{1,0:T(8,128)} %copy-done.29) | copy-start | bytes 786436
  76.6 10.3 %copy-start.38 = (f32[16,1024]{1,0:T(8,128)S(1)}, f32[16,1024]{1,0:T(8,128)}, u32[]{:S(2)}) copy-start(f32[16,1024]{1,0:T(8,128)} %copy-done.37) | copy-start | bytes 196612
  76.6 10.3 %copy-start.41 = (s32[2]{0:T(128)S(1)}, s32[2]{0:T(128)}, u32[]{:S(2)}) copy-start(s32[2]{0:T(128)} %copy-done.39) | copy-start | bytes 28
  76.7 9.4 %collective-permute-start.16 = (f32[2,104,640]{2,1,0:T(8,128)S(1)}, f32[2,104,640]{2,1,0:T(8,128)S(1)}, u32[]{:S(2)}, u32[]{:S(2)}) collective-permute-start(f32[2,104,640]{2,1,0:T(8,128)S(1)} %dynamic-slice_bitcast_fusion.1), channel_id=1, source_target_pairs={{0,8},{4,20},{8,0},{12,28},{16,24},{20,4},{24,16},{28,12},{1,9},{5... | collective-permute-start | bytes 1597448 | tf_op jit(solution)/shard_map/ppermute | solution.py:269
  76.9 3.8 %collective-permute-start.17 = (f32[16,128]{1,0:T(8,128)S(1)}, f32[16,128]{1,0:T(8,128)S(1)}, u32[]{:S(2)}, u32[]{:S(2)}) collective-permute-start(f32[16,128]{1,0:T(8,128)S(1)} %copy-done.49), channel_id=1, source_target_pairs={{0,16},{4,20},{8,24},{12,28},{16,0},{20,4},{24,8},{28,12},{1,17},{... | collective-permute-start | bytes 24584 | tf_op jit(solution)/shard_map/ppermute | solution.py:319
  77.8 2.8 %collective-permute-start.18 = (f32[16,128]{1,0:T(8,128)S(1)}, f32[16,128]{1,0:T(8,128)S(1)}, u32[]{:S(2)}, u32[]{:S(2)}) collective-permute-start(f32[16,128]{1,0:T(8,128)S(1)} %copy-done.47), channel_id=1, source_target_pairs={{0,4},{4,0},{8,12},{12,8},{16,20},{20,16},{24,28},{28,24},{1,5},{5... | collective-permute-start | bytes 24584 | tf_op jit(solution)/shard_map/ppermute | solution.py:319
  78.3 5.5 %collective-permute-start.19 = (f32[16,128]{1,0:T(8,128)S(1)}, f32[16,128]{1,0:T(8,128)S(1)}, u32[]{:S(2)}, u32[]{:S(2)}) collective-permute-start(f32[16,128]{1,0:T(8,128)S(1)} %copy-done.45), channel_id=1, source_target_pairs={{0,28},{4,8},{8,4},{12,16},{16,12},{20,24},{24,20},{28,0},{1,29},{... | collective-permute-start | bytes 24584 | tf_op jit(solution)/shard_map/ppermute | solution.py:319
  86.2 6.5 %collective-permute-start.20 = (f32[1,104,640]{2,1,0:T(8,128)S(1)}, f32[1,104,640]{2,1,0:T(8,128)S(1)}, u32[]{:S(2)}, u32[]{:S(2)}) collective-permute-start(f32[1,104,640]{2,1,0:T(8,128)S(1)} %constant_dynamic-slice_fusion), channel_id=1, source_target_pairs={{0,16},{4,12},{8,24},{12,4},{16,0},{20,28},{24,8},{28,20},{1,17},{... | collective-permute-start | bytes 798728 | tf_op jit(solution)/shard_map/ppermute | solution.py:269
  92.7 6.5 %collective-permute-start.21 = (f32[1,104,640]{2,1,0:T(8,128)S(1)}, f32[1,104,640]{2,1,0:T(8,128)S(1)}, u32[]{:S(2)}, u32[]{:S(2)}) collective-permute-start(f32[1,104,640]{2,1,0:T(8,128)S(1)} %dynamic-slice_add_fusion), channel_id=1, source_target_pairs={{0,16},{4,12},{8,24},{12,4},{16,0},{20,28},{24,8},{28,20},{1,17},{... | collective-permute-start | bytes 798728 | tf_op jit(solution)/shard_map/ppermute | solution.py:269
  99.3 9.3 %collective-permute-start.22 = (f32[2,104,640]{2,1,0:T(8,128)S(1)}, f32[2,104,640]{2,1,0:T(8,128)S(1)}, u32[]{:S(2)}, u32[]{:S(2)}) collective-permute-start(f32[2,104,640]{2,1,0:T(8,128)S(1)} %maximum_select_fusion.3), channel_id=1, source_target_pairs={{0,8},{4,20},{8,0},{12,28},{16,24},{20,4},{24,16},{28,12},{1,9},{5... | collective-permute-start | bytes 1597448 | tf_op jit(solution)/shard_map/ppermute | solution.py:269
  108.7 2.7 %collective-permute-start.23 = (f32[4,104,640]{2,1,0:T(8,128)S(1)}, f32[4,104,640]{2,1,0:T(8,128)S(1)}, u32[]{:S(2)}, u32[]{:S(2)}) collective-permute-start(f32[4,104,640]{2,1,0:T(8,128)S(1)} %bitcast.55), channel_id=1, source_target_pairs={{0,4},{4,0},{8,12},{12,8},{16,20},{20,16},{24,28},{28,24},{1,5},{5... | collective-permute-start | bytes 3194888 | tf_op jit(solution)/shard_map/ppermute | solution.py:269
  (26 other events, 31.3 us)

commit v5 on v4

--- a/solution.py
+++ b/solution.py
@@ -105,15 +105,28 @@
         to_ref[tracer * levels : (tracer + 1) * levels, :] = from_ref[pl.ds(start, levels), :]
 
 
-def gather_kernel(depths, info, edge_ref, land_ref, *refs):
+def prepare_kernel(edge_ref, land_ref, state_ref, b_in, b_mid, b_out, weight_ref, own_ref, in_ref, mid_ref, out_ref):
+    weight = edge_ref[...] * land_ref[...].astype(jnp.float32)
+    weight_ref[...] = jnp.broadcast_to(weight, weight_ref.shape)
+    own_ref[...] = state_ref[...]
+    in_ref[...] = b_in[...].reshape(in_ref.shape)
+    mid_ref[...] = b_mid[...].reshape(mid_ref.shape)
+    rest = b_out[...].reshape(1, FEATURES)
+    terms = []
+    for _ in range(3):
+        term = rest.astype(jnp.bfloat16)
+        terms.append(term)
+        rest = rest - term.astype(jnp.float32)
+    terms.append(jnp.zeros((5, FEATURES), jnp.bfloat16))
+    out_ref[...] = contract(jnp.concatenate(terms, axis=0), jnp.ones((8, LANES), jnp.bfloat16), (0, 0))
+
+
+def gather_kernel(depths, info, weight_ref, *refs):
     message_refs = refs[:depths]
-    state_ref, weight_ref = refs[depths : depths + 2]
-    edge_refs = refs[depths + 2 : depths + 5]
-    in_order(depths, info, message_refs, refs[depths + 5], state_ref)
-    weight = edge_ref[...] * land_ref[...].astype(jnp.float32)
-    weight_rows = jnp.broadcast_to(weight, weight_ref.shape)
-    weight_ref[...] = weight_rows
-    scaled = jnp.concatenate([state_ref[...] * weight, weight_rows], axis=0)
+    state_ref = refs[depths]
+    edge_refs = refs[depths + 1 : depths + 4]
+    in_order(depths, info, message_refs, refs[depths + 4], state_ref)
+    scaled = jnp.concatenate([state_ref[...] * weight_ref[0:1, :], weight_ref[...]], axis=0)
     for edge_out, edge in zip(edge_refs, edges_of(scaled, info)):
         edge_out[...] = edge
 
@@ -126,23 +139,26 @@
     return lax.dot_general(a, b, ((dims[:1], dims[1:]), ((), ())), preferred_element_type=jnp.float32)
 
 
-def forward_kernel(state_ref, w_in, b_in, w_mid, b_mid, w_out_t, b_out, q_ref, one_ref, slope_one_ref, two_ref, slope_two_ref):
-    inputs = state_ref[...].astype(jnp.bfloat16)
-    pre_one = contract(inputs, w_in[...], (0, 0)) + b_in[...]
-    gate = sigmoid(pre_one)
-    hidden = pre_one * gate
-    slope_one_ref[...] = gate + hidden * (1.0 - gate)
-    hidden_one = hidden.astype(jnp.bfloat16)
-    one_ref[...] = hidden_one
-    pre_two = contract(hidden_one, w_mid[...], (1, 0)) + b_mid[...]
-    gate = sigmoid(pre_two)
-    hidden = pre_two * gate
-    slope_two_ref[...] = gate + hidden * (1.0 - gate)
-    hidden_two = hidden.astype(jnp.bfloat16)
-    two_ref[...] = hidden_two
+def layer(pre):
+    gate = sigmoid(pre)
+    hidden = pre * gate
+    return hidden.astype(jnp.bfloat16), gate + hidden * (1.0 - gate)
+
+
+def hidden_layers(state, w_in, b_in, w_mid, b_mid):
+    inputs = state.astype(jnp.bfloat16)
+    hidden_one, slope_one = layer(contract(inputs, w_in[...], (0, 0)) + b_in[...])
+    hidden_two, slope_two = layer(contract(hidden_one, w_mid[...], (1, 0)) + b_mid[...])
+    return hidden_one, slope_one, hidden_two, slope_two
+
+
+def forward_kernel(state_ref, w_in, b_in, w_mid, b_mid, w_out_t, b_out, q_ref, *cache_refs):
+    layers = hidden_layers(state_ref[...], w_in, b_in, w_mid, b_mid)
     bias = b_out[...]
     bias = jnp.concatenate([bias] * (q_ref.shape[1] // LANES), axis=1)
-    q_ref[...] = contract(w_out_t[...], hidden_two, (1, 1)) + bias
+    q_ref[...] = contract(w_out_t[...], layers[2], (1, 1)) + bias
+    for cache_ref, value in zip(cache_refs, layers):
+        cache_ref[...] = value
 
 
 def first_step_kernel(info, state_ref, weight_ref, q_ref, e0, e1, e2, next_ref, sums_ref, o0, o1, o2):
@@ -199,46 +215,75 @@
     sensitivity_ref[...] = adjoint + diffuse_coef * diffused(adjoint, weight, sums_ref[0:1, :], received, info) + own[...]
 
 
-CHUNKS = 8
-
-
-def backward_kernel(with_sum, *refs):
-    state_ref, upstream_ref, one_ref, slope_one_ref, two_ref, slope_two_ref, w_in, w_mid, w_out_t = refs[:9]
-    if with_sum:
-        earlier_ref, back_ref, total_ref = refs[9:]
-    else:
-        back_ref, total_ref = refs[9:]
-    features = FEATURES
+HALVES = 2
+EXPONENT_ROW = 4
+TOP_EXPONENT = 14.0
+
+
+def exponent_of(part):
+    largest = jnp.max(jnp.max(jnp.abs(part), axis=0, keepdims=True), axis=1, keepdims=True)
+    exponent = jnp.ceil(jnp.log2(jnp.maximum(largest, 1e-37))) - TOP_EXPONENT
+    return jnp.clip(exponent, -110.0, 110.0)
+
+
+def gradient_parts(inputs, upstream, layers, w_in, w_mid, w_out_t):
+    hidden_one, slope_one, hidden_two, slope_two = layers
     width = w_mid.shape[0]
-    mid_rows = width // CHUNKS
-    side_rows = features // CHUNKS
-
-    def store(first_row, rows, matrix):
-        for c in range(CHUNKS):
-            piece = matrix[c * rows : (c + 1) * rows, :]
-            if with_sum:
-                piece = piece + earlier_ref[c, first_row : first_row + rows, :]
-            total_ref[c, first_row : first_row + rows, :] = piece
-
-    upstream = upstream_ref[...]
+    ones = jnp.ones((8, upstream.shape[1]), jnp.bfloat16)
+    slope_two = (contract(upstream, w_out_t[...], (0, 0)) * slope_two).astype(jnp.bfloat16)
+    slope_one = (contract(slope_two, w_mid[...], (1, 1)) * slope_one).astype(jnp.bfloat16)
+    back = contract(w_in[...], slope_one, (1, 1))
+    bias_out = contract(ones, upstream, (1, 1))
+    return back, (
+        contract(hidden_one, slope_two, (0, 0)),
+        contract(inputs, slope_one, (1, 0)),
+        contract(upstream, hidden_two, (1, 0)),
+        contract(ones, slope_one, (1, 0)),
+        contract(ones, slope_two, (1, 0)),
+        jnp.concatenate([bias_out, jnp.zeros((8, width - FEATURES), jnp.float32)], axis=1),
+    )
+
+
+def first_backward_kernel(state_ref, upstream_ref, w_in, b_in, w_mid, b_mid, w_out_t, back_ref, *part_refs):
+    state = state_ref[...]
+    layers = hidden_layers(state, w_in, b_in, w_mid, b_mid)
+    back, parts = gradient_parts(state.astype(jnp.bfloat16), upstream_ref[...], layers, w_in, w_mid, w_out_t)
+    back_ref[...] = back
+    for part_ref, part in zip(part_refs, parts):
+        part_ref[...] = part
+
+
+def last_backward_kernel(info, state_ref, upstream_ref, one_ref, slope_one_ref, two_ref, slope_two_ref, w_in, w_mid, w_out_t, *refs):
+    earlier_refs = refs[:6]
+    back_ref, kept_ref, sent_ref = refs[6:]
+    layers = (one_ref[...], slope_one_ref[...], two_ref[...], slope_two_ref[...])
     inputs = state_ref[...].astype(jnp.bfloat16)
-    ones = jnp.ones((8, upstream.shape[1]), jnp.bfloat16)
-    slope_two = (contract(upstream, w_out_t[...], (0, 0)) * slope_two_ref[...]).astype(jnp.bfloat16)
-    slope_one = (contract(slope_two, w_mid[...], (1, 1)) * slope_one_ref[...]).astype(jnp.bfloat16)
-    back_ref[...] = contract(w_in[...], slope_one, (1, 1))
-    store(0, mid_rows, contract(one_ref[...], slope_two, (0, 0)))
-    store(mid_rows, side_rows, contract(inputs, slope_one, (1, 0)))
-    store(mid_rows + side_rows, side_rows, contract(upstream, two_ref[...], (1, 0)))
-    bias_in = contract(ones, slope_one, (1, 0))
-    bias_mid = contract(ones, slope_two, (1, 0))
-    bias_out = contract(ones, upstream, (1, 1))
-    bias_out = jnp.concatenate([bias_out, jnp.zeros((8, width - features), jnp.float32)], axis=1)
-    first_row = mid_rows + 2 * side_rows
-    for c in range(CHUNKS):
-        rows = (bias_in, bias_mid, bias_out)[c] if c < 3 else jnp.zeros((8, width), jnp.float32)
-        if with_sum:
-            rows = rows + earlier_ref[c, first_row : first_row + 8, :]
-        total_ref[c, first_row : first_row + 8, :] = rows
+    back, parts = gradient_parts(inputs, upstream_ref[...], layers, w_in, w_mid, w_out_t)
+    back_ref[...] = back
+    mid, side_in, side_out, bias_in, bias_mid, bias_out = [part + ref[...] for part, ref in zip(parts, earlier_refs)]
+    row = lax.broadcasted_iota(jnp.int32, bias_in.shape, 0)
+    own = info[1] % HALVES
+    for half in range(HALVES):
+        pieces = []
+        for matrix in (mid, side_in, side_out):
+            count = matrix.shape[0] // HALVES
+            pieces.append(matrix[half * count : (half + 1) * count, :])
+        tail = jnp.where(row == 0, bias_mid if half else bias_in, 0.0)
+        if half == 0:
+            tail = jnp.where(row == 1, bias_out, tail)
+        pieces.append(tail)
+        for k, exponent in enumerate([exponent_of(piece) for piece in pieces]):
+            tail = jnp.where(row == EXPONENT_ROW + k, exponent, tail)
+        pieces[-1] = tail
+
+        def store(to_ref, pieces=pieces):
+            at = 0
+            for piece in pieces:
+                to_ref[at : at + piece.shape[0], :] = piece
+                at += piece.shape[0]
+
+        pl.when(own == half)(functools.partial(store, kept_ref))
+        pl.when(own != half)(functools.partial(store, sent_ref))
 
 
 def spec_of(shape, dtype=jnp.float32):
@@ -260,50 +305,64 @@
     )(*info, *args)
 
 
-def is_power_of_two(count):
-    return count & (count - 1) == 0
-
-
 def swapped(x, axis, even_bit, odd_bit):
     length = lax.axis_size(axis)
     return lax.ppermute(x, axis, [(i, i ^ (odd_bit if i & 1 else even_bit)) for i in range(length)])
 
 
-def tile_rounds(length):
-    bits = [1 << k for k in range(length.bit_length() - 1)]
-    rounds = [(bits[0], bits[0])] if bits else []
-    rest = bits[1:]
-    for k in range(len(rest)):
-        rounds.append((rest[k], rest[(k + 1) % len(rest)]))
-    return rounds
-
-
-def halving_applies():
-    tiles = lax.axis_size("tile")
-    return tiles == CHUNKS
-
-
-def all_summed(block, side_work):
-    tail = block.shape[1:]
-    tile = lax.axis_index("tile")
-    rounds = tile_rounds(lax.axis_size("tile"))
-    sides = []
-    for even_bit, odd_bit in rounds:
-        bit = jnp.where(tile & 1 == 1, odd_bit, even_bit)
-        sides.append(((tile & bit) != 0).astype(jnp.int32))
-    for (even_bit, odd_bit), side in zip(rounds, sides):
-        halves = block.reshape(2, block.shape[0] // 2, *tail)
-        sent = lax.dynamic_index_in_dim(halves, 1 - side, 0, False)
-        kept = lax.dynamic_index_in_dim(halves, side, 0, False)
-        sent = swapped(sent, "tile", even_bit, odd_bit)
-        sent = side_work.send(sent)
-        block = kept + sent
-    for (even_bit, odd_bit), side in zip(reversed(rounds), reversed(sides)):
-        other = swapped(block, "tile", even_bit, odd_bit)
-        other = side_work.send(other)
-        block = jnp.where(side == 0, jnp.stack([block, other]), jnp.stack([other, block]))
-        block = block.reshape(block.shape[0] * block.shape[1], *tail)
-    return block
+def by_part(rows, exponents):
+    width = exponents.shape[1]
+    starts = part_starts(rows)
+    row = lax.broadcasted_iota(jnp.int32, (rows, width), 0)
+    out = exponents[3:4]
+    for k in (2, 1, 0):
+        out = jnp.where(row < starts[k + 1], exponents[k : k + 1], out)
+    return out
+
+
+def part_starts(rows):
+    side = FEATURES // HALVES
+    return (0, rows - 8 - 2 * side, rows - 8 - side, rows - 8)
+
+
+def exponents_of(half):
+    return half[half.shape[0] - 8 + EXPONENT_ROW :, :].astype(jnp.float32)
+
+
+def with_exponents(half, exponents):
+    rows, width = half.shape
+    row = lax.broadcasted_iota(jnp.int32, (rows, width), 0)
+    out = half
+    for k in range(4):
+        out = jnp.where(row == rows - 8 + EXPONENT_ROW + k, exponents[k : k + 1], out)
+    return out.astype(jnp.float16)
+
+
+def exact_power(exponent):
+    count = jnp.clip(-exponent, 0.0, 31.0).astype(jnp.int32)
+    out = jnp.ones(exponent.shape, jnp.float32)
+    for bit in range(5):
+        out = out * jnp.where((count >> bit) & 1 == 1, 2.0 ** -(1 << bit), 1.0)
+    return out
+
+
+def summed_by_tile(kept, sent, side_work):
+    rows = kept.shape[0]
+    received = side_work.send(swapped(sent, "tile", 1, 1))
+    exponents = jnp.maximum(exponents_of(kept), exponents_of(received)) + 1.0
+    factors = lax.optimization_barrier(jnp.exp2(-exponents))
+    half = with_exponents((kept + received) * by_part(rows, factors), exponents)
+    for even_bit, odd_bit in ((2, 4), (4, 2)):
+        received = side_work.send(swapped(half, "tile", even_bit, odd_bit))
+        mine, other = exponents_of(half), exponents_of(received)
+        exponents = jnp.maximum(mine, other) + 1.0
+        factors = lax.optimization_barrier((exact_power(mine - exponents), exact_power(other - exponents)))
+        total = half.astype(jnp.float32) * by_part(rows, factors[0])
+        total = total + received.astype(jnp.float32) * by_part(rows, factors[1])
+        half = with_exponents(total, exponents)
+    other = swapped(half, "tile", 1, 1)
+    first = lax.axis_index("tile") % HALVES == 0
+    return jnp.where(first, jnp.stack([half, other]), jnp.stack([other, half]))
 
 
 def body(initial_state, observed, edge_weight, land, w_in, b_in, w_mid, b_mid, w_out, b_out):
@@ -321,11 +380,7 @@
     def from_depths(own):
         return (own, *(swapped(own, "depth", k, k) for k in range(1, depths)))
 
-    bias_in = b_in.reshape(1, width)
-    bias_mid = b_mid.reshape(1, width)
-    bias_out = jnp.broadcast_to(b_out[:, None], (FEATURES, LANES))
     w_out_t = w_out.T
-    weights = (w_in, bias_in, w_mid, bias_mid, w_out_t, bias_out)
     field = spec_of((FEATURES, TILE_CELLS))
     half_field = spec_of((FEATURES, TILE_CELLS), jnp.bfloat16)
     own_field = spec_of((rows, TILE_CELLS))
@@ -336,29 +391,40 @@
     held = pltpu.VMEM((depths, rows, TILE_CELLS), jnp.float32)
     whole = pltpu.VMEM((FEATURES, TILE_CELLS), jnp.float32)
     cached = (
-        field,
         spec_of((TILE_CELLS, width), jnp.bfloat16),
         spec_of((TILE_CELLS, width)),
         spec_of((TILE_CELLS, width), jnp.bfloat16),
         spec_of((TILE_CELLS, width)),
     )
-
-    def closure(state):
-        return called(forward_kernel, cached, (), (state, *weights), name="closure")
-
-    messages = from_depths(initial_state.reshape(rows, TILE_CELLS))
-    state_0, weight, *edges = called(
+    own_state = initial_state.reshape(rows, TILE_CELLS)
+    others = from_depths(own_state)[1:]
+    weight, own_state, bias_in, bias_mid, bias_out = called(
+        prepare_kernel,
+        (weight_rows, own_field, spec_of((1, width)), spec_of((1, width)), edge),
+        (),
+        (edge_weight.reshape(1, TILE_CELLS), land.reshape(1, TILE_CELLS), own_state, b_in, b_mid, b_out),
+        name="prepare",
+    )
+    others, weight, own_state, bias_in, bias_mid, bias_out = lax.optimization_barrier(
+        (others, weight, own_state, bias_in, bias_mid, bias_out)
+    )
+    weights = (w_in, bias_in, w_mid, bias_mid, w_out_t, bias_out)
+
+    def closure(state, outs):
+        return called(forward_kernel, (field, *outs), (), (state, *weights), name="closure")
+
+    state_0, *edges = called(
         functools.partial(gather_kernel, depths),
-        (field, weight_rows, first_edge, first_edge, first_edge),
+        (field, first_edge, first_edge, first_edge),
         info,
-        (edge_weight.reshape(1, TILE_CELLS), land.reshape(1, TILE_CELLS), *messages),
+        (weight, own_state, *others),
         scratch=[held],
         name="gather",
     )
     edges = exchanged(edges)
     state_0, target = lax.optimization_barrier((state_0, observed.reshape(rows, TILE_CELLS)))
     targets = from_depths(target)
-    q, *cache_0 = closure(state_0)
+    q, *cache_0 = closure(state_0, cached)
     state_1, weight_sums, *edges = called(
         first_step_kernel,
         (field, weight_rows, edge, edge, edge),
@@ -367,7 +433,7 @@
         name="step",
     )
     edges = exchanged(edges)
-    q, *cache_1 = closure(state_1)
+    (q,) = closure(state_1, ())
     final_state, adjoint, upstream, *edges = called(
         functools.partial(last_step_kernel, depths),
         (own_field, field, half_field, edge, edge, edge),
@@ -377,13 +443,14 @@
         name="last_step",
     )
     edges = exchanged(edges)
-    total = spec_of((CHUNKS, width // CHUNKS + 2 * (FEATURES // CHUNKS) + 8, width))
-    back, grads = called(
-        functools.partial(backward_kernel, False),
-        (field, total),
+    side = spec_of((FEATURES, width))
+    row_sum = spec_of((8, width))
+    back, *parts = called(
+        first_backward_kernel,
+        (field, spec_of((width, width)), side, side, row_sum, row_sum, row_sum),
         (),
-        (state_1, upstream, *cache_1, w_in, w_mid, w_out_t),
-        name="backward",
+        (state_1, upstream, *weights[:5]),
+        name="first_backward",
     )
     adjoint, upstream, *edges = called(
         functools.partial(adjoint_kernel, depths),
@@ -393,12 +460,13 @@
         scratch=[whole],
         name="adjoint",
     )
-    back, grads = called(
-        functools.partial(backward_kernel, True),
-        (field, total),
-        (),
-        (state_0, upstream, *cache_0, w_in, w_mid, w_out_t, grads),
-        name="backward_sum",
+    half = spec_of((width // HALVES + 2 * (FEATURES // HALVES) + 8, width))
+    back, kept, sent = called(
+        last_backward_kernel,
+        (field, half, half),
+        info,
+        (state_0, upstream, *cache_0, w_in, w_mid, w_out_t, *parts),
+        name="last_backward",
     )
     ended = []
 
@@ -424,30 +492,40 @@
 
     side_work = last_transfers()
     next(side_work)
-    if halving_applies():
-        grads = all_summed(grads, side_work)
+    if tiles == 8:
+        grads = summed_by_tile(kept, sent, side_work)
     else:
+        first = lax.axis_index("tile") % HALVES == 0
+        grads = jnp.where(first, jnp.stack([kept, sent]), jnp.stack([sent, kept]))
         grads = lax.psum(grads, "tile")
         for _ in range(3):
             grads = side_work.send(grads)
     (sensitivity,) = ended
-    grads = grads * (1.0 / (tiles * TILE_CELLS))
-    mid_rows = width // CHUNKS
-    side_rows = FEATURES // CHUNKS
-    first_row = mid_rows + 2 * side_rows
-    grad_w_mid = grads[:, :mid_rows, :].reshape(width, width)
-    grad_w_in = grads[:, mid_rows : mid_rows + side_rows, :].reshape(FEATURES, width)
-    grad_w_out = grads[:, mid_rows + side_rows : first_row, :].reshape(FEATURES, width).T
+    scale = 1.0 / (tiles * TILE_CELLS)
+    starts = part_starts(half.shape[0])
+
+    def part(k, count):
+        values = grads[:, starts[k] : starts[k] + count, :]
+        if grads.dtype != jnp.float16:
+            return values * scale
+        at = starts[3] + EXPONENT_ROW + k
+        exponent = grads[:, at : at + 1, :].astype(jnp.float32)
+        return values.astype(jnp.float32) * (jnp.exp2(exponent) * scale)
+
+    grad_w_mid = part(0, width // HALVES).reshape(width, width)
+    grad_w_in = part(1, FEATURES // HALVES).reshape(FEATURES, width)
+    grad_w_out = part(2, FEATURES // HALVES).reshape(FEATURES, width).T
+    biases = part(3, 2)
     shape = (TRACERS, levels, TILE_CELLS)
     return (
         final_state.reshape(shape),
         sensitivity.reshape(shape),
         grad_w_in,
-        grads[0, first_row],
+        biases[0, 0],
         grad_w_mid,
-        grads[1, first_row],
+        biases[1, 0],
         grad_w_out,
-        grads[2, first_row, :FEATURES],
+        biases[0, 1, :FEATURES],
     )
 
 

time: 115 us -> 82.8 us (0.72)
  local copies, waits for them, and re-layouts: 31 us -> 8.64 us
  waiting for transfers between devices: 36.5 us -> 19.8 us
  other arithmetic: 1.98 us -> 7.87 us
  Pallas kernels: 21.1 us -> 23.4 us
  starting transfers between devices: 23.1 us -> 21.7 us
    ppermute x12 -> x10, waiting for transfers between devices: 33 us -> 13.9 us  [swapped(): lax.ppermute(x, axis, [(i, i ^ (odd_bit if i & 1 else even_bit)) for i in...]
    unnamed x100 -> x30, local copies, waits for them, and re-layouts: 25.6 us -> 7.26 us
    convert_element_type x0 -> x3, other arithmetic: none -> 5.21 us  [with_exponents(): return out.astype(jnp.float16)]
    ppermute x12, starting transfers between devices: 11.9 us -> 9.19 us  [exchanged(): lax.ppermute(edge, 'tile', way)]
    ppermute x12, waiting for transfers between devices: 3.54 us -> 5.93 us  [exchanged(): lax.ppermute(edge, 'tile', way)]
    pallas_call x9 -> x10, Pallas kernels: 21.1 us -> 23.4 us  [called(): pl.pallas_call(kernel, out_shape=tuple(outs), in_specs=in_specs, out_spec...]
    mul x1 -> x4, other arithmetic: 0.14 us -> 2.08 us  [part(): return values.astype(jnp.float32) * (jnp.exp2(exponent) * scale)]
    add x3 -> x2, other arithmetic: 1.51 us -> 0.1 us  [summed_by_tile(): exponents = jnp.maximum(mine, other) + 1.0]
  transfers between devices with their start and end apart: 24 -> 22, of which waited for: 10 -> 9; matrix products, arithmetic and copies ran while one was open for 2% -> 0% of each run, Pallas kernels for 11% -> 17%
where the time goes in v5:
time: 82.8 us; the launch traced here: 82.4 us
  Pallas kernels  23.4 us (28%)
  starting transfers between devices  21.7 us (26%)
  waiting for transfers between devices  19.8 us (24%)
  local copies, waits for them, and re-layouts  8.64 us (10%)
  other arithmetic  7.87 us (10%)
  between operations  0.95 us (1%)
    pallas_call x10, Pallas kernels, called(): pl.pallas_call(kernel, out_shape=tuple(outs), in_specs=in_specs, out_spec...  23.4 us
    ppermute x10, waiting for transfers between devices, swapped(): lax.ppermute(x, axis, [(i, i ^ (odd_bit if i & 1 else even_bit)) for i in...  13.9 us
    ppermute x10, starting transfers between devices, swapped(): lax.ppermute(x, axis, [(i, i ^ (odd_bit if i & 1 else even_bit)) for i in...  12.5 us
    ppermute x12, starting transfers between devices, exchanged(): lax.ppermute(edge, 'tile', way)  9.19 us
    unnamed x30, local copies, waits for them, and re-layouts  7.26 us
    ppermute x12, waiting for transfers between devices, exchanged(): lax.ppermute(edge, 'tile', way)  5.93 us
    convert_element_type x3, other arithmetic, with_exponents(): return out.astype(jnp.float16)  5.21 us
    mul x4, other arithmetic, part(): return values.astype(jnp.float32) * (jnp.exp2(exponent) * scale)  2.08 us
  transfers between devices with their start and end apart: 22, of which 9 were waited for; matrix products, arithmetic and copies ran while one was open for 0% of the time, Pallas kernels for 17%

profile of v5, /device:TPU:0, one launch (start us, length us, event | category | flops | bytes accessed | tf_op | source)
XLA Modules:
  0.0 82.4 jit_solution(7478085867848315769)
XLA Ops:
  0.6 3.1 %collective-permute-start = (f32[16,1024]{1,0:T(8,128)}, f32[16,1024]{1,0:T(8,128)S(1)}, u32[]{:S(2)}, u32[]{:S(2)}) collective-permute-start(f32[16,1024]{1,0:T(8,128)} %bitcast.38), channel_id=1, source_target_pairs={{0,1},{1,0},{2,3},{3,2},{4,5},{5,4},{6,7},{7,6},{8,9},{9,8},{10,11... | collective-permute-start | bytes 196616 | tf_op jit(solution)/shard_map/ppermute | solution.py:310
  3.7 2.6 %collective-permute-start.1 = (f32[16,1024]{1,0:T(8,128)}, f32[16,1024]{1,0:T(8,128)S(1)}, u32[]{:S(2)}, u32[]{:S(2)}) collective-permute-start(f32[16,1024]{1,0:T(8,128)} %bitcast.39), channel_id=1, source_target_pairs={{0,2},{1,3},{2,0},{3,1},{4,6},{5,7},{6,4},{7,5},{8,10},{9,11},{10,... | collective-permute-start | bytes 196616 | tf_op jit(solution)/shard_map/ppermute | solution.py:310
  6.3 0.9 %copy-done.7 = f32[2,8,1024]{2,1,0:T(8,128)S(1)} copy-done((f32[2,8,1024]{2,1,0:T(8,128)S(1)}, f32[2,8,1024]{2,1,0:T(8,128)}, u32[]{:S(2)}) %copy-start.7) | copy-done | bytes 65560
  7.2 0.7 copy-done.8
  7.9 0.7 copy-done.9
  8.6 0.7 copy-done.10
  9.3 0.7 copy-done.11
  10.0 0.7 copy-done.12
  11.2 1.4 %collective-permute-done.2.refs_3_ = f32[16,1024]{1,0:T(8,128)S(1)} collective-permute-done((f32[16,1024]{1,0:T(8,128)}, f32[16,1024]{1,0:T(8,128)S(1)}, u32[]{:S(2)}, u32[]{:S(2)}) %collective-permute-start.2) | collective-permute-done | bytes 65568 | tf_op jit(solution)/shard_map/ppermute | solution.py:310
  12.6 1.0 %gather.1 = (f32[64,1024]{1,0:T(8,128)S(1)}, f32[72,128]{1,0:T(8,128)S(1)}, f32[72,128]{1,0:T(8,128)S(1)}, f32[72,128]{1,0:T(8,128)S(1)}) custom-call(s32[2]{0:T(128)S(1)} %pad_add_fusion.info, f32[8,1024]{1,0:T(8,128)S(1)} %get-tuple-element.77.weight_ref, f32[16,1024]{1,0:T(8,128)S(1)} %get-tuple-element.78.refs_0_, ...), custom_call_target="tpu_custom_call" | custom-call | tf_op jit(solution)/shard_map/gather/pallas_call | solution.py:297
  13.6 1.6 %collective-permute-start.3 = (f32[72,128]{1,0:T(8,128)S(1)}, f32[72,128]{1,0:T(8,128)S(1)}, u32[]{:S(2)}, u32[]{:S(2)}) collective-permute-start(f32[72,128]{1,0:T(8,128)S(1)} %get-tuple-element.88), channel_id=1, source_target_pairs={{0,16},{4,20},{8,24},{12,28},{16,0},{20,4},{24,8},{28,12},{1,17},{... | collective-permute-start | bytes 110600 | tf_op jit(solution)/shard_map/ppermute | solution.py:378
  15.2 1.5 %collective-permute-start.5 = (f32[72,128]{1,0:T(8,128)S(1)}, f32[72,128]{1,0:T(8,128)S(1)}, u32[]{:S(2)}, u32[]{:S(2)}) collective-permute-start(f32[72,128]{1,0:T(8,128)S(1)} %get-tuple-element.90), channel_id=1, source_target_pairs={{0,28},{4,8},{8,4},{12,16},{16,12},{20,24},{24,20},{28,0},{1,29},{... | collective-permute-start | bytes 110600 | tf_op jit(solution)/shard_map/ppermute | solution.py:378
  16.7 2.6 %collective-permute-start.10 = (f32[16,1024]{1,0:T(8,128)}, f32[16,1024]{1,0:T(8,128)S(1)}, u32[]{:S(2)}, u32[]{:S(2)}) collective-permute-start(f32[16,1024]{1,0:T(8,128)} %bitcast.35), channel_id=1, source_target_pairs={{0,2},{1,3},{2,0},{3,1},{4,6},{5,7},{6,4},{7,5},{8,10},{9,11},{10,... | collective-permute-start | bytes 196616 | tf_op jit(solution)/shard_map/ppermute | solution.py:310
  19.4 1.7 %collective-permute-start.11 = (f32[16,1024]{1,0:T(8,128)}, f32[16,1024]{1,0:T(8,128)S(1)}, u32[]{:S(2)}, u32[]{:S(2)}) collective-permute-start(f32[16,1024]{1,0:T(8,128)} %bitcast.36), channel_id=1, source_target_pairs={{0,3},{1,2},{2,1},{3,0},{4,7},{5,6},{6,5},{7,4},{8,11},{9,10},{10,... | collective-permute-start | bytes 196616 | tf_op jit(solution)/shard_map/ppermute | solution.py:310
  21.1 1.1 %copy-done = bf16[640,640]{1,0:T(8,128)(2,1)S(1)} copy-done((bf16[640,640]{1,0:T(8,128)(2,1)S(1)}, bf16[640,640]{1,0:T(8,128)(2,1)}, u32[]{:S(2)}) %copy-start) | copy-done | bytes 819224
  22.3 0.9 %copy-done.2 = bf16[64,640]{1,0:T(8,128)(2,1)S(1)} copy-done((bf16[64,640]{1,0:T(8,128)(2,1)S(1)}, bf16[64,640]{1,0:T(8,128)(2,1)}, u32[]{:S(2)}) %copy-start.2) | copy-done | bytes 81944
  23.2 0.9 %copy-done.4 = bf16[640,64]{0,1:T(8,128)(2,1)S(1)} copy-done((bf16[640,64]{0,1:T(8,128)(2,1)S(1)}, bf16[640,64]{0,1:T(8,128)(2,1)}, u32[]{:S(2)}) %copy-start.4) | copy-done | bytes 81944
  24.0 2.7 %closure.2 = (f32[64,1024]{1,0:T(8,128)S(1)}, bf16[1024,640]{1,0:T(8,128)(2,1)S(1)}, f32[1024,640]{1,0:T(8,128)S(1)}, bf16[1024,640]{1,0:T(8,128)(2,1)S(1)}, f32[1024,640]{1,0:T(8,128)S(1)}) custom-call(f32[64,1024]{1,0:T(8,128)S(1)} %get-tuple-element.83.state_ref, bf16[64,640]{1,0:T(8,128)(2,1)S(1)} %copy-done.2, f32[1,640]{1,0:T(1,128)S(1)} %get-tuple-element.84.b_in, ...), custom_call_target="tpu_custom_call" | custom-call | tf_op jit(solution)/shard_map/closure/pallas_call | solution.py:297
  26.8 1.6 %step.1 = (f32[64,1024]{1,0:T(8,128)S(1)}, f32[8,1024]{1,0:T(8,128)S(1)}, f32[64,128]{1,0:T(8,128)S(1)}, f32[64,128]{1,0:T(8,128)S(1)}, f32[64,128]{1,0:T(8,128)S(1)}) custom-call(s32[2]{0:T(128)S(1)} %pad_add_fusion.info, f32[64,1024]{1,0:T(8,128)S(1)} %get-tuple-element.83.state_ref, f32[8,1024]{1,0:T(8,128)S(1)} %get-tuple-element.77.weight_ref, ...), custom_call_target="tpu_custom_call" | custom-call | tf_op jit(solution)/shard_map/step/pallas_call | solution.py:297
  28.4 1.6 %collective-permute-start.6 = (f32[64,128]{1,0:T(8,128)S(1)}, f32[64,128]{1,0:T(8,128)S(1)}, u32[]{:S(2)}, u32[]{:S(2)}) collective-permute-start(f32[64,128]{1,0:T(8,128)S(1)} %get-tuple-element.93), channel_id=1, source_target_pairs={{0,16},{4,20},{8,24},{12,28},{16,0},{20,4},{24,8},{28,12},{1,17},{... | collective-permute-start | bytes 98312 | tf_op jit(solution)/shard_map/ppermute | solution.py:378
  30.0 0.7 collective-permute-start.8
  30.7 2.2 %closure.3.q_ref = f32[64,1024]{1,0:T(8,128)S(1)} custom-call(f32[64,1024]{1,0:T(8,128)S(1)} %get-tuple-element.91.state_ref, bf16[64,640]{1,0:T(8,128)(2,1)S(1)} %copy-done.2, f32[1,640]{1,0:T(1,128)S(1)} %get-tuple-element.84.b_in, bf16[640,640]{1,0:T(8,128)(2,1)S(1)} %copy-done.1, f32[1,640]{1,0:T(1,128)S(1)} %get-tuple-element.85.b_mid, ...), custom_call_target="tpu_custom_call" | custom-call | tf_op jit(solution)/shard_map/closure/pallas_call | solution.py:297
  33.0 1.4 %collective-permute-done.8.e2 = f32[64,128]{1,0:T(8,128)S(1)} collective-permute-done((f32[64,128]{1,0:T(8,128)S(1)}, f32[64,128]{1,0:T(8,128)S(1)}, u32[]{:S(2)}, u32[]{:S(2)}) %collective-permute-start.8) | collective-permute-done | bytes 32800 | tf_op jit(solution)/shard_map/ppermute | solution.py:378
  34.3 2.1 %last_step.1 = (f32[16,1024]{1,0:T(8,128)}, f32[64,1024]{1,0:T(8,128)S(1)}, bf16[64,1024]{1,0:T(8,128)(2,1)S(1)}, f32[64,128]{1,0:T(8,128)S(1)}, f32[64,128]{1,0:T(8,128)S(1)}, /*index=5*/f32[64,128]{1,0:T(8,128)S(1)}) custom-call(s32[2]{0:T(128)S(1)} %pad_add_fusion.info, f32[64,1024]{1,0:T(8,128)S(1)} %get-tuple-element.91.state_ref, ...), custom_call_target="tpu_custom_call" | custom-call | tf_op jit(solution)/shard_map/last_step/pallas_call | solution.py:297
  36.5 0.4 collective-permute-start.12
  36.9 1.3 %collective-permute-start.14 = (f32[64,128]{1,0:T(8,128)S(1)}, f32[64,128]{1,0:T(8,128)S(1)}, u32[]{:S(2)}, u32[]{:S(2)}) collective-permute-start(f32[64,128]{1,0:T(8,128)S(1)} %get-tuple-element.103), channel_id=1, source_target_pairs={{0,28},{4,8},{8,4},{12,16},{16,12},{20,24},{24,20},{28,0},{1,29},{... | collective-permute-start | bytes 98312 | tf_op jit(solution)/shard_map/ppermute | solution.py:378
  38.2 6.0 %first_backward.1 = (f32[64,1024]{1,0:T(8,128)S(1)}, f32[640,640]{1,0:T(8,128)S(1)}, f32[64,640]{1,0:T(8,128)S(1)}, f32[64,640]{1,0:T(8,128)S(1)}, f32[8,640]{1,...) custom-call(f32[64,1024]{1,0:T(8,128)S(1)} %get-tuple-element.91.state_ref, ...), custom_call_target="tpu_custom_call" | custom-call | tf_op jit(solution)/shard_map/first_backward/pallas_call | solution.py:297
  44.2 1.4 %adjoint.1 = (f32[16,1024]{1,0:T(8,128)S(1)}, bf16[64,1024]{1,0:T(8,128)(2,1)S(1)}, f32[16,128]{1,0:T(8,128)S(1)}, f32[16,128]{1,0:T(8,128)S(1)}, f32[16,128]{1,0:T(8,128)S(1)}) custom-call(s32[2]{0:T(128)S(1)} %pad_add_fusion.info, f32[64,1024]{1,0:T(8,128)S(1)} %get-tuple-element.98.adjoint_ref, f32[8,1024]{1,0:T(8,128)S(1)} %get-tuple-element.77.weight_ref, ...), custom_call_target="tpu_custom_call" | custom-call | tf_op jit(solution)/shard_map/adjoint/pallas_call | solution.py:297
  45.6 4.7 %last_backward.1 = (f32[64,1024]{1,0:T(8,128)S(1)}, f32[392,640]{1,0:T(8,128)S(1)}, f32[392,640]{1,0:T(8,128)S(1)}) custom-call(s32[2]{0:T(128)S(1)} %pad_add_fusion.info, f32[64,1024]{1,0:T(8,128)S(1)} %get-tuple-element.83.state_ref, bf16[64,1024]{1,0:T(8,128)(2,1)S(1)} %get-tuple-element.104.upstream_ref, ...), custom_call_target="tpu_custom_call" | custom-call | tf_op jit(solution)/shard_map/last_backward/pallas_call | solution.py:297
  50.5 2.5 %collective-permute-done.15 = f32[392,640]{1,0:T(8,128)S(1)} collective-permute-done((f32[392,640]{1,0:T(8,128)S(1)}, f32[392,640]{1,0:T(8,128)S(1)}, u32[]{:S(2)}, u32[]{:S(2)}) %collective-permute-start.15) | collective-permute-done | bytes 1003552 | tf_op jit(solution)/shard_map/ppermute | solution.py:310
  53.1 0.9 %select_convert_fusion.2 = f16[392,640]{1,0:T(8,128)(2,1)S(1)} fusion(f32[392,640]{1,0:T(8,128)S(1)} %get-tuple-element.115, f32[392,640]{1,0:T(8,128)S(1)} %collective-permute-done.15, f32[640]{0:T(1024)S(1)} %get-tuple-element.167, f32[640]{0:T(1024)S(1)} %get-tuple-element.168, f32[640]{0:T(1024)S(1)} %get-tuple-element.169, ...), kind=kLoop, calls=%fused_computation.4 | loop fusion | flops 2508800 | bytes 2532024 | tf_op jit(solution)/shard_map/convert_element_type | solution.py:338
  54.1 1.6 %collective-permute-start.16 = (f16[392,640]{1,0:T(8,128)(2,1)S(1)}, f16[392,640]{1,0:T(8,128)(2,1)S(1)}, u32[]{:S(2)}, u32[]{:S(2)}) collective-permute-start(f16[392,640]{1,0:T(8,128)(2,1)S(1)} %select_convert_fusion.2), channel_id=1, source_target_pairs={{0,8},{4,20},{8,0},{12,28},{16,24},{20,4},{24,16},{28,12},{1,9},{5... | collective-permute-start | bytes 1505288 | tf_op jit(solution)/shard_map/ppermute | solution.py:310
  55.6 0.9 %collective-permute-start.17 = (f32[16,128]{1,0:T(8,128)S(1)}, f32[16,128]{1,0:T(8,128)S(1)}, u32[]{:S(2)}, u32[]{:S(2)}) collective-permute-start(f32[16,128]{1,0:T(8,128)S(1)} %get-tuple-element.121), channel_id=1, source_target_pairs={{0,16},{4,20},{8,24},{12,28},{16,0},{20,4},{24,8},{28,12},{1,17},{... | collective-permute-start | bytes 24584 | tf_op jit(solution)/shard_map/ppermute | solution.py:378
  56.6 1.2 %collective-permute-start.19 = (f32[16,128]{1,0:T(8,128)S(1)}, f32[16,128]{1,0:T(8,128)S(1)}, u32[]{:S(2)}, u32[]{:S(2)}) collective-permute-start(f32[16,128]{1,0:T(8,128)S(1)} %get-tuple-element.123), channel_id=1, source_target_pairs={{0,28},{4,8},{8,4},{12,16},{16,12},{20,24},{24,20},{28,0},{1,29},{... | collective-permute-start | bytes 24584 | tf_op jit(solution)/shard_map/ppermute | solution.py:378
  57.7 1.7 %collective-permute-done.17.e0 = f32[16,128]{1,0:T(8,128)S(1)} collective-permute-done((f32[16,128]{1,0:T(8,128)S(1)}, f32[16,128]{1,0:T(8,128)S(1)}, u32[]{:S(2)}, u32[]{:S(2)}) %collective-permute-start.17) | collective-permute-done | bytes 8224 | tf_op jit(solution)/shard_map/ppermute | solution.py:378
  59.4 2.8 %collective-permute-done.19.e2 = f32[16,128]{1,0:T(8,128)S(1)} collective-permute-done((f32[16,128]{1,0:T(8,128)S(1)}, f32[16,128]{1,0:T(8,128)S(1)}, u32[]{:S(2)}, u32[]{:S(2)}) %collective-permute-start.19) | collective-permute-done | bytes 8224 | tf_op jit(solution)/shard_map/ppermute | solution.py:378
  62.3 0.9 %collective-permute-done.16 = f16[392,640]{1,0:T(8,128)(2,1)S(1)} collective-permute-done((f16[392,640]{1,0:T(8,128)(2,1)S(1)}, f16[392,640]{1,0:T(8,128)(2,1)S(1)}, u32[]{:S(2)}, u32[]{:S(2)}) %collective-permute-start.16) | collective-permute-done | bytes 501792 | tf_op jit(solution)/shard_map/ppermute | solution.py:310
  63.3 2.1 %select_convert_fusion.1 = f16[392,640]{1,0:T(8,128)(2,1)S(1)} fusion(f16[392,640]{1,0:T(8,128)(2,1)S(1)} %collective-permute-done.16, f16[392,640]{1,0:T(8,128)(2,1)S(1)} %select_convert_fusion.2, f32[640]{0:T(1024)S(1)} %get-tuple-element.159, f32[640]{0:T(1024)S(1)} %get-tuple-element.160, f32[640]{0:T(1024)S(1)} %get-tuple-element.161, ...), kind=kLoop, calls=%fused_computation.3 | loop fusion | flops 4014080 | bytes 1538744 | tf_op jit(solution)/shard_map/convert_element_type | solution.py:338
  65.5 0.7 collective-permute-start.20
  66.2 1.4 %end.1 = f32[16,1024]{1,0:T(8,128)} custom-call(s32[2]{0:T(128)S(1)} %pad_add_fusion.info, f32[16,1024]{1,0:T(8,128)S(1)} %get-tuple-element.127.adjoint_ref, f32[8,1024]{1,0:T(8,128)S(1)} %get-tuple-element.77.weight_ref, f32[8,1024]{1,0:T(8,128)S(1)} %get-tuple-element.92.sums_ref, f32[64,1024]{1,0:T(8,128)S(1)} %get-tuple-element.128.back_ref, ...), custom_call_target="tpu_custom_call" | custom-call | tf_op jit(solution)/shard_map/end/pallas_call | solution.py:297
  67.6 6.9 %collective-permute-done.20 = f16[392,640]{1,0:T(8,128)(2,1)S(1)} collective-permute-done((f16[392,640]{1,0:T(8,128)(2,1)S(1)}, f16[392,640]{1,0:T(8,128)(2,1)S(1)}, u32[]{:S(2)}, u32[]{:S(2)}) %collective-permute-start.20) | collective-permute-done | bytes 501792 | tf_op jit(solution)/shard_map/ppermute | solution.py:310
  74.7 2.1 %select_convert_fusion = f16[392,640]{1,0:T(8,128)(2,1)S(1)} fusion(f16[392,640]{1,0:T(8,128)(2,1)S(1)} %collective-permute-done.20, f16[392,640]{1,0:T(8,128)(2,1)S(1)} %select_convert_fusion.1, f32[640]{0:T(1024)S(1)} %get-tuple-element.147, f32[640]{0:T(1024)S(1)} %get-tuple-element.148, f32[640]{0:T(1024)S(1)} %get-tuple-element.149, ...), kind=kLoop, calls=%fused_computation.2 | loop fusion | flops 4014080 | bytes 1538744 | tf_op jit(solution)/shard_map/convert_element_type | solution.py:338
  76.9 1.9 %collective-permute-done.21 = f16[392,640]{1,0:T(8,128)(2,1)S(1)} collective-permute-done((f16[392,640]{1,0:T(8,128)(2,1)S(1)}, f16[392,640]{1,0:T(8,128)(2,1)S(1)}, u32[]{:S(2)}, u32[]{:S(2)}) %collective-permute-start.21) | collective-permute-done | bytes 501792 | tf_op jit(solution)/shard_map/ppermute | solution.py:310
  78.8 0.4 maximum_select_fusion
  79.2 0.6 slice_reduce_fusion
  79.8 0.5 slice_bitcast_fusion
  80.3 1.3 %convert_multiply_fusion = f32[2,320,640]{2,1,0:T(8,128)} fusion(f16[2,392,640]{2,1,0:T(8,128)(2,1)S(1)} %maximum_select_fusion, f32[2,640]{1,0:T(2,128)S(1)} %bitcast.52), kind=kLoop, calls=%fused_computation | loop fusion | flops 819200 | bytes 2462720 | tf_op jit(solution)/shard_map/mul | solution.py:513
  81.6 0.7 convert_multiply_fusion.1
  (61 shorter events, 1.3 us)
Async XLA Ops:
  0.6 10.3 %collective-permute-start = (f32[16,1024]{1,0:T(8,128)}, f32[16,1024]{1,0:T(8,128)S(1)}, u32[]{:S(2)}, u32[]{:S(2)}) collective-permute-start(f32[16,1024]{1,0:T(8,128)} %bitcast.38), channel_id=1, source_target_pairs={{0,1},{1,0},{2,3},{3,2},{4,5},{5,4},{6,7},{7,6},{8,9},{9,8},{10,11... | collective-permute-start | bytes 196616 | tf_op jit(solution)/shard_map/ppermute | solution.py:310
  3.7 7.5 %collective-permute-start.1 = (f32[16,1024]{1,0:T(8,128)}, f32[16,1024]{1,0:T(8,128)S(1)}, u32[]{:S(2)}, u32[]{:S(2)}) collective-permute-start(f32[16,1024]{1,0:T(8,128)} %bitcast.39), channel_id=1, source_target_pairs={{0,2},{1,3},{2,0},{3,1},{4,6},{5,7},{6,4},{7,5},{8,10},{9,11},{10,... | collective-permute-start | bytes 196616 | tf_op jit(solution)/shard_map/ppermute | solution.py:310
  6.3 6.3 %collective-permute-start.2 = (f32[16,1024]{1,0:T(8,128)}, f32[16,1024]{1,0:T(8,128)S(1)}, u32[]{:S(2)}, u32[]{:S(2)}) collective-permute-start(f32[16,1024]{1,0:T(8,128)} %bitcast.40), channel_id=1, source_target_pairs={{0,3},{1,2},{2,1},{3,0},{4,7},{5,6},{6,5},{7,4},{8,11},{9,10},{10,... | collective-permute-start | bytes 196616 | tf_op jit(solution)/shard_map/ppermute | solution.py:310
  6.3 0.9 %copy-start.7 = (f32[2,8,1024]{2,1,0:T(8,128)S(1)}, f32[2,8,1024]{2,1,0:T(8,128)}, u32[]{:S(2)}) copy-start(f32[2,8,1024]{2,1,0:T(8,128)} %param.10) | copy-start | bytes 196612
  7.2 0.7 copy-start.8
  7.9 0.7 copy-start.9
  8.6 0.7 copy-start.10
  9.3 0.7 copy-start.11
  10.0 0.7 copy-start.12
  13.6 5.8 %collective-permute-start.3 = (f32[72,128]{1,0:T(8,128)S(1)}, f32[72,128]{1,0:T(8,128)S(1)}, u32[]{:S(2)}, u32[]{:S(2)}) collective-permute-start(f32[72,128]{1,0:T(8,128)S(1)} %get-tuple-element.88), channel_id=1, source_target_pairs={{0,16},{4,20},{8,24},{12,28},{16,0},{20,4},{24,8},{28,12},{1,17},{... | collective-permute-start | bytes 110600 | tf_op jit(solution)/shard_map/ppermute | solution.py:378
  15.2 14.8 %collective-permute-start.9 = (f32[16,1024]{1,0:T(8,128)}, f32[16,1024]{1,0:T(8,128)S(1)}, u32[]{:S(2)}, u32[]{:S(2)}) collective-permute-start(f32[16,1024]{1,0:T(8,128)} %bitcast.34), channel_id=1, source_target_pairs={{0,1},{1,0},{2,3},{3,2},{4,5},{5,4},{6,7},{7,6},{8,9},{9,8},{10,11... | collective-permute-start | bytes 196616 | tf_op jit(solution)/shard_map/ppermute | solution.py:310
  15.2 11.6 %collective-permute-start.4 = (f32[72,128]{1,0:T(8,128)S(1)}, f32[72,128]{1,0:T(8,128)S(1)}, u32[]{:S(2)}, u32[]{:S(2)}) collective-permute-start(f32[72,128]{1,0:T(8,128)S(1)} %get-tuple-element.89), channel_id=1, source_target_pairs={{0,4},{4,0},{8,12},{12,8},{16,20},{20,16},{24,28},{28,24},{1,5},{5... | collective-permute-start | bytes 110600 | tf_op jit(solution)/shard_map/ppermute | solution.py:378
  15.2 11.6 %collective-permute-start.5 = (f32[72,128]{1,0:T(8,128)S(1)}, f32[72,128]{1,0:T(8,128)S(1)}, u32[]{:S(2)}, u32[]{:S(2)}) collective-permute-start(f32[72,128]{1,0:T(8,128)S(1)} %get-tuple-element.90), channel_id=1, source_target_pairs={{0,28},{4,8},{8,4},{12,16},{16,12},{20,24},{24,20},{28,0},{1,29},{... | collective-permute-start | bytes 110600 | tf_op jit(solution)/shard_map/ppermute | solution.py:378
  16.7 16.2 %collective-permute-start.10 = (f32[16,1024]{1,0:T(8,128)}, f32[16,1024]{1,0:T(8,128)S(1)}, u32[]{:S(2)}, u32[]{:S(2)}) collective-permute-start(f32[16,1024]{1,0:T(8,128)} %bitcast.35), channel_id=1, source_target_pairs={{0,2},{1,3},{2,0},{3,1},{4,6},{5,7},{6,4},{7,5},{8,10},{9,11},{10,... | collective-permute-start | bytes 196616 | tf_op jit(solution)/shard_map/ppermute | solution.py:310
  19.4 13.6 %collective-permute-start.11 = (f32[16,1024]{1,0:T(8,128)}, f32[16,1024]{1,0:T(8,128)S(1)}, u32[]{:S(2)}, u32[]{:S(2)}) collective-permute-start(f32[16,1024]{1,0:T(8,128)} %bitcast.36), channel_id=1, source_target_pairs={{0,3},{1,2},{2,1},{3,0},{4,7},{5,6},{6,5},{7,4},{8,11},{9,10},{10,... | collective-permute-start | bytes 196616 | tf_op jit(solution)/shard_map/ppermute | solution.py:310
  21.1 1.1 %copy-start = (bf16[640,640]{1,0:T(8,128)(2,1)S(1)}, bf16[640,640]{1,0:T(8,128)(2,1)}, u32[]{:S(2)}) copy-start(bf16[640,640]{1,0:T(8,128)(2,1)} %w_mid.7) | copy-start | bytes 2457604
  22.3 0.9 %copy-start.2 = (bf16[64,640]{1,0:T(8,128)(2,1)S(1)}, bf16[64,640]{1,0:T(8,128)(2,1)}, u32[]{:S(2)}) copy-start(bf16[64,640]{1,0:T(8,128)(2,1)} %w_in.7) | copy-start | bytes 245764
  23.1 0.9 %copy-start.4 = (bf16[640,64]{0,1:T(8,128)(2,1)S(1)}, bf16[640,64]{0,1:T(8,128)(2,1)}, u32[]{:S(2)}) copy-start(bf16[640,64]{0,1:T(8,128)(2,1)} %param.18) | copy-start | bytes 245764
  24.0 6.6 %copy-start.1 = (bf16[640,640]{1,0:T(8,128)(2,1)S(1)}, bf16[640,640]{1,0:T(8,128)(2,1)}, u32[]{:S(2)}) copy-start(bf16[640,640]{1,0:T(8,128)(2,1)} %w_mid.7) | copy-start | bytes 2457604
  24.0 10.3 %copy-start.6 = (f32[2,8,1024]{2,1,0:T(8,128)S(1)}, f32[2,8,1024]{2,1,0:T(8,128)}, u32[]{:S(2)}) copy-start(f32[2,8,1024]{2,1,0:T(8,128)} %param.11) | copy-start | bytes 196612
  26.7 11.5 %copy-start.5 = (bf16[640,64]{0,1:T(8,128)(2,1)S(1)}, bf16[640,64]{0,1:T(8,128)(2,1)}, u32[]{:S(2)}) copy-start(bf16[640,64]{0,1:T(8,128)(2,1)} %param.18) | copy-start | bytes 245764
  28.4 4.5 %collective-permute-start.6 = (f32[64,128]{1,0:T(8,128)S(1)}, f32[64,128]{1,0:T(8,128)S(1)}, u32[]{:S(2)}, u32[]{:S(2)}) collective-permute-start(f32[64,128]{1,0:T(8,128)S(1)} %get-tuple-element.93), channel_id=1, source_target_pairs={{0,16},{4,20},{8,24},{12,28},{16,0},{20,4},{24,8},{28,12},{1,17},{... | collective-permute-start | bytes 98312 | tf_op jit(solution)/shard_map/ppermute | solution.py:378
  30.0 3.0 %collective-permute-start.7 = (f32[64,128]{1,0:T(8,128)S(1)}, f32[64,128]{1,0:T(8,128)S(1)}, u32[]{:S(2)}, u32[]{:S(2)}) collective-permute-start(f32[64,128]{1,0:T(8,128)S(1)} %get-tuple-element.94), channel_id=1, source_target_pairs={{0,4},{4,0},{8,12},{12,8},{16,20},{20,16},{24,28},{28,24},{1,5},{5... | collective-permute-start | bytes 98312 | tf_op jit(solution)/shard_map/ppermute | solution.py:378
  30.0 4.3 %collective-permute-start.8 = (f32[64,128]{1,0:T(8,128)S(1)}, f32[64,128]{1,0:T(8,128)S(1)}, u32[]{:S(2)}, u32[]{:S(2)}) collective-permute-start(f32[64,128]{1,0:T(8,128)S(1)} %get-tuple-element.95), channel_id=1, source_target_pairs={{0,28},{4,8},{8,4},{12,16},{16,12},{20,24},{24,20},{28,0},{1,29},{... | collective-permute-start | bytes 98312 | tf_op jit(solution)/shard_map/ppermute | solution.py:378
  32.9 12.7 %copy-start.3 = (bf16[64,640]{1,0:T(8,128)(2,1)S(1)}, bf16[64,640]{1,0:T(8,128)(2,1)}, u32[]{:S(2)}) copy-start(bf16[64,640]{1,0:T(8,128)(2,1)} %w_in.7) | copy-start | bytes 245764
  36.5 7.7 %collective-permute-start.12 = (f32[64,128]{1,0:T(8,128)S(1)}, f32[64,128]{1,0:T(8,128)S(1)}, u32[]{:S(2)}, u32[]{:S(2)}) collective-permute-start(f32[64,128]{1,0:T(8,128)S(1)} %get-tuple-element.101), channel_id=1, source_target_pairs={{0,16},{4,20},{8,24},{12,28},{16,0},{20,4},{24,8},{28,12},{1,17},{... | collective-permute-start | bytes 98312 | tf_op jit(solution)/shard_map/ppermute | solution.py:378
  36.9 7.3 %collective-permute-start.13 = (f32[64,128]{1,0:T(8,128)S(1)}, f32[64,128]{1,0:T(8,128)S(1)}, u32[]{:S(2)}, u32[]{:S(2)}) collective-permute-start(f32[64,128]{1,0:T(8,128)S(1)} %get-tuple-element.102), channel_id=1, source_target_pairs={{0,4},{4,0},{8,12},{12,8},{16,20},{20,16},{24,28},{28,24},{1,5},{5... | collective-permute-start | bytes 98312 | tf_op jit(solution)/shard_map/ppermute | solution.py:378
  36.9 7.3 %collective-permute-start.14 = (f32[64,128]{1,0:T(8,128)S(1)}, f32[64,128]{1,0:T(8,128)S(1)}, u32[]{:S(2)}, u32[]{:S(2)}) collective-permute-start(f32[64,128]{1,0:T(8,128)S(1)} %get-tuple-element.103), channel_id=1, source_target_pairs={{0,28},{4,8},{8,4},{12,16},{16,12},{20,24},{24,20},{28,0},{1,29},{... | collective-permute-start | bytes 98312 | tf_op jit(solution)/shard_map/ppermute | solution.py:378
  50.4 2.7 %collective-permute-start.15 = (f32[392,640]{1,0:T(8,128)S(1)}, f32[392,640]{1,0:T(8,128)S(1)}, u32[]{:S(2)}, u32[]{:S(2)}) collective-permute-start(f32[392,640]{1,0:T(8,128)S(1)} %get-tuple-element.116), channel_id=1, source_target_pairs={{0,4},{4,0},{8,12},{12,8},{16,20},{20,16},{24,28},{28,24},{1,5},{5... | collective-permute-start | bytes 3010568 | tf_op jit(solution)/shard_map/ppermute | solution.py:310
  54.1 9.1 %collective-permute-start.16 = (f16[392,640]{1,0:T(8,128)(2,1)S(1)}, f16[392,640]{1,0:T(8,128)(2,1)S(1)}, u32[]{:S(2)}, u32[]{:S(2)}) collective-permute-start(f16[392,640]{1,0:T(8,128)(2,1)S(1)} %select_convert_fusion.2), channel_id=1, source_target_pairs={{0,8},{4,20},{8,0},{12,28},{16,24},{20,4},{24,16},{28,12},{1,9},{5... | collective-permute-start | bytes 1505288 | tf_op jit(solution)/shard_map/ppermute | solution.py:310
  55.6 3.8 %collective-permute-start.17 = (f32[16,128]{1,0:T(8,128)S(1)}, f32[16,128]{1,0:T(8,128)S(1)}, u32[]{:S(2)}, u32[]{:S(2)}) collective-permute-start(f32[16,128]{1,0:T(8,128)S(1)} %get-tuple-element.121), channel_id=1, source_target_pairs={{0,16},{4,20},{8,24},{12,28},{16,0},{20,4},{24,8},{28,12},{1,17},{... | collective-permute-start | bytes 24584 | tf_op jit(solution)/shard_map/ppermute | solution.py:378
  56.6 2.9 %collective-permute-start.18 = (f32[16,128]{1,0:T(8,128)S(1)}, f32[16,128]{1,0:T(8,128)S(1)}, u32[]{:S(2)}, u32[]{:S(2)}) collective-permute-start(f32[16,128]{1,0:T(8,128)S(1)} %get-tuple-element.122), channel_id=1, source_target_pairs={{0,4},{4,0},{8,12},{12,8},{16,20},{20,16},{24,28},{28,24},{1,5},{5... | collective-permute-start | bytes 24584 | tf_op jit(solution)/shard_map/ppermute | solution.py:378
  56.6 5.7 %collective-permute-start.19 = (f32[16,128]{1,0:T(8,128)S(1)}, f32[16,128]{1,0:T(8,128)S(1)}, u32[]{:S(2)}, u32[]{:S(2)}) collective-permute-start(f32[16,128]{1,0:T(8,128)S(1)} %get-tuple-element.123), channel_id=1, source_target_pairs={{0,28},{4,8},{8,4},{12,16},{16,12},{20,24},{24,20},{28,0},{1,29},{... | collective-permute-start | bytes 24584 | tf_op jit(solution)/shard_map/ppermute | solution.py:378
  65.5 9.0 %collective-permute-start.20 = (f16[392,640]{1,0:T(8,128)(2,1)S(1)}, f16[392,640]{1,0:T(8,128)(2,1)S(1)}, u32[]{:S(2)}, u32[]{:S(2)}) collective-permute-start(f16[392,640]{1,0:T(8,128)(2,1)S(1)} %select_convert_fusion.1), channel_id=1, source_target_pairs={{0,16},{4,12},{8,24},{12,4},{16,0},{20,28},{24,8},{28,20},{1,17},{... | collective-permute-start | bytes 1505288 | tf_op jit(solution)/shard_map/ppermute | solution.py:310
  76.8 1.9 %collective-permute-start.21 = (f16[392,640]{1,0:T(8,128)(2,1)S(1)}, f16[392,640]{1,0:T(8,128)(2,1)S(1)}, u32[]{:S(2)}, u32[]{:S(2)}) collective-permute-start(f16[392,640]{1,0:T(8,128)(2,1)S(1)} %select_convert_fusion), channel_id=1, source_target_pairs={{0,4},{4,0},{8,12},{12,8},{16,20},{20,16},{24,28},{28,24},{1,5},{5... | collective-permute-start | bytes 1505288 | tf_op jit(solution)/shard_map/ppermute | solution.py:310

commit v6 on v5

--- a/solution.py
+++ b/solution.py
@@ -105,13 +105,29 @@
         to_ref[tracer * levels : (tracer + 1) * levels, :] = from_ref[pl.ds(start, levels), :]
 
 
-def prepare_kernel(edge_ref, land_ref, state_ref, b_in, b_mid, b_out, weight_ref, own_ref, in_ref, mid_ref, out_ref):
-    weight = edge_ref[...] * land_ref[...].astype(jnp.float32)
-    weight_ref[...] = jnp.broadcast_to(weight, weight_ref.shape)
-    own_ref[...] = state_ref[...]
-    in_ref[...] = b_in[...].reshape(in_ref.shape)
-    mid_ref[...] = b_mid[...].reshape(mid_ref.shape)
-    rest = b_out[...].reshape(1, FEATURES)
+def prepare_kernel(*refs):
+    edge_ref, land_ref, state_ref, b_in, b_mid, b_out, *weight_refs = refs[:9]
+    weight_out, own_ref, in_ref, mid_ref, out_ref, *held_refs = refs[9:17]
+    edge, land, bias_in, bias_mid, bias_out, sems = refs[17:]
+    pairs = [
+        (edge_ref, edge),
+        (land_ref, land),
+        (b_in, bias_in),
+        (b_mid, bias_mid),
+        (b_out, bias_out),
+        (state_ref, own_ref),
+        *zip(weight_refs, held_refs),
+    ]
+    copies = [pltpu.make_async_copy(source, to, sems.at[k]) for k, (source, to) in enumerate(pairs)]
+    for copy in copies:
+        copy.start()
+    for copy in copies:
+        copy.wait()
+    weight = edge[...] * land[...].astype(jnp.float32)
+    weight_out[...] = jnp.broadcast_to(weight, weight_out.shape)
+    in_ref[...] = bias_in[...].reshape(in_ref.shape)
+    mid_ref[...] = bias_mid[...].reshape(mid_ref.shape)
+    rest = bias_out[...].reshape(1, FEATURES)
     terms = []
     for _ in range(3):
         term = rest.astype(jnp.bfloat16)
@@ -176,9 +192,9 @@
         edge_out[...] = edge
 
 
-def last_step_kernel(depths, info, state_ref, weight_ref, sums_ref, q_ref, e0, e1, e2, *refs):
-    message_refs = refs[:depths]
-    final_ref, adjoint_ref, upstream_ref, o0, o1, o2, held, ordered = refs[depths:]
+def last_step_kernel(
+    depths, info, state_ref, weight_ref, sums_ref, q_ref, e0, e1, e2, target_ref, final_ref, adjoint_ref, upstream_ref, o0, o1, o2, held, ordered
+):
     weight = weight_ref[0:1, :]
     mask = mask_of(weight)
     state = state_ref[...]
@@ -187,7 +203,7 @@
     state = state + diffuse_coef * change + step_size * mask * q_ref[...]
     adjoint_ref[...] = state
     own_levels(depths, info, adjoint_ref, final_ref)
-    in_order(depths, info, message_refs, held, ordered)
+    in_order(depths, info, [target_ref.at[k] for k in range(depths)], held, ordered)
     adjoint = mask * (state - ordered[...])
     adjoint_ref[...] = adjoint
     upstream_ref[...] = (step_size * mask * adjoint).astype(jnp.bfloat16)
@@ -218,6 +234,12 @@
 HALVES = 2
 EXPONENT_ROW = 4
 TOP_EXPONENT = 14.0
+
+
+def block_parts(width):
+    side = FEATURES // HALVES
+    second = (width // HALVES - 2 * side) // 2 // 16 * 16
+    return (width // HALVES - second,), (second, side, side)
 
 
 def exponent_of(part):
@@ -255,7 +277,7 @@
 
 def last_backward_kernel(info, state_ref, upstream_ref, one_ref, slope_one_ref, two_ref, slope_two_ref, w_in, w_mid, w_out_t, *refs):
     earlier_refs = refs[:6]
-    back_ref, kept_ref, sent_ref = refs[6:]
+    back_ref, *block_refs = refs[6:]
     layers = (one_ref[...], slope_one_ref[...], two_ref[...], slope_two_ref[...])
     inputs = state_ref[...].astype(jnp.bfloat16)
     back, parts = gradient_parts(inputs, upstream_ref[...], layers, w_in, w_mid, w_out_t)
@@ -263,37 +285,45 @@
     mid, side_in, side_out, bias_in, bias_mid, bias_out = [part + ref[...] for part, ref in zip(parts, earlier_refs)]
     row = lax.broadcasted_iota(jnp.int32, bias_in.shape, 0)
     own = info[1] % HALVES
+    (top,), (_, side, _) = block_parts(w_mid.shape[0])
     for half in range(HALVES):
-        pieces = []
-        for matrix in (mid, side_in, side_out):
-            count = matrix.shape[0] // HALVES
-            pieces.append(matrix[half * count : (half + 1) * count, :])
+        count = mid.shape[0] // HALVES
+        rows = mid[half * count : (half + 1) * count, :]
         tail = jnp.where(row == 0, bias_mid if half else bias_in, 0.0)
         if half == 0:
             tail = jnp.where(row == 1, bias_out, tail)
-        pieces.append(tail)
-        for k, exponent in enumerate([exponent_of(piece) for piece in pieces]):
-            tail = jnp.where(row == EXPONENT_ROW + k, exponent, tail)
-        pieces[-1] = tail
-
-        def store(to_ref, pieces=pieces):
-            at = 0
-            for piece in pieces:
-                to_ref[at : at + piece.shape[0], :] = piece
-                at += piece.shape[0]
-
-        pl.when(own == half)(functools.partial(store, kept_ref))
-        pl.when(own != half)(functools.partial(store, sent_ref))
+        at = slice(half * side, (half + 1) * side)
+        blocks = ([rows[:top, :], jnp.zeros_like(tail)], [rows[top:, :], side_in[at, :], side_out[at, :], tail])
+        for k, pieces in enumerate(blocks):
+            last = pieces[-1]
+            for j, piece in enumerate(pieces if k else pieces[:1]):
+                last = jnp.where(row == EXPONENT_ROW + j, exponent_of(piece), last)
+            pieces[-1] = last
+
+            def store(to_ref, pieces=pieces):
+                at = 0
+                for piece in pieces:
+                    to_ref[at : at + piece.shape[0], :] = piece
+                    at += piece.shape[0]
+
+            pl.when(own == half)(functools.partial(store, block_refs[k]))
+            pl.when(own != half)(functools.partial(store, block_refs[2 + k]))
 
 
 def spec_of(shape, dtype=jnp.float32):
     return jax.ShapeDtypeStruct(shape, dtype)
 
 
-def called(kernel, outs, info, args, scratch=(), name=None):
+def closure_cost(passes):
+    width = 640
+    macs = TILE_CELLS * width * (2 * FEATURES + width) * passes
+    return pl.CostEstimate(flops=2 * macs, transcendentals=2 * TILE_CELLS * width, bytes_accessed=8 * TILE_CELLS * width * passes)
+
+
+def called(kernel, outs, info, args, scratch=(), name=None, fetches=False, passes=0):
     smem = pl.BlockSpec(memory_space=pltpu.SMEM)
     vmem = pl.BlockSpec(memory_space=pltpu.VMEM)
-    in_specs = [smem] * len(info) + [vmem] * len(args)
+    in_specs = [smem] * len(info) + [pl.BlockSpec(memory_space=pltpu.HBM) if fetches else vmem] * len(args)
     return pl.pallas_call(
         kernel,
         out_shape=tuple(outs),
@@ -301,8 +331,9 @@
         out_specs=tuple(vmem for _ in outs),
         scratch_shapes=list(scratch),
         compiler_params=pltpu.CompilerParams(vmem_limit_bytes=VMEM_LIMIT),
+        cost_estimate=closure_cost(passes) if passes else None,
         name=name,
-    )(*info, *args)
+    )(*info, *[pltpu.with_memory_space_constraint(arg, pltpu.HBM) if fetches else arg for arg in args])
 
 
 def swapped(x, axis, even_bit, odd_bit):
@@ -310,19 +341,15 @@
     return lax.ppermute(x, axis, [(i, i ^ (odd_bit if i & 1 else even_bit)) for i in range(length)])
 
 
-def by_part(rows, exponents):
-    width = exponents.shape[1]
-    starts = part_starts(rows)
-    row = lax.broadcasted_iota(jnp.int32, (rows, width), 0)
+def by_part(parts, exponents):
+    if len(parts) == 1:
+        return exponents[0:1]
+    rows = sum(parts) + 8
+    row = lax.broadcasted_iota(jnp.int32, (rows, exponents.shape[1]), 0)
     out = exponents[3:4]
     for k in (2, 1, 0):
-        out = jnp.where(row < starts[k + 1], exponents[k : k + 1], out)
+        out = jnp.where(row < sum(parts[: k + 1]), exponents[k : k + 1], out)
     return out
-
-
-def part_starts(rows):
-    side = FEATURES // HALVES
-    return (0, rows - 8 - 2 * side, rows - 8 - side, rows - 8)
 
 
 def exponents_of(half):
@@ -346,23 +373,33 @@
     return out
 
 
-def summed_by_tile(kept, sent, side_work):
-    rows = kept.shape[0]
-    received = side_work.send(swapped(sent, "tile", 1, 1))
-    exponents = jnp.maximum(exponents_of(kept), exponents_of(received)) + 1.0
-    factors = lax.optimization_barrier(jnp.exp2(-exponents))
-    half = with_exponents((kept + received) * by_part(rows, factors), exponents)
+def summed_by_tile(kept, sent, all_parts, side_work):
+    received = [swapped(block, "tile", 1, 1) for block in sent]
+    received[1] = side_work.send(received[1])
+    blocks = []
+    for block, other, parts in zip(kept, received, all_parts):
+        exponents = jnp.maximum(exponents_of(block), exponents_of(other)) + 1.0
+        factors = lax.optimization_barrier(jnp.exp2(-exponents))
+        blocks.append(with_exponents((block + other) * by_part(parts, factors), exponents))
     for even_bit, odd_bit in ((2, 4), (4, 2)):
-        received = side_work.send(swapped(half, "tile", even_bit, odd_bit))
-        mine, other = exponents_of(half), exponents_of(received)
-        exponents = jnp.maximum(mine, other) + 1.0
-        factors = lax.optimization_barrier((exact_power(mine - exponents), exact_power(other - exponents)))
-        total = half.astype(jnp.float32) * by_part(rows, factors[0])
-        total = total + received.astype(jnp.float32) * by_part(rows, factors[1])
-        half = with_exponents(total, exponents)
-    other = swapped(half, "tile", 1, 1)
+        received = [swapped(block, "tile", even_bit, odd_bit) for block in blocks]
+        received[1] = side_work.send(received[1])
+        added = []
+        for block, other, parts in zip(blocks, received, all_parts):
+            mine, others = exponents_of(block), exponents_of(other)
+            exponents = jnp.maximum(mine, others) + 1.0
+            factors = lax.optimization_barrier((exact_power(mine - exponents), exact_power(others - exponents)))
+            total = block.astype(jnp.float32) * by_part(parts, factors[0])
+            total = total + other.astype(jnp.float32) * by_part(parts, factors[1])
+            added.append(with_exponents(total, exponents))
+        blocks = added
+    others = [swapped(block, "tile", 1, 1) for block in blocks]
+    return by_half(blocks, others)
+
+
+def by_half(own, others):
     first = lax.axis_index("tile") % HALVES == 0
-    return jnp.where(first, jnp.stack([half, other]), jnp.stack([other, half]))
+    return [jnp.where(first, jnp.stack([a, b]), jnp.stack([b, a])) for a, b in zip(own, others)]
 
 
 def body(initial_state, observed, edge_weight, land, w_in, b_in, w_mid, b_mid, w_out, b_out):
@@ -376,6 +413,9 @@
 
     def exchanged(edges):
         return tuple(lax.ppermute(edge, "tile", way) for edge, way in zip(edges, ways))
+
+    def with_partner(blocks, bit):
+        return jnp.concatenate([blocks, swapped(blocks, "depth", bit, bit)], axis=0)
 
     def from_depths(own):
         return (own, *(swapped(own, "depth", k, k) for k in range(1, depths)))
@@ -397,21 +437,41 @@
         spec_of((TILE_CELLS, width)),
     )
     own_state = initial_state.reshape(rows, TILE_CELLS)
+    target = observed.reshape(rows, TILE_CELLS)
     others = from_depths(own_state)[1:]
-    weight, own_state, bias_in, bias_mid, bias_out = called(
+    prepared = called(
         prepare_kernel,
-        (weight_rows, own_field, spec_of((1, width)), spec_of((1, width)), edge),
+        (
+            weight_rows,
+            own_field,
+            spec_of((1, width)),
+            spec_of((1, width)),
+            edge,
+            spec_of(w_in.shape, w_in.dtype),
+            spec_of(w_mid.shape, w_mid.dtype),
+            spec_of(w_out_t.shape, w_out_t.dtype),
+        ),
         (),
-        (edge_weight.reshape(1, TILE_CELLS), land.reshape(1, TILE_CELLS), own_state, b_in, b_mid, b_out),
+        (edge_weight.reshape(1, TILE_CELLS), land.reshape(1, TILE_CELLS), own_state, b_in, b_mid, b_out, w_in, w_mid, w_out_t),
+        scratch=[
+            pltpu.VMEM((1, TILE_CELLS), jnp.float32),
+            pltpu.VMEM((1, TILE_CELLS), jnp.int32),
+            pltpu.VMEM((width,), jnp.float32),
+            pltpu.VMEM((width,), jnp.float32),
+            pltpu.VMEM((FEATURES,), jnp.float32),
+            pltpu.SemaphoreType.DMA((9,)),
+        ],
         name="prepare",
-    )
-    others, weight, own_state, bias_in, bias_mid, bias_out = lax.optimization_barrier(
-        (others, weight, own_state, bias_in, bias_mid, bias_out)
-    )
+        fetches=True,
+    )
+    prepared, target = lax.optimization_barrier((prepared, target))
+    targets = with_partner(target[None], 1)
+    others, prepared = lax.optimization_barrier((others, prepared))
+    weight, own_state, bias_in, bias_mid, bias_out, w_in, w_mid, w_out_t = prepared
     weights = (w_in, bias_in, w_mid, bias_mid, w_out_t, bias_out)
 
     def closure(state, outs):
-        return called(forward_kernel, (field, *outs), (), (state, *weights), name="closure")
+        return called(forward_kernel, (field, *outs), (), (state, *weights), name="closure", passes=1)
 
     state_0, *edges = called(
         functools.partial(gather_kernel, depths),
@@ -422,8 +482,11 @@
         name="gather",
     )
     edges = exchanged(edges)
-    state_0, target = lax.optimization_barrier((state_0, observed.reshape(rows, TILE_CELLS)))
-    targets = from_depths(target)
+    state_0, targets = lax.optimization_barrier((state_0, targets))
+    bit = 2
+    while bit < depths:
+        targets = with_partner(targets, bit)
+        bit *= 2
     q, *cache_0 = closure(state_0, cached)
     state_1, weight_sums, *edges = called(
         first_step_kernel,
@@ -438,7 +501,7 @@
         functools.partial(last_step_kernel, depths),
         (own_field, field, half_field, edge, edge, edge),
         info,
-        (state_1, weight, weight_sums, q, *edges, *targets),
+        (state_1, weight, weight_sums, q, *edges, targets),
         scratch=[held, whole],
         name="last_step",
     )
@@ -451,6 +514,7 @@
         (),
         (state_1, upstream, *weights[:5]),
         name="first_backward",
+        passes=3,
     )
     adjoint, upstream, *edges = called(
         functools.partial(adjoint_kernel, depths),
@@ -460,14 +524,17 @@
         scratch=[whole],
         name="adjoint",
     )
-    half = spec_of((width // HALVES + 2 * (FEATURES // HALVES) + 8, width))
-    back, kept, sent = called(
+    all_parts = block_parts(width)
+    blocks = [spec_of((sum(parts) + 8, width)) for parts in all_parts]
+    back, *blocks = called(
         last_backward_kernel,
-        (field, half, half),
+        (field, *blocks, *blocks),
         info,
         (state_0, upstream, *cache_0, w_in, w_mid, w_out_t, *parts),
         name="last_backward",
-    )
+        passes=2,
+    )
+    kept, sent = blocks[:2], blocks[2:]
     ended = []
 
     def last_transfers():
@@ -493,29 +560,28 @@
     side_work = last_transfers()
     next(side_work)
     if tiles == 8:
-        grads = summed_by_tile(kept, sent, side_work)
+        grads = summed_by_tile(kept, sent, all_parts, side_work)
     else:
-        first = lax.axis_index("tile") % HALVES == 0
-        grads = jnp.where(first, jnp.stack([kept, sent]), jnp.stack([sent, kept]))
-        grads = lax.psum(grads, "tile")
+        grads = lax.psum(by_half(kept, sent), "tile")
         for _ in range(3):
-            grads = side_work.send(grads)
+            grads[0] = side_work.send(grads[0])
     (sensitivity,) = ended
     scale = 1.0 / (tiles * TILE_CELLS)
-    starts = part_starts(half.shape[0])
-
-    def part(k, count):
-        values = grads[:, starts[k] : starts[k] + count, :]
-        if grads.dtype != jnp.float16:
+
+    def part(b, k, count=None):
+        start = sum(all_parts[b][:k])
+        count = all_parts[b][k] if count is None else count
+        values = grads[b][:, start : start + count, :]
+        if values.dtype != jnp.float16:
             return values * scale
-        at = starts[3] + EXPONENT_ROW + k
-        exponent = grads[:, at : at + 1, :].astype(jnp.float32)
+        at = sum(all_parts[b]) + EXPONENT_ROW + k
+        exponent = grads[b][:, at : at + 1, :].astype(jnp.float32)
         return values.astype(jnp.float32) * (jnp.exp2(exponent) * scale)
 
-    grad_w_mid = part(0, width // HALVES).reshape(width, width)
-    grad_w_in = part(1, FEATURES // HALVES).reshape(FEATURES, width)
-    grad_w_out = part(2, FEATURES // HALVES).reshape(FEATURES, width).T
-    biases = part(3, 2)
+    grad_w_mid = jnp.concatenate([part(0, 0), part(1, 0)], axis=1).reshape(width, width)
+    grad_w_in = part(1, 1).reshape(FEATURES, width)
+    grad_w_out = part(1, 2).reshape(FEATURES, width).T
+    biases = part(1, 3, 2)
     shape = (TRACERS, levels, TILE_CELLS)
     return (
         final_state.reshape(shape),

time: 82.8 us -> 69.6 us (0.84)
  local copies, waits for them, and re-layouts: 8.64 us -> 1.57 us
  waiting for transfers between devices: 19.8 us -> 13.3 us
  other arithmetic: 7.87 us -> 6.42 us
  Pallas kernels: 23.4 us -> 24.8 us
    unnamed x30 -> x5, local copies, waits for them, and re-layouts: 7.26 us -> 0.02 us
    ppermute x10 -> x13, waiting for transfers between devices: 13.9 us -> 10.3 us  [swapped(): lax.ppermute(x, axis, [(i, i ^ (odd_bit if i & 1 else even_bit)) for i in...]
    ppermute x12, waiting for transfers between devices: 5.93 us -> 2.95 us  [exchanged(): lax.ppermute(edge, 'tile', way)]
    convert_element_type x3 -> x6, other arithmetic: 5.21 us -> 2.63 us  [with_exponents(): return out.astype(jnp.float16)]
    concatenate x0 -> x3, other arithmetic: none -> 2.15 us  [the longest x1 1.27 us: body(): jnp.concatenate([part(0, 0), part(1, 0)], axis=1).reshape(width, width)]
    pallas_call x10, Pallas kernels: 23.4 us -> 24.8 us  [called(): pl.pallas_call(kernel, out_shape=tuple(outs), in_specs=in_specs, out_spec...]
    mul x4 -> x6, other arithmetic: 2.08 us -> 0.94 us  [part(): return values.astype(jnp.float32) * (jnp.exp2(exponent) * scale)]
    ppermute x10 -> x13, starting transfers between devices: 12.5 us -> 13 us  [swapped(): lax.ppermute(x, axis, [(i, i ^ (odd_bit if i & 1 else even_bit)) for i in...]
  transfers between devices with their start and end apart: 22 -> 25, of which waited for: 9 -> 9; matrix products, arithmetic and copies ran while one was open for 0% -> 7% of each run, Pallas kernels for 17% -> 23%
where the time goes in v6:
time: 69.6 us; the launch traced here: 69.4 us
  Pallas kernels  24.8 us (36%)
  starting transfers between devices  22.2 us (32%)
  waiting for transfers between devices  13.3 us (19%)
  other arithmetic  6.42 us (9%)
  local copies, waits for them, and re-layouts  1.57 us (2%)
  between operations  1.07 us (2%)
    pallas_call x10, Pallas kernels, called(): pl.pallas_call(kernel, out_shape=tuple(outs), in_specs=in_specs, out_spec...  24.8 us
    ppermute x13, starting transfers between devices, swapped(): lax.ppermute(x, axis, [(i, i ^ (odd_bit if i & 1 else even_bit)) for i in...  13 us
    ppermute x13, waiting for transfers between devices, swapped(): lax.ppermute(x, axis, [(i, i ^ (odd_bit if i & 1 else even_bit)) for i in...  10.3 us
    ppermute x12, starting transfers between devices, exchanged(): lax.ppermute(edge, 'tile', way)  9.27 us
    ppermute x12, waiting for transfers between devices, exchanged(): lax.ppermute(edge, 'tile', way)  2.95 us
    convert_element_type x6, other arithmetic, with_exponents(): return out.astype(jnp.float16)  2.63 us
  transfers between devices with their start and end apart: 25, of which 9 were waited for; matrix products, arithmetic and copies ran while one was open for 7% of the time, Pallas kernels for 23%

profile of v6, /device:TPU:0, one launch (start us, length us, event | category | flops | bytes accessed | tf_op | source)
XLA Modules:
  0.0 69.4 jit_solution(10789297398322405980)
XLA Ops:
  0.6 3.1 %collective-permute-start = (f32[16,1024]{1,0:T(8,128)}, f32[16,1024]{1,0:T(8,128)S(1)}, u32[]{:S(2)}, u32[]{:S(2)}) collective-permute-start(f32[16,1024]{1,0:T(8,128)} %bitcast.47), channel_id=1, source_target_pairs={{0,1},{1,0},{2,3},{3,2},{4,5},{5,4},{6,7},{7,6},{8,9},{9,8},{10,11... | collective-permute-start | bytes 196616 | tf_op jit(solution)/shard_map/ppermute | solution.py:341
  3.7 2.6 %collective-permute-start.1 = (f32[16,1024]{1,0:T(8,128)}, f32[16,1024]{1,0:T(8,128)S(1)}, u32[]{:S(2)}, u32[]{:S(2)}) collective-permute-start(f32[16,1024]{1,0:T(8,128)} %bitcast.48), channel_id=1, source_target_pairs={{0,2},{1,3},{2,0},{3,1},{4,6},{5,7},{6,4},{7,5},{8,10},{9,11},{10,... | collective-permute-start | bytes 196616 | tf_op jit(solution)/shard_map/ppermute | solution.py:341
  6.3 1.6 %prepare.1 = (f32[8,1024]{1,0:T(8,128)S(1)}, f32[16,1024]{1,0:T(8,128)S(1)}, f32[1,640]{1,0:T(1,128)S(1)}, f32[1,640]{1,0:T(1,128)S(1)}, f32[64,128]{1,0:T(8,128...) custom-call(f32[1,1024]{1,0:T(1,128)} %bitcast.56, ...), custom_call_target="tpu_custom_call" | custom-call | tf_op jit(solution)/shard_map/prepare/pallas_call | solution.py:327
  7.9 1.0 %collective-permute-start.3 = (f32[1,16,1024]{2,1,0:T(8,128)}, f32[1,16,1024]{2,1,0:T(8,128)S(1)}, u32[]{:S(2)}, u32[]{:S(2)}) collective-permute-start(f32[1,16,1024]{2,1,0:T(8,128)} %bitcast.44), channel_id=1, source_target_pairs={{0,1},{1,0},{2,3},{3,2},{4,5},{5,4},{6,7},{7,6},{8,9},{9,8},{10,11... | collective-permute-start | bytes 196616 | tf_op jit(solution)/shard_map/ppermute | solution.py:341
  8.9 2.3 %collective-permute-done.1.refs_2_ = f32[16,1024]{1,0:T(8,128)S(1)} collective-permute-done((f32[16,1024]{1,0:T(8,128)}, f32[16,1024]{1,0:T(8,128)S(1)}, u32[]{:S(2)}, u32[]{:S(2)}) %collective-permute-start.1) | collective-permute-done | bytes 65568 | tf_op jit(solution)/shard_map/ppermute | solution.py:341
  11.2 2.0 %collective-permute-done.2.refs_3_ = f32[16,1024]{1,0:T(8,128)S(1)} collective-permute-done((f32[16,1024]{1,0:T(8,128)}, f32[16,1024]{1,0:T(8,128)S(1)}, u32[]{:S(2)}, u32[]{:S(2)}) %collective-permute-start.2) | collective-permute-done | bytes 65568 | tf_op jit(solution)/shard_map/ppermute | solution.py:341
  13.2 1.0 %gather.1 = (f32[64,1024]{1,0:T(8,128)S(1)}, f32[72,128]{1,0:T(8,128)S(1)}, f32[72,128]{1,0:T(8,128)S(1)}, f32[72,128]{1,0:T(8,128)S(1)}) custom-call(s32[2]{0:T(128)S(1)} %pad_add_fusion.info, f32[8,1024]{1,0:T(8,128)S(1)} %get-tuple-element.109.weight_ref, f32[16,1024]{1,0:T(8,128)S(1)} %get-tuple-element.110.refs_0_, ...), custom_call_target="tpu_custom_call" | custom-call | tf_op jit(solution)/shard_map/gather/pallas_call | solution.py:327
  14.2 0.9 %pad_maximum_fusion.2 = f32[2,16,1024]{2,1,0:T(8,128)S(1)} fusion(f32[1,16,1024]{2,1,0:T(8,128)S(1)} %collective-permute-done.3, f32[1,16,1024]{2,1,0:T(8,128)} %bitcast.45), kind=kLoop, calls=%fused_computation.14 | loop fusion | flops 32768 | bytes 262144 | tf_op jit(solution)/shard_map/concatenate | solution.py:418
  15.1 1.7 %collective-permute-start.4 = (f32[72,128]{1,0:T(8,128)S(1)}, f32[72,128]{1,0:T(8,128)S(1)}, u32[]{:S(2)}, u32[]{:S(2)}) collective-permute-start(f32[72,128]{1,0:T(8,128)S(1)} %get-tuple-element.124), channel_id=1, source_target_pairs={{0,16},{4,20},{8,24},{12,28},{16,0},{20,4},{24,8},{28,12},{1,17},{... | collective-permute-start | bytes 110600 | tf_op jit(solution)/shard_map/ppermute | solution.py:415
  16.7 1.5 %collective-permute-start.6 = (f32[72,128]{1,0:T(8,128)S(1)}, f32[72,128]{1,0:T(8,128)S(1)}, u32[]{:S(2)}, u32[]{:S(2)}) collective-permute-start(f32[72,128]{1,0:T(8,128)S(1)} %get-tuple-element.126), channel_id=1, source_target_pairs={{0,28},{4,8},{8,4},{12,16},{16,12},{20,24},{24,20},{28,0},{1,29},{... | collective-permute-start | bytes 110600 | tf_op jit(solution)/shard_map/ppermute | solution.py:415
  18.3 0.9 %collective-permute-start.10 = (f32[2,16,1024]{2,1,0:T(8,128)S(1)}, f32[2,16,1024]{2,1,0:T(8,128)S(1)}, u32[]{:S(2)}, u32[]{:S(2)}) collective-permute-start(f32[2,16,1024]{2,1,0:T(8,128)S(1)} %pad_maximum_fusion.2), channel_id=1, source_target_pairs={{0,2},{1,3},{2,0},{3,1},{4,6},{5,7},{6,4},{7,5},{8,10},{9,11},{10,... | collective-permute-start | bytes 393224 | tf_op jit(solution)/shard_map/ppermute | solution.py:341
  19.2 2.7 %closure.2 = (f32[64,1024]{1,0:T(8,128)S(1)}, bf16[1024,640]{1,0:T(8,128)(2,1)S(1)}, f32[1024,640]{1,0:T(8,128)S(1)}, bf16[1024,640]{1,0:T(8,128)(2,1)S(1)}, f32[1024,640]{1,0:T(8,128)S(1)}) custom-call(f32[64,1024]{1,0:T(8,128)S(1)} %get-tuple-element.116.state_ref, bf16[64,640]{1,0:T(8,128)(2,1)S(1)} %get-tuple-element.117.w_in, ...), custom_call_target="tpu_custom_call" | custom-call | flops 1006632960 | bytes 5242880 | tf_op jit(solution)/shard_map/closure/pallas_call | solution.py:327
  21.9 1.6 %step.1 = (f32[64,1024]{1,0:T(8,128)S(1)}, f32[8,1024]{1,0:T(8,128)S(1)}, f32[64,128]{1,0:T(8,128)S(1)}, f32[64,128]{1,0:T(8,128)S(1)}, f32[64,128]{1,0:T(8,128)S(1)}) custom-call(s32[2]{0:T(128)S(1)} %pad_add_fusion.info, f32[64,1024]{1,0:T(8,128)S(1)} %get-tuple-element.116.state_ref, f32[8,1024]{1,0:T(8,128)S(1)} %get-tuple-element.109.weight_ref, ...), custom_call_target="tpu_custom_call" | custom-call | tf_op jit(solution)/shard_map/step/pallas_call | solution.py:327
  23.5 1.6 %collective-permute-start.7 = (f32[64,128]{1,0:T(8,128)S(1)}, f32[64,128]{1,0:T(8,128)S(1)}, u32[]{:S(2)}, u32[]{:S(2)}) collective-permute-start(f32[64,128]{1,0:T(8,128)S(1)} %get-tuple-element.129), channel_id=1, source_target_pairs={{0,16},{4,20},{8,24},{12,28},{16,0},{20,4},{24,8},{28,12},{1,17},{... | collective-permute-start | bytes 98312 | tf_op jit(solution)/shard_map/ppermute | solution.py:415
  25.1 0.6 collective-permute-start.9
  25.7 2.2 %closure.3.q_ref = f32[64,1024]{1,0:T(8,128)S(1)} custom-call(f32[64,1024]{1,0:T(8,128)S(1)} %get-tuple-element.127.state_ref, bf16[64,640]{1,0:T(8,128)(2,1)S(1)} %get-tuple-element.117.w_in, f32[1,640]{1,0:T(1,128)S(1)} %get-tuple-element.118.b_in, bf16[640,640]{1,0:T(8,128)(2,1)S(1)} %get-tuple-element.119.w_mid, f32[1,640]{1,0:T(1,128)S(1)} %get-tuple-element.120.b_mid, ...), custom_call_target="tpu_custom_call" | custom-call | flops 1006632960 | bytes 5242880 | tf_op jit(solution)/shard_map/closure/pallas_call | solution.py:327
  28.0 1.4 %collective-permute-done.9.e2 = f32[64,128]{1,0:T(8,128)S(1)} collective-permute-done((f32[64,128]{1,0:T(8,128)S(1)}, f32[64,128]{1,0:T(8,128)S(1)}, u32[]{:S(2)}, u32[]{:S(2)}) %collective-permute-start.9) | collective-permute-done | bytes 32800 | tf_op jit(solution)/shard_map/ppermute | solution.py:415
  29.4 2.1 %last_step.1 = (f32[16,1024]{1,0:T(8,128)}, f32[64,1024]{1,0:T(8,128)S(1)}, bf16[64,1024]{1,0:T(8,128)(2,1)S(1)}, f32[64,128]{1,0:T(8,128)S(1)}, f32[64,128]{1,0:T(8,128)S(1)}, /*index=5*/f32[64,128]{1,0:T(8,128)S(1)}) custom-call(s32[2]{0:T(128)S(1)} %pad_add_fusion.info, f32[64,1024]{1,0:T(8,128)S(1)} %get-tuple-element.127.state_ref, ...), custom_call_target="tpu_custom_call" | custom-call | tf_op jit(solution)/shard_map/last_step/pallas_call | solution.py:327
  31.5 0.4 collective-permute-start.11
  32.0 1.3 %collective-permute-start.13 = (f32[64,128]{1,0:T(8,128)S(1)}, f32[64,128]{1,0:T(8,128)S(1)}, u32[]{:S(2)}, u32[]{:S(2)}) collective-permute-start(f32[64,128]{1,0:T(8,128)S(1)} %get-tuple-element.139), channel_id=1, source_target_pairs={{0,28},{4,8},{8,4},{12,16},{16,12},{20,24},{24,20},{28,0},{1,29},{... | collective-permute-start | bytes 98312 | tf_op jit(solution)/shard_map/ppermute | solution.py:415
  33.2 5.8 %first_backward.1 = (f32[64,1024]{1,0:T(8,128)S(1)}, f32[640,640]{1,0:T(8,128)S(1)}, f32[64,640]{1,0:T(8,128)S(1)}, f32[64,640]{1,0:T(8,128)S(1)}, f32[8,640]{1,...) custom-call(f32[64,1024]{1,0:T(8,128)S(1)} %get-tuple-element.127.state_ref, ...), custom_call_target="tpu_custom_call" | custom-call | flops 3019898880 | bytes 15728640 | tf_op jit(solution)/shard_map/first_backward/pallas_call | solution.py:327
  39.0 1.6 %adjoint.1 = (f32[16,1024]{1,0:T(8,128)S(1)}, bf16[64,1024]{1,0:T(8,128)(2,1)S(1)}, f32[16,128]{1,0:T(8,128)S(1)}, f32[16,128]{1,0:T(8,128)S(1)}, f32[16,128]{1,0:T(8,128)S(1)}) custom-call(s32[2]{0:T(128)S(1)} %pad_add_fusion.info, f32[64,1024]{1,0:T(8,128)S(1)} %get-tuple-element.134.adjoint_ref, f32[8,1024]{1,0:T(8,128)S(1)} %get-tuple-element.109.weight_ref, ...), custom_call_target="tpu_custom_call" | custom-call | tf_op jit(solution)/shard_map/adjoint/pallas_call | solution.py:327
  40.6 5.0 %last_backward.1 = (f32[64,1024]{1,0:T(8,128)S(1)}, f32[200,640]{1,0:T(8,128)S(1)}, f32[200,640]{1,0:T(8,128)S(1)}, f32[200,640]{1,0:T(8,128)S(1)}, f32[200,640]{1,0:T(8,128)S(1)}) custom-call(s32[2]{0:T(128)S(1)} %pad_add_fusion.info, f32[64,1024]{1,0:T(8,128)S(1)} %get-tuple-element.116.state_ref, bf16[64,1024]{1,0:T(8,128)(2,1)S(1)} %get-tuple-element.140.upstream_ref, ...), custom_call_target="tpu_custom_call" | custom-call | flops 2013265920 | bytes 10485760 | tf_op jit(solution)/shard_map/last_backward/pallas_call | solution.py:327
  45.7 0.5 collective-permute-start.21
  46.3 1.3 %collective-permute-done.14 = f32[200,640]{1,0:T(8,128)S(1)} collective-permute-done((f32[200,640]{1,0:T(8,128)S(1)}, f32[200,640]{1,0:T(8,128)S(1)}, u32[]{:S(2)}, u32[]{:S(2)}) %collective-permute-start.14) | collective-permute-done | bytes 512032 | tf_op jit(solution)/shard_map/ppermute | solution.py:341
  47.6 0.3 select_convert_fusion.5
  48.0 1.6 %collective-permute-start.15 = (f16[200,640]{1,0:T(8,128)(2,1)S(1)}, f16[200,640]{1,0:T(8,128)(2,1)S(1)}, u32[]{:S(2)}, u32[]{:S(2)}) collective-permute-start(f16[200,640]{1,0:T(8,128)(2,1)S(1)} %select_convert_fusion.5), channel_id=1, source_target_pairs={{0,8},{4,20},{8,0},{12,28},{16,24},{20,4},{24,16},{28,12},{1,9},{5... | collective-permute-start | bytes 768008 | tf_op jit(solution)/shard_map/ppermute | solution.py:341
  49.5 0.9 %collective-permute-start.16 = (f32[16,128]{1,0:T(8,128)S(1)}, f32[16,128]{1,0:T(8,128)S(1)}, u32[]{:S(2)}, u32[]{:S(2)}) collective-permute-start(f32[16,128]{1,0:T(8,128)S(1)} %get-tuple-element.157), channel_id=1, source_target_pairs={{0,16},{4,20},{8,24},{12,28},{16,0},{20,4},{24,8},{28,12},{1,17},{... | collective-permute-start | bytes 24584 | tf_op jit(solution)/shard_map/ppermute | solution.py:415
  50.5 1.1 %collective-permute-start.18 = (f32[16,128]{1,0:T(8,128)S(1)}, f32[16,128]{1,0:T(8,128)S(1)}, u32[]{:S(2)}, u32[]{:S(2)}) collective-permute-start(f32[16,128]{1,0:T(8,128)S(1)} %get-tuple-element.159), channel_id=1, source_target_pairs={{0,28},{4,8},{8,4},{12,16},{16,12},{20,24},{24,20},{28,0},{1,29},{... | collective-permute-start | bytes 24584 | tf_op jit(solution)/shard_map/ppermute | solution.py:415
  51.7 0.2 select_convert_fusion.2
  51.9 1.1 %collective-permute-start.22 = (f16[200,640]{1,0:T(8,128)(2,1)S(1)}, f16[200,640]{1,0:T(8,128)(2,1)S(1)}, u32[]{:S(2)}, u32[]{:S(2)}) collective-permute-start(f16[200,640]{1,0:T(8,128)(2,1)S(1)} %select_convert_fusion.2), channel_id=1, source_target_pairs={{0,8},{4,20},{8,0},{12,28},{16,24},{20,4},{24,16},{28,12},{1,9},{5... | collective-permute-start | bytes 768008 | tf_op jit(solution)/shard_map/ppermute | solution.py:341
  53.0 0.3 collective-permute-done.16.e0
  53.3 1.2 %collective-permute-done.18.e2 = f32[16,128]{1,0:T(8,128)S(1)} collective-permute-done((f32[16,128]{1,0:T(8,128)S(1)}, f32[16,128]{1,0:T(8,128)S(1)}, u32[]{:S(2)}, u32[]{:S(2)}) %collective-permute-start.18) | collective-permute-done | bytes 8224 | tf_op jit(solution)/shard_map/ppermute | solution.py:415
  54.7 0.8 %select_convert_fusion.4 = f16[200,640]{1,0:T(8,128)(2,1)S(1)} fusion(f16[200,640]{1,0:T(8,128)(2,1)S(1)} %collective-permute-done.15, f16[200,640]{1,0:T(8,128)(2,1)S(1)} %select_convert_fusion.5, f32[640]{0:T(1024)S(1)} %get-tuple-element.213, f32[640]{0:T(1024)S(1)} %get-tuple-element.214, f32[640]{0:T(1024)S(1)} %get-tuple-element.215, ...), kind=kLoop, calls=%fused_computation.9 | loop fusion | flops 2048000 | bytes 800120 | tf_op jit(solution)/shard_map/convert_element_type | solution.py:365
  55.5 1.2 %collective-permute-start.19 = (f16[200,640]{1,0:T(8,128)(2,1)S(1)}, f16[200,640]{1,0:T(8,128)(2,1)S(1)}, u32[]{:S(2)}, u32[]{:S(2)}) collective-permute-start(f16[200,640]{1,0:T(8,128)(2,1)S(1)} %select_convert_fusion.4), channel_id=1, source_target_pairs={{0,16},{4,12},{8,24},{12,4},{16,0},{20,28},{24,8},{28,20},{1,17},{... | collective-permute-start | bytes 768008 | tf_op jit(solution)/shard_map/ppermute | solution.py:341
  56.7 1.6 %collective-permute-done.22 = f16[200,640]{1,0:T(8,128)(2,1)S(1)} collective-permute-done((f16[200,640]{1,0:T(8,128)(2,1)S(1)}, f16[200,640]{1,0:T(8,128)(2,1)S(1)}, u32[]{:S(2)}, u32[]{:S(2)}) %collective-permute-start.22) | collective-permute-done | bytes 256032 | tf_op jit(solution)/shard_map/ppermute | solution.py:341
  58.4 0.3 select_convert_fusion.1
  58.7 0.9 %collective-permute-start.23 = (f16[200,640]{1,0:T(8,128)(2,1)S(1)}, f16[200,640]{1,0:T(8,128)(2,1)S(1)}, u32[]{:S(2)}, u32[]{:S(2)}) collective-permute-start(f16[200,640]{1,0:T(8,128)(2,1)S(1)} %select_convert_fusion.1), channel_id=1, source_target_pairs={{0,16},{4,12},{8,24},{12,4},{16,0},{20,28},{24,8},{28,20},{1,17},{... | collective-permute-start | bytes 768008 | tf_op jit(solution)/shard_map/ppermute | solution.py:341
  59.6 1.4 %end.1 = f32[16,1024]{1,0:T(8,128)} custom-call(s32[2]{0:T(128)S(1)} %pad_add_fusion.info, f32[16,1024]{1,0:T(8,128)S(1)} %get-tuple-element.163.adjoint_ref, f32[8,1024]{1,0:T(8,128)S(1)} %get-tuple-element.109.weight_ref, f32[8,1024]{1,0:T(8,128)S(1)} %get-tuple-element.128.sums_ref, f32[64,1024]{1,0:T(8,128)S(1)} %get-tuple-element.164.back_ref, ...), custom_call_target="tpu_custom_call" | custom-call | tf_op jit(solution)/shard_map/end/pallas_call | solution.py:327
  60.9 0.9 %collective-permute-done.19 = f16[200,640]{1,0:T(8,128)(2,1)S(1)} collective-permute-done((f16[200,640]{1,0:T(8,128)(2,1)S(1)}, f16[200,640]{1,0:T(8,128)(2,1)S(1)}, u32[]{:S(2)}, u32[]{:S(2)}) %collective-permute-start.19) | collective-permute-done | bytes 256032 | tf_op jit(solution)/shard_map/ppermute | solution.py:341
  62.1 0.8 %select_convert_fusion.3 = f16[200,640]{1,0:T(8,128)(2,1)S(1)} fusion(f16[200,640]{1,0:T(8,128)(2,1)S(1)} %collective-permute-done.19, f16[200,640]{1,0:T(8,128)(2,1)S(1)} %select_convert_fusion.4, f32[640]{0:T(1024)S(1)} %get-tuple-element.201, f32[640]{0:T(1024)S(1)} %get-tuple-element.202, f32[640]{0:T(1024)S(1)} %get-tuple-element.203, ...), kind=kLoop, calls=%fused_computation.8 | loop fusion | flops 2048000 | bytes 800120 | tf_op jit(solution)/shard_map/convert_element_type | solution.py:365
  62.9 2.2 %collective-permute-done.23 = f16[200,640]{1,0:T(8,128)(2,1)S(1)} collective-permute-done((f16[200,640]{1,0:T(8,128)(2,1)S(1)}, f16[200,640]{1,0:T(8,128)(2,1)S(1)}, u32[]{:S(2)}, u32[]{:S(2)}) %collective-permute-start.23) | collective-permute-done | bytes 256032 | tf_op jit(solution)/shard_map/ppermute | solution.py:341
  65.2 0.3 select_convert_fusion
  65.6 0.2 maximum_select_fusion
  65.9 0.5 slice_bitcast_fusion
  66.4 0.6 slice_reduce_fusion
  67.4 0.8 %convert_multiply_fusion.2 = (f32[2,32,640]{2,1,0:T(8,128)}, f32[2,32,640]{2,1,0:T(8,128)}) fusion(f16[2,200,640]{2,1,0:T(8,128)(2,1)S(1)} %maximum_select_fusion, f32[2,640]{1,0:T(2,128)S(1)} %bitcast.51, f32[2,640]{1,0:T(2,128)S(1)} %bitcast.52), kind=kLoop, calls=%fused_computation.12 | loop fusion | flops 163840 | bytes 501760 | tf_op jit(solution)/shard_map/mul | solution.py:579
  68.1 1.3 %pad_maximum_fusion = f32[2,320,640]{2,1,0:T(8,128)} fusion(f32[2,128,640]{2,1,0:T(8,128)S(1)} %convert_multiply_fusion.1, f32[2,192,640]{2,1,0:T(8,128)S(1)} %convert_multiply_fusion), kind=kLoop, calls=%fused_computation | loop fusion | flops 409600 | bytes 3276800 | tf_op jit(solution)/shard_map/concatenate | solution.py:581
  (61 shorter events, 1.5 us)
Async XLA Ops:
  0.6 8.3 %collective-permute-start = (f32[16,1024]{1,0:T(8,128)}, f32[16,1024]{1,0:T(8,128)S(1)}, u32[]{:S(2)}, u32[]{:S(2)}) collective-permute-start(f32[16,1024]{1,0:T(8,128)} %bitcast.47), channel_id=1, source_target_pairs={{0,1},{1,0},{2,3},{3,2},{4,5},{5,4},{6,7},{7,6},{8,9},{9,8},{10,11... | collective-permute-start | bytes 196616 | tf_op jit(solution)/shard_map/ppermute | solution.py:341
  3.7 7.5 %collective-permute-start.1 = (f32[16,1024]{1,0:T(8,128)}, f32[16,1024]{1,0:T(8,128)S(1)}, u32[]{:S(2)}, u32[]{:S(2)}) collective-permute-start(f32[16,1024]{1,0:T(8,128)} %bitcast.48), channel_id=1, source_target_pairs={{0,2},{1,3},{2,0},{3,1},{4,6},{5,7},{6,4},{7,5},{8,10},{9,11},{10,... | collective-permute-start | bytes 196616 | tf_op jit(solution)/shard_map/ppermute | solution.py:341
  6.3 6.9 %collective-permute-start.2 = (f32[16,1024]{1,0:T(8,128)}, f32[16,1024]{1,0:T(8,128)S(1)}, u32[]{:S(2)}, u32[]{:S(2)}) collective-permute-start(f32[16,1024]{1,0:T(8,128)} %bitcast.49), channel_id=1, source_target_pairs={{0,3},{1,2},{2,1},{3,0},{4,7},{5,6},{6,5},{7,4},{8,11},{9,10},{10,... | collective-permute-start | bytes 196616 | tf_op jit(solution)/shard_map/ppermute | solution.py:341
  7.9 6.3 %collective-permute-start.3 = (f32[1,16,1024]{2,1,0:T(8,128)}, f32[1,16,1024]{2,1,0:T(8,128)S(1)}, u32[]{:S(2)}, u32[]{:S(2)}) collective-permute-start(f32[1,16,1024]{2,1,0:T(8,128)} %bitcast.44), channel_id=1, source_target_pairs={{0,1},{1,0},{2,3},{3,2},{4,5},{5,4},{6,7},{7,6},{8,9},{9,8},{10,11... | collective-permute-start | bytes 196616 | tf_op jit(solution)/shard_map/ppermute | solution.py:341
  15.1 6.7 %collective-permute-start.4 = (f32[72,128]{1,0:T(8,128)S(1)}, f32[72,128]{1,0:T(8,128)S(1)}, u32[]{:S(2)}, u32[]{:S(2)}) collective-permute-start(f32[72,128]{1,0:T(8,128)S(1)} %get-tuple-element.124), channel_id=1, source_target_pairs={{0,16},{4,20},{8,24},{12,28},{16,0},{20,4},{24,8},{28,12},{1,17},{... | collective-permute-start | bytes 110600 | tf_op jit(solution)/shard_map/ppermute | solution.py:415
  16.7 5.1 %collective-permute-start.5 = (f32[72,128]{1,0:T(8,128)S(1)}, f32[72,128]{1,0:T(8,128)S(1)}, u32[]{:S(2)}, u32[]{:S(2)}) collective-permute-start(f32[72,128]{1,0:T(8,128)S(1)} %get-tuple-element.125), channel_id=1, source_target_pairs={{0,4},{4,0},{8,12},{12,8},{16,20},{20,16},{24,28},{28,24},{1,5},{5... | collective-permute-start | bytes 110600 | tf_op jit(solution)/shard_map/ppermute | solution.py:415
  16.7 5.1 %collective-permute-start.6 = (f32[72,128]{1,0:T(8,128)S(1)}, f32[72,128]{1,0:T(8,128)S(1)}, u32[]{:S(2)}, u32[]{:S(2)}) collective-permute-start(f32[72,128]{1,0:T(8,128)S(1)} %get-tuple-element.126), channel_id=1, source_target_pairs={{0,28},{4,8},{8,4},{12,16},{16,12},{20,24},{24,20},{28,0},{1,29},{... | collective-permute-start | bytes 110600 | tf_op jit(solution)/shard_map/ppermute | solution.py:415
  18.3 9.7 %collective-permute-start.10 = (f32[2,16,1024]{2,1,0:T(8,128)S(1)}, f32[2,16,1024]{2,1,0:T(8,128)S(1)}, u32[]{:S(2)}, u32[]{:S(2)}) collective-permute-start(f32[2,16,1024]{2,1,0:T(8,128)S(1)} %pad_maximum_fusion.2), channel_id=1, source_target_pairs={{0,2},{1,3},{2,0},{3,1},{4,6},{5,7},{6,4},{7,5},{8,10},{9,11},{10,... | collective-permute-start | bytes 393224 | tf_op jit(solution)/shard_map/ppermute | solution.py:341
  23.5 4.5 %collective-permute-start.7 = (f32[64,128]{1,0:T(8,128)S(1)}, f32[64,128]{1,0:T(8,128)S(1)}, u32[]{:S(2)}, u32[]{:S(2)}) collective-permute-start(f32[64,128]{1,0:T(8,128)S(1)} %get-tuple-element.129), channel_id=1, source_target_pairs={{0,16},{4,20},{8,24},{12,28},{16,0},{20,4},{24,8},{28,12},{1,17},{... | collective-permute-start | bytes 98312 | tf_op jit(solution)/shard_map/ppermute | solution.py:415
  25.1 2.9 %collective-permute-start.8 = (f32[64,128]{1,0:T(8,128)S(1)}, f32[64,128]{1,0:T(8,128)S(1)}, u32[]{:S(2)}, u32[]{:S(2)}) collective-permute-start(f32[64,128]{1,0:T(8,128)S(1)} %get-tuple-element.130), channel_id=1, source_target_pairs={{0,4},{4,0},{8,12},{12,8},{16,20},{20,16},{24,28},{28,24},{1,5},{5... | collective-permute-start | bytes 98312 | tf_op jit(solution)/shard_map/ppermute | solution.py:415
  25.1 4.3 %collective-permute-start.9 = (f32[64,128]{1,0:T(8,128)S(1)}, f32[64,128]{1,0:T(8,128)S(1)}, u32[]{:S(2)}, u32[]{:S(2)}) collective-permute-start(f32[64,128]{1,0:T(8,128)S(1)} %get-tuple-element.131), channel_id=1, source_target_pairs={{0,28},{4,8},{8,4},{12,16},{16,12},{20,24},{24,20},{28,0},{1,29},{... | collective-permute-start | bytes 98312 | tf_op jit(solution)/shard_map/ppermute | solution.py:415
  31.5 7.5 %collective-permute-start.11 = (f32[64,128]{1,0:T(8,128)S(1)}, f32[64,128]{1,0:T(8,128)S(1)}, u32[]{:S(2)}, u32[]{:S(2)}) collective-permute-start(f32[64,128]{1,0:T(8,128)S(1)} %get-tuple-element.137), channel_id=1, source_target_pairs={{0,16},{4,20},{8,24},{12,28},{16,0},{20,4},{24,8},{28,12},{1,17},{... | collective-permute-start | bytes 98312 | tf_op jit(solution)/shard_map/ppermute | solution.py:415
  31.9 7.1 %collective-permute-start.12 = (f32[64,128]{1,0:T(8,128)S(1)}, f32[64,128]{1,0:T(8,128)S(1)}, u32[]{:S(2)}, u32[]{:S(2)}) collective-permute-start(f32[64,128]{1,0:T(8,128)S(1)} %get-tuple-element.138), channel_id=1, source_target_pairs={{0,4},{4,0},{8,12},{12,8},{16,20},{20,16},{24,28},{28,24},{1,5},{5... | collective-permute-start | bytes 98312 | tf_op jit(solution)/shard_map/ppermute | solution.py:415
  32.0 7.1 %collective-permute-start.13 = (f32[64,128]{1,0:T(8,128)S(1)}, f32[64,128]{1,0:T(8,128)S(1)}, u32[]{:S(2)}, u32[]{:S(2)}) collective-permute-start(f32[64,128]{1,0:T(8,128)S(1)} %get-tuple-element.139), channel_id=1, source_target_pairs={{0,28},{4,8},{8,4},{12,16},{16,12},{20,24},{24,20},{28,0},{1,29},{... | collective-permute-start | bytes 98312 | tf_op jit(solution)/shard_map/ppermute | solution.py:415
  45.6 2.0 %collective-permute-start.14 = (f32[200,640]{1,0:T(8,128)S(1)}, f32[200,640]{1,0:T(8,128)S(1)}, u32[]{:S(2)}, u32[]{:S(2)}) collective-permute-start(f32[200,640]{1,0:T(8,128)S(1)} %get-tuple-element.152), channel_id=1, source_target_pairs={{0,4},{4,0},{8,12},{12,8},{16,20},{20,16},{24,28},{28,24},{1,5},{5... | collective-permute-start | bytes 1536008 | tf_op jit(solution)/shard_map/ppermute | solution.py:341
  45.7 5.9 %collective-permute-start.21 = (f32[200,640]{1,0:T(8,128)S(1)}, f32[200,640]{1,0:T(8,128)S(1)}, u32[]{:S(2)}, u32[]{:S(2)}) collective-permute-start(f32[200,640]{1,0:T(8,128)S(1)} %get-tuple-element.173), channel_id=1, source_target_pairs={{0,4},{4,0},{8,12},{12,8},{16,20},{20,16},{24,28},{28,24},{1,5},{5... | collective-permute-start | bytes 1536008 | tf_op jit(solution)/shard_map/ppermute | solution.py:341
  48.0 6.6 %collective-permute-start.15 = (f16[200,640]{1,0:T(8,128)(2,1)S(1)}, f16[200,640]{1,0:T(8,128)(2,1)S(1)}, u32[]{:S(2)}, u32[]{:S(2)}) collective-permute-start(f16[200,640]{1,0:T(8,128)(2,1)S(1)} %select_convert_fusion.5), channel_id=1, source_target_pairs={{0,8},{4,20},{8,0},{12,28},{16,24},{20,4},{24,16},{28,12},{1,9},{5... | collective-permute-start | bytes 768008 | tf_op jit(solution)/shard_map/ppermute | solution.py:341
  49.5 3.8 %collective-permute-start.16 = (f32[16,128]{1,0:T(8,128)S(1)}, f32[16,128]{1,0:T(8,128)S(1)}, u32[]{:S(2)}, u32[]{:S(2)}) collective-permute-start(f32[16,128]{1,0:T(8,128)S(1)} %get-tuple-element.157), channel_id=1, source_target_pairs={{0,16},{4,20},{8,24},{12,28},{16,0},{20,4},{24,8},{28,12},{1,17},{... | collective-permute-start | bytes 24584 | tf_op jit(solution)/shard_map/ppermute | solution.py:415
  50.5 2.9 %collective-permute-start.17 = (f32[16,128]{1,0:T(8,128)S(1)}, f32[16,128]{1,0:T(8,128)S(1)}, u32[]{:S(2)}, u32[]{:S(2)}) collective-permute-start(f32[16,128]{1,0:T(8,128)S(1)} %get-tuple-element.158), channel_id=1, source_target_pairs={{0,4},{4,0},{8,12},{12,8},{16,20},{20,16},{24,28},{28,24},{1,5},{5... | collective-permute-start | bytes 24584 | tf_op jit(solution)/shard_map/ppermute | solution.py:415
  50.5 4.0 %collective-permute-start.18 = (f32[16,128]{1,0:T(8,128)S(1)}, f32[16,128]{1,0:T(8,128)S(1)}, u32[]{:S(2)}, u32[]{:S(2)}) collective-permute-start(f32[16,128]{1,0:T(8,128)S(1)} %get-tuple-element.159), channel_id=1, source_target_pairs={{0,28},{4,8},{8,4},{12,16},{16,12},{20,24},{24,20},{28,0},{1,29},{... | collective-permute-start | bytes 24584 | tf_op jit(solution)/shard_map/ppermute | solution.py:415
  51.9 6.4 %collective-permute-start.22 = (f16[200,640]{1,0:T(8,128)(2,1)S(1)}, f16[200,640]{1,0:T(8,128)(2,1)S(1)}, u32[]{:S(2)}, u32[]{:S(2)}) collective-permute-start(f16[200,640]{1,0:T(8,128)(2,1)S(1)} %select_convert_fusion.2), channel_id=1, source_target_pairs={{0,8},{4,20},{8,0},{12,28},{16,24},{20,4},{24,16},{28,12},{1,9},{5... | collective-permute-start | bytes 768008 | tf_op jit(solution)/shard_map/ppermute | solution.py:341
  55.5 6.4 %collective-permute-start.19 = (f16[200,640]{1,0:T(8,128)(2,1)S(1)}, f16[200,640]{1,0:T(8,128)(2,1)S(1)}, u32[]{:S(2)}, u32[]{:S(2)}) collective-permute-start(f16[200,640]{1,0:T(8,128)(2,1)S(1)} %select_convert_fusion.4), channel_id=1, source_target_pairs={{0,16},{4,12},{8,24},{12,4},{16,0},{20,28},{24,8},{28,20},{1,17},{... | collective-permute-start | bytes 768008 | tf_op jit(solution)/shard_map/ppermute | solution.py:341
  58.7 6.4 %collective-permute-start.23 = (f16[200,640]{1,0:T(8,128)(2,1)S(1)}, f16[200,640]{1,0:T(8,128)(2,1)S(1)}, u32[]{:S(2)}, u32[]{:S(2)}) collective-permute-start(f16[200,640]{1,0:T(8,128)(2,1)S(1)} %select_convert_fusion.1), channel_id=1, source_target_pairs={{0,16},{4,12},{8,24},{12,4},{16,0},{20,28},{24,8},{28,20},{1,17},{... | collective-permute-start | bytes 768008 | tf_op jit(solution)/shard_map/ppermute | solution.py:341
  62.8 2.7 %collective-permute-start.20 = (f16[200,640]{1,0:T(8,128)(2,1)S(1)}, f16[200,640]{1,0:T(8,128)(2,1)S(1)}, u32[]{:S(2)}, u32[]{:S(2)}) collective-permute-start(f16[200,640]{1,0:T(8,128)(2,1)S(1)} %select_convert_fusion.3), channel_id=1, source_target_pairs={{0,4},{4,0},{8,12},{12,8},{16,20},{20,16},{24,28},{28,24},{1,5},{5... | collective-permute-start | bytes 768008 | tf_op jit(solution)/shard_map/ppermute | solution.py:341
  65.5 1.6 %collective-permute-start.24 = (f16[200,640]{1,0:T(8,128)(2,1)S(1)}, f16[200,640]{1,0:T(8,128)(2,1)S(1)}, u32[]{:S(2)}, u32[]{:S(2)}) collective-permute-start(f16[200,640]{1,0:T(8,128)(2,1)S(1)} %select_convert_fusion), channel_id=1, source_target_pairs={{0,4},{4,0},{8,12},{12,8},{16,20},{20,16},{24,28},{28,24},{1,5},{5... | collective-permute-start | bytes 768008 | tf_op jit(solution)/shard_map/ppermute | solution.py:341

commit v7 on v6

--- a/solution.py
+++ b/solution.py
@@ -125,8 +125,10 @@
         copy.wait()
     weight = edge[...] * land[...].astype(jnp.float32)
     weight_out[...] = jnp.broadcast_to(weight, weight_out.shape)
-    in_ref[...] = bias_in[...].reshape(in_ref.shape)
-    mid_ref[...] = bias_mid[...].reshape(mid_ref.shape)
+    in_ref[...] = 0.5 * bias_in[...].reshape(in_ref.shape)
+    mid_ref[...] = 0.5 * bias_mid[...].reshape(mid_ref.shape)
+    for held_ref in held_refs[:2]:
+        held_ref[...] = (0.5 * held_ref[...].astype(jnp.float32)).astype(jnp.bfloat16)
     rest = bias_out[...].reshape(1, FEATURES)
     terms = []
     for _ in range(3):
@@ -147,18 +149,14 @@
         edge_out[...] = edge
 
 
-def sigmoid(z):
-    return 0.5 * jnp.tanh(0.5 * z) + 0.5
-
-
 def contract(a, b, dims):
     return lax.dot_general(a, b, ((dims[:1], dims[1:]), ((), ())), preferred_element_type=jnp.float32)
 
 
-def layer(pre):
-    gate = sigmoid(pre)
-    hidden = pre * gate
-    return hidden.astype(jnp.bfloat16), gate + hidden * (1.0 - gate)
+def layer(y):
+    a = 1.0 + jnp.tanh(y)
+    hidden = y * a
+    return hidden.astype(jnp.bfloat16), a * ((1.0 + (y + y)) - hidden)
 
 
 def hidden_layers(state, w_in, b_in, w_mid, b_mid):
@@ -192,9 +190,9 @@
         edge_out[...] = edge
 
 
-def last_step_kernel(
-    depths, info, state_ref, weight_ref, sums_ref, q_ref, e0, e1, e2, target_ref, final_ref, adjoint_ref, upstream_ref, o0, o1, o2, held, ordered
-):
+def last_step_kernel(depths, info, state_ref, weight_ref, sums_ref, q_ref, e0, e1, e2, *refs):
+    target_refs = refs[:depths]
+    final_ref, adjoint_ref, upstream_ref, o0, o1, o2, held, ordered = refs[depths:]
     weight = weight_ref[0:1, :]
     mask = mask_of(weight)
     state = state_ref[...]
@@ -203,7 +201,7 @@
     state = state + diffuse_coef * change + step_size * mask * q_ref[...]
     adjoint_ref[...] = state
     own_levels(depths, info, adjoint_ref, final_ref)
-    in_order(depths, info, [target_ref.at[k] for k in range(depths)], held, ordered)
+    in_order(depths, info, target_refs, held, ordered)
     adjoint = mask * (state - ordered[...])
     adjoint_ref[...] = adjoint
     upstream_ref[...] = (step_size * mask * adjoint).astype(jnp.bfloat16)
@@ -239,7 +237,7 @@
 def block_parts(width):
     side = FEATURES // HALVES
     second = (width // HALVES - 2 * side) // 2 // 16 * 16
-    return (width // HALVES - second,), (second, side, side)
+    return (second, side, side), (width // HALVES - second,)
 
 
 def exponent_of(part):
@@ -252,9 +250,10 @@
     hidden_one, slope_one, hidden_two, slope_two = layers
     width = w_mid.shape[0]
     ones = jnp.ones((8, upstream.shape[1]), jnp.bfloat16)
-    slope_two = (contract(upstream, w_out_t[...], (0, 0)) * slope_two).astype(jnp.bfloat16)
+    half = (0.5 * upstream.astype(jnp.float32)).astype(jnp.bfloat16)
+    slope_two = (contract(half, w_out_t[...], (0, 0)) * slope_two).astype(jnp.bfloat16)
     slope_one = (contract(slope_two, w_mid[...], (1, 1)) * slope_one).astype(jnp.bfloat16)
-    back = contract(w_in[...], slope_one, (1, 1))
+    back = 2.0 * contract(w_in[...], slope_one, (1, 1))
     bias_out = contract(ones, upstream, (1, 1))
     return back, (
         contract(hidden_one, slope_two, (0, 0)),
@@ -266,10 +265,12 @@
     )
 
 
-def first_backward_kernel(state_ref, upstream_ref, w_in, b_in, w_mid, b_mid, w_out_t, back_ref, *part_refs):
-    state = state_ref[...]
-    layers = hidden_layers(state, w_in, b_in, w_mid, b_mid)
-    back, parts = gradient_parts(state.astype(jnp.bfloat16), upstream_ref[...], layers, w_in, w_mid, w_out_t)
+def first_backward_kernel(
+    state_ref, upstream_ref, one_ref, slope_one_ref, two_ref, slope_two_ref, w_in, w_mid, w_out_t, back_ref, *part_refs
+):
+    layers = (one_ref[...], slope_one_ref[...], two_ref[...], slope_two_ref[...])
+    inputs = state_ref[...].astype(jnp.bfloat16)
+    back, parts = gradient_parts(inputs, upstream_ref[...], layers, w_in, w_mid, w_out_t)
     back_ref[...] = back
     for part_ref, part in zip(part_refs, parts):
         part_ref[...] = part
@@ -284,30 +285,32 @@
     back_ref[...] = back
     mid, side_in, side_out, bias_in, bias_mid, bias_out = [part + ref[...] for part, ref in zip(parts, earlier_refs)]
     row = lax.broadcasted_iota(jnp.int32, bias_in.shape, 0)
-    own = info[1] % HALVES
-    (top,), (_, side, _) = block_parts(w_mid.shape[0])
-    for half in range(HALVES):
-        count = mid.shape[0] // HALVES
-        rows = mid[half * count : (half + 1) * count, :]
-        tail = jnp.where(row == 0, bias_mid if half else bias_in, 0.0)
-        if half == 0:
-            tail = jnp.where(row == 1, bias_out, tail)
-        at = slice(half * side, (half + 1) * side)
-        blocks = ([rows[:top, :], jnp.zeros_like(tail)], [rows[top:, :], side_in[at, :], side_out[at, :], tail])
-        for k, pieces in enumerate(blocks):
-            last = pieces[-1]
-            for j, piece in enumerate(pieces if k else pieces[:1]):
-                last = jnp.where(row == EXPONENT_ROW + j, exponent_of(piece), last)
-            pieces[-1] = last
-
-            def store(to_ref, pieces=pieces):
-                at = 0
-                for piece in pieces:
-                    to_ref[at : at + piece.shape[0], :] = piece
-                    at += piece.shape[0]
-
-            pl.when(own == half)(functools.partial(store, block_refs[k]))
-            pl.when(own != half)(functools.partial(store, block_refs[2 + k]))
+    is_first = info[1] % HALVES == 0
+    (top, side, _), _ = block_parts(w_mid.shape[0])
+    count = mid.shape[0] // HALVES
+    tails = (
+        jnp.where(row == 0, bias_in, jnp.where(row == 1, bias_out, 0.0)),
+        jnp.where(row == 0, bias_mid, 0.0),
+    )
+    for other in (False, True):
+
+        def one(halves):
+            return jnp.where(is_first, halves[other], halves[not other])
+
+        first = [
+            one((mid[:top, :], mid[count : count + top, :])),
+            one((side_in[:side, :], side_in[side:, :])),
+            one((side_out[:side, :], side_out[side:, :])),
+            one(tails),
+        ]
+        second = [one((mid[top:count, :], mid[count + top :, :])), jnp.zeros_like(tails[0])]
+        for pieces, to_ref, coded_parts in zip((first, second), block_refs[2 * other :], (4, 1)):
+            for k in range(coded_parts):
+                pieces[-1] = jnp.where(row == EXPONENT_ROW + k, exponent_of(pieces[k]), pieces[-1])
+            at = 0
+            for piece in pieces:
+                to_ref[at : at + piece.shape[0], :] = piece
+                at += piece.shape[0]
 
 
 def spec_of(shape, dtype=jnp.float32):
@@ -373,33 +376,44 @@
     return out
 
 
-def summed_by_tile(kept, sent, all_parts, side_work):
-    received = [swapped(block, "tile", 1, 1) for block in sent]
-    received[1] = side_work.send(received[1])
-    blocks = []
-    for block, other, parts in zip(kept, received, all_parts):
-        exponents = jnp.maximum(exponents_of(block), exponents_of(other)) + 1.0
-        factors = lax.optimization_barrier(jnp.exp2(-exponents))
-        blocks.append(with_exponents((block + other) * by_part(parts, factors), exponents))
-    for even_bit, odd_bit in ((2, 4), (4, 2)):
-        received = [swapped(block, "tile", even_bit, odd_bit) for block in blocks]
-        received[1] = side_work.send(received[1])
-        added = []
-        for block, other, parts in zip(blocks, received, all_parts):
-            mine, others = exponents_of(block), exponents_of(other)
-            exponents = jnp.maximum(mine, others) + 1.0
-            factors = lax.optimization_barrier((exact_power(mine - exponents), exact_power(others - exponents)))
-            total = block.astype(jnp.float32) * by_part(parts, factors[0])
-            total = total + other.astype(jnp.float32) * by_part(parts, factors[1])
-            added.append(with_exponents(total, exponents))
-        blocks = added
-    others = [swapped(block, "tile", 1, 1) for block in blocks]
-    return by_half(blocks, others)
-
-
-def by_half(own, others):
+def coded_sum(block, other, parts):
+    exponents = jnp.maximum(exponents_of(block), exponents_of(other)) + 1.0
+    factors = lax.optimization_barrier(jnp.exp2(-exponents))
+    return with_exponents((block + other) * by_part(parts, factors), exponents)
+
+
+def sum_of_coded(block, other, parts):
+    mine, others = exponents_of(block), exponents_of(other)
+    exponents = jnp.maximum(mine, others) + 1.0
+    factors = lax.optimization_barrier((exact_power(mine - exponents), exact_power(others - exponents)))
+    total = block.astype(jnp.float32) * by_part(parts, factors[0])
+    total = total + other.astype(jnp.float32) * by_part(parts, factors[1])
+    return with_exponents(total, exponents)
+
+
+def summed_by_tile(kept, sent, all_parts, edges, exchanged, end, finish_first):
+    tied = lax.optimization_barrier
+    others = [swapped(block, "tile", 1, 1) for block in sent]
+    first = coded_sum(kept[0], others[0], all_parts[0])
+    second = coded_sum(kept[1], others[1], all_parts[1])
+    later, edges = tied((second, edges))
+    arrived = exchanged(edges)
+    others = [swapped(block, "tile", 2, 4) for block in (first, second)]
+    others[0], second = tied((others[0], later))
+    first = sum_of_coded(first, others[0], all_parts[0])
+    others[1], held, arrived = tied((others[1], first, arrived))
+    second = sum_of_coded(second, others[1], all_parts[1])
+    others = [swapped(block, "tile", 4, 2) for block in (first, second)]
+    others[0], later, ended = tied((others[0], second, end(arrived)))
+    first = sum_of_coded(held, others[0], all_parts[0])
+    finished = finish_first(by_half(first, swapped(first, "tile", 1, 1)))
+    second = sum_of_coded(later, others[1], all_parts[1])
+    return ended, finished, by_half(second, swapped(second, "tile", 1, 1))
+
+
+def by_half(own, other):
     first = lax.axis_index("tile") % HALVES == 0
-    return [jnp.where(first, jnp.stack([a, b]), jnp.stack([b, a])) for a, b in zip(own, others)]
+    return jnp.where(first, jnp.stack([own, other]), jnp.stack([other, own]))
 
 
 def body(initial_state, observed, edge_weight, land, w_in, b_in, w_mid, b_mid, w_out, b_out):
@@ -413,9 +427,6 @@
 
     def exchanged(edges):
         return tuple(lax.ppermute(edge, "tile", way) for edge, way in zip(edges, ways))
-
-    def with_partner(blocks, bit):
-        return jnp.concatenate([blocks, swapped(blocks, "depth", bit, bit)], axis=0)
 
     def from_depths(own):
         return (own, *(swapped(own, "depth", k, k) for k in range(1, depths)))
@@ -465,7 +476,7 @@
         fetches=True,
     )
     prepared, target = lax.optimization_barrier((prepared, target))
-    targets = with_partner(target[None], 1)
+    targets = from_depths(target)
     others, prepared = lax.optimization_barrier((others, prepared))
     weight, own_state, bias_in, bias_mid, bias_out, w_in, w_mid, w_out_t = prepared
     weights = (w_in, bias_in, w_mid, bias_mid, w_out_t, bias_out)
@@ -482,12 +493,8 @@
         name="gather",
     )
     edges = exchanged(edges)
-    state_0, targets = lax.optimization_barrier((state_0, targets))
-    bit = 2
-    while bit < depths:
-        targets = with_partner(targets, bit)
-        bit *= 2
     q, *cache_0 = closure(state_0, cached)
+    q, targets = lax.optimization_barrier((q, targets))
     state_1, weight_sums, *edges = called(
         first_step_kernel,
         (field, weight_rows, edge, edge, edge),
@@ -496,12 +503,12 @@
         name="step",
     )
     edges = exchanged(edges)
-    (q,) = closure(state_1, ())
+    q, *cache_1 = closure(state_1, cached)
     final_state, adjoint, upstream, *edges = called(
         functools.partial(last_step_kernel, depths),
         (own_field, field, half_field, edge, edge, edge),
         info,
-        (state_1, weight, weight_sums, q, *edges, targets),
+        (state_1, weight, weight_sums, q, *edges, *targets),
         scratch=[held, whole],
         name="last_step",
     )
@@ -512,9 +519,9 @@
         first_backward_kernel,
         (field, spec_of((width, width)), side, side, row_sum, row_sum, row_sum),
         (),
-        (state_1, upstream, *weights[:5]),
+        (state_1, upstream, *cache_1, w_in, w_mid, w_out_t),
         name="first_backward",
-        passes=3,
+        passes=2,
     )
     adjoint, upstream, *edges = called(
         functools.partial(adjoint_kernel, depths),
@@ -535,63 +542,53 @@
         passes=2,
     )
     kept, sent = blocks[:2], blocks[2:]
-    ended = []
-
-    def last_transfers():
-        arrived = yield None
-        arrived, *held = lax.optimization_barrier((arrived, *edges))
-        arrived = yield arrived
-        got = exchanged(held)
-        arrived, *got = lax.optimization_barrier((arrived, *got))
-        arrived = yield arrived
+    scale = 1.0 / (tiles * TILE_CELLS)
+
+    def end(arrived):
         (sensitivity,) = called(
             functools.partial(end_kernel, depths),
             (own_field,),
             info,
-            (adjoint, weight, weight_sums, back, *got),
+            (adjoint, weight, weight_sums, back, *arrived),
             scratch=[pltpu.VMEM((rows, TILE_CELLS), jnp.float32)],
             name="end",
         )
-        arrived, sensitivity = lax.optimization_barrier((arrived, sensitivity))
-        ended.append(sensitivity)
-        while True:
-            arrived = yield arrived
-
-    side_work = last_transfers()
-    next(side_work)
-    if tiles == 8:
-        grads = summed_by_tile(kept, sent, all_parts, side_work)
-    else:
-        grads = lax.psum(by_half(kept, sent), "tile")
-        for _ in range(3):
-            grads[0] = side_work.send(grads[0])
-    (sensitivity,) = ended
-    scale = 1.0 / (tiles * TILE_CELLS)
-
-    def part(b, k, count=None):
+        return sensitivity
+
+    def part(block, b, k, count=None):
         start = sum(all_parts[b][:k])
         count = all_parts[b][k] if count is None else count
-        values = grads[b][:, start : start + count, :]
+        values = block[:, start : start + count, :]
         if values.dtype != jnp.float16:
             return values * scale
         at = sum(all_parts[b]) + EXPONENT_ROW + k
-        exponent = grads[b][:, at : at + 1, :].astype(jnp.float32)
+        exponent = block[:, at : at + 1, :].astype(jnp.float32)
         return values.astype(jnp.float32) * (jnp.exp2(exponent) * scale)
 
-    grad_w_mid = jnp.concatenate([part(0, 0), part(1, 0)], axis=1).reshape(width, width)
-    grad_w_in = part(1, 1).reshape(FEATURES, width)
-    grad_w_out = part(1, 2).reshape(FEATURES, width).T
-    biases = part(1, 3, 2)
+    def finish_first(block):
+        grad_w_in = part(block, 0, 1).reshape(FEATURES, width)
+        grad_w_out = part(block, 0, 2).reshape(FEATURES, width).T
+        biases = part(block, 0, 3, 2)
+        return grad_w_in, biases[0, 0], biases[1, 0], grad_w_out, biases[0, 1, :FEATURES], block
+
+    if tiles == 8:
+        sensitivity, finished, second = summed_by_tile(kept, sent, all_parts, tuple(edges), exchanged, end, finish_first)
+    else:
+        first, second = lax.psum([by_half(*args) for args in zip(kept, sent)], "tile")
+        finished = finish_first(first)
+        sensitivity = end(exchanged(edges))
+    grad_w_in, grad_b_in, grad_b_mid, grad_w_out, grad_b_out, first = finished
+    grad_w_mid = jnp.concatenate([part(first, 0, 0), part(second, 1, 0)], axis=1).reshape(width, width)
     shape = (TRACERS, levels, TILE_CELLS)
     return (
         final_state.reshape(shape),
         sensitivity.reshape(shape),
         grad_w_in,
-        biases[0, 0],
+        grad_b_in,
         grad_w_mid,
-        biases[1, 0],
+        grad_b_mid,
         grad_w_out,
-        biases[0, 1, :FEATURES],
+        grad_b_out,
     )
 
 

time: 69.6 us -> 66.6 us (0.957)
  waiting for transfers between devices: 13.3 us -> 9.18 us
  starting transfers between devices: 22.2 us -> 26 us
  Pallas kernels: 24.8 us -> 23 us
  other arithmetic: 6.42 us -> 5.55 us
    ppermute x12, waiting for transfers between devices: 2.95 us -> 0.25 us  [exchanged(): lax.ppermute(edge, 'tile', way)]
    ppermute x12, starting transfers between devices: 9.27 us -> 11.3 us  [exchanged(): lax.ppermute(edge, 'tile', way)]
    pallas_call x10, Pallas kernels: 24.8 us -> 23 us  [called(): pl.pallas_call(kernel, out_shape=tuple(outs), in_specs=in_specs, out_spec...]
    ppermute x13 -> x14, starting transfers between devices: 13 us -> 14.7 us  [swapped(): lax.ppermute(x, axis, [(i, i ^ (odd_bit if i & 1 else even_bit)) for i in...]
    ppermute x13 -> x14, waiting for transfers between devices: 10.3 us -> 8.93 us  [swapped(): lax.ppermute(x, axis, [(i, i ^ (odd_bit if i & 1 else even_bit)) for i in...]
    concatenate x3 -> x1, other arithmetic: 2.15 us -> 1.27 us  [body(): jnp.concatenate([part(first, 0, 0), part(second, 1, 0)], axis=1)]
  transfers between devices with their start and end apart: 25 -> 26, of which waited for: 9 -> 8; matrix products, arithmetic and copies ran while one was open for 7% -> 7% of each run, Pallas kernels for 23% -> 20%
where the time goes in v7:
time: 66.6 us; the launch traced here: 66.4 us
  starting transfers between devices  26 us (39%)
  Pallas kernels  23 us (35%)
  waiting for transfers between devices  9.18 us (14%)
  other arithmetic  5.55 us (8%)
  local copies, waits for them, and re-layouts  1.58 us (2%)
  between operations  1.09 us (2%)
    pallas_call x10, Pallas kernels, called(): pl.pallas_call(kernel, out_shape=tuple(outs), in_specs=in_specs, out_spec...  23 us
    ppermute x14, starting transfers between devices, swapped(): lax.ppermute(x, axis, [(i, i ^ (odd_bit if i & 1 else even_bit)) for i in...  14.7 us
    ppermute x12, starting transfers between devices, exchanged(): lax.ppermute(edge, 'tile', way)  11.3 us
    ppermute x14, waiting for transfers between devices, swapped(): lax.ppermute(x, axis, [(i, i ^ (odd_bit if i & 1 else even_bit)) for i in...  8.93 us
    convert_element_type x6, other arithmetic, with_exponents(): return out.astype(jnp.float16)  2.64 us
  transfers between devices with their start and end apart: 26, of which 8 were waited for; matrix products, arithmetic and copies ran while one was open for 7% of the time, Pallas kernels for 20%

profile of v7, /device:TPU:0, one launch (start us, length us, event | category | flops | bytes accessed | tf_op | source)
XLA Modules:
  0.0 66.4 jit_solution(13991982657189011785)
XLA Ops:
  0.6 3.1 %collective-permute-start = (f32[16,1024]{1,0:T(8,128)}, f32[16,1024]{1,0:T(8,128)S(1)}, u32[]{:S(2)}, u32[]{:S(2)}) collective-permute-start(f32[16,1024]{1,0:T(8,128)} %bitcast.48), channel_id=1, source_target_pairs={{0,1},{1,0},{2,3},{3,2},{4,5},{5,4},{6,7},{7,6},{8,9},{9,8},{10,11... | collective-permute-start | bytes 196616 | tf_op jit(solution)/shard_map/ppermute | solution.py:344
  3.7 2.6 %collective-permute-start.1 = (f32[16,1024]{1,0:T(8,128)}, f32[16,1024]{1,0:T(8,128)S(1)}, u32[]{:S(2)}, u32[]{:S(2)}) collective-permute-start(f32[16,1024]{1,0:T(8,128)} %bitcast.49), channel_id=1, source_target_pairs={{0,2},{1,3},{2,0},{3,1},{4,6},{5,7},{6,4},{7,5},{8,10},{9,11},{10,... | collective-permute-start | bytes 196616 | tf_op jit(solution)/shard_map/ppermute | solution.py:344
  6.3 1.7 %prepare.1 = (f32[8,1024]{1,0:T(8,128)S(1)}, f32[16,1024]{1,0:T(8,128)S(1)}, f32[1,640]{1,0:T(1,128)S(1)}, f32[1,640]{1,0:T(1,128)S(1)}, f32[64,128]{1,0:T(8,128...) custom-call(f32[1,1024]{1,0:T(1,128)} %bitcast.57, ...), custom_call_target="tpu_custom_call" | custom-call | tf_op jit(solution)/shard_map/prepare/pallas_call | solution.py:330
  8.0 1.0 %collective-permute-start.3 = (f32[16,1024]{1,0:T(8,128)}, f32[16,1024]{1,0:T(8,128)S(1)}, u32[]{:S(2)}, u32[]{:S(2)}) collective-permute-start(f32[16,1024]{1,0:T(8,128)} %bitcast.35), channel_id=1, source_target_pairs={{0,1},{1,0},{2,3},{3,2},{4,5},{5,4},{6,7},{7,6},{8,9},{9,8},{10,11... | collective-permute-start | bytes 196616 | tf_op jit(solution)/shard_map/ppermute | solution.py:344
  9.0 3.5 %collective-permute-start.4 = (f32[16,1024]{1,0:T(8,128)}, f32[16,1024]{1,0:T(8,128)S(1)}, u32[]{:S(2)}, u32[]{:S(2)}) collective-permute-start(f32[16,1024]{1,0:T(8,128)} %bitcast.36), channel_id=1, source_target_pairs={{0,2},{1,3},{2,0},{3,1},{4,6},{5,7},{6,4},{7,5},{8,10},{9,11},{10,... | collective-permute-start | bytes 196616 | tf_op jit(solution)/shard_map/ppermute | solution.py:344
  12.4 0.1 pad_add_fusion.info
  12.6 0.7 %collective-permute-done.2.refs_3_ = f32[16,1024]{1,0:T(8,128)S(1)} collective-permute-done((f32[16,1024]{1,0:T(8,128)}, f32[16,1024]{1,0:T(8,128)S(1)}, u32[]{:S(2)}, u32[]{:S(2)}) %collective-permute-start.2) | collective-permute-done | bytes 65568 | tf_op jit(solution)/shard_map/ppermute | solution.py:344
  13.3 1.0 %gather.1 = (f32[64,1024]{1,0:T(8,128)S(1)}, f32[72,128]{1,0:T(8,128)S(1)}, f32[72,128]{1,0:T(8,128)S(1)}, f32[72,128]{1,0:T(8,128)S(1)}) custom-call(s32[2]{0:T(128)S(1)} %pad_add_fusion.info, f32[8,1024]{1,0:T(8,128)S(1)} %get-tuple-element.121.weight_ref, f32[16,1024]{1,0:T(8,128)S(1)} %get-tuple-element.122.refs_0_, ...), custom_call_target="tpu_custom_call" | custom-call | tf_op jit(solution)/shard_map/gather/pallas_call | solution.py:330
  14.3 1.6 %collective-permute-start.6 = (f32[72,128]{1,0:T(8,128)S(1)}, f32[72,128]{1,0:T(8,128)S(1)}, u32[]{:S(2)}, u32[]{:S(2)}) collective-permute-start(f32[72,128]{1,0:T(8,128)S(1)} %get-tuple-element.136), channel_id=1, source_target_pairs={{0,16},{4,20},{8,24},{12,28},{16,0},{20,4},{24,8},{28,12},{1,17},{... | collective-permute-start | bytes 110600 | tf_op jit(solution)/shard_map/ppermute | solution.py:429
  15.9 1.5 %collective-permute-start.8 = (f32[72,128]{1,0:T(8,128)S(1)}, f32[72,128]{1,0:T(8,128)S(1)}, u32[]{:S(2)}, u32[]{:S(2)}) collective-permute-start(f32[72,128]{1,0:T(8,128)S(1)} %get-tuple-element.138), channel_id=1, source_target_pairs={{0,28},{4,8},{8,4},{12,16},{16,12},{20,24},{24,20},{28,0},{1,29},{... | collective-permute-start | bytes 110600 | tf_op jit(solution)/shard_map/ppermute | solution.py:429
  17.4 2.6 %closure.2 = (f32[64,1024]{1,0:T(8,128)S(1)}, bf16[1024,640]{1,0:T(8,128)(2,1)S(1)}, f32[1024,640]{1,0:T(8,128)S(1)}, bf16[1024,640]{1,0:T(8,128)(2,1)S(1)}, f32[1024,640]{1,0:T(8,128)S(1)}) custom-call(f32[64,1024]{1,0:T(8,128)S(1)} %get-tuple-element.126.state_ref, bf16[64,640]{1,0:T(8,128)(2,1)S(1)} %get-tuple-element.127.w_in, ...), custom_call_target="tpu_custom_call" | custom-call | flops 1006632960 | bytes 5242880 | tf_op jit(solution)/shard_map/closure/pallas_call | solution.py:330
  20.1 0.2 collective-permute-done.8.e2
  20.3 1.6 %step.1 = (f32[64,1024]{1,0:T(8,128)S(1)}, f32[8,1024]{1,0:T(8,128)S(1)}, f32[64,128]{1,0:T(8,128)S(1)}, f32[64,128]{1,0:T(8,128)S(1)}, f32[64,128]{1,0:T(8,128)S(1)}) custom-call(s32[2]{0:T(128)S(1)} %pad_add_fusion.info, f32[64,1024]{1,0:T(8,128)S(1)} %get-tuple-element.126.state_ref, f32[8,1024]{1,0:T(8,128)S(1)} %get-tuple-element.121.weight_ref, ...), custom_call_target="tpu_custom_call" | custom-call | tf_op jit(solution)/shard_map/step/pallas_call | solution.py:330
  22.0 1.5 %collective-permute-start.11 = (f32[64,128]{1,0:T(8,128)S(1)}, f32[64,128]{1,0:T(8,128)S(1)}, u32[]{:S(2)}, u32[]{:S(2)}) collective-permute-start(f32[64,128]{1,0:T(8,128)S(1)} %get-tuple-element.144), channel_id=1, source_target_pairs={{0,28},{4,8},{8,4},{12,16},{16,12},{20,24},{24,20},{28,0},{1,29},{... | collective-permute-start | bytes 98312 | tf_op jit(solution)/shard_map/ppermute | solution.py:429
  23.5 1.5 %collective-permute-start.9 = (f32[64,128]{1,0:T(8,128)S(1)}, f32[64,128]{1,0:T(8,128)S(1)}, u32[]{:S(2)}, u32[]{:S(2)}) collective-permute-start(f32[64,128]{1,0:T(8,128)S(1)} %get-tuple-element.142), channel_id=1, source_target_pairs={{0,16},{4,20},{8,24},{12,28},{16,0},{20,4},{24,8},{28,12},{1,17},{... | collective-permute-start | bytes 98312 | tf_op jit(solution)/shard_map/ppermute | solution.py:429
  25.0 2.6 %closure.3 = (f32[64,1024]{1,0:T(8,128)S(1)}, bf16[1024,640]{1,0:T(8,128)(2,1)S(1)}, f32[1024,640]{1,0:T(8,128)S(1)}, bf16[1024,640]{1,0:T(8,128)(2,1)S(1)}, f32[1024,640]{1,0:T(8,128)S(1)}) custom-call(f32[64,1024]{1,0:T(8,128)S(1)} %get-tuple-element.139.state_ref, bf16[64,640]{1,0:T(8,128)(2,1)S(1)} %get-tuple-element.127.w_in, ...), custom_call_target="tpu_custom_call" | custom-call | flops 1006632960 | bytes 5242880 | tf_op jit(solution)/shard_map/closure/pallas_call | solution.py:330
  27.6 2.1 %last_step.1 = (f32[16,1024]{1,0:T(8,128)}, f32[64,1024]{1,0:T(8,128)S(1)}, bf16[64,1024]{1,0:T(8,128)(2,1)S(1)}, f32[64,128]{1,0:T(8,128)S(1)}, f32[64,128]{1,0:T(8,128)S(1)}, /*index=5*/f32[64,128]{1,0:T(8,128)S(1)}) custom-call(s32[2]{0:T(128)S(1)} %pad_add_fusion.info, f32[64,1024]{1,0:T(8,128)S(1)} %get-tuple-element.139.state_ref, ...), custom_call_target="tpu_custom_call" | custom-call | tf_op jit(solution)/shard_map/last_step/pallas_call | solution.py:330
  29.8 1.3 %collective-permute-start.12 = (f32[64,128]{1,0:T(8,128)S(1)}, f32[64,128]{1,0:T(8,128)S(1)}, u32[]{:S(2)}, u32[]{:S(2)}) collective-permute-start(f32[64,128]{1,0:T(8,128)S(1)} %get-tuple-element.157), channel_id=1, source_target_pairs={{0,16},{4,20},{8,24},{12,28},{16,0},{20,4},{24,8},{28,12},{1,17},{... | collective-permute-start | bytes 98312 | tf_op jit(solution)/shard_map/ppermute | solution.py:429
  31.1 1.2 %collective-permute-start.14 = (f32[64,128]{1,0:T(8,128)S(1)}, f32[64,128]{1,0:T(8,128)S(1)}, u32[]{:S(2)}, u32[]{:S(2)}) collective-permute-start(f32[64,128]{1,0:T(8,128)S(1)} %get-tuple-element.159), channel_id=1, source_target_pairs={{0,28},{4,8},{8,4},{12,16},{16,12},{20,24},{24,20},{28,0},{1,29},{... | collective-permute-start | bytes 98312 | tf_op jit(solution)/shard_map/ppermute | solution.py:429
  32.3 3.9 %first_backward.1 = (f32[64,1024]{1,0:T(8,128)S(1)}, f32[640,640]{1,0:T(8,128)S(1)}, f32[64,640]{1,0:T(8,128)S(1)}, f32[64,640]{1,0:T(8,128)S(1)}, f32[8,640]{1,...) custom-call(f32[64,1024]{1,0:T(8,128)S(1)} %get-tuple-element.139.state_ref, ...), custom_call_target="tpu_custom_call" | custom-call | flops 2013265920 | bytes 10485760 | tf_op jit(solution)/shard_map/first_backward/pallas_call | solution.py:330
  36.2 1.4 %adjoint.1 = (f32[16,1024]{1,0:T(8,128)S(1)}, bf16[64,1024]{1,0:T(8,128)(2,1)S(1)}, f32[16,128]{1,0:T(8,128)S(1)}, f32[16,128]{1,0:T(8,128)S(1)}, f32[16,128]{1,0:T(8,128)S(1)}) custom-call(s32[2]{0:T(128)S(1)} %pad_add_fusion.info, f32[64,1024]{1,0:T(8,128)S(1)} %get-tuple-element.150.adjoint_ref, f32[8,1024]{1,0:T(8,128)S(1)} %get-tuple-element.121.weight_ref, ...), custom_call_target="tpu_custom_call" | custom-call | tf_op jit(solution)/shard_map/adjoint/pallas_call | solution.py:330
  37.7 4.8 %last_backward.1 = (f32[64,1024]{1,0:T(8,128)S(1)}, f32[200,640]{1,0:T(8,128)S(1)}, f32[200,640]{1,0:T(8,128)S(1)}, f32[200,640]{1,0:T(8,128)S(1)}, f32[200,640]{1,0:T(8,128)S(1)}) custom-call(s32[2]{0:T(128)S(1)} %pad_add_fusion.info, f32[64,1024]{1,0:T(8,128)S(1)} %get-tuple-element.126.state_ref, bf16[64,1024]{1,0:T(8,128)(2,1)S(1)} %get-tuple-element.160.upstream_ref, ...), custom_call_target="tpu_custom_call" | custom-call | flops 2013265920 | bytes 10485760 | tf_op jit(solution)/shard_map/last_backward/pallas_call | solution.py:330
  42.6 0.5 collective-permute-start.15
  43.1 1.4 %collective-permute-done.17 = f32[200,640]{1,0:T(8,128)S(1)} collective-permute-done((f32[200,640]{1,0:T(8,128)S(1)}, f32[200,640]{1,0:T(8,128)S(1)}, u32[]{:S(2)}, u32[]{:S(2)}) %collective-permute-start.17) | collective-permute-done | bytes 512032 | tf_op jit(solution)/shard_map/ppermute | solution.py:344
  44.5 0.7 %collective-permute-done.15 = f32[200,640]{1,0:T(8,128)S(1)} collective-permute-done((f32[200,640]{1,0:T(8,128)S(1)}, f32[200,640]{1,0:T(8,128)S(1)}, u32[]{:S(2)}, u32[]{:S(2)}) %collective-permute-start.15) | collective-permute-done | bytes 512032 | tf_op jit(solution)/shard_map/ppermute | solution.py:344
  45.3 0.3 select_convert_fusion.5
  45.6 1.0 %collective-permute-start.16 = (f16[200,640]{1,0:T(8,128)(2,1)S(1)}, f16[200,640]{1,0:T(8,128)(2,1)S(1)}, u32[]{:S(2)}, u32[]{:S(2)}) collective-permute-start(f16[200,640]{1,0:T(8,128)(2,1)S(1)} %select_convert_fusion.5), channel_id=1, source_target_pairs={{0,8},{4,20},{8,0},{12,28},{16,24},{20,4},{24,16},{28,12},{1,9},{5... | collective-permute-start | bytes 768008 | tf_op jit(solution)/shard_map/ppermute | solution.py:344
  46.6 0.2 select_convert_fusion.4
  46.9 1.2 %collective-permute-start.19 = (f16[200,640]{1,0:T(8,128)(2,1)S(1)}, f16[200,640]{1,0:T(8,128)(2,1)S(1)}, u32[]{:S(2)}, u32[]{:S(2)}) collective-permute-start(f16[200,640]{1,0:T(8,128)(2,1)S(1)} %select_convert_fusion.4), channel_id=1, source_target_pairs={{0,8},{4,20},{8,0},{12,28},{16,24},{20,4},{24,16},{28,12},{1,9},{5... | collective-permute-start | bytes 768008 | tf_op jit(solution)/shard_map/ppermute | solution.py:344
  48.0 0.8 %collective-permute-start.20 = (f32[16,128]{1,0:T(8,128)S(1)}, f32[16,128]{1,0:T(8,128)S(1)}, u32[]{:S(2)}, u32[]{:S(2)}) collective-permute-start(f32[16,128]{1,0:T(8,128)S(1)} %get-tuple-element.183), channel_id=1, source_target_pairs={{0,16},{4,20},{8,24},{12,28},{16,0},{20,4},{24,8},{28,12},{1,17},{... | collective-permute-start | bytes 24584 | tf_op jit(solution)/shard_map/ppermute | solution.py:429
  48.8 1.7 %collective-permute-start.22 = (f32[16,128]{1,0:T(8,128)S(1)}, f32[16,128]{1,0:T(8,128)S(1)}, u32[]{:S(2)}, u32[]{:S(2)}) collective-permute-start(f32[16,128]{1,0:T(8,128)S(1)} %get-tuple-element.185), channel_id=1, source_target_pairs={{0,28},{4,8},{8,4},{12,16},{16,12},{20,24},{24,20},{28,0},{1,29},{... | collective-permute-start | bytes 24584 | tf_op jit(solution)/shard_map/ppermute | solution.py:429
  50.5 1.5 %collective-permute-done.16 = f16[200,640]{1,0:T(8,128)(2,1)S(1)} collective-permute-done((f16[200,640]{1,0:T(8,128)(2,1)S(1)}, f16[200,640]{1,0:T(8,128)(2,1)S(1)}, u32[]{:S(2)}, u32[]{:S(2)}) %collective-permute-start.16) | collective-permute-done | bytes 256032 | tf_op jit(solution)/shard_map/ppermute | solution.py:344
  52.2 0.8 %select_convert_fusion.3 = f16[200,640]{1,0:T(8,128)(2,1)S(1)} fusion(f16[200,640]{1,0:T(8,128)(2,1)S(1)} %collective-permute-done.16, f16[200,640]{1,0:T(8,128)(2,1)S(1)} %select_convert_fusion.5, f32[640]{0:T(1024)S(1)} %get-tuple-element.233, f32[640]{0:T(1024)S(1)} %get-tuple-element.234, f32[640]{0:T(1024)S(1)} %get-tuple-element.235, ...), kind=kLoop, calls=%fused_computation.8 | loop fusion | flops 2048000 | bytes 800120 | tf_op jit(solution)/shard_map/convert_element_type | solution.py:368
  52.9 0.8 %collective-permute-start.18 = (f16[200,640]{1,0:T(8,128)(2,1)S(1)}, f16[200,640]{1,0:T(8,128)(2,1)S(1)}, u32[]{:S(2)}, u32[]{:S(2)}) collective-permute-start(f16[200,640]{1,0:T(8,128)(2,1)S(1)} %select_convert_fusion.3), channel_id=1, source_target_pairs={{0,16},{4,12},{8,24},{12,4},{16,0},{20,28},{24,8},{28,20},{1,17},{... | collective-permute-start | bytes 768008 | tf_op jit(solution)/shard_map/ppermute | solution.py:344
  53.8 1.0 %collective-permute-done.19 = f16[200,640]{1,0:T(8,128)(2,1)S(1)} collective-permute-done((f16[200,640]{1,0:T(8,128)(2,1)S(1)}, f16[200,640]{1,0:T(8,128)(2,1)S(1)}, u32[]{:S(2)}, u32[]{:S(2)}) %collective-permute-start.19) | collective-permute-done | bytes 256032 | tf_op jit(solution)/shard_map/ppermute | solution.py:344
  54.9 0.3 select_convert_fusion.2
  55.2 0.8 %collective-permute-start.24 = (f16[200,640]{1,0:T(8,128)(2,1)S(1)}, f16[200,640]{1,0:T(8,128)(2,1)S(1)}, u32[]{:S(2)}, u32[]{:S(2)}) collective-permute-start(f16[200,640]{1,0:T(8,128)(2,1)S(1)} %select_convert_fusion.2), channel_id=1, source_target_pairs={{0,16},{4,12},{8,24},{12,4},{16,0},{20,28},{24,8},{28,20},{1,17},{... | collective-permute-start | bytes 768008 | tf_op jit(solution)/shard_map/ppermute | solution.py:344
  56.1 1.4 %end.1 = f32[16,1024]{1,0:T(8,128)} custom-call(s32[2]{0:T(128)S(1)} %pad_add_fusion.info, f32[16,1024]{1,0:T(8,128)S(1)} %get-tuple-element.189.adjoint_ref, f32[8,1024]{1,0:T(8,128)S(1)} %get-tuple-element.121.weight_ref, f32[8,1024]{1,0:T(8,128)S(1)} %get-tuple-element.140.sums_ref, f32[64,1024]{1,0:T(8,128)S(1)} %get-tuple-element.190.back_ref, ...), custom_call_target="tpu_custom_call" | custom-call | tf_op jit(solution)/shard_map/end/pallas_call | solution.py:330
  57.4 1.9 %collective-permute-done.18 = f16[200,640]{1,0:T(8,128)(2,1)S(1)} collective-permute-done((f16[200,640]{1,0:T(8,128)(2,1)S(1)}, f16[200,640]{1,0:T(8,128)(2,1)S(1)}, u32[]{:S(2)}, u32[]{:S(2)}) %collective-permute-start.18) | collective-permute-done | bytes 256032 | tf_op jit(solution)/shard_map/ppermute | solution.py:344
  59.5 0.8 %select_convert_fusion.1 = f16[200,640]{1,0:T(8,128)(2,1)S(1)} fusion(f16[200,640]{1,0:T(8,128)(2,1)S(1)} %collective-permute-done.18, f16[200,640]{1,0:T(8,128)(2,1)S(1)} %select_convert_fusion.3, f32[640]{0:T(1024)S(1)} %get-tuple-element.217, f32[640]{0:T(1024)S(1)} %get-tuple-element.218, f32[640]{0:T(1024)S(1)} %get-tuple-element.219, ...), kind=kLoop, calls=%fused_computation.6 | loop fusion | flops 2048000 | bytes 800120 | tf_op jit(solution)/shard_map/convert_element_type | solution.py:368
  60.4 1.7 %collective-permute-done.24 = f16[200,640]{1,0:T(8,128)(2,1)S(1)} collective-permute-done((f16[200,640]{1,0:T(8,128)(2,1)S(1)}, f16[200,640]{1,0:T(8,128)(2,1)S(1)}, u32[]{:S(2)}, u32[]{:S(2)}) %collective-permute-start.24) | collective-permute-done | bytes 256032 | tf_op jit(solution)/shard_map/ppermute | solution.py:344
  62.2 0.3 select_convert_fusion
  62.5 0.2 maximum_select_fusion
  62.8 0.5 slice_bitcast_fusion
  63.3 0.6 slice_reduce_fusion
  64.0 0.2 maximum_select_fusion.1
  64.4 1.3 %pad_maximum_fusion = f32[2,320,640]{2,1,0:T(8,128)} fusion(f32[2,192,640]{2,1,0:T(8,128)S(1)} %convert_multiply_fusion, f32[2,128,640]{2,1,0:T(8,128)S(1)} %convert_multiply_fusion.1), kind=kLoop, calls=%fused_computation | loop fusion | flops 409600 | bytes 3276800 | tf_op jit(solution)/shard_map/concatenate | solution.py:581
  65.7 0.7 %convert_multiply_fusion.2 = (f32[2,32,640]{2,1,0:T(8,128)}, f32[2,32,640]{2,1,0:T(8,128)}) fusion(f16[2,200,640]{2,1,0:T(8,128)(2,1)S(1)} %maximum_select_fusion, f32[2,640]{1,0:T(2,128)S(1)} %bitcast.52, f32[2,640]{1,0:T(2,128)S(1)} %bitcast.53), kind=kLoop, calls=%fused_computation.11 | loop fusion | flops 163840 | bytes 501760 | tf_op jit(solution)/shard_map/mul | solution.py:566
  (63 shorter events, 1.3 us)
Async XLA Ops:
  0.6 11.9 %collective-permute-start = (f32[16,1024]{1,0:T(8,128)}, f32[16,1024]{1,0:T(8,128)S(1)}, u32[]{:S(2)}, u32[]{:S(2)}) collective-permute-start(f32[16,1024]{1,0:T(8,128)} %bitcast.48), channel_id=1, source_target_pairs={{0,1},{1,0},{2,3},{3,2},{4,5},{5,4},{6,7},{7,6},{8,9},{9,8},{10,11... | collective-permute-start | bytes 196616 | tf_op jit(solution)/shard_map/ppermute | solution.py:344
  3.7 8.8 %collective-permute-start.1 = (f32[16,1024]{1,0:T(8,128)}, f32[16,1024]{1,0:T(8,128)S(1)}, u32[]{:S(2)}, u32[]{:S(2)}) collective-permute-start(f32[16,1024]{1,0:T(8,128)} %bitcast.49), channel_id=1, source_target_pairs={{0,2},{1,3},{2,0},{3,1},{4,6},{5,7},{6,4},{7,5},{8,10},{9,11},{10,... | collective-permute-start | bytes 196616 | tf_op jit(solution)/shard_map/ppermute | solution.py:344
  6.3 7.0 %collective-permute-start.2 = (f32[16,1024]{1,0:T(8,128)}, f32[16,1024]{1,0:T(8,128)S(1)}, u32[]{:S(2)}, u32[]{:S(2)}) collective-permute-start(f32[16,1024]{1,0:T(8,128)} %bitcast.50), channel_id=1, source_target_pairs={{0,3},{1,2},{2,1},{3,0},{4,7},{5,6},{6,5},{7,4},{8,11},{9,10},{10,... | collective-permute-start | bytes 196616 | tf_op jit(solution)/shard_map/ppermute | solution.py:344
  8.0 7.9 %collective-permute-start.3 = (f32[16,1024]{1,0:T(8,128)}, f32[16,1024]{1,0:T(8,128)S(1)}, u32[]{:S(2)}, u32[]{:S(2)}) collective-permute-start(f32[16,1024]{1,0:T(8,128)} %bitcast.35), channel_id=1, source_target_pairs={{0,1},{1,0},{2,3},{3,2},{4,5},{5,4},{6,7},{7,6},{8,9},{9,8},{10,11... | collective-permute-start | bytes 196616 | tf_op jit(solution)/shard_map/ppermute | solution.py:344
  9.0 11.1 %collective-permute-start.4 = (f32[16,1024]{1,0:T(8,128)}, f32[16,1024]{1,0:T(8,128)S(1)}, u32[]{:S(2)}, u32[]{:S(2)}) collective-permute-start(f32[16,1024]{1,0:T(8,128)} %bitcast.36), channel_id=1, source_target_pairs={{0,2},{1,3},{2,0},{3,1},{4,6},{5,7},{6,4},{7,5},{8,10},{9,11},{10,... | collective-permute-start | bytes 196616 | tf_op jit(solution)/shard_map/ppermute | solution.py:344
  12.5 7.5 %collective-permute-start.5 = (f32[16,1024]{1,0:T(8,128)}, f32[16,1024]{1,0:T(8,128)S(1)}, u32[]{:S(2)}, u32[]{:S(2)}) collective-permute-start(f32[16,1024]{1,0:T(8,128)} %bitcast.37), channel_id=1, source_target_pairs={{0,3},{1,2},{2,1},{3,0},{4,7},{5,6},{6,5},{7,4},{8,11},{9,10},{10,... | collective-permute-start | bytes 196616 | tf_op jit(solution)/shard_map/ppermute | solution.py:344
  14.3 5.8 %collective-permute-start.6 = (f32[72,128]{1,0:T(8,128)S(1)}, f32[72,128]{1,0:T(8,128)S(1)}, u32[]{:S(2)}, u32[]{:S(2)}) collective-permute-start(f32[72,128]{1,0:T(8,128)S(1)} %get-tuple-element.136), channel_id=1, source_target_pairs={{0,16},{4,20},{8,24},{12,28},{16,0},{20,4},{24,8},{28,12},{1,17},{... | collective-permute-start | bytes 110600 | tf_op jit(solution)/shard_map/ppermute | solution.py:429
  15.9 4.2 %collective-permute-start.7 = (f32[72,128]{1,0:T(8,128)S(1)}, f32[72,128]{1,0:T(8,128)S(1)}, u32[]{:S(2)}, u32[]{:S(2)}) collective-permute-start(f32[72,128]{1,0:T(8,128)S(1)} %get-tuple-element.137), channel_id=1, source_target_pairs={{0,4},{4,0},{8,12},{12,8},{16,20},{20,16},{24,28},{28,24},{1,5},{5... | collective-permute-start | bytes 110600 | tf_op jit(solution)/shard_map/ppermute | solution.py:429
  15.9 4.4 %collective-permute-start.8 = (f32[72,128]{1,0:T(8,128)S(1)}, f32[72,128]{1,0:T(8,128)S(1)}, u32[]{:S(2)}, u32[]{:S(2)}) collective-permute-start(f32[72,128]{1,0:T(8,128)S(1)} %get-tuple-element.138), channel_id=1, source_target_pairs={{0,28},{4,8},{8,4},{12,16},{16,12},{20,24},{24,20},{28,0},{1,29},{... | collective-permute-start | bytes 110600 | tf_op jit(solution)/shard_map/ppermute | solution.py:429
  21.9 5.7 %collective-permute-start.10 = (f32[64,128]{1,0:T(8,128)S(1)}, f32[64,128]{1,0:T(8,128)S(1)}, u32[]{:S(2)}, u32[]{:S(2)}) collective-permute-start(f32[64,128]{1,0:T(8,128)S(1)} %get-tuple-element.143), channel_id=1, source_target_pairs={{0,4},{4,0},{8,12},{12,8},{16,20},{20,16},{24,28},{28,24},{1,5},{5... | collective-permute-start | bytes 98312 | tf_op jit(solution)/shard_map/ppermute | solution.py:429
  22.0 5.6 %collective-permute-start.11 = (f32[64,128]{1,0:T(8,128)S(1)}, f32[64,128]{1,0:T(8,128)S(1)}, u32[]{:S(2)}, u32[]{:S(2)}) collective-permute-start(f32[64,128]{1,0:T(8,128)S(1)} %get-tuple-element.144), channel_id=1, source_target_pairs={{0,28},{4,8},{8,4},{12,16},{16,12},{20,24},{24,20},{28,0},{1,29},{... | collective-permute-start | bytes 98312 | tf_op jit(solution)/shard_map/ppermute | solution.py:429
  23.5 4.1 %collective-permute-start.9 = (f32[64,128]{1,0:T(8,128)S(1)}, f32[64,128]{1,0:T(8,128)S(1)}, u32[]{:S(2)}, u32[]{:S(2)}) collective-permute-start(f32[64,128]{1,0:T(8,128)S(1)} %get-tuple-element.142), channel_id=1, source_target_pairs={{0,16},{4,20},{8,24},{12,28},{16,0},{20,4},{24,8},{28,12},{1,17},{... | collective-permute-start | bytes 98312 | tf_op jit(solution)/shard_map/ppermute | solution.py:429
  25.0 2.6 %copy-start = (f32[2,8,1024]{2,1,0:T(8,128)S(1)}, f32[2,8,1024]{2,1,0:T(8,128)}, u32[]{:S(2)}) copy-start(f32[2,8,1024]{2,1,0:T(8,128)} %param.11) | copy-start | bytes 196612
  29.8 6.4 %collective-permute-start.12 = (f32[64,128]{1,0:T(8,128)S(1)}, f32[64,128]{1,0:T(8,128)S(1)}, u32[]{:S(2)}, u32[]{:S(2)}) collective-permute-start(f32[64,128]{1,0:T(8,128)S(1)} %get-tuple-element.157), channel_id=1, source_target_pairs={{0,16},{4,20},{8,24},{12,28},{16,0},{20,4},{24,8},{28,12},{1,17},{... | collective-permute-start | bytes 98312 | tf_op jit(solution)/shard_map/ppermute | solution.py:429
  31.1 5.1 %collective-permute-start.13 = (f32[64,128]{1,0:T(8,128)S(1)}, f32[64,128]{1,0:T(8,128)S(1)}, u32[]{:S(2)}, u32[]{:S(2)}) collective-permute-start(f32[64,128]{1,0:T(8,128)S(1)} %get-tuple-element.158), channel_id=1, source_target_pairs={{0,4},{4,0},{8,12},{12,8},{16,20},{20,16},{24,28},{28,24},{1,5},{5... | collective-permute-start | bytes 98312 | tf_op jit(solution)/shard_map/ppermute | solution.py:429
  31.1 5.2 %collective-permute-start.14 = (f32[64,128]{1,0:T(8,128)S(1)}, f32[64,128]{1,0:T(8,128)S(1)}, u32[]{:S(2)}, u32[]{:S(2)}) collective-permute-start(f32[64,128]{1,0:T(8,128)S(1)} %get-tuple-element.159), channel_id=1, source_target_pairs={{0,28},{4,8},{8,4},{12,16},{16,12},{20,24},{24,20},{28,0},{1,29},{... | collective-permute-start | bytes 98312 | tf_op jit(solution)/shard_map/ppermute | solution.py:429
  42.5 2.0 %collective-permute-start.17 = (f32[200,640]{1,0:T(8,128)S(1)}, f32[200,640]{1,0:T(8,128)S(1)}, u32[]{:S(2)}, u32[]{:S(2)}) collective-permute-start(f32[200,640]{1,0:T(8,128)S(1)} %get-tuple-element.174), channel_id=1, source_target_pairs={{0,4},{4,0},{8,12},{12,8},{16,20},{20,16},{24,28},{28,24},{1,5},{5... | collective-permute-start | bytes 1536008 | tf_op jit(solution)/shard_map/ppermute | solution.py:344
  42.6 2.6 %collective-permute-start.15 = (f32[200,640]{1,0:T(8,128)S(1)}, f32[200,640]{1,0:T(8,128)S(1)}, u32[]{:S(2)}, u32[]{:S(2)}) collective-permute-start(f32[200,640]{1,0:T(8,128)S(1)} %get-tuple-element.172), channel_id=1, source_target_pairs={{0,4},{4,0},{8,12},{12,8},{16,20},{20,16},{24,28},{28,24},{1,5},{5... | collective-permute-start | bytes 1536008 | tf_op jit(solution)/shard_map/ppermute | solution.py:344
  45.6 6.4 %collective-permute-start.16 = (f16[200,640]{1,0:T(8,128)(2,1)S(1)}, f16[200,640]{1,0:T(8,128)(2,1)S(1)}, u32[]{:S(2)}, u32[]{:S(2)}) collective-permute-start(f16[200,640]{1,0:T(8,128)(2,1)S(1)} %select_convert_fusion.5), channel_id=1, source_target_pairs={{0,8},{4,20},{8,0},{12,28},{16,24},{20,4},{24,16},{28,12},{1,9},{5... | collective-permute-start | bytes 768008 | tf_op jit(solution)/shard_map/ppermute | solution.py:344
  46.9 8.0 %collective-permute-start.19 = (f16[200,640]{1,0:T(8,128)(2,1)S(1)}, f16[200,640]{1,0:T(8,128)(2,1)S(1)}, u32[]{:S(2)}, u32[]{:S(2)}) collective-permute-start(f16[200,640]{1,0:T(8,128)(2,1)S(1)} %select_convert_fusion.4), channel_id=1, source_target_pairs={{0,8},{4,20},{8,0},{12,28},{16,24},{20,4},{24,16},{28,12},{1,9},{5... | collective-permute-start | bytes 768008 | tf_op jit(solution)/shard_map/ppermute | solution.py:344
  48.0 5.8 %collective-permute-start.20 = (f32[16,128]{1,0:T(8,128)S(1)}, f32[16,128]{1,0:T(8,128)S(1)}, u32[]{:S(2)}, u32[]{:S(2)}) collective-permute-start(f32[16,128]{1,0:T(8,128)S(1)} %get-tuple-element.183), channel_id=1, source_target_pairs={{0,16},{4,20},{8,24},{12,28},{16,0},{20,4},{24,8},{28,12},{1,17},{... | collective-permute-start | bytes 24584 | tf_op jit(solution)/shard_map/ppermute | solution.py:429
  48.8 5.0 %collective-permute-start.21 = (f32[16,128]{1,0:T(8,128)S(1)}, f32[16,128]{1,0:T(8,128)S(1)}, u32[]{:S(2)}, u32[]{:S(2)}) collective-permute-start(f32[16,128]{1,0:T(8,128)S(1)} %get-tuple-element.184), channel_id=1, source_target_pairs={{0,4},{4,0},{8,12},{12,8},{16,20},{20,16},{24,28},{28,24},{1,5},{5... | collective-permute-start | bytes 24584 | tf_op jit(solution)/shard_map/ppermute | solution.py:429
  48.8 5.0 %collective-permute-start.22 = (f32[16,128]{1,0:T(8,128)S(1)}, f32[16,128]{1,0:T(8,128)S(1)}, u32[]{:S(2)}, u32[]{:S(2)}) collective-permute-start(f32[16,128]{1,0:T(8,128)S(1)} %get-tuple-element.185), channel_id=1, source_target_pairs={{0,28},{4,8},{8,4},{12,16},{16,12},{20,24},{24,20},{28,0},{1,29},{... | collective-permute-start | bytes 24584 | tf_op jit(solution)/shard_map/ppermute | solution.py:429
  52.9 6.4 %collective-permute-start.18 = (f16[200,640]{1,0:T(8,128)(2,1)S(1)}, f16[200,640]{1,0:T(8,128)(2,1)S(1)}, u32[]{:S(2)}, u32[]{:S(2)}) collective-permute-start(f16[200,640]{1,0:T(8,128)(2,1)S(1)} %select_convert_fusion.3), channel_id=1, source_target_pairs={{0,16},{4,12},{8,24},{12,4},{16,0},{20,28},{24,8},{28,20},{1,17},{... | collective-permute-start | bytes 768008 | tf_op jit(solution)/shard_map/ppermute | solution.py:344
  55.2 6.8 %collective-permute-start.24 = (f16[200,640]{1,0:T(8,128)(2,1)S(1)}, f16[200,640]{1,0:T(8,128)(2,1)S(1)}, u32[]{:S(2)}, u32[]{:S(2)}) collective-permute-start(f16[200,640]{1,0:T(8,128)(2,1)S(1)} %select_convert_fusion.2), channel_id=1, source_target_pairs={{0,16},{4,12},{8,24},{12,4},{16,0},{20,28},{24,8},{28,20},{1,17},{... | collective-permute-start | bytes 768008 | tf_op jit(solution)/shard_map/ppermute | solution.py:344
  60.3 2.3 %collective-permute-start.23 = (f16[200,640]{1,0:T(8,128)(2,1)S(1)}, f16[200,640]{1,0:T(8,128)(2,1)S(1)}, u32[]{:S(2)}, u32[]{:S(2)}) collective-permute-start(f16[200,640]{1,0:T(8,128)(2,1)S(1)} %select_convert_fusion.1), channel_id=1, source_target_pairs={{0,4},{4,0},{8,12},{12,8},{16,20},{20,16},{24,28},{28,24},{1,5},{5... | collective-permute-start | bytes 768008 | tf_op jit(solution)/shard_map/ppermute | solution.py:344
  62.5 1.6 %collective-permute-start.25 = (f16[200,640]{1,0:T(8,128)(2,1)S(1)}, f16[200,640]{1,0:T(8,128)(2,1)S(1)}, u32[]{:S(2)}, u32[]{:S(2)}) collective-permute-start(f16[200,640]{1,0:T(8,128)(2,1)S(1)} %select_convert_fusion), channel_id=1, source_target_pairs={{0,4},{4,0},{8,12},{12,8},{16,20},{20,16},{24,28},{28,24},{1,5},{5... | collective-permute-start | bytes 768008 | tf_op jit(solution)/shard_map/ppermute | solution.py:344

commit v8 on v7

--- a/solution.py
+++ b/solution.py
@@ -30,9 +30,22 @@
     return lax.broadcasted_iota(jnp.int32, shape, 1)
 
 
+def is_even_tile(info, shape):
+    return (jnp.broadcast_to(info[1:2, : shape[1]], shape) & 1) == 0
+
+
+def by_depth(depths, info, choices):
+    shape = choices[0].shape
+    depth = jnp.broadcast_to(info[0:1, : shape[1]], shape)
+    out = choices[depths - 1]
+    for d in range(depths - 1):
+        out = jnp.where(depth == d, choices[d], out)
+    return out
+
+
 def edges_of(scaled, info):
-    even_tile = info[1] % 2 == 0
     rows, whole = scaled.shape
+    even_tile = is_even_tile(info, (rows, LANES))
     lane = lane_of((rows, LANES))
     across = jnp.where(lane < LANES // 2, scaled[:, :LANES], scaled[:, whole - LANES :])
     bit = 1
@@ -41,7 +54,7 @@
         down = pltpu.roll(across, LANES - bit, 1)
         across = jnp.where((lane & bit) != 0, up, down)
         bit *= 2
-    place = lane % TILE_SIDE
+    place = lane & (TILE_SIDE - 1)
 
     def squeezed(last):
         shift = LANES - (TILE_SIDE - 1) if last else 0
@@ -58,12 +71,12 @@
 
 
 def neighbour_sum(scaled, received, info):
-    even_tile = info[1] % 2 == 0
     across, inside, outside = received
+    even_tile = is_even_tile(info, inside.shape)
     whole = scaled.shape[1]
     count = whole // LANES
     lane = lane_of(scaled.shape)
-    place = lane % TILE_SIDE
+    place = lane & (TILE_SIDE - 1)
     west = jnp.where(even_tile, outside, inside)
     east = jnp.where(even_tile, inside, outside)
 
@@ -88,21 +101,21 @@
     return jnp.where(weight > 0.0, 1.0, 0.0)
 
 
-def in_order(depths, info, message_refs, held, out_ref):
-    for k in range(depths):
-        held[info[0] ^ k] = message_refs[k][...]
+def in_order(depths, info, message_refs, out_ref):
     levels = LEVELS // depths
-    for tracer in range(TRACERS):
-        for d in range(depths):
+    for d in range(depths):
+        values = by_depth(depths, info, [message_refs[own ^ d][...] for own in range(depths)])
+        for tracer in range(TRACERS):
             to = tracer * LEVELS + d * levels
-            out_ref[to : to + levels, :] = held[d, tracer * levels : (tracer + 1) * levels, :]
+            out_ref[to : to + levels, :] = values[tracer * levels : (tracer + 1) * levels, :]
 
 
 def own_levels(depths, info, from_ref, to_ref):
     levels = LEVELS // depths
     for tracer in range(TRACERS):
-        start = pl.multiple_of(tracer * LEVELS + info[0] * levels, levels)
-        to_ref[tracer * levels : (tracer + 1) * levels, :] = from_ref[pl.ds(start, levels), :]
+        starts = [tracer * LEVELS + d * levels for d in range(depths)]
+        values = by_depth(depths, info, [from_ref[at : at + levels, :] for at in starts])
+        to_ref[tracer * levels : (tracer + 1) * levels, :] = values
 
 
 def prepare_kernel(*refs):
@@ -143,7 +156,7 @@
     message_refs = refs[:depths]
     state_ref = refs[depths]
     edge_refs = refs[depths + 1 : depths + 4]
-    in_order(depths, info, message_refs, refs[depths + 4], state_ref)
+    in_order(depths, info, message_refs, state_ref)
     scaled = jnp.concatenate([state_ref[...] * weight_ref[0:1, :], weight_ref[...]], axis=0)
     for edge_out, edge in zip(edge_refs, edges_of(scaled, info)):
         edge_out[...] = edge
@@ -192,7 +205,7 @@
 
 def last_step_kernel(depths, info, state_ref, weight_ref, sums_ref, q_ref, e0, e1, e2, *refs):
     target_refs = refs[:depths]
-    final_ref, adjoint_ref, upstream_ref, o0, o1, o2, held, ordered = refs[depths:]
+    final_ref, adjoint_ref, upstream_ref, o0, o1, o2, ordered = refs[depths:]
     weight = weight_ref[0:1, :]
     mask = mask_of(weight)
     state = state_ref[...]
@@ -201,7 +214,7 @@
     state = state + diffuse_coef * change + step_size * mask * q_ref[...]
     adjoint_ref[...] = state
     own_levels(depths, info, adjoint_ref, final_ref)
-    in_order(depths, info, target_refs, held, ordered)
+    in_order(depths, info, target_refs, ordered)
     adjoint = mask * (state - ordered[...])
     adjoint_ref[...] = adjoint
     upstream_ref[...] = (step_size * mask * adjoint).astype(jnp.bfloat16)
@@ -285,7 +298,6 @@
     back_ref[...] = back
     mid, side_in, side_out, bias_in, bias_mid, bias_out = [part + ref[...] for part, ref in zip(parts, earlier_refs)]
     row = lax.broadcasted_iota(jnp.int32, bias_in.shape, 0)
-    is_first = info[1] % HALVES == 0
     (top, side, _), _ = block_parts(w_mid.shape[0])
     count = mid.shape[0] // HALVES
     tails = (
@@ -295,7 +307,7 @@
     for other in (False, True):
 
         def one(halves):
-            return jnp.where(is_first, halves[other], halves[not other])
+            return jnp.where(is_even_tile(info, halves[0].shape), halves[other], halves[not other])
 
         first = [
             one((mid[:top, :], mid[count : count + top, :])),
@@ -324,9 +336,8 @@
 
 
 def called(kernel, outs, info, args, scratch=(), name=None, fetches=False, passes=0):
-    smem = pl.BlockSpec(memory_space=pltpu.SMEM)
     vmem = pl.BlockSpec(memory_space=pltpu.VMEM)
-    in_specs = [smem] * len(info) + [pl.BlockSpec(memory_space=pltpu.HBM) if fetches else vmem] * len(args)
+    in_specs = [vmem] * len(info) + [pl.BlockSpec(memory_space=pltpu.HBM) if fetches else vmem] * len(args)
     return pl.pallas_call(
         kernel,
         out_shape=tuple(outs),
@@ -395,12 +406,13 @@
     tied = lax.optimization_barrier
     others = [swapped(block, "tile", 1, 1) for block in sent]
     first = coded_sum(kept[0], others[0], all_parts[0])
+    others[1], held = tied((others[1], first))
     second = coded_sum(kept[1], others[1], all_parts[1])
     later, edges = tied((second, edges))
     arrived = exchanged(edges)
     others = [swapped(block, "tile", 2, 4) for block in (first, second)]
     others[0], second = tied((others[0], later))
-    first = sum_of_coded(first, others[0], all_parts[0])
+    first = sum_of_coded(held, others[0], all_parts[0])
     others[1], held, arrived = tied((others[1], first, arrived))
     second = sum_of_coded(second, others[1], all_parts[1])
     others = [swapped(block, "tile", 4, 2) for block in (first, second)]
@@ -419,7 +431,8 @@
 def body(initial_state, observed, edge_weight, land, w_in, b_in, w_mid, b_mid, w_out, b_out):
     tiles = lax.axis_size("tile")
     depths = lax.axis_size("depth")
-    info = (jnp.stack([lax.axis_index("depth"), lax.axis_index("tile")]).astype(jnp.int32),)
+    row = lax.broadcasted_iota(jnp.int32, (8, TILE_CELLS), 0)
+    info = (jnp.where(row == 0, lax.axis_index("depth"), lax.axis_index("tile")).astype(jnp.int32),)
     width = w_mid.shape[0]
     levels = LEVELS // depths
     rows = TRACERS * levels
@@ -439,7 +452,6 @@
     edge = spec_of((FEATURES, LANES))
     first_edge = spec_of((FEATURES + 8, LANES))
     own_edge = spec_of((rows, LANES))
-    held = pltpu.VMEM((depths, rows, TILE_CELLS), jnp.float32)
     whole = pltpu.VMEM((FEATURES, TILE_CELLS), jnp.float32)
     cached = (
         spec_of((TILE_CELLS, width), jnp.bfloat16),
@@ -489,7 +501,6 @@
         (field, first_edge, first_edge, first_edge),
         info,
         (weight, own_state, *others),
-        scratch=[held],
         name="gather",
     )
     edges = exchanged(edges)
@@ -509,7 +520,7 @@
         (own_field, field, half_field, edge, edge, edge),
         info,
         (state_1, weight, weight_sums, q, *edges, *targets),
-        scratch=[held, whole],
+        scratch=[whole],
         name="last_step",
     )
     edges = exchanged(edges)

time: 66.6 us -> 63.1 us (0.947)
  Pallas kernels: 23 us -> 19.6 us
    pallas_call x10, Pallas kernels: 23 us -> 19.6 us  [called(): pl.pallas_call(kernel, out_shape=tuple(outs), in_specs=in_specs, out_spec...]
  transfers between devices with their start and end apart: 26 -> 26, of which waited for: 8 -> 7; matrix products, arithmetic and copies ran while one was open for 7% -> 8% of each run, Pallas kernels for 20% -> 19%
where the time goes in v8:
time: 63.1 us; the launch traced here: 62.9 us
  starting transfers between devices  26.1 us (41%)
  Pallas kernels  19.6 us (31%)
  waiting for transfers between devices  8.9 us (14%)
  other arithmetic  5.48 us (9%)
  local copies, waits for them, and re-layouts  1.66 us (3%)
  between operations  1.12 us (2%)
    pallas_call x10, Pallas kernels, called(): pl.pallas_call(kernel, out_shape=tuple(outs), in_specs=in_specs, out_spec...  19.6 us
    ppermute x14, starting transfers between devices, swapped(): lax.ppermute(x, axis, [(i, i ^ (odd_bit if i & 1 else even_bit)) for i in...  14.8 us
    ppermute x12, starting transfers between devices, exchanged(): lax.ppermute(edge, 'tile', way)  11.3 us
    ppermute x14, waiting for transfers between devices, swapped(): lax.ppermute(x, axis, [(i, i ^ (odd_bit if i & 1 else even_bit)) for i in...  8.64 us
    convert_element_type x6, other arithmetic, with_exponents(): return out.astype(jnp.float16)  2.63 us
    concatenate x1, other arithmetic, body(): jnp.concatenate([part(first, 0, 0), part(second, 1, 0)], axis=1)  1.27 us
  transfers between devices with their start and end apart: 26, of which 7 were waited for; matrix products, arithmetic and copies ran while one was open for 8% of the time, Pallas kernels for 19%

profile of v8, /device:TPU:0, one launch (start us, length us, event | category | flops | bytes accessed | tf_op | source)
XLA Modules:
  0.0 62.9 jit_solution(17788646221012694151)
XLA Ops:
  0.6 3.1 %collective-permute-start = (f32[16,1024]{1,0:T(8,128)}, f32[16,1024]{1,0:T(8,128)S(1)}, u32[]{:S(2)}, u32[]{:S(2)}) collective-permute-start(f32[16,1024]{1,0:T(8,128)} %bitcast.46), channel_id=1, source_target_pairs={{0,1},{1,0},{2,3},{3,2},{4,5},{5,4},{6,7},{7,6},{8,9},{9,8},{10,11... | collective-permute-start | bytes 196616 | tf_op jit(solution)/shard_map/ppermute | solution.py:355
  3.7 2.6 %collective-permute-start.1 = (f32[16,1024]{1,0:T(8,128)}, f32[16,1024]{1,0:T(8,128)S(1)}, u32[]{:S(2)}, u32[]{:S(2)}) collective-permute-start(f32[16,1024]{1,0:T(8,128)} %bitcast.47), channel_id=1, source_target_pairs={{0,2},{1,3},{2,0},{3,1},{4,6},{5,7},{6,4},{7,5},{8,10},{9,11},{10,... | collective-permute-start | bytes 196616 | tf_op jit(solution)/shard_map/ppermute | solution.py:355
  6.3 1.7 %prepare.1 = (f32[8,1024]{1,0:T(8,128)S(1)}, f32[16,1024]{1,0:T(8,128)S(1)}, f32[1,640]{1,0:T(1,128)S(1)}, f32[1,640]{1,0:T(1,128)S(1)}, f32[64,128]{1,0:T(8,128...) custom-call(f32[1,1024]{1,0:T(1,128)} %bitcast.55, ...), custom_call_target="tpu_custom_call" | custom-call | tf_op jit(solution)/shard_map/prepare/pallas_call | solution.py:341
  8.0 1.0 %collective-permute-start.3 = (f32[16,1024]{1,0:T(8,128)}, f32[16,1024]{1,0:T(8,128)S(1)}, u32[]{:S(2)}, u32[]{:S(2)}) collective-permute-start(f32[16,1024]{1,0:T(8,128)} %bitcast.33), channel_id=1, source_target_pairs={{0,1},{1,0},{2,3},{3,2},{4,5},{5,4},{6,7},{7,6},{8,9},{9,8},{10,11... | collective-permute-start | bytes 196616 | tf_op jit(solution)/shard_map/ppermute | solution.py:355
  9.0 3.5 %collective-permute-start.4 = (f32[16,1024]{1,0:T(8,128)}, f32[16,1024]{1,0:T(8,128)S(1)}, u32[]{:S(2)}, u32[]{:S(2)}) collective-permute-start(f32[16,1024]{1,0:T(8,128)} %bitcast.34), channel_id=1, source_target_pairs={{0,2},{1,3},{2,0},{3,1},{4,6},{5,7},{6,4},{7,5},{8,10},{9,11},{10,... | collective-permute-start | bytes 196616 | tf_op jit(solution)/shard_map/ppermute | solution.py:355
  12.5 0.8 %collective-permute-done.2.refs_3_ = f32[16,1024]{1,0:T(8,128)S(1)} collective-permute-done((f32[16,1024]{1,0:T(8,128)}, f32[16,1024]{1,0:T(8,128)S(1)}, u32[]{:S(2)}, u32[]{:S(2)}) %collective-permute-start.2) | collective-permute-done | bytes 65568 | tf_op jit(solution)/shard_map/ppermute | solution.py:355
  13.4 0.4 gather.1
  13.8 1.6 %collective-permute-start.6 = (f32[72,128]{1,0:T(8,128)S(1)}, f32[72,128]{1,0:T(8,128)S(1)}, u32[]{:S(2)}, u32[]{:S(2)}) collective-permute-start(f32[72,128]{1,0:T(8,128)S(1)} %get-tuple-element.138), channel_id=1, source_target_pairs={{0,16},{4,20},{8,24},{12,28},{16,0},{20,4},{24,8},{28,12},{1,17},{... | collective-permute-start | bytes 110600 | tf_op jit(solution)/shard_map/ppermute | solution.py:442
  15.4 1.5 %collective-permute-start.8 = (f32[72,128]{1,0:T(8,128)S(1)}, f32[72,128]{1,0:T(8,128)S(1)}, u32[]{:S(2)}, u32[]{:S(2)}) collective-permute-start(f32[72,128]{1,0:T(8,128)S(1)} %get-tuple-element.140), channel_id=1, source_target_pairs={{0,28},{4,8},{8,4},{12,16},{16,12},{20,24},{24,20},{28,0},{1,29},{... | collective-permute-start | bytes 110600 | tf_op jit(solution)/shard_map/ppermute | solution.py:442
  17.0 2.6 %closure.2 = (f32[64,1024]{1,0:T(8,128)S(1)}, bf16[1024,640]{1,0:T(8,128)(2,1)S(1)}, f32[1024,640]{1,0:T(8,128)S(1)}, bf16[1024,640]{1,0:T(8,128)(2,1)S(1)}, f32[1024,640]{1,0:T(8,128)S(1)}) custom-call(f32[64,1024]{1,0:T(8,128)S(1)} %get-tuple-element.128.state_ref, bf16[64,640]{1,0:T(8,128)(2,1)S(1)} %get-tuple-element.129.w_in, ...), custom_call_target="tpu_custom_call" | custom-call | flops 1006632960 | bytes 5242880 | tf_op jit(solution)/shard_map/closure/pallas_call | solution.py:341
  19.6 0.2 collective-permute-done.8.e2
  19.8 1.1 %step.1 = (f32[64,1024]{1,0:T(8,128)S(1)}, f32[8,1024]{1,0:T(8,128)S(1)}, f32[64,128]{1,0:T(8,128)S(1)}, f32[64,128]{1,0:T(8,128)S(1)}, f32[64,128]{1,0:T(8,128)S(1)}) custom-call(s32[8,1024]{1,0:T(8,128)S(1)} %iota.185.info, f32[64,1024]{1,0:T(8,128)S(1)} %get-tuple-element.128.state_ref, f32[8,1024]{1,0:T(8,128)S(1)} %get-tuple-element.123.weight_ref, ...), custom_call_target="tpu_custom_call" | custom-call | tf_op jit(solution)/shard_map/step/pallas_call | solution.py:341
  21.0 1.5 %collective-permute-start.11 = (f32[64,128]{1,0:T(8,128)S(1)}, f32[64,128]{1,0:T(8,128)S(1)}, u32[]{:S(2)}, u32[]{:S(2)}) collective-permute-start(f32[64,128]{1,0:T(8,128)S(1)} %get-tuple-element.146), channel_id=1, source_target_pairs={{0,28},{4,8},{8,4},{12,16},{16,12},{20,24},{24,20},{28,0},{1,29},{... | collective-permute-start | bytes 98312 | tf_op jit(solution)/shard_map/ppermute | solution.py:442
  22.5 1.5 %collective-permute-start.9 = (f32[64,128]{1,0:T(8,128)S(1)}, f32[64,128]{1,0:T(8,128)S(1)}, u32[]{:S(2)}, u32[]{:S(2)}) collective-permute-start(f32[64,128]{1,0:T(8,128)S(1)} %get-tuple-element.144), channel_id=1, source_target_pairs={{0,16},{4,20},{8,24},{12,28},{16,0},{20,4},{24,8},{28,12},{1,17},{... | collective-permute-start | bytes 98312 | tf_op jit(solution)/shard_map/ppermute | solution.py:442
  24.0 2.6 %closure.3 = (f32[64,1024]{1,0:T(8,128)S(1)}, bf16[1024,640]{1,0:T(8,128)(2,1)S(1)}, f32[1024,640]{1,0:T(8,128)S(1)}, bf16[1024,640]{1,0:T(8,128)(2,1)S(1)}, f32[1024,640]{1,0:T(8,128)S(1)}) custom-call(f32[64,1024]{1,0:T(8,128)S(1)} %get-tuple-element.141.state_ref, bf16[64,640]{1,0:T(8,128)(2,1)S(1)} %get-tuple-element.129.w_in, ...), custom_call_target="tpu_custom_call" | custom-call | flops 1006632960 | bytes 5242880 | tf_op jit(solution)/shard_map/closure/pallas_call | solution.py:341
  26.6 1.6 %last_step.1 = (f32[16,1024]{1,0:T(8,128)}, f32[64,1024]{1,0:T(8,128)S(1)}, bf16[64,1024]{1,0:T(8,128)(2,1)S(1)}, f32[64,128]{1,0:T(8,128)S(1)}, f32[64,128]{1,0:T(8,128)S(1)}, /*index=5*/f32[64,128]{1,0:T(8,128)S(1)}) custom-call(s32[8,1024]{1,0:T(8,128)S(1)} %iota.185.info, f32[64,1024]{1,0:T(8,128)S(1)} %get-tuple-element.141.state_ref, ...), custom_call_target="tpu_custom_call" | custom-call | tf_op jit(solution)/shard_map/last_step/pallas_call | solution.py:341
  28.2 1.3 %collective-permute-start.12 = (f32[64,128]{1,0:T(8,128)S(1)}, f32[64,128]{1,0:T(8,128)S(1)}, u32[]{:S(2)}, u32[]{:S(2)}) collective-permute-start(f32[64,128]{1,0:T(8,128)S(1)} %get-tuple-element.159), channel_id=1, source_target_pairs={{0,16},{4,20},{8,24},{12,28},{16,0},{20,4},{24,8},{28,12},{1,17},{... | collective-permute-start | bytes 98312 | tf_op jit(solution)/shard_map/ppermute | solution.py:442
  29.5 1.2 %collective-permute-start.14 = (f32[64,128]{1,0:T(8,128)S(1)}, f32[64,128]{1,0:T(8,128)S(1)}, u32[]{:S(2)}, u32[]{:S(2)}) collective-permute-start(f32[64,128]{1,0:T(8,128)S(1)} %get-tuple-element.161), channel_id=1, source_target_pairs={{0,28},{4,8},{8,4},{12,16},{16,12},{20,24},{24,20},{28,0},{1,29},{... | collective-permute-start | bytes 98312 | tf_op jit(solution)/shard_map/ppermute | solution.py:442
  30.7 3.9 %first_backward.1 = (f32[64,1024]{1,0:T(8,128)S(1)}, f32[640,640]{1,0:T(8,128)S(1)}, f32[64,640]{1,0:T(8,128)S(1)}, f32[64,640]{1,0:T(8,128)S(1)}, f32[8,640]{1,...) custom-call(f32[64,1024]{1,0:T(8,128)S(1)} %get-tuple-element.141.state_ref, ...), custom_call_target="tpu_custom_call" | custom-call | flops 2013265920 | bytes 10485760 | tf_op jit(solution)/shard_map/first_backward/pallas_call | solution.py:341
  34.7 0.8 %adjoint.1 = (f32[16,1024]{1,0:T(8,128)S(1)}, bf16[64,1024]{1,0:T(8,128)(2,1)S(1)}, f32[16,128]{1,0:T(8,128)S(1)}, f32[16,128]{1,0:T(8,128)S(1)}, f32[16,128]{1,0:T(8,128)S(1)}) custom-call(s32[8,1024]{1,0:T(8,128)S(1)} %iota.185.info, f32[64,1024]{1,0:T(8,128)S(1)} %get-tuple-element.152.adjoint_ref, f32[8,1024]{1,0:T(8,128)S(1)} %get-tuple-element.123.weight_ref, ...), custom_call_target="tpu_custom_call" | custom-call | tf_op jit(solution)/shard_map/adjoint/pallas_call | solution.py:341
  35.4 4.3 %last_backward.1 = (f32[64,1024]{1,0:T(8,128)S(1)}, f32[200,640]{1,0:T(8,128)S(1)}, f32[200,640]{1,0:T(8,128)S(1)}, f32[200,640]{1,0:T(8,128)S(1)}, f32[200,640]{1,0:T(8,128)S(1)}) custom-call(s32[8,1024]{1,0:T(8,128)S(1)} %iota.185.info, f32[64,1024]{1,0:T(8,128)S(1)} %get-tuple-element.128.state_ref, bf16[64,1024]{1,0:T(8,128)(2,1)S(1)} %get-tuple-element.162.upstream_ref, ...), custom_call_target="tpu_custom_call" | custom-call | flops 2013265920 | bytes 10485760 | tf_op jit(solution)/shard_map/last_backward/pallas_call | solution.py:341
  39.7 0.1 collective-permute-start.16
  39.9 0.5 collective-permute-start.15
  40.4 1.3 %collective-permute-done.16 = f32[200,640]{1,0:T(8,128)S(1)} collective-permute-done((f32[200,640]{1,0:T(8,128)S(1)}, f32[200,640]{1,0:T(8,128)S(1)}, u32[]{:S(2)}, u32[]{:S(2)}) %collective-permute-start.16) | collective-permute-done | bytes 512032 | tf_op jit(solution)/shard_map/ppermute | solution.py:355
  41.8 0.3 select_convert_fusion.5
  42.1 1.0 %collective-permute-start.17 = (f16[200,640]{1,0:T(8,128)(2,1)S(1)}, f16[200,640]{1,0:T(8,128)(2,1)S(1)}, u32[]{:S(2)}, u32[]{:S(2)}) collective-permute-start(f16[200,640]{1,0:T(8,128)(2,1)S(1)} %select_convert_fusion.5), channel_id=1, source_target_pairs={{0,8},{4,20},{8,0},{12,28},{16,24},{20,4},{24,16},{28,12},{1,9},{5... | collective-permute-start | bytes 768008 | tf_op jit(solution)/shard_map/ppermute | solution.py:355
  43.2 0.2 select_convert_fusion.4
  43.4 1.2 %collective-permute-start.19 = (f16[200,640]{1,0:T(8,128)(2,1)S(1)}, f16[200,640]{1,0:T(8,128)(2,1)S(1)}, u32[]{:S(2)}, u32[]{:S(2)}) collective-permute-start(f16[200,640]{1,0:T(8,128)(2,1)S(1)} %select_convert_fusion.4), channel_id=1, source_target_pairs={{0,8},{4,20},{8,0},{12,28},{16,24},{20,4},{24,16},{28,12},{1,9},{5... | collective-permute-start | bytes 768008 | tf_op jit(solution)/shard_map/ppermute | solution.py:355
  44.6 0.8 %collective-permute-start.20 = (f32[16,128]{1,0:T(8,128)S(1)}, f32[16,128]{1,0:T(8,128)S(1)}, u32[]{:S(2)}, u32[]{:S(2)}) collective-permute-start(f32[16,128]{1,0:T(8,128)S(1)} %get-tuple-element.187), channel_id=1, source_target_pairs={{0,16},{4,20},{8,24},{12,28},{16,0},{20,4},{24,8},{28,12},{1,17},{... | collective-permute-start | bytes 24584 | tf_op jit(solution)/shard_map/ppermute | solution.py:442
  45.4 1.7 %collective-permute-start.22 = (f32[16,128]{1,0:T(8,128)S(1)}, f32[16,128]{1,0:T(8,128)S(1)}, u32[]{:S(2)}, u32[]{:S(2)}) collective-permute-start(f32[16,128]{1,0:T(8,128)S(1)} %get-tuple-element.189), channel_id=1, source_target_pairs={{0,28},{4,8},{8,4},{12,16},{16,12},{20,24},{24,20},{28,0},{1,29},{... | collective-permute-start | bytes 24584 | tf_op jit(solution)/shard_map/ppermute | solution.py:442
  47.1 1.4 %collective-permute-done.17 = f16[200,640]{1,0:T(8,128)(2,1)S(1)} collective-permute-done((f16[200,640]{1,0:T(8,128)(2,1)S(1)}, f16[200,640]{1,0:T(8,128)(2,1)S(1)}, u32[]{:S(2)}, u32[]{:S(2)}) %collective-permute-start.17) | collective-permute-done | bytes 256032 | tf_op jit(solution)/shard_map/ppermute | solution.py:355
  48.7 0.8 %select_convert_fusion.3 = f16[200,640]{1,0:T(8,128)(2,1)S(1)} fusion(f16[200,640]{1,0:T(8,128)(2,1)S(1)} %collective-permute-done.17, f16[200,640]{1,0:T(8,128)(2,1)S(1)} %select_convert_fusion.5, f32[640]{0:T(1024)S(1)} %get-tuple-element.237, f32[640]{0:T(1024)S(1)} %get-tuple-element.238, f32[640]{0:T(1024)S(1)} %get-tuple-element.239, ...), kind=kLoop, calls=%fused_computation.8 | loop fusion | flops 2048000 | bytes 800120 | tf_op jit(solution)/shard_map/convert_element_type | solution.py:379
  49.4 0.9 %collective-permute-start.18 = (f16[200,640]{1,0:T(8,128)(2,1)S(1)}, f16[200,640]{1,0:T(8,128)(2,1)S(1)}, u32[]{:S(2)}, u32[]{:S(2)}) collective-permute-start(f16[200,640]{1,0:T(8,128)(2,1)S(1)} %select_convert_fusion.3), channel_id=1, source_target_pairs={{0,16},{4,12},{8,24},{12,4},{16,0},{20,28},{24,8},{28,20},{1,17},{... | collective-permute-start | bytes 768008 | tf_op jit(solution)/shard_map/ppermute | solution.py:355
  50.3 1.0 %collective-permute-done.19 = f16[200,640]{1,0:T(8,128)(2,1)S(1)} collective-permute-done((f16[200,640]{1,0:T(8,128)(2,1)S(1)}, f16[200,640]{1,0:T(8,128)(2,1)S(1)}, u32[]{:S(2)}, u32[]{:S(2)}) %collective-permute-start.19) | collective-permute-done | bytes 256032 | tf_op jit(solution)/shard_map/ppermute | solution.py:355
  51.5 0.3 select_convert_fusion.2
  51.7 0.9 %collective-permute-start.24 = (f16[200,640]{1,0:T(8,128)(2,1)S(1)}, f16[200,640]{1,0:T(8,128)(2,1)S(1)}, u32[]{:S(2)}, u32[]{:S(2)}) collective-permute-start(f16[200,640]{1,0:T(8,128)(2,1)S(1)} %select_convert_fusion.2), channel_id=1, source_target_pairs={{0,16},{4,12},{8,24},{12,4},{16,0},{20,28},{24,8},{28,20},{1,17},{... | collective-permute-start | bytes 768008 | tf_op jit(solution)/shard_map/ppermute | solution.py:355
  52.6 0.8 %end.1 = f32[16,1024]{1,0:T(8,128)} custom-call(s32[8,1024]{1,0:T(8,128)S(1)} %iota.185.info, f32[16,1024]{1,0:T(8,128)S(1)} %get-tuple-element.193.adjoint_ref, f32[8,1024]{1,0:T(8,128)S(1)} %get-tuple-element.123.weight_ref, f32[8,1024]{1,0:T(8,128)S(1)} %get-tuple-element.142.sums_ref, f32[64,1024]{1,0:T(8,128)S(1)} %get-tuple-element.194.back_ref, ...), custom_call_target="tpu_custom_call" | custom-call | tf_op jit(solution)/shard_map/end/pallas_call | solution.py:341
  53.4 2.4 %collective-permute-done.18 = f16[200,640]{1,0:T(8,128)(2,1)S(1)} collective-permute-done((f16[200,640]{1,0:T(8,128)(2,1)S(1)}, f16[200,640]{1,0:T(8,128)(2,1)S(1)}, u32[]{:S(2)}, u32[]{:S(2)}) %collective-permute-start.18) | collective-permute-done | bytes 256032 | tf_op jit(solution)/shard_map/ppermute | solution.py:355
  56.0 0.8 %select_convert_fusion.1 = f16[200,640]{1,0:T(8,128)(2,1)S(1)} fusion(f16[200,640]{1,0:T(8,128)(2,1)S(1)} %collective-permute-done.18, f16[200,640]{1,0:T(8,128)(2,1)S(1)} %select_convert_fusion.3, f32[640]{0:T(1024)S(1)} %get-tuple-element.221, f32[640]{0:T(1024)S(1)} %get-tuple-element.222, f32[640]{0:T(1024)S(1)} %get-tuple-element.223, ...), kind=kLoop, calls=%fused_computation.6 | loop fusion | flops 2048000 | bytes 800120 | tf_op jit(solution)/shard_map/convert_element_type | solution.py:379
  56.9 1.7 %collective-permute-done.24 = f16[200,640]{1,0:T(8,128)(2,1)S(1)} collective-permute-done((f16[200,640]{1,0:T(8,128)(2,1)S(1)}, f16[200,640]{1,0:T(8,128)(2,1)S(1)}, u32[]{:S(2)}, u32[]{:S(2)}) %collective-permute-start.24) | collective-permute-done | bytes 256032 | tf_op jit(solution)/shard_map/ppermute | solution.py:355
  58.7 0.3 select_convert_fusion
  59.0 0.1 collective-permute-start.25
  59.0 0.2 maximum_select_fusion
  59.3 0.5 slice_bitcast_fusion
  59.8 0.6 slice_reduce_fusion
  60.5 0.2 maximum_select_fusion.1
  60.9 1.3 %pad_maximum_fusion = f32[2,320,640]{2,1,0:T(8,128)} fusion(f32[2,192,640]{2,1,0:T(8,128)S(1)} %convert_multiply_fusion, f32[2,128,640]{2,1,0:T(8,128)S(1)} %convert_multiply_fusion.1), kind=kLoop, calls=%fused_computation | loop fusion | flops 409600 | bytes 3276800 | tf_op jit(solution)/shard_map/concatenate | solution.py:592
  62.2 0.7 %convert_multiply_fusion.2 = (f32[2,32,640]{2,1,0:T(8,128)}, f32[2,32,640]{2,1,0:T(8,128)}) fusion(f16[2,200,640]{2,1,0:T(8,128)(2,1)S(1)} %maximum_select_fusion, f32[2,640]{1,0:T(2,128)S(1)} %bitcast.50, f32[2,640]{1,0:T(2,128)S(1)} %bitcast.51), kind=kLoop, calls=%fused_computation.11 | loop fusion | flops 163840 | bytes 501760 | tf_op jit(solution)/shard_map/mul | solution.py:577
  (65 shorter events, 1.2 us)
Async XLA Ops:
  0.6 11.8 %collective-permute-start = (f32[16,1024]{1,0:T(8,128)}, f32[16,1024]{1,0:T(8,128)S(1)}, u32[]{:S(2)}, u32[]{:S(2)}) collective-permute-start(f32[16,1024]{1,0:T(8,128)} %bitcast.46), channel_id=1, source_target_pairs={{0,1},{1,0},{2,3},{3,2},{4,5},{5,4},{6,7},{7,6},{8,9},{9,8},{10,11... | collective-permute-start | bytes 196616 | tf_op jit(solution)/shard_map/ppermute | solution.py:355
  3.7 8.7 %collective-permute-start.1 = (f32[16,1024]{1,0:T(8,128)}, f32[16,1024]{1,0:T(8,128)S(1)}, u32[]{:S(2)}, u32[]{:S(2)}) collective-permute-start(f32[16,1024]{1,0:T(8,128)} %bitcast.47), channel_id=1, source_target_pairs={{0,2},{1,3},{2,0},{3,1},{4,6},{5,7},{6,4},{7,5},{8,10},{9,11},{10,... | collective-permute-start | bytes 196616 | tf_op jit(solution)/shard_map/ppermute | solution.py:355
  6.3 7.0 %collective-permute-start.2 = (f32[16,1024]{1,0:T(8,128)}, f32[16,1024]{1,0:T(8,128)S(1)}, u32[]{:S(2)}, u32[]{:S(2)}) collective-permute-start(f32[16,1024]{1,0:T(8,128)} %bitcast.48), channel_id=1, source_target_pairs={{0,3},{1,2},{2,1},{3,0},{4,7},{5,6},{6,5},{7,4},{8,11},{9,10},{10,... | collective-permute-start | bytes 196616 | tf_op jit(solution)/shard_map/ppermute | solution.py:355
  8.0 7.4 %collective-permute-start.3 = (f32[16,1024]{1,0:T(8,128)}, f32[16,1024]{1,0:T(8,128)S(1)}, u32[]{:S(2)}, u32[]{:S(2)}) collective-permute-start(f32[16,1024]{1,0:T(8,128)} %bitcast.33), channel_id=1, source_target_pairs={{0,1},{1,0},{2,3},{3,2},{4,5},{5,4},{6,7},{7,6},{8,9},{9,8},{10,11... | collective-permute-start | bytes 196616 | tf_op jit(solution)/shard_map/ppermute | solution.py:355
  9.0 10.6 %collective-permute-start.4 = (f32[16,1024]{1,0:T(8,128)}, f32[16,1024]{1,0:T(8,128)S(1)}, u32[]{:S(2)}, u32[]{:S(2)}) collective-permute-start(f32[16,1024]{1,0:T(8,128)} %bitcast.34), channel_id=1, source_target_pairs={{0,2},{1,3},{2,0},{3,1},{4,6},{5,7},{6,4},{7,5},{8,10},{9,11},{10,... | collective-permute-start | bytes 196616 | tf_op jit(solution)/shard_map/ppermute | solution.py:355
  12.5 7.1 %collective-permute-start.5 = (f32[16,1024]{1,0:T(8,128)}, f32[16,1024]{1,0:T(8,128)S(1)}, u32[]{:S(2)}, u32[]{:S(2)}) collective-permute-start(f32[16,1024]{1,0:T(8,128)} %bitcast.35), channel_id=1, source_target_pairs={{0,3},{1,2},{2,1},{3,0},{4,7},{5,6},{6,5},{7,4},{8,11},{9,10},{10,... | collective-permute-start | bytes 196616 | tf_op jit(solution)/shard_map/ppermute | solution.py:355
  13.8 5.8 %collective-permute-start.6 = (f32[72,128]{1,0:T(8,128)S(1)}, f32[72,128]{1,0:T(8,128)S(1)}, u32[]{:S(2)}, u32[]{:S(2)}) collective-permute-start(f32[72,128]{1,0:T(8,128)S(1)} %get-tuple-element.138), channel_id=1, source_target_pairs={{0,16},{4,20},{8,24},{12,28},{16,0},{20,4},{24,8},{28,12},{1,17},{... | collective-permute-start | bytes 110600 | tf_op jit(solution)/shard_map/ppermute | solution.py:442
  15.4 4.1 %collective-permute-start.7 = (f32[72,128]{1,0:T(8,128)S(1)}, f32[72,128]{1,0:T(8,128)S(1)}, u32[]{:S(2)}, u32[]{:S(2)}) collective-permute-start(f32[72,128]{1,0:T(8,128)S(1)} %get-tuple-element.139), channel_id=1, source_target_pairs={{0,4},{4,0},{8,12},{12,8},{16,20},{20,16},{24,28},{28,24},{1,5},{5... | collective-permute-start | bytes 110600 | tf_op jit(solution)/shard_map/ppermute | solution.py:442
  15.4 4.4 %collective-permute-start.8 = (f32[72,128]{1,0:T(8,128)S(1)}, f32[72,128]{1,0:T(8,128)S(1)}, u32[]{:S(2)}, u32[]{:S(2)}) collective-permute-start(f32[72,128]{1,0:T(8,128)S(1)} %get-tuple-element.140), channel_id=1, source_target_pairs={{0,28},{4,8},{8,4},{12,16},{16,12},{20,24},{24,20},{28,0},{1,29},{... | collective-permute-start | bytes 110600 | tf_op jit(solution)/shard_map/ppermute | solution.py:442
  20.9 5.7 %collective-permute-start.10 = (f32[64,128]{1,0:T(8,128)S(1)}, f32[64,128]{1,0:T(8,128)S(1)}, u32[]{:S(2)}, u32[]{:S(2)}) collective-permute-start(f32[64,128]{1,0:T(8,128)S(1)} %get-tuple-element.145), channel_id=1, source_target_pairs={{0,4},{4,0},{8,12},{12,8},{16,20},{20,16},{24,28},{28,24},{1,5},{5... | collective-permute-start | bytes 98312 | tf_op jit(solution)/shard_map/ppermute | solution.py:442
  21.0 5.6 %collective-permute-start.11 = (f32[64,128]{1,0:T(8,128)S(1)}, f32[64,128]{1,0:T(8,128)S(1)}, u32[]{:S(2)}, u32[]{:S(2)}) collective-permute-start(f32[64,128]{1,0:T(8,128)S(1)} %get-tuple-element.146), channel_id=1, source_target_pairs={{0,28},{4,8},{8,4},{12,16},{16,12},{20,24},{24,20},{28,0},{1,29},{... | collective-permute-start | bytes 98312 | tf_op jit(solution)/shard_map/ppermute | solution.py:442
  22.5 4.1 %collective-permute-start.9 = (f32[64,128]{1,0:T(8,128)S(1)}, f32[64,128]{1,0:T(8,128)S(1)}, u32[]{:S(2)}, u32[]{:S(2)}) collective-permute-start(f32[64,128]{1,0:T(8,128)S(1)} %get-tuple-element.144), channel_id=1, source_target_pairs={{0,16},{4,20},{8,24},{12,28},{16,0},{20,4},{24,8},{28,12},{1,17},{... | collective-permute-start | bytes 98312 | tf_op jit(solution)/shard_map/ppermute | solution.py:442
  24.0 2.6 %copy-start = (f32[2,8,1024]{2,1,0:T(8,128)S(1)}, f32[2,8,1024]{2,1,0:T(8,128)}, u32[]{:S(2)}) copy-start(f32[2,8,1024]{2,1,0:T(8,128)} %param.11) | copy-start | bytes 196612
  28.2 6.4 %collective-permute-start.12 = (f32[64,128]{1,0:T(8,128)S(1)}, f32[64,128]{1,0:T(8,128)S(1)}, u32[]{:S(2)}, u32[]{:S(2)}) collective-permute-start(f32[64,128]{1,0:T(8,128)S(1)} %get-tuple-element.159), channel_id=1, source_target_pairs={{0,16},{4,20},{8,24},{12,28},{16,0},{20,4},{24,8},{28,12},{1,17},{... | collective-permute-start | bytes 98312 | tf_op jit(solution)/shard_map/ppermute | solution.py:442
  29.5 5.2 %collective-permute-start.13 = (f32[64,128]{1,0:T(8,128)S(1)}, f32[64,128]{1,0:T(8,128)S(1)}, u32[]{:S(2)}, u32[]{:S(2)}) collective-permute-start(f32[64,128]{1,0:T(8,128)S(1)} %get-tuple-element.160), channel_id=1, source_target_pairs={{0,4},{4,0},{8,12},{12,8},{16,20},{20,16},{24,28},{28,24},{1,5},{5... | collective-permute-start | bytes 98312 | tf_op jit(solution)/shard_map/ppermute | solution.py:442
  29.5 5.2 %collective-permute-start.14 = (f32[64,128]{1,0:T(8,128)S(1)}, f32[64,128]{1,0:T(8,128)S(1)}, u32[]{:S(2)}, u32[]{:S(2)}) collective-permute-start(f32[64,128]{1,0:T(8,128)S(1)} %get-tuple-element.161), channel_id=1, source_target_pairs={{0,28},{4,8},{8,4},{12,16},{16,12},{20,24},{24,20},{28,0},{1,29},{... | collective-permute-start | bytes 98312 | tf_op jit(solution)/shard_map/ppermute | solution.py:442
  39.7 2.0 %collective-permute-start.16 = (f32[200,640]{1,0:T(8,128)S(1)}, f32[200,640]{1,0:T(8,128)S(1)}, u32[]{:S(2)}, u32[]{:S(2)}) collective-permute-start(f32[200,640]{1,0:T(8,128)S(1)} %get-tuple-element.175), channel_id=1, source_target_pairs={{0,4},{4,0},{8,12},{12,8},{16,20},{20,16},{24,28},{28,24},{1,5},{5... | collective-permute-start | bytes 1536008 | tf_op jit(solution)/shard_map/ppermute | solution.py:355
  39.9 3.2 %collective-permute-start.15 = (f32[200,640]{1,0:T(8,128)S(1)}, f32[200,640]{1,0:T(8,128)S(1)}, u32[]{:S(2)}, u32[]{:S(2)}) collective-permute-start(f32[200,640]{1,0:T(8,128)S(1)} %get-tuple-element.173), channel_id=1, source_target_pairs={{0,4},{4,0},{8,12},{12,8},{16,20},{20,16},{24,28},{28,24},{1,5},{5... | collective-permute-start | bytes 1536008 | tf_op jit(solution)/shard_map/ppermute | solution.py:355
  42.1 6.4 %collective-permute-start.17 = (f16[200,640]{1,0:T(8,128)(2,1)S(1)}, f16[200,640]{1,0:T(8,128)(2,1)S(1)}, u32[]{:S(2)}, u32[]{:S(2)}) collective-permute-start(f16[200,640]{1,0:T(8,128)(2,1)S(1)} %select_convert_fusion.5), channel_id=1, source_target_pairs={{0,8},{4,20},{8,0},{12,28},{16,24},{20,4},{24,16},{28,12},{1,9},{5... | collective-permute-start | bytes 768008 | tf_op jit(solution)/shard_map/ppermute | solution.py:355
  43.4 7.9 %collective-permute-start.19 = (f16[200,640]{1,0:T(8,128)(2,1)S(1)}, f16[200,640]{1,0:T(8,128)(2,1)S(1)}, u32[]{:S(2)}, u32[]{:S(2)}) collective-permute-start(f16[200,640]{1,0:T(8,128)(2,1)S(1)} %select_convert_fusion.4), channel_id=1, source_target_pairs={{0,8},{4,20},{8,0},{12,28},{16,24},{20,4},{24,16},{28,12},{1,9},{5... | collective-permute-start | bytes 768008 | tf_op jit(solution)/shard_map/ppermute | solution.py:355
  44.6 5.7 %collective-permute-start.20 = (f32[16,128]{1,0:T(8,128)S(1)}, f32[16,128]{1,0:T(8,128)S(1)}, u32[]{:S(2)}, u32[]{:S(2)}) collective-permute-start(f32[16,128]{1,0:T(8,128)S(1)} %get-tuple-element.187), channel_id=1, source_target_pairs={{0,16},{4,20},{8,24},{12,28},{16,0},{20,4},{24,8},{28,12},{1,17},{... | collective-permute-start | bytes 24584 | tf_op jit(solution)/shard_map/ppermute | solution.py:442
  45.4 4.9 %collective-permute-start.21 = (f32[16,128]{1,0:T(8,128)S(1)}, f32[16,128]{1,0:T(8,128)S(1)}, u32[]{:S(2)}, u32[]{:S(2)}) collective-permute-start(f32[16,128]{1,0:T(8,128)S(1)} %get-tuple-element.188), channel_id=1, source_target_pairs={{0,4},{4,0},{8,12},{12,8},{16,20},{20,16},{24,28},{28,24},{1,5},{5... | collective-permute-start | bytes 24584 | tf_op jit(solution)/shard_map/ppermute | solution.py:442
  45.4 4.9 %collective-permute-start.22 = (f32[16,128]{1,0:T(8,128)S(1)}, f32[16,128]{1,0:T(8,128)S(1)}, u32[]{:S(2)}, u32[]{:S(2)}) collective-permute-start(f32[16,128]{1,0:T(8,128)S(1)} %get-tuple-element.189), channel_id=1, source_target_pairs={{0,28},{4,8},{8,4},{12,16},{16,12},{20,24},{24,20},{28,0},{1,29},{... | collective-permute-start | bytes 24584 | tf_op jit(solution)/shard_map/ppermute | solution.py:442
  49.4 6.4 %collective-permute-start.18 = (f16[200,640]{1,0:T(8,128)(2,1)S(1)}, f16[200,640]{1,0:T(8,128)(2,1)S(1)}, u32[]{:S(2)}, u32[]{:S(2)}) collective-permute-start(f16[200,640]{1,0:T(8,128)(2,1)S(1)} %select_convert_fusion.3), channel_id=1, source_target_pairs={{0,16},{4,12},{8,24},{12,4},{16,0},{20,28},{24,8},{28,20},{1,17},{... | collective-permute-start | bytes 768008 | tf_op jit(solution)/shard_map/ppermute | solution.py:355
  51.7 6.8 %collective-permute-start.24 = (f16[200,640]{1,0:T(8,128)(2,1)S(1)}, f16[200,640]{1,0:T(8,128)(2,1)S(1)}, u32[]{:S(2)}, u32[]{:S(2)}) collective-permute-start(f16[200,640]{1,0:T(8,128)(2,1)S(1)} %select_convert_fusion.2), channel_id=1, source_target_pairs={{0,16},{4,12},{8,24},{12,4},{16,0},{20,28},{24,8},{28,20},{1,17},{... | collective-permute-start | bytes 768008 | tf_op jit(solution)/shard_map/ppermute | solution.py:355
  56.8 2.3 %collective-permute-start.23 = (f16[200,640]{1,0:T(8,128)(2,1)S(1)}, f16[200,640]{1,0:T(8,128)(2,1)S(1)}, u32[]{:S(2)}, u32[]{:S(2)}) collective-permute-start(f16[200,640]{1,0:T(8,128)(2,1)S(1)} %select_convert_fusion.1), channel_id=1, source_target_pairs={{0,4},{4,0},{8,12},{12,8},{16,20},{20,16},{24,28},{28,24},{1,5},{5... | collective-permute-start | bytes 768008 | tf_op jit(solution)/shard_map/ppermute | solution.py:355
  59.0 1.6 %collective-permute-start.25 = (f16[200,640]{1,0:T(8,128)(2,1)S(1)}, f16[200,640]{1,0:T(8,128)(2,1)S(1)}, u32[]{:S(2)}, u32[]{:S(2)}) collective-permute-start(f16[200,640]{1,0:T(8,128)(2,1)S(1)} %select_convert_fusion), channel_id=1, source_target_pairs={{0,4},{4,0},{8,12},{12,8},{16,20},{20,16},{24,28},{28,24},{1,5},{5... | collective-permute-start | bytes 768008 | tf_op jit(solution)/shard_map/ppermute | solution.py:355

commit v9 on v8

--- a/solution.py
+++ b/solution.py
@@ -325,6 +325,49 @@
                 at += piece.shape[0]
 
 
+def decoded(scale, info, half, own, other, start, rows, exponent_row):
+    def rows_of(at, number):
+        pair = (own[at : at + number, :], other[at : at + number, :])
+        return jnp.where(is_even_tile(info, pair[0].shape), pair[half], pair[1 - half])
+
+    return rows_of(start, rows) * (jnp.exp2(rows_of(exponent_row, 1)) * scale)
+
+
+def first_finish_kernel(scale, info, own, other, mid_ref, in_ref, out_ref, b_in, b_mid, b_out, held, sems):
+    width = own.shape[1]
+    (top, side, _), _ = block_parts(width)
+    at = top + 2 * side + EXPONENT_ROW
+    copies = []
+    for half in range(HALVES):
+        part = functools.partial(decoded, scale, info, half, own, other)
+        held[half] = part(0, top, at)
+        copies.append(pltpu.make_async_copy(held.at[half], mid_ref.at[pl.ds(half * (width // HALVES), top)], sems.at[half]))
+        copies[half].start()
+        in_ref[half * side : (half + 1) * side, :] = part(top, side, at + 1)
+        out_ref[half * side : (half + 1) * side, :] = part(top + side, side, at + 2)
+        tail = part(top + 2 * side, 8, at + 3)
+        if half == 0:
+            b_in[...] = tail[0:1, :].reshape(b_in.shape)
+            b_out[...] = tail[1:2, : b_out.shape[0]].reshape(b_out.shape)
+        else:
+            b_mid[...] = tail[0:1, :].reshape(b_mid.shape)
+    for copy in copies:
+        copy.wait()
+
+
+def second_finish_kernel(scale, info, own, other, begun_ref, mid_ref, held, sems):
+    width = own.shape[1]
+    (top, _, _), (rest,) = block_parts(width)
+    copies = []
+    for half in range(HALVES):
+        held[half] = decoded(scale, info, half, own, other, 0, rest, rest + EXPONENT_ROW)
+        to = mid_ref.at[pl.ds(half * (width // HALVES) + top, rest)]
+        copies.append(pltpu.make_async_copy(held.at[half], to, sems.at[half]))
+        copies[half].start()
+    for copy in copies:
+        copy.wait()
+
+
 def spec_of(shape, dtype=jnp.float32):
     return jax.ShapeDtypeStruct(shape, dtype)
 
@@ -402,7 +445,7 @@
     return with_exponents(total, exponents)
 
 
-def summed_by_tile(kept, sent, all_parts, edges, exchanged, end, finish_first):
+def summed_by_tile(kept, sent, all_parts, edges, exchanged, end):
     tied = lax.optimization_barrier
     others = [swapped(block, "tile", 1, 1) for block in sent]
     first = coded_sum(kept[0], others[0], all_parts[0])
@@ -418,9 +461,10 @@
     others = [swapped(block, "tile", 4, 2) for block in (first, second)]
     others[0], later, ended = tied((others[0], second, end(arrived)))
     first = sum_of_coded(held, others[0], all_parts[0])
-    finished = finish_first(by_half(first, swapped(first, "tile", 1, 1)))
+    others[1], held = tied((others[1], first))
     second = sum_of_coded(later, others[1], all_parts[1])
-    return ended, finished, by_half(second, swapped(second, "tile", 1, 1))
+    blocks = [held, swapped(first, "tile", 1, 1), second, swapped(second, "tile", 1, 1)]
+    return ended, [block.astype(jnp.float32) for block in blocks]
 
 
 def by_half(own, other):
@@ -569,27 +613,41 @@
     def part(block, b, k, count=None):
         start = sum(all_parts[b][:k])
         count = all_parts[b][k] if count is None else count
-        values = block[:, start : start + count, :]
-        if values.dtype != jnp.float16:
-            return values * scale
-        at = sum(all_parts[b]) + EXPONENT_ROW + k
-        exponent = block[:, at : at + 1, :].astype(jnp.float32)
-        return values.astype(jnp.float32) * (jnp.exp2(exponent) * scale)
-
-    def finish_first(block):
-        grad_w_in = part(block, 0, 1).reshape(FEATURES, width)
-        grad_w_out = part(block, 0, 2).reshape(FEATURES, width).T
-        biases = part(block, 0, 3, 2)
-        return grad_w_in, biases[0, 0], biases[1, 0], grad_w_out, biases[0, 1, :FEATURES], block
+        return block[:, start : start + count, :] * scale
 
     if tiles == 8:
-        sensitivity, finished, second = summed_by_tile(kept, sent, all_parts, tuple(edges), exchanged, end, finish_first)
+        sensitivity, blocks = summed_by_tile(kept, sent, all_parts, tuple(edges), exchanged, end)
+        whole_mid = spec_of((width, width))
+        vmem, hbm = (pl.BlockSpec(memory_space=space) for space in (pltpu.VMEM, pltpu.HBM))
+        limit = pltpu.CompilerParams(vmem_limit_bytes=VMEM_LIMIT)
+        begun, grad_w_in, grad_w_out, grad_b_in, grad_b_mid, grad_b_out = pl.pallas_call(
+            functools.partial(first_finish_kernel, scale),
+            out_shape=(whole_mid, side, side, spec_of((width,)), spec_of((width,)), spec_of((FEATURES,))),
+            in_specs=[vmem, vmem, vmem],
+            out_specs=(hbm, vmem, vmem, vmem, vmem, vmem),
+            scratch_shapes=[pltpu.VMEM((HALVES, all_parts[0][0], width), jnp.float32), pltpu.SemaphoreType.DMA((HALVES,))],
+            compiler_params=limit,
+            name="first_finish",
+        )(*info, *blocks[:2])
+        (grad_w_mid,) = pl.pallas_call(
+            functools.partial(second_finish_kernel, scale),
+            out_shape=(whole_mid,),
+            in_specs=[vmem, vmem, vmem, hbm],
+            out_specs=(hbm,),
+            scratch_shapes=[pltpu.VMEM((HALVES, all_parts[1][0], width), jnp.float32), pltpu.SemaphoreType.DMA((HALVES,))],
+            input_output_aliases={3: 0},
+            compiler_params=limit,
+            name="second_finish",
+        )(*info, *blocks[2:], begun)
+        grad_w_out = grad_w_out.T
     else:
         first, second = lax.psum([by_half(*args) for args in zip(kept, sent)], "tile")
-        finished = finish_first(first)
         sensitivity = end(exchanged(edges))
-    grad_w_in, grad_b_in, grad_b_mid, grad_w_out, grad_b_out, first = finished
-    grad_w_mid = jnp.concatenate([part(first, 0, 0), part(second, 1, 0)], axis=1).reshape(width, width)
+        grad_w_mid = jnp.concatenate([part(first, 0, 0), part(second, 1, 0)], axis=1).reshape(width, width)
+        grad_w_in = part(first, 0, 1).reshape(FEATURES, width)
+        grad_w_out = part(first, 0, 2).reshape(FEATURES, width).T
+        biases = part(first, 0, 3, 2)
+        grad_b_in, grad_b_mid, grad_b_out = biases[0, 0], biases[1, 0], biases[0, 1, :FEATURES]
     shape = (TRACERS, levels, TILE_CELLS)
     return (
         final_state.reshape(shape),

time: 63.1 us -> 62.2 us (0.986)
  Pallas kernels: 19.6 us -> 22.3 us
  other arithmetic: 5.48 us -> 3.03 us
  local copies, waits for them, and re-layouts: 1.66 us -> 0.51 us
    pallas_call x0 -> x2, Pallas kernels: none -> 2.67 us  [the longest x1 1.64 us: body(): pl.pallas_call(functools.partial(first_finish_kernel, scale), out_shape=(...]
    concatenate x1 -> x0, other arithmetic: 1.27 us -> none  [body(): jnp.concatenate([part(first, 0, 0), part(second, 1, 0)], axis=1)]
    mul x6 -> x0, other arithmetic: 0.94 us -> none  [part(): return values.astype(jnp.float32) * (jnp.exp2(exponent) * scale)]
    convert_element_type x6 -> x5, other arithmetic: 2.63 us -> 2.4 us  [with_exponents(): return out.astype(jnp.float16)]
  transfers between devices with their start and end apart: 26 -> 26, of which waited for: 7 -> 7; matrix products, arithmetic and copies ran while one was open for 8% -> 6% of each run, Pallas kernels for 19% -> 22%
where the time goes in v9:
time: 62.2 us; the launch traced here: 62 us
  starting transfers between devices  26.1 us (42%)
  Pallas kernels  22.3 us (36%)
  waiting for transfers between devices  8.87 us (14%)
  other arithmetic  3.03 us (5%)
  between operations  1.23 us (2%)
    pallas_call x10, Pallas kernels, called(): pl.pallas_call(kernel, out_shape=tuple(outs), in_specs=in_specs, out_spec...  19.6 us
    ppermute x14, starting transfers between devices, swapped(): lax.ppermute(x, axis, [(i, i ^ (odd_bit if i & 1 else even_bit)) for i in...  14.8 us
    ppermute x12, starting transfers between devices, exchanged(): lax.ppermute(edge, 'tile', way)  11.3 us
    ppermute x14, waiting for transfers between devices, swapped(): lax.ppermute(x, axis, [(i, i ^ (odd_bit if i & 1 else even_bit)) for i in...  8.61 us
    convert_element_type x5, other arithmetic, with_exponents(): return out.astype(jnp.float16)  2.4 us
    pallas_call x1, Pallas kernels, body(): pl.pallas_call(functools.partial(first_finish_kernel, scale), out_shape=(...  1.64 us
  transfers between devices with their start and end apart: 26, of which 7 were waited for; matrix products, arithmetic and copies ran while one was open for 6% of the time, Pallas kernels for 22%

profile of v9, /device:TPU:0, one launch (start us, length us, event | category | flops | bytes accessed | tf_op | source)
XLA Modules:
  0.0 62.0 jit_solution(10622120527164972640)
XLA Ops:
  0.6 3.1 %collective-permute-start = (f32[16,1024]{1,0:T(8,128)}, f32[16,1024]{1,0:T(8,128)S(1)}, u32[]{:S(2)}, u32[]{:S(2)}) collective-permute-start(f32[16,1024]{1,0:T(8,128)} %bitcast.14), channel_id=1, source_target_pairs={{0,1},{1,0},{2,3},{3,2},{4,5},{5,4},{6,7},{7,6},{8,9},{9,8},{10,11... | collective-permute-start | bytes 196616 | tf_op jit(solution)/shard_map/ppermute | solution.py:398
  3.7 2.6 %collective-permute-start.1 = (f32[16,1024]{1,0:T(8,128)}, f32[16,1024]{1,0:T(8,128)S(1)}, u32[]{:S(2)}, u32[]{:S(2)}) collective-permute-start(f32[16,1024]{1,0:T(8,128)} %bitcast.15), channel_id=1, source_target_pairs={{0,2},{1,3},{2,0},{3,1},{4,6},{5,7},{6,4},{7,5},{8,10},{9,11},{10,... | collective-permute-start | bytes 196616 | tf_op jit(solution)/shard_map/ppermute | solution.py:398
  6.3 1.7 %prepare.1 = (f32[8,1024]{1,0:T(8,128)S(1)}, f32[16,1024]{1,0:T(8,128)S(1)}, f32[1,640]{1,0:T(1,128)S(1)}, f32[1,640]{1,0:T(1,128)S(1)}, f32[64,128]{1,0:T(8,128...) custom-call(f32[1,1024]{1,0:T(1,128)} %bitcast.18, ...), custom_call_target="tpu_custom_call" | custom-call | tf_op jit(solution)/shard_map/prepare/pallas_call | solution.py:384
  8.0 1.0 %collective-permute-start.3 = (f32[16,1024]{1,0:T(8,128)}, f32[16,1024]{1,0:T(8,128)S(1)}, u32[]{:S(2)}, u32[]{:S(2)}) collective-permute-start(f32[16,1024]{1,0:T(8,128)} %bitcast.8), channel_id=1, source_target_pairs={{0,1},{1,0},{2,3},{3,2},{4,5},{5,4},{6,7},{7,6},{8,9},{9,8},{10,11... | collective-permute-start | bytes 196616 | tf_op jit(solution)/shard_map/ppermute | solution.py:398
  9.0 3.5 %collective-permute-start.4 = (f32[16,1024]{1,0:T(8,128)}, f32[16,1024]{1,0:T(8,128)S(1)}, u32[]{:S(2)}, u32[]{:S(2)}) collective-permute-start(f32[16,1024]{1,0:T(8,128)} %bitcast.9), channel_id=1, source_target_pairs={{0,2},{1,3},{2,0},{3,1},{4,6},{5,7},{6,4},{7,5},{8,10},{9,11},{10,... | collective-permute-start | bytes 196616 | tf_op jit(solution)/shard_map/ppermute | solution.py:398
  12.5 0.8 %collective-permute-done.2.refs_3_ = f32[16,1024]{1,0:T(8,128)S(1)} collective-permute-done((f32[16,1024]{1,0:T(8,128)}, f32[16,1024]{1,0:T(8,128)S(1)}, u32[]{:S(2)}, u32[]{:S(2)}) %collective-permute-start.2) | collective-permute-done | bytes 65568 | tf_op jit(solution)/shard_map/ppermute | solution.py:398
  13.3 0.1 iota.185.info
  13.4 0.4 gather.1
  13.8 1.6 %collective-permute-start.6 = (f32[72,128]{1,0:T(8,128)S(1)}, f32[72,128]{1,0:T(8,128)S(1)}, u32[]{:S(2)}, u32[]{:S(2)}) collective-permute-start(f32[72,128]{1,0:T(8,128)S(1)} %get-tuple-element.146), channel_id=1, source_target_pairs={{0,16},{4,20},{8,24},{12,28},{16,0},{20,4},{24,8},{28,12},{1,17},{... | collective-permute-start | bytes 110600 | tf_op jit(solution)/shard_map/ppermute | solution.py:486
  15.4 1.5 %collective-permute-start.8 = (f32[72,128]{1,0:T(8,128)S(1)}, f32[72,128]{1,0:T(8,128)S(1)}, u32[]{:S(2)}, u32[]{:S(2)}) collective-permute-start(f32[72,128]{1,0:T(8,128)S(1)} %get-tuple-element.148), channel_id=1, source_target_pairs={{0,28},{4,8},{8,4},{12,16},{16,12},{20,24},{24,20},{28,0},{1,29},{... | collective-permute-start | bytes 110600 | tf_op jit(solution)/shard_map/ppermute | solution.py:486
  17.0 2.6 %closure.2 = (f32[64,1024]{1,0:T(8,128)S(1)}, bf16[1024,640]{1,0:T(8,128)(2,1)S(1)}, f32[1024,640]{1,0:T(8,128)S(1)}, bf16[1024,640]{1,0:T(8,128)(2,1)S(1)}, f32[1024,640]{1,0:T(8,128)S(1)}) custom-call(f32[64,1024]{1,0:T(8,128)S(1)} %get-tuple-element.136.state_ref, bf16[64,640]{1,0:T(8,128)(2,1)S(1)} %get-tuple-element.137.w_in, ...), custom_call_target="tpu_custom_call" | custom-call | flops 1006632960 | bytes 5242880 | tf_op jit(solution)/shard_map/closure/pallas_call | solution.py:384
  19.6 0.2 collective-permute-done.8.e2
  19.8 1.1 %step.1 = (f32[64,1024]{1,0:T(8,128)S(1)}, f32[8,1024]{1,0:T(8,128)S(1)}, f32[64,128]{1,0:T(8,128)S(1)}, f32[64,128]{1,0:T(8,128)S(1)}, f32[64,128]{1,0:T(8,128)S(1)}) custom-call(s32[8,1024]{1,0:T(8,128)S(1)} %iota.185.info, f32[64,1024]{1,0:T(8,128)S(1)} %get-tuple-element.136.state_ref, f32[8,1024]{1,0:T(8,128)S(1)} %get-tuple-element.131.weight_ref, ...), custom_call_target="tpu_custom_call" | custom-call | tf_op jit(solution)/shard_map/step/pallas_call | solution.py:384
  20.9 0.1 collective-permute-start.10
  21.0 1.5 %collective-permute-start.11 = (f32[64,128]{1,0:T(8,128)S(1)}, f32[64,128]{1,0:T(8,128)S(1)}, u32[]{:S(2)}, u32[]{:S(2)}) collective-permute-start(f32[64,128]{1,0:T(8,128)S(1)} %get-tuple-element.154), channel_id=1, source_target_pairs={{0,28},{4,8},{8,4},{12,16},{16,12},{20,24},{24,20},{28,0},{1,29},{... | collective-permute-start | bytes 98312 | tf_op jit(solution)/shard_map/ppermute | solution.py:486
  22.5 1.5 %collective-permute-start.9 = (f32[64,128]{1,0:T(8,128)S(1)}, f32[64,128]{1,0:T(8,128)S(1)}, u32[]{:S(2)}, u32[]{:S(2)}) collective-permute-start(f32[64,128]{1,0:T(8,128)S(1)} %get-tuple-element.152), channel_id=1, source_target_pairs={{0,16},{4,20},{8,24},{12,28},{16,0},{20,4},{24,8},{28,12},{1,17},{... | collective-permute-start | bytes 98312 | tf_op jit(solution)/shard_map/ppermute | solution.py:486
  24.0 2.6 %closure.3 = (f32[64,1024]{1,0:T(8,128)S(1)}, bf16[1024,640]{1,0:T(8,128)(2,1)S(1)}, f32[1024,640]{1,0:T(8,128)S(1)}, bf16[1024,640]{1,0:T(8,128)(2,1)S(1)}, f32[1024,640]{1,0:T(8,128)S(1)}) custom-call(f32[64,1024]{1,0:T(8,128)S(1)} %get-tuple-element.149.state_ref, bf16[64,640]{1,0:T(8,128)(2,1)S(1)} %get-tuple-element.137.w_in, ...), custom_call_target="tpu_custom_call" | custom-call | flops 1006632960 | bytes 5242880 | tf_op jit(solution)/shard_map/closure/pallas_call | solution.py:384
  26.6 1.6 %last_step.1 = (f32[16,1024]{1,0:T(8,128)}, f32[64,1024]{1,0:T(8,128)S(1)}, bf16[64,1024]{1,0:T(8,128)(2,1)S(1)}, f32[64,128]{1,0:T(8,128)S(1)}, f32[64,128]{1,0:T(8,128)S(1)}, /*index=5*/f32[64,128]{1,0:T(8,128)S(1)}) custom-call(s32[8,1024]{1,0:T(8,128)S(1)} %iota.185.info, f32[64,1024]{1,0:T(8,128)S(1)} %get-tuple-element.149.state_ref, ...), custom_call_target="tpu_custom_call" | custom-call | tf_op jit(solution)/shard_map/last_step/pallas_call | solution.py:384
  28.2 1.3 %collective-permute-start.12 = (f32[64,128]{1,0:T(8,128)S(1)}, f32[64,128]{1,0:T(8,128)S(1)}, u32[]{:S(2)}, u32[]{:S(2)}) collective-permute-start(f32[64,128]{1,0:T(8,128)S(1)} %get-tuple-element.167), channel_id=1, source_target_pairs={{0,16},{4,20},{8,24},{12,28},{16,0},{20,4},{24,8},{28,12},{1,17},{... | collective-permute-start | bytes 98312 | tf_op jit(solution)/shard_map/ppermute | solution.py:486
  29.5 1.2 %collective-permute-start.14 = (f32[64,128]{1,0:T(8,128)S(1)}, f32[64,128]{1,0:T(8,128)S(1)}, u32[]{:S(2)}, u32[]{:S(2)}) collective-permute-start(f32[64,128]{1,0:T(8,128)S(1)} %get-tuple-element.169), channel_id=1, source_target_pairs={{0,28},{4,8},{8,4},{12,16},{16,12},{20,24},{24,20},{28,0},{1,29},{... | collective-permute-start | bytes 98312 | tf_op jit(solution)/shard_map/ppermute | solution.py:486
  30.7 3.9 %first_backward.1 = (f32[64,1024]{1,0:T(8,128)S(1)}, f32[640,640]{1,0:T(8,128)S(1)}, f32[64,640]{1,0:T(8,128)S(1)}, f32[64,640]{1,0:T(8,128)S(1)}, f32[8,640]{1,...) custom-call(f32[64,1024]{1,0:T(8,128)S(1)} %get-tuple-element.149.state_ref, ...), custom_call_target="tpu_custom_call" | custom-call | flops 2013265920 | bytes 10485760 | tf_op jit(solution)/shard_map/first_backward/pallas_call | solution.py:384
  34.6 0.8 %adjoint.1 = (f32[16,1024]{1,0:T(8,128)S(1)}, bf16[64,1024]{1,0:T(8,128)(2,1)S(1)}, f32[16,128]{1,0:T(8,128)S(1)}, f32[16,128]{1,0:T(8,128)S(1)}, f32[16,128]{1,0:T(8,128)S(1)}) custom-call(s32[8,1024]{1,0:T(8,128)S(1)} %iota.185.info, f32[64,1024]{1,0:T(8,128)S(1)} %get-tuple-element.160.adjoint_ref, f32[8,1024]{1,0:T(8,128)S(1)} %get-tuple-element.131.weight_ref, ...), custom_call_target="tpu_custom_call" | custom-call | tf_op jit(solution)/shard_map/adjoint/pallas_call | solution.py:384
  35.4 4.3 %last_backward.1 = (f32[64,1024]{1,0:T(8,128)S(1)}, f32[200,640]{1,0:T(8,128)S(1)}, f32[200,640]{1,0:T(8,128)S(1)}, f32[200,640]{1,0:T(8,128)S(1)}, f32[200,640]{1,0:T(8,128)S(1)}) custom-call(s32[8,1024]{1,0:T(8,128)S(1)} %iota.185.info, f32[64,1024]{1,0:T(8,128)S(1)} %get-tuple-element.136.state_ref, bf16[64,1024]{1,0:T(8,128)(2,1)S(1)} %get-tuple-element.170.upstream_ref, ...), custom_call_target="tpu_custom_call" | custom-call | flops 2013265920 | bytes 10485760 | tf_op jit(solution)/shard_map/last_backward/pallas_call | solution.py:384
  39.7 0.1 collective-permute-start.16
  39.8 0.5 collective-permute-start.15
  40.4 1.3 %collective-permute-done.16 = f32[200,640]{1,0:T(8,128)S(1)} collective-permute-done((f32[200,640]{1,0:T(8,128)S(1)}, f32[200,640]{1,0:T(8,128)S(1)}, u32[]{:S(2)}, u32[]{:S(2)}) %collective-permute-start.16) | collective-permute-done | bytes 512032 | tf_op jit(solution)/shard_map/ppermute | solution.py:398
  41.7 0.1 slice_reduce_fusion.24
  41.8 0.3 select_convert_fusion.5
  42.1 1.0 %collective-permute-start.17 = (f16[200,640]{1,0:T(8,128)(2,1)S(1)}, f16[200,640]{1,0:T(8,128)(2,1)S(1)}, u32[]{:S(2)}, u32[]{:S(2)}) collective-permute-start(f16[200,640]{1,0:T(8,128)(2,1)S(1)} %select_convert_fusion.5), channel_id=1, source_target_pairs={{0,8},{4,20},{8,0},{12,28},{16,24},{20,4},{24,16},{28,12},{1,9},{5... | collective-permute-start | bytes 768008 | tf_op jit(solution)/shard_map/ppermute | solution.py:398
  43.2 0.2 select_convert_fusion.4
  43.4 1.2 %collective-permute-start.19 = (f16[200,640]{1,0:T(8,128)(2,1)S(1)}, f16[200,640]{1,0:T(8,128)(2,1)S(1)}, u32[]{:S(2)}, u32[]{:S(2)}) collective-permute-start(f16[200,640]{1,0:T(8,128)(2,1)S(1)} %select_convert_fusion.4), channel_id=1, source_target_pairs={{0,8},{4,20},{8,0},{12,28},{16,24},{20,4},{24,16},{28,12},{1,9},{5... | collective-permute-start | bytes 768008 | tf_op jit(solution)/shard_map/ppermute | solution.py:398
  44.6 0.8 %collective-permute-start.20 = (f32[16,128]{1,0:T(8,128)S(1)}, f32[16,128]{1,0:T(8,128)S(1)}, u32[]{:S(2)}, u32[]{:S(2)}) collective-permute-start(f32[16,128]{1,0:T(8,128)S(1)} %get-tuple-element.195), channel_id=1, source_target_pairs={{0,16},{4,20},{8,24},{12,28},{16,0},{20,4},{24,8},{28,12},{1,17},{... | collective-permute-start | bytes 24584 | tf_op jit(solution)/shard_map/ppermute | solution.py:486
  45.4 1.7 %collective-permute-start.22 = (f32[16,128]{1,0:T(8,128)S(1)}, f32[16,128]{1,0:T(8,128)S(1)}, u32[]{:S(2)}, u32[]{:S(2)}) collective-permute-start(f32[16,128]{1,0:T(8,128)S(1)} %get-tuple-element.197), channel_id=1, source_target_pairs={{0,28},{4,8},{8,4},{12,16},{16,12},{20,24},{24,20},{28,0},{1,29},{... | collective-permute-start | bytes 24584 | tf_op jit(solution)/shard_map/ppermute | solution.py:486
  47.1 1.4 %collective-permute-done.17 = f16[200,640]{1,0:T(8,128)(2,1)S(1)} collective-permute-done((f16[200,640]{1,0:T(8,128)(2,1)S(1)}, f16[200,640]{1,0:T(8,128)(2,1)S(1)}, u32[]{:S(2)}, u32[]{:S(2)}) %collective-permute-start.17) | collective-permute-done | bytes 256032 | tf_op jit(solution)/shard_map/ppermute | solution.py:398
  48.6 0.8 %select_convert_fusion.3 = f16[200,640]{1,0:T(8,128)(2,1)S(1)} fusion(f16[200,640]{1,0:T(8,128)(2,1)S(1)} %collective-permute-done.17, f16[200,640]{1,0:T(8,128)(2,1)S(1)} %select_convert_fusion.5, f32[640]{0:T(1024)S(1)} %get-tuple-element.251, f32[640]{0:T(1024)S(1)} %get-tuple-element.252, f32[640]{0:T(1024)S(1)} %get-tuple-element.253, ...), kind=kLoop, calls=%fused_computation.3 | loop fusion | flops 2048000 | bytes 800120 | tf_op jit(solution)/shard_map/convert_element_type | solution.py:422
  49.4 0.9 %collective-permute-start.18 = (f16[200,640]{1,0:T(8,128)(2,1)S(1)}, f16[200,640]{1,0:T(8,128)(2,1)S(1)}, u32[]{:S(2)}, u32[]{:S(2)}) collective-permute-start(f16[200,640]{1,0:T(8,128)(2,1)S(1)} %select_convert_fusion.3), channel_id=1, source_target_pairs={{0,16},{4,12},{8,24},{12,4},{16,0},{20,28},{24,8},{28,20},{1,17},{... | collective-permute-start | bytes 768008 | tf_op jit(solution)/shard_map/ppermute | solution.py:398
  50.3 1.0 %collective-permute-done.19 = f16[200,640]{1,0:T(8,128)(2,1)S(1)} collective-permute-done((f16[200,640]{1,0:T(8,128)(2,1)S(1)}, f16[200,640]{1,0:T(8,128)(2,1)S(1)}, u32[]{:S(2)}, u32[]{:S(2)}) %collective-permute-start.19) | collective-permute-done | bytes 256032 | tf_op jit(solution)/shard_map/ppermute | solution.py:398
  51.4 0.3 select_convert_fusion.2
  51.7 0.9 %collective-permute-start.23 = (f16[200,640]{1,0:T(8,128)(2,1)S(1)}, f16[200,640]{1,0:T(8,128)(2,1)S(1)}, u32[]{:S(2)}, u32[]{:S(2)}) collective-permute-start(f16[200,640]{1,0:T(8,128)(2,1)S(1)} %select_convert_fusion.2), channel_id=1, source_target_pairs={{0,16},{4,12},{8,24},{12,4},{16,0},{20,28},{24,8},{28,20},{1,17},{... | collective-permute-start | bytes 768008 | tf_op jit(solution)/shard_map/ppermute | solution.py:398
  52.6 0.8 %end.1 = f32[16,1024]{1,0:T(8,128)} custom-call(s32[8,1024]{1,0:T(8,128)S(1)} %iota.185.info, f32[16,1024]{1,0:T(8,128)S(1)} %get-tuple-element.201.adjoint_ref, f32[8,1024]{1,0:T(8,128)S(1)} %get-tuple-element.131.weight_ref, f32[8,1024]{1,0:T(8,128)S(1)} %get-tuple-element.150.sums_ref, f32[64,1024]{1,0:T(8,128)S(1)} %get-tuple-element.202.back_ref, ...), custom_call_target="tpu_custom_call" | custom-call | tf_op jit(solution)/shard_map/end/pallas_call | solution.py:384
  53.4 2.4 %collective-permute-done.18 = f16[200,640]{1,0:T(8,128)(2,1)S(1)} collective-permute-done((f16[200,640]{1,0:T(8,128)(2,1)S(1)}, f16[200,640]{1,0:T(8,128)(2,1)S(1)}, u32[]{:S(2)}, u32[]{:S(2)}) %collective-permute-start.18) | collective-permute-done | bytes 256032 | tf_op jit(solution)/shard_map/ppermute | solution.py:398
  56.0 0.8 %select_convert_fusion.1 = f16[200,640]{1,0:T(8,128)(2,1)S(1)} fusion(f16[200,640]{1,0:T(8,128)(2,1)S(1)} %collective-permute-done.18, f16[200,640]{1,0:T(8,128)(2,1)S(1)} %select_convert_fusion.3, f32[640]{0:T(1024)S(1)} %get-tuple-element.235, f32[640]{0:T(1024)S(1)} %get-tuple-element.236, f32[640]{0:T(1024)S(1)} %get-tuple-element.237, ...), kind=kLoop, calls=%fused_computation.1 | loop fusion | flops 2048000 | bytes 800120 | tf_op jit(solution)/shard_map/convert_element_type | solution.py:422
  56.8 0.1 collective-permute-start.24
  56.8 1.7 %collective-permute-done.23 = f16[200,640]{1,0:T(8,128)(2,1)S(1)} collective-permute-done((f16[200,640]{1,0:T(8,128)(2,1)S(1)}, f16[200,640]{1,0:T(8,128)(2,1)S(1)}, u32[]{:S(2)}, u32[]{:S(2)}) %collective-permute-start.23) | collective-permute-done | bytes 256032 | tf_op jit(solution)/shard_map/ppermute | solution.py:398
  58.7 0.3 fusion.29
  59.0 0.1 collective-permute-start.25
  59.1 1.6 %first_finish.1 = (f32[640,640]{1,0:T(8,128)}, f32[64,640]{1,0:T(8,128)}, f32[64,640]{1,0:T(8,128)}, f32[640]{0:T(1024)}, f32[640]{0:T(1024)}, /*index=5*/f32[64]{0:T(128)}) custom-call(s32[8,1024]{1,0:T(8,128)S(1)} %iota.185.info, f32[200,640]{1,0:T(8,128)S(1)} %convert_element_type.125.own, f32[200,640]{1,0:T(8,128)S(1)} %convert_element_type.126.other), custom_call_target="tpu_custom_call" | custom-call | tf_op jit(solution)/shard_map/first_finish/pallas_call | solution.py:623
  60.8 1.0 %second_finish.1 = f32[640,640]{1,0:T(8,128)} custom-call(s32[8,1024]{1,0:T(8,128)S(1)} %iota.185.info, f32[200,640]{1,0:T(8,128)S(1)} %get-tuple-element.266.own, f32[200,640]{1,0:T(8,128)S(1)} %convert_element_type.135.other, f32[640,640]{1,0:T(8,128)} %get-tuple-element.218.begun_ref), custom_call_target="tpu_custom_call", output_to_operand_aliasing={{}: (3, {})} | custom-call | tf_op jit(solution)/shard_map/second_finish/pallas_call | solution.py:632
  (54 shorter events, 0.8 us)
Async XLA Ops:
  0.6 11.8 %collective-permute-start = (f32[16,1024]{1,0:T(8,128)}, f32[16,1024]{1,0:T(8,128)S(1)}, u32[]{:S(2)}, u32[]{:S(2)}) collective-permute-start(f32[16,1024]{1,0:T(8,128)} %bitcast.14), channel_id=1, source_target_pairs={{0,1},{1,0},{2,3},{3,2},{4,5},{5,4},{6,7},{7,6},{8,9},{9,8},{10,11... | collective-permute-start | bytes 196616 | tf_op jit(solution)/shard_map/ppermute | solution.py:398
  3.7 8.7 %collective-permute-start.1 = (f32[16,1024]{1,0:T(8,128)}, f32[16,1024]{1,0:T(8,128)S(1)}, u32[]{:S(2)}, u32[]{:S(2)}) collective-permute-start(f32[16,1024]{1,0:T(8,128)} %bitcast.15), channel_id=1, source_target_pairs={{0,2},{1,3},{2,0},{3,1},{4,6},{5,7},{6,4},{7,5},{8,10},{9,11},{10,... | collective-permute-start | bytes 196616 | tf_op jit(solution)/shard_map/ppermute | solution.py:398
  6.3 7.0 %collective-permute-start.2 = (f32[16,1024]{1,0:T(8,128)}, f32[16,1024]{1,0:T(8,128)S(1)}, u32[]{:S(2)}, u32[]{:S(2)}) collective-permute-start(f32[16,1024]{1,0:T(8,128)} %bitcast.16), channel_id=1, source_target_pairs={{0,3},{1,2},{2,1},{3,0},{4,7},{5,6},{6,5},{7,4},{8,11},{9,10},{10,... | collective-permute-start | bytes 196616 | tf_op jit(solution)/shard_map/ppermute | solution.py:398
  8.0 7.4 %collective-permute-start.3 = (f32[16,1024]{1,0:T(8,128)}, f32[16,1024]{1,0:T(8,128)S(1)}, u32[]{:S(2)}, u32[]{:S(2)}) collective-permute-start(f32[16,1024]{1,0:T(8,128)} %bitcast.8), channel_id=1, source_target_pairs={{0,1},{1,0},{2,3},{3,2},{4,5},{5,4},{6,7},{7,6},{8,9},{9,8},{10,11... | collective-permute-start | bytes 196616 | tf_op jit(solution)/shard_map/ppermute | solution.py:398
  9.0 10.6 %collective-permute-start.4 = (f32[16,1024]{1,0:T(8,128)}, f32[16,1024]{1,0:T(8,128)S(1)}, u32[]{:S(2)}, u32[]{:S(2)}) collective-permute-start(f32[16,1024]{1,0:T(8,128)} %bitcast.9), channel_id=1, source_target_pairs={{0,2},{1,3},{2,0},{3,1},{4,6},{5,7},{6,4},{7,5},{8,10},{9,11},{10,... | collective-permute-start | bytes 196616 | tf_op jit(solution)/shard_map/ppermute | solution.py:398
  12.5 7.1 %collective-permute-start.5 = (f32[16,1024]{1,0:T(8,128)}, f32[16,1024]{1,0:T(8,128)S(1)}, u32[]{:S(2)}, u32[]{:S(2)}) collective-permute-start(f32[16,1024]{1,0:T(8,128)} %bitcast.10), channel_id=1, source_target_pairs={{0,3},{1,2},{2,1},{3,0},{4,7},{5,6},{6,5},{7,4},{8,11},{9,10},{10,... | collective-permute-start | bytes 196616 | tf_op jit(solution)/shard_map/ppermute | solution.py:398
  13.8 5.8 %collective-permute-start.6 = (f32[72,128]{1,0:T(8,128)S(1)}, f32[72,128]{1,0:T(8,128)S(1)}, u32[]{:S(2)}, u32[]{:S(2)}) collective-permute-start(f32[72,128]{1,0:T(8,128)S(1)} %get-tuple-element.146), channel_id=1, source_target_pairs={{0,16},{4,20},{8,24},{12,28},{16,0},{20,4},{24,8},{28,12},{1,17},{... | collective-permute-start | bytes 110600 | tf_op jit(solution)/shard_map/ppermute | solution.py:486
  15.4 4.2 %collective-permute-start.7 = (f32[72,128]{1,0:T(8,128)S(1)}, f32[72,128]{1,0:T(8,128)S(1)}, u32[]{:S(2)}, u32[]{:S(2)}) collective-permute-start(f32[72,128]{1,0:T(8,128)S(1)} %get-tuple-element.147), channel_id=1, source_target_pairs={{0,4},{4,0},{8,12},{12,8},{16,20},{20,16},{24,28},{28,24},{1,5},{5... | collective-permute-start | bytes 110600 | tf_op jit(solution)/shard_map/ppermute | solution.py:486
  15.4 4.4 %collective-permute-start.8 = (f32[72,128]{1,0:T(8,128)S(1)}, f32[72,128]{1,0:T(8,128)S(1)}, u32[]{:S(2)}, u32[]{:S(2)}) collective-permute-start(f32[72,128]{1,0:T(8,128)S(1)} %get-tuple-element.148), channel_id=1, source_target_pairs={{0,28},{4,8},{8,4},{12,16},{16,12},{20,24},{24,20},{28,0},{1,29},{... | collective-permute-start | bytes 110600 | tf_op jit(solution)/shard_map/ppermute | solution.py:486
  20.9 5.7 %collective-permute-start.10 = (f32[64,128]{1,0:T(8,128)S(1)}, f32[64,128]{1,0:T(8,128)S(1)}, u32[]{:S(2)}, u32[]{:S(2)}) collective-permute-start(f32[64,128]{1,0:T(8,128)S(1)} %get-tuple-element.153), channel_id=1, source_target_pairs={{0,4},{4,0},{8,12},{12,8},{16,20},{20,16},{24,28},{28,24},{1,5},{5... | collective-permute-start | bytes 98312 | tf_op jit(solution)/shard_map/ppermute | solution.py:486
  21.0 5.6 %collective-permute-start.11 = (f32[64,128]{1,0:T(8,128)S(1)}, f32[64,128]{1,0:T(8,128)S(1)}, u32[]{:S(2)}, u32[]{:S(2)}) collective-permute-start(f32[64,128]{1,0:T(8,128)S(1)} %get-tuple-element.154), channel_id=1, source_target_pairs={{0,28},{4,8},{8,4},{12,16},{16,12},{20,24},{24,20},{28,0},{1,29},{... | collective-permute-start | bytes 98312 | tf_op jit(solution)/shard_map/ppermute | solution.py:486
  22.5 4.1 %collective-permute-start.9 = (f32[64,128]{1,0:T(8,128)S(1)}, f32[64,128]{1,0:T(8,128)S(1)}, u32[]{:S(2)}, u32[]{:S(2)}) collective-permute-start(f32[64,128]{1,0:T(8,128)S(1)} %get-tuple-element.152), channel_id=1, source_target_pairs={{0,16},{4,20},{8,24},{12,28},{16,0},{20,4},{24,8},{28,12},{1,17},{... | collective-permute-start | bytes 98312 | tf_op jit(solution)/shard_map/ppermute | solution.py:486
  24.0 2.6 %copy-start = (f32[2,8,1024]{2,1,0:T(8,128)S(1)}, f32[2,8,1024]{2,1,0:T(8,128)}, u32[]{:S(2)}) copy-start(f32[2,8,1024]{2,1,0:T(8,128)} %param.11) | copy-start | bytes 196612
  28.2 6.4 %collective-permute-start.12 = (f32[64,128]{1,0:T(8,128)S(1)}, f32[64,128]{1,0:T(8,128)S(1)}, u32[]{:S(2)}, u32[]{:S(2)}) collective-permute-start(f32[64,128]{1,0:T(8,128)S(1)} %get-tuple-element.167), channel_id=1, source_target_pairs={{0,16},{4,20},{8,24},{12,28},{16,0},{20,4},{24,8},{28,12},{1,17},{... | collective-permute-start | bytes 98312 | tf_op jit(solution)/shard_map/ppermute | solution.py:486
  29.5 5.2 %collective-permute-start.13 = (f32[64,128]{1,0:T(8,128)S(1)}, f32[64,128]{1,0:T(8,128)S(1)}, u32[]{:S(2)}, u32[]{:S(2)}) collective-permute-start(f32[64,128]{1,0:T(8,128)S(1)} %get-tuple-element.168), channel_id=1, source_target_pairs={{0,4},{4,0},{8,12},{12,8},{16,20},{20,16},{24,28},{28,24},{1,5},{5... | collective-permute-start | bytes 98312 | tf_op jit(solution)/shard_map/ppermute | solution.py:486
  29.5 5.2 %collective-permute-start.14 = (f32[64,128]{1,0:T(8,128)S(1)}, f32[64,128]{1,0:T(8,128)S(1)}, u32[]{:S(2)}, u32[]{:S(2)}) collective-permute-start(f32[64,128]{1,0:T(8,128)S(1)} %get-tuple-element.169), channel_id=1, source_target_pairs={{0,28},{4,8},{8,4},{12,16},{16,12},{20,24},{24,20},{28,0},{1,29},{... | collective-permute-start | bytes 98312 | tf_op jit(solution)/shard_map/ppermute | solution.py:486
  39.7 2.0 %collective-permute-start.16 = (f32[200,640]{1,0:T(8,128)S(1)}, f32[200,640]{1,0:T(8,128)S(1)}, u32[]{:S(2)}, u32[]{:S(2)}) collective-permute-start(f32[200,640]{1,0:T(8,128)S(1)} %get-tuple-element.183), channel_id=1, source_target_pairs={{0,4},{4,0},{8,12},{12,8},{16,20},{20,16},{24,28},{28,24},{1,5},{5... | collective-permute-start | bytes 1536008 | tf_op jit(solution)/shard_map/ppermute | solution.py:398
  39.8 3.3 %collective-permute-start.15 = (f32[200,640]{1,0:T(8,128)S(1)}, f32[200,640]{1,0:T(8,128)S(1)}, u32[]{:S(2)}, u32[]{:S(2)}) collective-permute-start(f32[200,640]{1,0:T(8,128)S(1)} %get-tuple-element.181), channel_id=1, source_target_pairs={{0,4},{4,0},{8,12},{12,8},{16,20},{20,16},{24,28},{28,24},{1,5},{5... | collective-permute-start | bytes 1536008 | tf_op jit(solution)/shard_map/ppermute | solution.py:398
  42.1 6.4 %collective-permute-start.17 = (f16[200,640]{1,0:T(8,128)(2,1)S(1)}, f16[200,640]{1,0:T(8,128)(2,1)S(1)}, u32[]{:S(2)}, u32[]{:S(2)}) collective-permute-start(f16[200,640]{1,0:T(8,128)(2,1)S(1)} %select_convert_fusion.5), channel_id=1, source_target_pairs={{0,8},{4,20},{8,0},{12,28},{16,24},{20,4},{24,16},{28,12},{1,9},{5... | collective-permute-start | bytes 768008 | tf_op jit(solution)/shard_map/ppermute | solution.py:398
  43.4 7.9 %collective-permute-start.19 = (f16[200,640]{1,0:T(8,128)(2,1)S(1)}, f16[200,640]{1,0:T(8,128)(2,1)S(1)}, u32[]{:S(2)}, u32[]{:S(2)}) collective-permute-start(f16[200,640]{1,0:T(8,128)(2,1)S(1)} %select_convert_fusion.4), channel_id=1, source_target_pairs={{0,8},{4,20},{8,0},{12,28},{16,24},{20,4},{24,16},{28,12},{1,9},{5... | collective-permute-start | bytes 768008 | tf_op jit(solution)/shard_map/ppermute | solution.py:398
  44.6 5.7 %collective-permute-start.20 = (f32[16,128]{1,0:T(8,128)S(1)}, f32[16,128]{1,0:T(8,128)S(1)}, u32[]{:S(2)}, u32[]{:S(2)}) collective-permute-start(f32[16,128]{1,0:T(8,128)S(1)} %get-tuple-element.195), channel_id=1, source_target_pairs={{0,16},{4,20},{8,24},{12,28},{16,0},{20,4},{24,8},{28,12},{1,17},{... | collective-permute-start | bytes 24584 | tf_op jit(solution)/shard_map/ppermute | solution.py:486
  45.4 4.9 %collective-permute-start.21 = (f32[16,128]{1,0:T(8,128)S(1)}, f32[16,128]{1,0:T(8,128)S(1)}, u32[]{:S(2)}, u32[]{:S(2)}) collective-permute-start(f32[16,128]{1,0:T(8,128)S(1)} %get-tuple-element.196), channel_id=1, source_target_pairs={{0,4},{4,0},{8,12},{12,8},{16,20},{20,16},{24,28},{28,24},{1,5},{5... | collective-permute-start | bytes 24584 | tf_op jit(solution)/shard_map/ppermute | solution.py:486
  45.4 4.9 %collective-permute-start.22 = (f32[16,128]{1,0:T(8,128)S(1)}, f32[16,128]{1,0:T(8,128)S(1)}, u32[]{:S(2)}, u32[]{:S(2)}) collective-permute-start(f32[16,128]{1,0:T(8,128)S(1)} %get-tuple-element.197), channel_id=1, source_target_pairs={{0,28},{4,8},{8,4},{12,16},{16,12},{20,24},{24,20},{28,0},{1,29},{... | collective-permute-start | bytes 24584 | tf_op jit(solution)/shard_map/ppermute | solution.py:486
  49.4 6.4 %collective-permute-start.18 = (f16[200,640]{1,0:T(8,128)(2,1)S(1)}, f16[200,640]{1,0:T(8,128)(2,1)S(1)}, u32[]{:S(2)}, u32[]{:S(2)}) collective-permute-start(f16[200,640]{1,0:T(8,128)(2,1)S(1)} %select_convert_fusion.3), channel_id=1, source_target_pairs={{0,16},{4,12},{8,24},{12,4},{16,0},{20,28},{24,8},{28,20},{1,17},{... | collective-permute-start | bytes 768008 | tf_op jit(solution)/shard_map/ppermute | solution.py:398
  51.7 6.9 %collective-permute-start.23 = (f16[200,640]{1,0:T(8,128)(2,1)S(1)}, f16[200,640]{1,0:T(8,128)(2,1)S(1)}, u32[]{:S(2)}, u32[]{:S(2)}) collective-permute-start(f16[200,640]{1,0:T(8,128)(2,1)S(1)} %select_convert_fusion.2), channel_id=1, source_target_pairs={{0,16},{4,12},{8,24},{12,4},{16,0},{20,28},{24,8},{28,20},{1,17},{... | collective-permute-start | bytes 768008 | tf_op jit(solution)/shard_map/ppermute | solution.py:398
  56.8 2.3 %collective-permute-start.24 = (f16[200,640]{1,0:T(8,128)(2,1)S(1)}, f16[200,640]{1,0:T(8,128)(2,1)S(1)}, u32[]{:S(2)}, u32[]{:S(2)}) collective-permute-start(f16[200,640]{1,0:T(8,128)(2,1)S(1)} %select_convert_fusion.1), channel_id=1, source_target_pairs={{0,4},{4,0},{8,12},{12,8},{16,20},{20,16},{24,28},{28,24},{1,5},{5... | collective-permute-start | bytes 768008 | tf_op jit(solution)/shard_map/ppermute | solution.py:398
  59.0 1.8 %collective-permute-start.25 = (f16[200,640]{1,0:T(8,128)(2,1)S(1)}, f16[200,640]{1,0:T(8,128)(2,1)S(1)}, u32[]{:S(2)}, u32[]{:S(2)}) collective-permute-start(f16[200,640]{1,0:T(8,128)(2,1)S(1)} %get-tuple-element.267), channel_id=1, source_target_pairs={{0,4},{4,0},{8,12},{12,8},{16,20},{20,16},{24,28},{28,24},{1,5},{5... | collective-permute-start | bytes 768008 | tf_op jit(solution)/shard_map/ppermute | solution.py:398

commit v10 on v9

--- a/solution.py
+++ b/solution.py
@@ -372,6 +372,12 @@
     return jax.ShapeDtypeStruct(shape, dtype)
 
 
+def adjoint_backward_kernel(depths, info, *refs):
+    upstream, held = refs[-2:]
+    adjoint_kernel(depths, info, *refs[:7], refs[21], upstream, *refs[22:25], held)
+    last_backward_kernel(info, refs[7], upstream, *refs[8:21], *refs[25:-2])
+
+
 def closure_cost(passes):
     width = 640
     macs = TILE_CELLS * width * (2 * FEATURES + width) * passes
@@ -578,24 +584,18 @@
         name="first_backward",
         passes=2,
     )
-    adjoint, upstream, *edges = called(
-        functools.partial(adjoint_kernel, depths),
-        (own_field, half_field, own_edge, own_edge, own_edge),
-        info,
-        (adjoint, weight, weight_sums, back, *edges),
-        scratch=[whole],
-        name="adjoint",
-    )
     all_parts = block_parts(width)
     blocks = [spec_of((sum(parts) + 8, width)) for parts in all_parts]
-    back, *blocks = called(
-        last_backward_kernel,
-        (field, *blocks, *blocks),
+    adjoint, *outs = called(
+        functools.partial(adjoint_backward_kernel, depths),
+        (own_field, own_edge, own_edge, own_edge, field, *blocks, *blocks),
         info,
-        (state_0, upstream, *cache_0, w_in, w_mid, w_out_t, *parts),
-        name="last_backward",
+        (adjoint, weight, weight_sums, back, *edges, state_0, *cache_0, w_in, w_mid, w_out_t, *parts),
+        scratch=[pltpu.VMEM((FEATURES, TILE_CELLS), jnp.bfloat16), whole],
+        name="adjoint_backward",
         passes=2,
     )
+    edges, back, blocks = outs[:3], outs[3], outs[4:]
     kept, sent = blocks[:2], blocks[2:]
     scale = 1.0 / (tiles * TILE_CELLS)
 

time: 62.2 us -> 62.1 us (level)
    pallas_call x10 -> x9, Pallas kernels: 19.6 us -> 19.5 us  [called(): pl.pallas_call(kernel, out_shape=tuple(outs), in_specs=in_specs, out_spec...]
where the time goes in v10:
time: 62.1 us; the launch traced here: 61.9 us
  starting transfers between devices  26.1 us (42%)
  Pallas kernels  22.2 us (36%)
  waiting for transfers between devices  8.9 us (14%)
  other arithmetic  3.03 us (5%)
  between operations  1.22 us (2%)
    pallas_call x9, Pallas kernels, called(): pl.pallas_call(kernel, out_shape=tuple(outs), in_specs=in_specs, out_spec...  19.5 us
    ppermute x14, starting transfers between devices, swapped(): lax.ppermute(x, axis, [(i, i ^ (odd_bit if i & 1 else even_bit)) for i in...  14.8 us
    ppermute x12, starting transfers between devices, exchanged(): lax.ppermute(edge, 'tile', way)  11.3 us
    ppermute x14, waiting for transfers between devices, swapped(): lax.ppermute(x, axis, [(i, i ^ (odd_bit if i & 1 else even_bit)) for i in...  8.65 us
    convert_element_type x5, other arithmetic, with_exponents(): return out.astype(jnp.float16)  2.4 us
    pallas_call x1, Pallas kernels, body(): pl.pallas_call(functools.partial(first_finish_kernel, scale), out_shape=(...  1.64 us
  transfers between devices with their start and end apart: 26, of which 7 were waited for; matrix products, arithmetic and copies ran while one was open for 6% of the time, Pallas kernels for 22%

profile of v10, /device:TPU:0, one launch (start us, length us, event | category | flops | bytes accessed | tf_op | source)
XLA Modules:
  0.0 61.9 jit_solution(18116291287025129838)
XLA Ops:
  0.6 3.1 %collective-permute-start = (f32[16,1024]{1,0:T(8,128)}, f32[16,1024]{1,0:T(8,128)S(1)}, u32[]{:S(2)}, u32[]{:S(2)}) collective-permute-start(f32[16,1024]{1,0:T(8,128)} %bitcast.14), channel_id=1, source_target_pairs={{0,1},{1,0},{2,3},{3,2},{4,5},{5,4},{6,7},{7,6},{8,9},{9,8},{10,11... | collective-permute-start | bytes 196616 | tf_op jit(solution)/shard_map/ppermute | solution.py:404
  3.7 2.6 %collective-permute-start.1 = (f32[16,1024]{1,0:T(8,128)}, f32[16,1024]{1,0:T(8,128)S(1)}, u32[]{:S(2)}, u32[]{:S(2)}) collective-permute-start(f32[16,1024]{1,0:T(8,128)} %bitcast.15), channel_id=1, source_target_pairs={{0,2},{1,3},{2,0},{3,1},{4,6},{5,7},{6,4},{7,5},{8,10},{9,11},{10,... | collective-permute-start | bytes 196616 | tf_op jit(solution)/shard_map/ppermute | solution.py:404
  6.3 1.7 %prepare.1 = (f32[8,1024]{1,0:T(8,128)S(1)}, f32[16,1024]{1,0:T(8,128)S(1)}, f32[1,640]{1,0:T(1,128)S(1)}, f32[1,640]{1,0:T(1,128)S(1)}, f32[64,128]{1,0:T(8,128...) custom-call(f32[1,1024]{1,0:T(1,128)} %bitcast.18, ...), custom_call_target="tpu_custom_call" | custom-call | tf_op jit(solution)/shard_map/prepare/pallas_call | solution.py:390
  8.0 1.0 %collective-permute-start.3 = (f32[16,1024]{1,0:T(8,128)}, f32[16,1024]{1,0:T(8,128)S(1)}, u32[]{:S(2)}, u32[]{:S(2)}) collective-permute-start(f32[16,1024]{1,0:T(8,128)} %bitcast.8), channel_id=1, source_target_pairs={{0,1},{1,0},{2,3},{3,2},{4,5},{5,4},{6,7},{7,6},{8,9},{9,8},{10,11... | collective-permute-start | bytes 196616 | tf_op jit(solution)/shard_map/ppermute | solution.py:404
  9.0 3.5 %collective-permute-start.4 = (f32[16,1024]{1,0:T(8,128)}, f32[16,1024]{1,0:T(8,128)S(1)}, u32[]{:S(2)}, u32[]{:S(2)}) collective-permute-start(f32[16,1024]{1,0:T(8,128)} %bitcast.9), channel_id=1, source_target_pairs={{0,2},{1,3},{2,0},{3,1},{4,6},{5,7},{6,4},{7,5},{8,10},{9,11},{10,... | collective-permute-start | bytes 196616 | tf_op jit(solution)/shard_map/ppermute | solution.py:404
  12.5 0.8 %collective-permute-done.2.refs_3_ = f32[16,1024]{1,0:T(8,128)S(1)} collective-permute-done((f32[16,1024]{1,0:T(8,128)}, f32[16,1024]{1,0:T(8,128)S(1)}, u32[]{:S(2)}, u32[]{:S(2)}) %collective-permute-start.2) | collective-permute-done | bytes 65568 | tf_op jit(solution)/shard_map/ppermute | solution.py:404
  13.3 0.1 iota.185.info
  13.4 0.4 gather.1
  13.8 1.6 %collective-permute-start.6 = (f32[72,128]{1,0:T(8,128)S(1)}, f32[72,128]{1,0:T(8,128)S(1)}, u32[]{:S(2)}, u32[]{:S(2)}) collective-permute-start(f32[72,128]{1,0:T(8,128)S(1)} %get-tuple-element.145), channel_id=1, source_target_pairs={{0,16},{4,20},{8,24},{12,28},{16,0},{20,4},{24,8},{28,12},{1,17},{... | collective-permute-start | bytes 110600 | tf_op jit(solution)/shard_map/ppermute | solution.py:492
  15.4 1.5 %collective-permute-start.8 = (f32[72,128]{1,0:T(8,128)S(1)}, f32[72,128]{1,0:T(8,128)S(1)}, u32[]{:S(2)}, u32[]{:S(2)}) collective-permute-start(f32[72,128]{1,0:T(8,128)S(1)} %get-tuple-element.147), channel_id=1, source_target_pairs={{0,28},{4,8},{8,4},{12,16},{16,12},{20,24},{24,20},{28,0},{1,29},{... | collective-permute-start | bytes 110600 | tf_op jit(solution)/shard_map/ppermute | solution.py:492
  17.0 2.6 %closure.2 = (f32[64,1024]{1,0:T(8,128)S(1)}, bf16[1024,640]{1,0:T(8,128)(2,1)S(1)}, f32[1024,640]{1,0:T(8,128)S(1)}, bf16[1024,640]{1,0:T(8,128)(2,1)S(1)}, f32[1024,640]{1,0:T(8,128)S(1)}) custom-call(f32[64,1024]{1,0:T(8,128)S(1)} %get-tuple-element.135.state_ref.refs_7_, bf16[64,640]{1,0:T(8,128)(2,1)S(1)} %get-tuple-element.136.w_in.refs_12_, ...), custom_call_target="tpu_custom_call" | custom-call | flops 1006632960 | bytes 5242880 | tf_op jit(solution)/shard_map/closure/pallas_call | solution.py:390
  19.6 0.2 collective-permute-done.8.e2
  19.8 1.1 %step.1 = (f32[64,1024]{1,0:T(8,128)S(1)}, f32[8,1024]{1,0:T(8,128)S(1)}, f32[64,128]{1,0:T(8,128)S(1)}, f32[64,128]{1,0:T(8,128)S(1)}, f32[64,128]{1,0:T(8,128)S(1)}) custom-call(s32[8,1024]{1,0:T(8,128)S(1)} %iota.185.info, f32[64,1024]{1,0:T(8,128)S(1)} %get-tuple-element.135.state_ref.refs_7_, f32[8,1024]{1,0:T(8,128)S(1)} %get-tuple-element.130.weight_ref.refs_1_, ...), custom_call_target="tpu_custom_call" | custom-call | tf_op jit(solution)/shard_map/step/pallas_call | solution.py:390
  20.9 0.1 collective-permute-start.10
  21.0 1.5 %collective-permute-start.11 = (f32[64,128]{1,0:T(8,128)S(1)}, f32[64,128]{1,0:T(8,128)S(1)}, u32[]{:S(2)}, u32[]{:S(2)}) collective-permute-start(f32[64,128]{1,0:T(8,128)S(1)} %get-tuple-element.153), channel_id=1, source_target_pairs={{0,28},{4,8},{8,4},{12,16},{16,12},{20,24},{24,20},{28,0},{1,29},{... | collective-permute-start | bytes 98312 | tf_op jit(solution)/shard_map/ppermute | solution.py:492
  22.5 1.5 %collective-permute-start.9 = (f32[64,128]{1,0:T(8,128)S(1)}, f32[64,128]{1,0:T(8,128)S(1)}, u32[]{:S(2)}, u32[]{:S(2)}) collective-permute-start(f32[64,128]{1,0:T(8,128)S(1)} %get-tuple-element.151), channel_id=1, source_target_pairs={{0,16},{4,20},{8,24},{12,28},{16,0},{20,4},{24,8},{28,12},{1,17},{... | collective-permute-start | bytes 98312 | tf_op jit(solution)/shard_map/ppermute | solution.py:492
  24.0 2.6 %closure.3 = (f32[64,1024]{1,0:T(8,128)S(1)}, bf16[1024,640]{1,0:T(8,128)(2,1)S(1)}, f32[1024,640]{1,0:T(8,128)S(1)}, bf16[1024,640]{1,0:T(8,128)(2,1)S(1)}, f32[1024,640]{1,0:T(8,128)S(1)}) custom-call(f32[64,1024]{1,0:T(8,128)S(1)} %get-tuple-element.148.state_ref, bf16[64,640]{1,0:T(8,128)(2,1)S(1)} %get-tuple-element.136.w_in.refs_12_, ...), custom_call_target="tpu_custom_call" | custom-call | flops 1006632960 | bytes 5242880 | tf_op jit(solution)/shard_map/closure/pallas_call | solution.py:390
  26.6 1.6 %last_step.1 = (f32[16,1024]{1,0:T(8,128)}, f32[64,1024]{1,0:T(8,128)S(1)}, bf16[64,1024]{1,0:T(8,128)(2,1)S(1)}, f32[64,128]{1,0:T(8,128)S(1)}, f32[64,128]{1,0:T(8,128)S(1)}, /*index=5*/f32[64,128]{1,0:T(8,128)S(1)}) custom-call(s32[8,1024]{1,0:T(8,128)S(1)} %iota.185.info, f32[64,1024]{1,0:T(8,128)S(1)} %get-tuple-element.148.state_ref, ...), custom_call_target="tpu_custom_call" | custom-call | tf_op jit(solution)/shard_map/last_step/pallas_call | solution.py:390
  28.2 1.3 %collective-permute-start.12 = (f32[64,128]{1,0:T(8,128)S(1)}, f32[64,128]{1,0:T(8,128)S(1)}, u32[]{:S(2)}, u32[]{:S(2)}) collective-permute-start(f32[64,128]{1,0:T(8,128)S(1)} %get-tuple-element.166), channel_id=1, source_target_pairs={{0,16},{4,20},{8,24},{12,28},{16,0},{20,4},{24,8},{28,12},{1,17},{... | collective-permute-start | bytes 98312 | tf_op jit(solution)/shard_map/ppermute | solution.py:492
  29.5 1.2 %collective-permute-start.14 = (f32[64,128]{1,0:T(8,128)S(1)}, f32[64,128]{1,0:T(8,128)S(1)}, u32[]{:S(2)}, u32[]{:S(2)}) collective-permute-start(f32[64,128]{1,0:T(8,128)S(1)} %get-tuple-element.168), channel_id=1, source_target_pairs={{0,28},{4,8},{8,4},{12,16},{16,12},{20,24},{24,20},{28,0},{1,29},{... | collective-permute-start | bytes 98312 | tf_op jit(solution)/shard_map/ppermute | solution.py:492
  30.7 3.9 %first_backward.1 = (f32[64,1024]{1,0:T(8,128)S(1)}, f32[640,640]{1,0:T(8,128)S(1)}, f32[64,640]{1,0:T(8,128)S(1)}, f32[64,640]{1,0:T(8,128)S(1)}, f32[8,640]{1,...) custom-call(f32[64,1024]{1,0:T(8,128)S(1)} %get-tuple-element.148.state_ref, ...), custom_call_target="tpu_custom_call" | custom-call | flops 2013265920 | bytes 10485760 | tf_op jit(solution)/shard_map/first_backward/pallas_call | solution.py:390
  34.6 0.0 collective-permute-done.13.refs_5_
  34.7 4.9 %adjoint_backward.1 = (f32[16,1024]{1,0:T(8,128)S(1)}, f32[16,128]{1,0:T(8,128)S(1)}, f32[16,128]{1,0:T(8,128)S(1)}, f32[16,128]{1,0:T(8,128)S(1)}, f32[64,1024]...) custom-call(s32[8,1024]{1,0:T(8,128)S(1)} %iota.185.info, ...), custom_call_target="tpu_custom_call" | custom-call | flops 2013265920 | bytes 10485760 | tf_op jit(solution)/shard_map/adjoint_backward/pallas_call | solution.py:390
  39.6 0.1 collective-permute-start.16
  39.7 0.5 collective-permute-start.15
  40.3 1.3 %collective-permute-done.16 = f32[200,640]{1,0:T(8,128)S(1)} collective-permute-done((f32[200,640]{1,0:T(8,128)S(1)}, f32[200,640]{1,0:T(8,128)S(1)}, u32[]{:S(2)}, u32[]{:S(2)}) %collective-permute-start.16) | collective-permute-done | bytes 512032 | tf_op jit(solution)/shard_map/ppermute | solution.py:404
  41.6 0.1 slice_reduce_fusion.24
  41.7 0.3 select_convert_fusion.5
  42.0 1.0 %collective-permute-start.17 = (f16[200,640]{1,0:T(8,128)(2,1)S(1)}, f16[200,640]{1,0:T(8,128)(2,1)S(1)}, u32[]{:S(2)}, u32[]{:S(2)}) collective-permute-start(f16[200,640]{1,0:T(8,128)(2,1)S(1)} %select_convert_fusion.5), channel_id=1, source_target_pairs={{0,8},{4,20},{8,0},{12,28},{16,24},{20,4},{24,16},{28,12},{1,9},{5... | collective-permute-start | bytes 768008 | tf_op jit(solution)/shard_map/ppermute | solution.py:404
  43.1 0.2 select_convert_fusion.4
  43.3 1.2 %collective-permute-start.19 = (f16[200,640]{1,0:T(8,128)(2,1)S(1)}, f16[200,640]{1,0:T(8,128)(2,1)S(1)}, u32[]{:S(2)}, u32[]{:S(2)}) collective-permute-start(f16[200,640]{1,0:T(8,128)(2,1)S(1)} %select_convert_fusion.4), channel_id=1, source_target_pairs={{0,8},{4,20},{8,0},{12,28},{16,24},{20,4},{24,16},{28,12},{1,9},{5... | collective-permute-start | bytes 768008 | tf_op jit(solution)/shard_map/ppermute | solution.py:404
  44.5 0.8 %collective-permute-start.20 = (f32[16,128]{1,0:T(8,128)S(1)}, f32[16,128]{1,0:T(8,128)S(1)}, u32[]{:S(2)}, u32[]{:S(2)}) collective-permute-start(f32[16,128]{1,0:T(8,128)S(1)} %get-tuple-element.193), channel_id=1, source_target_pairs={{0,16},{4,20},{8,24},{12,28},{16,0},{20,4},{24,8},{28,12},{1,17},{... | collective-permute-start | bytes 24584 | tf_op jit(solution)/shard_map/ppermute | solution.py:492
  45.3 1.7 %collective-permute-start.22 = (f32[16,128]{1,0:T(8,128)S(1)}, f32[16,128]{1,0:T(8,128)S(1)}, u32[]{:S(2)}, u32[]{:S(2)}) collective-permute-start(f32[16,128]{1,0:T(8,128)S(1)} %get-tuple-element.195), channel_id=1, source_target_pairs={{0,28},{4,8},{8,4},{12,16},{16,12},{20,24},{24,20},{28,0},{1,29},{... | collective-permute-start | bytes 24584 | tf_op jit(solution)/shard_map/ppermute | solution.py:492
  47.0 1.4 %collective-permute-done.17 = f16[200,640]{1,0:T(8,128)(2,1)S(1)} collective-permute-done((f16[200,640]{1,0:T(8,128)(2,1)S(1)}, f16[200,640]{1,0:T(8,128)(2,1)S(1)}, u32[]{:S(2)}, u32[]{:S(2)}) %collective-permute-start.17) | collective-permute-done | bytes 256032 | tf_op jit(solution)/shard_map/ppermute | solution.py:404
  48.5 0.8 %select_convert_fusion.3 = f16[200,640]{1,0:T(8,128)(2,1)S(1)} fusion(f16[200,640]{1,0:T(8,128)(2,1)S(1)} %collective-permute-done.17, f16[200,640]{1,0:T(8,128)(2,1)S(1)} %select_convert_fusion.5, f32[640]{0:T(1024)S(1)} %get-tuple-element.249, f32[640]{0:T(1024)S(1)} %get-tuple-element.250, f32[640]{0:T(1024)S(1)} %get-tuple-element.251, ...), kind=kLoop, calls=%fused_computation.3 | loop fusion | flops 2048000 | bytes 800120 | tf_op jit(solution)/shard_map/convert_element_type | solution.py:428
  49.3 0.9 %collective-permute-start.18 = (f16[200,640]{1,0:T(8,128)(2,1)S(1)}, f16[200,640]{1,0:T(8,128)(2,1)S(1)}, u32[]{:S(2)}, u32[]{:S(2)}) collective-permute-start(f16[200,640]{1,0:T(8,128)(2,1)S(1)} %select_convert_fusion.3), channel_id=1, source_target_pairs={{0,16},{4,12},{8,24},{12,4},{16,0},{20,28},{24,8},{28,20},{1,17},{... | collective-permute-start | bytes 768008 | tf_op jit(solution)/shard_map/ppermute | solution.py:404
  50.2 1.0 %collective-permute-done.19 = f16[200,640]{1,0:T(8,128)(2,1)S(1)} collective-permute-done((f16[200,640]{1,0:T(8,128)(2,1)S(1)}, f16[200,640]{1,0:T(8,128)(2,1)S(1)}, u32[]{:S(2)}, u32[]{:S(2)}) %collective-permute-start.19) | collective-permute-done | bytes 256032 | tf_op jit(solution)/shard_map/ppermute | solution.py:404
  51.3 0.3 select_convert_fusion.2
  51.6 0.9 %collective-permute-start.23 = (f16[200,640]{1,0:T(8,128)(2,1)S(1)}, f16[200,640]{1,0:T(8,128)(2,1)S(1)}, u32[]{:S(2)}, u32[]{:S(2)}) collective-permute-start(f16[200,640]{1,0:T(8,128)(2,1)S(1)} %select_convert_fusion.2), channel_id=1, source_target_pairs={{0,16},{4,12},{8,24},{12,4},{16,0},{20,28},{24,8},{28,20},{1,17},{... | collective-permute-start | bytes 768008 | tf_op jit(solution)/shard_map/ppermute | solution.py:404
  52.5 0.8 %end.1 = f32[16,1024]{1,0:T(8,128)} custom-call(s32[8,1024]{1,0:T(8,128)S(1)} %iota.185.info, f32[16,1024]{1,0:T(8,128)S(1)} %get-tuple-element.199.adjoint_ref, f32[8,1024]{1,0:T(8,128)S(1)} %get-tuple-element.130.weight_ref.refs_1_, f32[8,1024]{1,0:T(8,128)S(1)} %get-tuple-element.149.sums_ref.refs_2_, f32[64,1024]{1,0:T(8,128)S(1)} %get-tuple-element.200.back_ref, ...), custom_call_target="tpu_custom_call" | custom-call | tf_op jit(solution)/shard_map/end/pallas_call | solution.py:390
  53.3 2.4 %collective-permute-done.18 = f16[200,640]{1,0:T(8,128)(2,1)S(1)} collective-permute-done((f16[200,640]{1,0:T(8,128)(2,1)S(1)}, f16[200,640]{1,0:T(8,128)(2,1)S(1)}, u32[]{:S(2)}, u32[]{:S(2)}) %collective-permute-start.18) | collective-permute-done | bytes 256032 | tf_op jit(solution)/shard_map/ppermute | solution.py:404
  55.9 0.8 %select_convert_fusion.1 = f16[200,640]{1,0:T(8,128)(2,1)S(1)} fusion(f16[200,640]{1,0:T(8,128)(2,1)S(1)} %collective-permute-done.18, f16[200,640]{1,0:T(8,128)(2,1)S(1)} %select_convert_fusion.3, f32[640]{0:T(1024)S(1)} %get-tuple-element.233, f32[640]{0:T(1024)S(1)} %get-tuple-element.234, f32[640]{0:T(1024)S(1)} %get-tuple-element.235, ...), kind=kLoop, calls=%fused_computation.1 | loop fusion | flops 2048000 | bytes 800120 | tf_op jit(solution)/shard_map/convert_element_type | solution.py:428
  56.7 0.1 collective-permute-start.24
  56.7 1.7 %collective-permute-done.23 = f16[200,640]{1,0:T(8,128)(2,1)S(1)} collective-permute-done((f16[200,640]{1,0:T(8,128)(2,1)S(1)}, f16[200,640]{1,0:T(8,128)(2,1)S(1)}, u32[]{:S(2)}, u32[]{:S(2)}) %collective-permute-start.23) | collective-permute-done | bytes 256032 | tf_op jit(solution)/shard_map/ppermute | solution.py:404
  58.6 0.3 fusion.29
  58.9 0.1 collective-permute-start.25
  59.0 1.6 %first_finish.1 = (f32[640,640]{1,0:T(8,128)}, f32[64,640]{1,0:T(8,128)}, f32[64,640]{1,0:T(8,128)}, f32[640]{0:T(1024)}, f32[640]{0:T(1024)}, /*index=5*/f32[64]{0:T(128)}) custom-call(s32[8,1024]{1,0:T(8,128)S(1)} %iota.185.info, f32[200,640]{1,0:T(8,128)S(1)} %convert_element_type.125.own, f32[200,640]{1,0:T(8,128)S(1)} %convert_element_type.126.other), custom_call_target="tpu_custom_call" | custom-call | tf_op jit(solution)/shard_map/first_finish/pallas_call | solution.py:623
  60.7 1.0 %second_finish.1 = f32[640,640]{1,0:T(8,128)} custom-call(s32[8,1024]{1,0:T(8,128)S(1)} %iota.185.info, f32[200,640]{1,0:T(8,128)S(1)} %get-tuple-element.264.own, f32[200,640]{1,0:T(8,128)S(1)} %convert_element_type.135.other, f32[640,640]{1,0:T(8,128)} %get-tuple-element.216.begun_ref), custom_call_target="tpu_custom_call", output_to_operand_aliasing={{}: (3, {})} | custom-call | tf_op jit(solution)/shard_map/second_finish/pallas_call | solution.py:632
  (53 shorter events, 0.8 us)
Async XLA Ops:
  0.6 11.8 %collective-permute-start = (f32[16,1024]{1,0:T(8,128)}, f32[16,1024]{1,0:T(8,128)S(1)}, u32[]{:S(2)}, u32[]{:S(2)}) collective-permute-start(f32[16,1024]{1,0:T(8,128)} %bitcast.14), channel_id=1, source_target_pairs={{0,1},{1,0},{2,3},{3,2},{4,5},{5,4},{6,7},{7,6},{8,9},{9,8},{10,11... | collective-permute-start | bytes 196616 | tf_op jit(solution)/shard_map/ppermute | solution.py:404
  3.7 8.7 %collective-permute-start.1 = (f32[16,1024]{1,0:T(8,128)}, f32[16,1024]{1,0:T(8,128)S(1)}, u32[]{:S(2)}, u32[]{:S(2)}) collective-permute-start(f32[16,1024]{1,0:T(8,128)} %bitcast.15), channel_id=1, source_target_pairs={{0,2},{1,3},{2,0},{3,1},{4,6},{5,7},{6,4},{7,5},{8,10},{9,11},{10,... | collective-permute-start | bytes 196616 | tf_op jit(solution)/shard_map/ppermute | solution.py:404
  6.3 7.0 %collective-permute-start.2 = (f32[16,1024]{1,0:T(8,128)}, f32[16,1024]{1,0:T(8,128)S(1)}, u32[]{:S(2)}, u32[]{:S(2)}) collective-permute-start(f32[16,1024]{1,0:T(8,128)} %bitcast.16), channel_id=1, source_target_pairs={{0,3},{1,2},{2,1},{3,0},{4,7},{5,6},{6,5},{7,4},{8,11},{9,10},{10,... | collective-permute-start | bytes 196616 | tf_op jit(solution)/shard_map/ppermute | solution.py:404
  8.0 7.4 %collective-permute-start.3 = (f32[16,1024]{1,0:T(8,128)}, f32[16,1024]{1,0:T(8,128)S(1)}, u32[]{:S(2)}, u32[]{:S(2)}) collective-permute-start(f32[16,1024]{1,0:T(8,128)} %bitcast.8), channel_id=1, source_target_pairs={{0,1},{1,0},{2,3},{3,2},{4,5},{5,4},{6,7},{7,6},{8,9},{9,8},{10,11... | collective-permute-start | bytes 196616 | tf_op jit(solution)/shard_map/ppermute | solution.py:404
  9.0 10.6 %collective-permute-start.4 = (f32[16,1024]{1,0:T(8,128)}, f32[16,1024]{1,0:T(8,128)S(1)}, u32[]{:S(2)}, u32[]{:S(2)}) collective-permute-start(f32[16,1024]{1,0:T(8,128)} %bitcast.9), channel_id=1, source_target_pairs={{0,2},{1,3},{2,0},{3,1},{4,6},{5,7},{6,4},{7,5},{8,10},{9,11},{10,... | collective-permute-start | bytes 196616 | tf_op jit(solution)/shard_map/ppermute | solution.py:404
  12.5 7.1 %collective-permute-start.5 = (f32[16,1024]{1,0:T(8,128)}, f32[16,1024]{1,0:T(8,128)S(1)}, u32[]{:S(2)}, u32[]{:S(2)}) collective-permute-start(f32[16,1024]{1,0:T(8,128)} %bitcast.10), channel_id=1, source_target_pairs={{0,3},{1,2},{2,1},{3,0},{4,7},{5,6},{6,5},{7,4},{8,11},{9,10},{10,... | collective-permute-start | bytes 196616 | tf_op jit(solution)/shard_map/ppermute | solution.py:404
  13.8 5.8 %collective-permute-start.6 = (f32[72,128]{1,0:T(8,128)S(1)}, f32[72,128]{1,0:T(8,128)S(1)}, u32[]{:S(2)}, u32[]{:S(2)}) collective-permute-start(f32[72,128]{1,0:T(8,128)S(1)} %get-tuple-element.145), channel_id=1, source_target_pairs={{0,16},{4,20},{8,24},{12,28},{16,0},{20,4},{24,8},{28,12},{1,17},{... | collective-permute-start | bytes 110600 | tf_op jit(solution)/shard_map/ppermute | solution.py:492
  15.4 4.2 %collective-permute-start.7 = (f32[72,128]{1,0:T(8,128)S(1)}, f32[72,128]{1,0:T(8,128)S(1)}, u32[]{:S(2)}, u32[]{:S(2)}) collective-permute-start(f32[72,128]{1,0:T(8,128)S(1)} %get-tuple-element.146), channel_id=1, source_target_pairs={{0,4},{4,0},{8,12},{12,8},{16,20},{20,16},{24,28},{28,24},{1,5},{5... | collective-permute-start | bytes 110600 | tf_op jit(solution)/shard_map/ppermute | solution.py:492
  15.4 4.4 %collective-permute-start.8 = (f32[72,128]{1,0:T(8,128)S(1)}, f32[72,128]{1,0:T(8,128)S(1)}, u32[]{:S(2)}, u32[]{:S(2)}) collective-permute-start(f32[72,128]{1,0:T(8,128)S(1)} %get-tuple-element.147), channel_id=1, source_target_pairs={{0,28},{4,8},{8,4},{12,16},{16,12},{20,24},{24,20},{28,0},{1,29},{... | collective-permute-start | bytes 110600 | tf_op jit(solution)/shard_map/ppermute | solution.py:492
  20.9 5.7 %collective-permute-start.10 = (f32[64,128]{1,0:T(8,128)S(1)}, f32[64,128]{1,0:T(8,128)S(1)}, u32[]{:S(2)}, u32[]{:S(2)}) collective-permute-start(f32[64,128]{1,0:T(8,128)S(1)} %get-tuple-element.152), channel_id=1, source_target_pairs={{0,4},{4,0},{8,12},{12,8},{16,20},{20,16},{24,28},{28,24},{1,5},{5... | collective-permute-start | bytes 98312 | tf_op jit(solution)/shard_map/ppermute | solution.py:492
  21.0 5.6 %collective-permute-start.11 = (f32[64,128]{1,0:T(8,128)S(1)}, f32[64,128]{1,0:T(8,128)S(1)}, u32[]{:S(2)}, u32[]{:S(2)}) collective-permute-start(f32[64,128]{1,0:T(8,128)S(1)} %get-tuple-element.153), channel_id=1, source_target_pairs={{0,28},{4,8},{8,4},{12,16},{16,12},{20,24},{24,20},{28,0},{1,29},{... | collective-permute-start | bytes 98312 | tf_op jit(solution)/shard_map/ppermute | solution.py:492
  22.5 4.1 %collective-permute-start.9 = (f32[64,128]{1,0:T(8,128)S(1)}, f32[64,128]{1,0:T(8,128)S(1)}, u32[]{:S(2)}, u32[]{:S(2)}) collective-permute-start(f32[64,128]{1,0:T(8,128)S(1)} %get-tuple-element.151), channel_id=1, source_target_pairs={{0,16},{4,20},{8,24},{12,28},{16,0},{20,4},{24,8},{28,12},{1,17},{... | collective-permute-start | bytes 98312 | tf_op jit(solution)/shard_map/ppermute | solution.py:492
  24.0 2.6 %copy-start = (f32[2,8,1024]{2,1,0:T(8,128)S(1)}, f32[2,8,1024]{2,1,0:T(8,128)}, u32[]{:S(2)}) copy-start(f32[2,8,1024]{2,1,0:T(8,128)} %param.11) | copy-start | bytes 196612
  28.2 6.4 %collective-permute-start.12 = (f32[64,128]{1,0:T(8,128)S(1)}, f32[64,128]{1,0:T(8,128)S(1)}, u32[]{:S(2)}, u32[]{:S(2)}) collective-permute-start(f32[64,128]{1,0:T(8,128)S(1)} %get-tuple-element.166), channel_id=1, source_target_pairs={{0,16},{4,20},{8,24},{12,28},{16,0},{20,4},{24,8},{28,12},{1,17},{... | collective-permute-start | bytes 98312 | tf_op jit(solution)/shard_map/ppermute | solution.py:492
  29.5 5.2 %collective-permute-start.13 = (f32[64,128]{1,0:T(8,128)S(1)}, f32[64,128]{1,0:T(8,128)S(1)}, u32[]{:S(2)}, u32[]{:S(2)}) collective-permute-start(f32[64,128]{1,0:T(8,128)S(1)} %get-tuple-element.167), channel_id=1, source_target_pairs={{0,4},{4,0},{8,12},{12,8},{16,20},{20,16},{24,28},{28,24},{1,5},{5... | collective-permute-start | bytes 98312 | tf_op jit(solution)/shard_map/ppermute | solution.py:492
  29.5 5.2 %collective-permute-start.14 = (f32[64,128]{1,0:T(8,128)S(1)}, f32[64,128]{1,0:T(8,128)S(1)}, u32[]{:S(2)}, u32[]{:S(2)}) collective-permute-start(f32[64,128]{1,0:T(8,128)S(1)} %get-tuple-element.168), channel_id=1, source_target_pairs={{0,28},{4,8},{8,4},{12,16},{16,12},{20,24},{24,20},{28,0},{1,29},{... | collective-permute-start | bytes 98312 | tf_op jit(solution)/shard_map/ppermute | solution.py:492
  39.6 2.0 %collective-permute-start.16 = (f32[200,640]{1,0:T(8,128)S(1)}, f32[200,640]{1,0:T(8,128)S(1)}, u32[]{:S(2)}, u32[]{:S(2)}) collective-permute-start(f32[200,640]{1,0:T(8,128)S(1)} %get-tuple-element.181), channel_id=1, source_target_pairs={{0,4},{4,0},{8,12},{12,8},{16,20},{20,16},{24,28},{28,24},{1,5},{5... | collective-permute-start | bytes 1536008 | tf_op jit(solution)/shard_map/ppermute | solution.py:404
  39.7 3.2 %collective-permute-start.15 = (f32[200,640]{1,0:T(8,128)S(1)}, f32[200,640]{1,0:T(8,128)S(1)}, u32[]{:S(2)}, u32[]{:S(2)}) collective-permute-start(f32[200,640]{1,0:T(8,128)S(1)} %get-tuple-element.179), channel_id=1, source_target_pairs={{0,4},{4,0},{8,12},{12,8},{16,20},{20,16},{24,28},{28,24},{1,5},{5... | collective-permute-start | bytes 1536008 | tf_op jit(solution)/shard_map/ppermute | solution.py:404
  42.0 6.4 %collective-permute-start.17 = (f16[200,640]{1,0:T(8,128)(2,1)S(1)}, f16[200,640]{1,0:T(8,128)(2,1)S(1)}, u32[]{:S(2)}, u32[]{:S(2)}) collective-permute-start(f16[200,640]{1,0:T(8,128)(2,1)S(1)} %select_convert_fusion.5), channel_id=1, source_target_pairs={{0,8},{4,20},{8,0},{12,28},{16,24},{20,4},{24,16},{28,12},{1,9},{5... | collective-permute-start | bytes 768008 | tf_op jit(solution)/shard_map/ppermute | solution.py:404
  43.3 7.9 %collective-permute-start.19 = (f16[200,640]{1,0:T(8,128)(2,1)S(1)}, f16[200,640]{1,0:T(8,128)(2,1)S(1)}, u32[]{:S(2)}, u32[]{:S(2)}) collective-permute-start(f16[200,640]{1,0:T(8,128)(2,1)S(1)} %select_convert_fusion.4), channel_id=1, source_target_pairs={{0,8},{4,20},{8,0},{12,28},{16,24},{20,4},{24,16},{28,12},{1,9},{5... | collective-permute-start | bytes 768008 | tf_op jit(solution)/shard_map/ppermute | solution.py:404
  44.5 5.7 %collective-permute-start.20 = (f32[16,128]{1,0:T(8,128)S(1)}, f32[16,128]{1,0:T(8,128)S(1)}, u32[]{:S(2)}, u32[]{:S(2)}) collective-permute-start(f32[16,128]{1,0:T(8,128)S(1)} %get-tuple-element.193), channel_id=1, source_target_pairs={{0,16},{4,20},{8,24},{12,28},{16,0},{20,4},{24,8},{28,12},{1,17},{... | collective-permute-start | bytes 24584 | tf_op jit(solution)/shard_map/ppermute | solution.py:492
  45.3 4.9 %collective-permute-start.21 = (f32[16,128]{1,0:T(8,128)S(1)}, f32[16,128]{1,0:T(8,128)S(1)}, u32[]{:S(2)}, u32[]{:S(2)}) collective-permute-start(f32[16,128]{1,0:T(8,128)S(1)} %get-tuple-element.194), channel_id=1, source_target_pairs={{0,4},{4,0},{8,12},{12,8},{16,20},{20,16},{24,28},{28,24},{1,5},{5... | collective-permute-start | bytes 24584 | tf_op jit(solution)/shard_map/ppermute | solution.py:492
  45.3 4.9 %collective-permute-start.22 = (f32[16,128]{1,0:T(8,128)S(1)}, f32[16,128]{1,0:T(8,128)S(1)}, u32[]{:S(2)}, u32[]{:S(2)}) collective-permute-start(f32[16,128]{1,0:T(8,128)S(1)} %get-tuple-element.195), channel_id=1, source_target_pairs={{0,28},{4,8},{8,4},{12,16},{16,12},{20,24},{24,20},{28,0},{1,29},{... | collective-permute-start | bytes 24584 | tf_op jit(solution)/shard_map/ppermute | solution.py:492
  49.3 6.4 %collective-permute-start.18 = (f16[200,640]{1,0:T(8,128)(2,1)S(1)}, f16[200,640]{1,0:T(8,128)(2,1)S(1)}, u32[]{:S(2)}, u32[]{:S(2)}) collective-permute-start(f16[200,640]{1,0:T(8,128)(2,1)S(1)} %select_convert_fusion.3), channel_id=1, source_target_pairs={{0,16},{4,12},{8,24},{12,4},{16,0},{20,28},{24,8},{28,20},{1,17},{... | collective-permute-start | bytes 768008 | tf_op jit(solution)/shard_map/ppermute | solution.py:404
  51.6 6.8 %collective-permute-start.23 = (f16[200,640]{1,0:T(8,128)(2,1)S(1)}, f16[200,640]{1,0:T(8,128)(2,1)S(1)}, u32[]{:S(2)}, u32[]{:S(2)}) collective-permute-start(f16[200,640]{1,0:T(8,128)(2,1)S(1)} %select_convert_fusion.2), channel_id=1, source_target_pairs={{0,16},{4,12},{8,24},{12,4},{16,0},{20,28},{24,8},{28,20},{1,17},{... | collective-permute-start | bytes 768008 | tf_op jit(solution)/shard_map/ppermute | solution.py:404
  56.7 2.3 %collective-permute-start.24 = (f16[200,640]{1,0:T(8,128)(2,1)S(1)}, f16[200,640]{1,0:T(8,128)(2,1)S(1)}, u32[]{:S(2)}, u32[]{:S(2)}) collective-permute-start(f16[200,640]{1,0:T(8,128)(2,1)S(1)} %select_convert_fusion.1), channel_id=1, source_target_pairs={{0,4},{4,0},{8,12},{12,8},{16,20},{20,16},{24,28},{28,24},{1,5},{5... | collective-permute-start | bytes 768008 | tf_op jit(solution)/shard_map/ppermute | solution.py:404
  58.9 1.8 %collective-permute-start.25 = (f16[200,640]{1,0:T(8,128)(2,1)S(1)}, f16[200,640]{1,0:T(8,128)(2,1)S(1)}, u32[]{:S(2)}, u32[]{:S(2)}) collective-permute-start(f16[200,640]{1,0:T(8,128)(2,1)S(1)} %get-tuple-element.265), channel_id=1, source_target_pairs={{0,4},{4,0},{8,12},{12,8},{16,20},{20,16},{24,28},{28,24},{1,5},{5... | collective-permute-start | bytes 768008 | tf_op jit(solution)/shard_map/ppermute | solution.py:404
